TPU v7x, 512 devices: a whole 4x4x16 slice. The times are simulated.
512 devices in a mesh: ent: 128 (over z, y, core), rep: 4 (over x).
Axes of the slice: x: 4, y: 4, z: 16, core: 2. Of those that a mesh axis runs over, the one named last changes fastest.
Arguments:
- entity_table: float32 [65536, 400], P('ent'), may hold values from -1.8 to 1.8
- adagrad_state: float32 [65536], P('ent'), may hold values from 0.05 to 0.5
- head_owner: int32 [65536, 1], P(('ent', 'rep')), may hold values from 0 to 127; in each aligned block of 128 rows (0 to 127, 128 to 255, ...) at most 2 rows name the same one
- head_row: int32 [65536], P(('ent', 'rep')), may hold values from 0 to 511
- relation_ids: int32 [65536], P(('ent', 'rep')), may hold values from 0 to 63
- tail_owner: int32 [65536, 1], P(('ent', 'rep')), may hold values from 0 to 127; in each aligned block of 128 rows (0 to 127, 128 to 255, ...) at most 2 rows name the same one
- tail_row: int32 [65536], P(('ent', 'rep')), may hold values from 0 to 511
- neg_rows: int32 [512], P('ent'), may hold values from 0 to 511
- relations: float32 [64, 400], replicated, may hold values from -6 to 6
Outputs:
- table_new: float32 [65536, 400], P('ent')
- state_new: float32 [65536], P('ent')
Inputs may be any that keep to these rules, and one draw needn't show every extreme that they name: `head_owner`: among the 128 rows of one device no owner is named more than 2 times; in some device one owner is named exactly 2 times. `tail_owner`: among the 128 rows of one device no owner is named more than 2 times; in some device one owner is named exactly 2 times.
All inputs are finite; a program needn't handle non-finite values.
Results may differ from a plain program's by a relative error of at most 0.0001.
Values sent between devices are 32-bit elements; how exact they have to be, the bound alone decides.
No kernel may reach another device: no remote copies, remote signals or barrier semaphores. Data moves between devices by JAX's collectives and lax.ppermute only.
A program may use at most 64 MiB of HBM per device.

v0:
```python
import math

import jax
import jax.numpy as jnp
from jax import lax
from jax.sharding import PartitionSpec as P

learn_rate = 0.1


def complex_mul(left_re, left_im, right_re, right_im):
    return (left_re * right_re - left_im * right_im, left_re * right_im + left_im * right_re)


def edge_terms(heads, tails, rel_vecs, negatives):
    half = heads.shape[1] // 2
    head_re, head_im = (heads[:, :half], heads[:, half:])
    tail_re, tail_im = (tails[:, :half], tails[:, half:])
    rel_re, rel_im = (rel_vecs[:, :half], rel_vecs[:, half:])
    query = jnp.concatenate(complex_mul(head_re, head_im, rel_re, rel_im), 1)
    probe = jnp.concatenate(complex_mul(rel_re, -rel_im, tail_re, tail_im), 1)
    pos_score = jnp.sum(heads * probe, 1)
    dims = (((1,), (1,)), ((), ()))
    tail_scores = lax.dot_general(query, negatives, dims, precision=lax.Precision.HIGHEST)
    head_scores = lax.dot_general(probe, negatives, dims, precision=lax.Precision.HIGHEST)
    neg_weight = 1.0 / math.sqrt(negatives.shape[0])
    tail_coef = jax.nn.sigmoid(tail_scores) * neg_weight
    head_coef = jax.nn.sigmoid(head_scores) * neg_weight
    pos_coef = -jax.nn.sigmoid(-pos_score)[:, None]
    query_grad = jnp.dot(tail_coef, negatives, precision=lax.Precision.HIGHEST)
    probe_grad = jnp.dot(head_coef, negatives, precision=lax.Precision.HIGHEST)
    head_grad = pos_coef * probe + jnp.concatenate(
        complex_mul(query_grad[:, :half], query_grad[:, half:], rel_re, -rel_im), 1
    )
    tail_grad = pos_coef * query + jnp.concatenate(
        complex_mul(probe_grad[:, :half], probe_grad[:, half:], rel_re, rel_im), 1
    )
    back = (((0,), (0,)), ((), ()))
    negs_grad = lax.dot_general(tail_coef, query, back, precision=lax.Precision.HIGHEST)
    negs_grad = negs_grad + lax.dot_general(head_coef, probe, back, precision=lax.Precision.HIGHEST)
    return (head_grad, tail_grad, negs_grad)


def slot_rank(owners, owners_count):
    member = (owners[:, None] == jnp.arange(owners_count, dtype=jnp.int32)[None, :]).astype(
        jnp.int32
    )
    return jnp.sum(jnp.cumsum(member, 0) * member, 1) - 1


def fetch_single(asks, entity_table):
    received = lax.all_to_all(asks, "ent", split_axis=0, concat_axis=0, tiled=True)
    found = entity_table[received]
    returned = lax.all_to_all(found, "ent", split_axis=0, concat_axis=0, tiled=True)
    return (returned, received)


def on_device(
    entity_table,
    adagrad_state,
    head_owner,
    head_row,
    relation_ids,
    tail_owner,
    tail_row,
    neg_rows,
    relations,
):
    owners_count = lax.axis_size("ent")
    edge_count = head_row.shape[0]
    capacity = max(2, 3 * edge_count // (2 * owners_count))
    width = entity_table.shape[1]
    head_dest = head_owner[:, 0]
    tail_dest = tail_owner[:, 0]
    head_slot = slot_rank(head_dest, owners_count)
    tail_slot = slot_rank(tail_dest, owners_count)
    head_asks = (
        jnp.zeros((owners_count, capacity), jnp.int32).at[head_dest, head_slot].set(head_row)
    )
    tail_asks = (
        jnp.zeros((owners_count, capacity), jnp.int32).at[tail_dest, tail_slot].set(tail_row)
    )
    head_back, head_recv = fetch_single(head_asks, entity_table)
    tail_back, tail_recv = fetch_single(tail_asks, entity_table)
    negatives = lax.all_gather(entity_table[neg_rows], "ent", axis=0, tiled=True)
    heads = head_back[head_dest, head_slot]
    tails = tail_back[tail_dest, tail_slot]
    relation_pick = (
        relation_ids[:, None] == jnp.arange(relations.shape[0], dtype=jnp.int32)[None, :]
    ).astype(jnp.float32)
    rel_vecs = jnp.dot(relation_pick, relations, precision=lax.Precision.HIGHEST)
    head_grad, tail_grad, negs_grad = edge_terms(heads, tails, rel_vecs, negatives)
    head_buffer = (
        jnp.zeros((owners_count, capacity, width), jnp.float32)
        .at[head_dest, head_slot]
        .set(head_grad)
    )
    tail_buffer = (
        jnp.zeros((owners_count, capacity, width), jnp.float32)
        .at[tail_dest, tail_slot]
        .set(tail_grad)
    )
    head_home, tail_home = (
        lax.all_to_all(head_buffer, "ent", split_axis=0, concat_axis=0, tiled=True),
        lax.all_to_all(tail_buffer, "ent", split_axis=0, concat_axis=0, tiled=True),
    )
    grad_table = (
        jnp.zeros_like(entity_table).at[head_recv].add(head_home).at[tail_recv].add(tail_home)
    )
    owned_negs = lax.psum_scatter(negs_grad, "ent", scatter_dimension=0, tiled=True)
    grad_table = grad_table.at[neg_rows].add(owned_negs)
    total_grad = lax.psum(grad_table, "rep")
    state_new = adagrad_state + jnp.mean(total_grad * total_grad, 1)
    table_new = entity_table - learn_rate * total_grad / jnp.sqrt(state_new)[:, None]
    return (table_new, state_new)


def solution(mesh):
    placed = (
        P("ent", None),
        P("ent"),
        P(("ent", "rep"), None),
        P(("ent", "rep")),
        P(("ent", "rep")),
        P(("ent", "rep"), None),
        P(("ent", "rep")),
        P("ent"),
        P(),
    )
    return jax.shard_map(
        on_device, mesh=mesh, in_specs=placed, out_specs=(P("ent", None), P("ent")), check_vma=False
    )
```

profile of v0, /device:TPU:24, one launch (start us, length us, event | category | flops | bytes accessed | tf_op | source)
XLA Modules:
  0.0 747.0 jit_solution(8857684919178705889)
XLA Ops:
  8.6 6.4 scatter_fusion.1
  15.7 19.3 %all-to-all-start.2 = ((s32[128,1,2]{2,1,0:T(1,128)}), s32[128,1,2]{2,1,0:T(1,128)S(1)}, u32[]{:S(2)}, u32[]{:S(2)}) async-start(s32[128,1,2]{2,1,0:T(1,128)} %copy.35), calls=%async_computation.2 | async-start | bytes 131072 | tf_op jit(solution)/shard_map/all_to_all | solution.py:52
  37.1 6.4 scatter_fusion
  44.2 4.5 all-to-all-done.2
  48.7 11.6 %all-to-all-start = ((s32[128,1,2]{2,1,0:T(1,128)}), s32[128,1,2]{2,1,0:T(1,128)S(1)}, u32[]{:S(2)}, u32[]{:S(2)}) async-start(s32[128,1,2]{2,1,0:T(1,128)} %copy.33), calls=%async_computation | async-start | bytes 131072 | tf_op jit(solution)/shard_map/all_to_all | solution.py:52
  62.6 11.5 %all-to-all-done = s32[128,1,2]{2,1,0:T(1,128)S(1)} async-done(((s32[128,1,2]{2,1,0:T(1,128)}), s32[128,1,2]{2,1,0:T(1,128)S(1)}, u32[]{:S(2)}, u32[]{:S(2)}) %all-to-all-start) | async-done | bytes 1056 | tf_op jit(solution)/shard_map/all_to_all | solution.py:52
  74.1 6.8 all-to-all-start.3
  83.2 31.0 %all-to-all-done.3 = f32[128,2,400]{2,1,0:T(2,128)S(1)} async-done(((f32[128,2,400]{2,1,0:T(2,128)}), f32[128,2,400]{2,1,0:T(2,128)S(1)}, u32[]{:S(2)}, u32[]{:S(2)}) %all-to-all-start.3) | async-done | bytes 409632 | tf_op jit(solution)/shard_map/all_to_all | solution.py:54
  114.2 6.8 all-to-all-start.1
  121.6 127.4 %all-gather.1 = f32[128,4,400]{2,1,0:T(4,128)} all-gather(f32[1,4,400]{2,1,0:T(4,128)S(1)} %bitcast.61), channel_id=2, replica_groups=mesh['ent'=128,'rep'=4] {'ent'}, dimensions={0}, use_global_device_ids=true | all-gather | bytes 825600 | tf_op jit(solution)/shard_map/all_gather | solution.py:85
  248.9 1.6 reshape.205
  251.0 1.8 gather_fusion.3
  254.7 1.8 gather_fusion.1
  257.7 1.3 fusion.7
  259.0 1.8 fusion.30
  260.9 1.3 fusion.4
  262.2 1.8 fusion.29
  265.2 16.1 %scatter_fusion.2 = f32[128,2,400]{2,1,0:T(2,128)} fusion(f32[128,2,400]{2,1,0:T(2,128)} %broadcast.142.clone, s32[128]{0:T(128)S(1)} %get-tuple-element.10, f32[128,400]{1,0:T(8,128)S(1)} %copy.43), kind=kCustom, calls=%fused_computation.7 | custom fusion | bytes 615424 | tf_op jit(solution)/shard_map/scatter | solution.py:96
  281.3 13.7 %all-to-all-start.4 = ((f32[128,2,400]{2,1,0:T(2,128)}), f32[128,2,400]{2,1,0:T(2,128)S(1)}, u32[]{:S(2)}, u32[]{:S(2)}) async-start(f32[128,2,400]{2,1,0:T(2,128)} %scatter_fusion.2), calls=%async_computation.4 | async-start | bytes 1048576 | tf_op jit(solution)/shard_map/all_to_all | solution.py:104
  296.1 15.1 %scatter_fusion.3 = f32[128,2,400]{2,1,0:T(2,128)} fusion(f32[128,2,400]{2,1,0:T(2,128)} %broadcast.142.clone.1, s32[128]{0:T(128)S(1)} %get-tuple-element.8, f32[128,400]{1,0:T(8,128)S(1)} %copy.44), kind=kCustom, calls=%fused_computation.9 | custom fusion | bytes 615424 | tf_op jit(solution)/shard_map/scatter | solution.py:101
  311.2 16.8 %all-to-all-done.4 = f32[128,2,400]{2,1,0:T(2,128)S(1)} async-done(((f32[128,2,400]{2,1,0:T(2,128)}), f32[128,2,400]{2,1,0:T(2,128)S(1)}, u32[]{:S(2)}, u32[]{:S(2)}) %all-to-all-start.4) | async-done | bytes 409632 | tf_op jit(solution)/shard_map/all_to_all | solution.py:104
  328.0 7.0 all-to-all-start.5
  336.1 2.1 convolution_add_fusion
  338.3 1.3 dynamic-slice
  340.6 2.3 scatter_custom_fusion.3
  342.9 25.1 %all-to-all-done.5 = f32[128,2,400]{2,1,0:T(2,128)S(1)} async-done(((f32[128,2,400]{2,1,0:T(2,128)}), f32[128,2,400]{2,1,0:T(2,128)S(1)}, u32[]{:S(2)}, u32[]{:S(2)}) %all-to-all-start.5) | async-done | bytes 409632 | tf_op jit(solution)/shard_map/all_to_all | solution.py:105
  368.3 2.5 scatter_fusion.4
  370.8 304.4 %all-reduce.6.cloned.1.call-done = f32[512,400]{1,0:T(8,128)} async-done(((f32[512,400]{1,0:T(8,128)}), f32[512,400]{1,0:T(8,128)}) %all-reduce.6.cloned.1.call-update) | async-done | bytes 819216
  675.3 1.2 scatter_custom_fusion.6
  677.6 59.2 %all-reduce.4.cloned.1.call-done = f32[512,400]{1,0:T(8,128)} async-done(((f32[512,400]{1,0:T(8,128)}), f32[512,400]{1,0:T(8,128)}) %all-reduce.4.cloned.1.call-update) | async-done | bytes 819216 | tf_op jit(solution)/shard_map/psum | solution.py:112
  736.7 1.5 multiply_reduce_fusion
  739.0 1.2 copy.46
  (82 shorter events, 19.6 us)
Async XLA Ops:
  7.2 243.4 %copy-start = (f32[64,400]{1,0:T(8,128)S(1)}, f32[64,400]{1,0:T(8,128)}, u32[]{:S(2)}) copy-start(f32[64,400]{1,0:T(8,128)} %param.17) | copy-start | bytes 307204
  7.2 0.7 copy-start.9
  8.0 0.7 copy-start.12
  8.1 28.0 %copy-start.7 = (f32[512,400]{0,1:T(8,128)S(1)}, f32[512,400]{0,1:T(8,128)}, u32[]{:S(2)}) copy-start(f32[512,400]{0,1:T(8,128)} %param.9) | copy-start | bytes 2457604
  15.7 33.0 %all-to-all-start.2 = ((s32[128,1,2]{2,1,0:T(1,128)}), s32[128,1,2]{2,1,0:T(1,128)S(1)}, u32[]{:S(2)}, u32[]{:S(2)}) async-start(s32[128,1,2]{2,1,0:T(1,128)} %copy.35), calls=%async_computation.2 | async-start | bytes 131072 | tf_op jit(solution)/shard_map/all_to_all | solution.py:52
  35.0 0.7 copy-start.10
  36.5 0.7 copy-start.13
  48.7 25.4 %all-to-all-start = ((s32[128,1,2]{2,1,0:T(1,128)}), s32[128,1,2]{2,1,0:T(1,128)S(1)}, u32[]{:S(2)}, u32[]{:S(2)}) async-start(s32[128,1,2]{2,1,0:T(1,128)} %copy.33), calls=%async_computation | async-start | bytes 131072 | tf_op jit(solution)/shard_map/all_to_all | solution.py:52
  74.1 40.1 %all-to-all-start.3 = ((f32[128,2,400]{2,1,0:T(2,128)}), f32[128,2,400]{2,1,0:T(2,128)S(1)}, u32[]{:S(2)}, u32[]{:S(2)}) async-start(f32[128,2,400]{2,1,0:T(2,128)} %reshape.128), calls=%async_computation.3 | async-start | bytes 1048576 | tf_op jit(solution)/shard_map/all_to_all | solution.py:54
  83.2 37.7 %copy-start.15 = (s32[4]{0:T(128)S(1)}, s32[4]{0:T(128)}, u32[]{:S(2)}) copy-start(s32[4]{0:T(128)} %param.16) | copy-start | bytes 52
  114.2 140.5 %all-to-all-start.1 = ((f32[128,2,400]{2,1,0:T(2,128)}), f32[128,2,400]{2,1,0:T(2,128)S(1)}, u32[]{:S(2)}, u32[]{:S(2)}) async-start(f32[128,2,400]{2,1,0:T(2,128)} %reshape.114), calls=%async_computation.1 | async-start | bytes 1048576 | tf_op jit(solution)/shard_map/all_to_all | solution.py:54
  248.9 1.6 copy-start.14
  256.5 1.1 copy-start.8
  257.6 6.4 copy-start.3
  257.6 6.4 copy-start.5
  281.3 46.7 %all-to-all-start.4 = ((f32[128,2,400]{2,1,0:T(2,128)}), f32[128,2,400]{2,1,0:T(2,128)S(1)}, u32[]{:S(2)}, u32[]{:S(2)}) async-start(f32[128,2,400]{2,1,0:T(2,128)} %scatter_fusion.2), calls=%async_computation.4 | async-start | bytes 1048576 | tf_op jit(solution)/shard_map/all_to_all | solution.py:104
  311.2 23.8 %copy-start.4 = (f32[128,200]{0,1:T(8,128)S(1)}, f32[128,200]{0,1:T(8,128)}, u32[]{:S(2)}) copy-start(f32[128,200]{0,1:T(8,128)} %copy-done.3) | copy-start | bytes 307204
  311.2 23.8 %copy-start.6 = (f32[128,200]{0,1:T(8,128)S(1)}, f32[128,200]{0,1:T(8,128)}, u32[]{:S(2)}) copy-start(f32[128,200]{0,1:T(8,128)} %copy-done.5) | copy-start | bytes 307204
  328.0 40.0 %all-to-all-start.5 = ((f32[128,2,400]{2,1,0:T(2,128)}), f32[128,2,400]{2,1,0:T(2,128)S(1)}, u32[]{:S(2)}, u32[]{:S(2)}) async-start(f32[128,2,400]{2,1,0:T(2,128)} %scatter_fusion.3), calls=%async_computation.5 | async-start | bytes 1048576 | tf_op jit(solution)/shard_map/all_to_all | solution.py:105
  335.0 340.3 %all-reduce.6.cloned.1.call-start = ((), (), s32[]{:S(2)}) async-start(), calls=%async_computation.7 | async-start | bytes 2097152
  338.2 398.5 %all-reduce.4.cloned.1.call-start = ((), (), s32[]{:S(2)}) async-start(), calls=%async_computation.6 | async-start | bytes 2097152 | tf_op jit(solution)/shard_map/psum | solution.py:112
  676.5 1.0 copy-start.1
  677.5 60.6 %copy-start.11 = (f32[512]{0:T(512)S(1)}, f32[512]{0:T(512)}, u32[]{:S(2)}) copy-start(f32[512]{0:T(512)} %param.10) | copy-start | bytes 6148
  736.7 2.1 copy-start.2
Sparse Core Ops, SparseCore 0:
  339.3 335.9 all-reduce.5
  677.8 58.9 all-reduce.3
where the time goes:
time: 749 us; the launch traced here: 747 us
  waiting for transfers between devices  452 us (60%)
  blocking collectives  127 us (17%)
  local copies, waits for them, and re-layouts  67.6 us (9%)
  starting transfers between devices  65.3 us (9%)
  between operations  15.2 us (2%)
  matrix products  9.73 us (1%)
  other arithmetic  9.47 us (1%)
    unnamed x3, waiting for transfers between devices  304 us
    all_gather x1, blocking collectives, on_device(): lax.all_gather(entity_table[neg_rows], 'ent', axis=0, tiled=True)  127 us
    psum x1, waiting for transfers between devices, on_device(): total_grad = lax.psum(grad_table, 'rep')  59.2 us
    all_to_all x2, waiting for transfers between devices, fetch_single(): lax.all_to_all(found, 'ent', split_axis=0, concat_axis=0, tiled=True)  31 us
    all_to_all x2, starting transfers between devices, fetch_single(): lax.all_to_all(asks, 'ent', split_axis=0, concat_axis=0, tiled=True)  30.9 us
    all_to_all x1, waiting for transfers between devices, on_device(): lax.all_to_all(tail_buffer, 'ent', split_axis=0, concat_axis=0, tiled=True)  25.1 us
    all_to_all x1, waiting for transfers between devices, on_device(): lax.all_to_all(head_buffer, 'ent', split_axis=0, concat_axis=0, tiled=True)  16.8 us
    scatter x1, local copies, waits for them, and re-layouts, on_device(): head_buffer = jnp.zeros((owners_count, capacity, width), jnp.float32).at[...  16.1 us
  transfers between devices with their start and end apart: 8, of which 7 were waited for; matrix products, arithmetic and copies ran while one was open for 6% of the time, Pallas kernels for 0%

commit v1 on v0

v1 whole, which is shorter than its diff:
```python
import math

import jax
import jax.numpy as jnp
from jax import lax
from jax.experimental import pallas as pl
from jax.experimental.pallas import tpu as pltpu
from jax.sharding import PartitionSpec as P

learn_rate = 0.1

LANE = 128
f32 = jnp.float32
bf16 = jnp.bfloat16
NN = (((1,), (0,)), ((), ()))
NT = (((1,), (1,)), ((), ()))
TN = (((0,), (0,)), ((), ()))
TILES1 = 4
TILES2 = 13
TILES3 = 16


def dot(a, b, dims):
    return lax.dot_general(a, b, dims, preferred_element_type=f32)


def parts(x, count):
    out = []
    for _ in range(count):
        head = x.astype(bf16)
        out.append(head)
        x = x - head.astype(f32)
    return out


def pick(onehot, pieces, dims):
    total = dot(onehot, pieces[0], dims)
    for piece in pieces[1:]:
        total = total + dot(onehot, piece, dims)
    return total


def dot3(a, b, dims):
    a0, a1 = parts(a, 2)
    b0, b1 = parts(b, 2)
    return dot(a0, b0, dims) + (dot(a0, b1, dims) + dot(a1, b0, dims))


def lanes(shape):
    return lax.broadcasted_iota(jnp.int32, shape, len(shape) - 1)


def cmul(a, b):
    return (a[0] * b[0] - a[1] * b[1], a[0] * b[1] + a[1] * b[0])


def conj(a):
    return (a[0], -a[1])


def sigmoid(x):
    return 1.0 / (1.0 + jnp.exp(-x))


def column(tile, lane):
    return jnp.sum(jnp.where(lanes(tile.shape) == lane, tile, 0.0), 1, keepdims=True)


def pack(ref, tiles, halves):
    n = halves[0].shape[0]
    at = lanes((n, LANE))
    tail = jnp.zeros((n, LANE), f32)
    for i, half in enumerate(halves):
        ref[pl.ds(i, n, stride=tiles), :] = half[:, :LANE]
        rest = half[:, LANE:]
        shift = (8 * i - 64) % LANE
        moved = pltpu.roll(rest, shift, 1) if shift else rest
        tail = jnp.where((at >= 8 * i) & (at < 8 * i + 8), moved, tail)
    for i in range(0, len(halves), 2):
        low, high = halves[i][:, LANE:], halves[i + 1][:, LANE:]
        ref[pl.ds(len(halves) + i // 2, n, stride=tiles), :] = jnp.where(
            at < 64, low, pltpu.roll(high, 64, 1)
        )
    ref[pl.ds(len(halves) * 3 // 2, n, stride=tiles), :] = tail


def unpack(ref, tiles, count, n):
    at = lanes((n, LANE))
    tail = ref[pl.ds(count * 3 // 2, n, stride=tiles), :]
    out = []
    for i in range(count):
        full = ref[pl.ds(i, n, stride=tiles), :]
        pair = ref[pl.ds(count + i // 2, n, stride=tiles), :]
        if i % 2:
            pair = pltpu.roll(pair, 64, 1)
        shift = (64 - 8 * i) % LANE
        moved = pltpu.roll(tail, shift, 1) if shift else tail
        rest = jnp.where(at < 64, pair, jnp.where(at < 72, moved, 0.0))
        out.append(jnp.concatenate([full, rest], 1))
    return out


def ask_kernel(neg_at, ints, table_t, send, head_edge, tail_edge):
    n = LANE
    vals = ints[...].astype(f32)
    sub = lax.broadcasted_iota(jnp.int32, (n, n), 0)
    lane = lanes((n, n))

    def row(i):
        return jnp.broadcast_to(vals[i : i + 1, :], (n, n))

    head_owner, head_row, rel, tail_owner, tail_row = (row(i) for i in range(5))
    owner_id = sub.astype(f32)
    columns = []

    def slots(owner, named):
        owner_c = owner.T
        rank = jnp.sum(jnp.where((owner == owner_c) & (sub < lane), 1.0, 0.0), 0, keepdims=True)
        rank = jnp.broadcast_to(rank, (n, n))
        edges = []
        for s in range(2):
            here = (owner == owner_id) & (rank == float(s))
            columns.append(jnp.sum(jnp.where(here, named + 1.0, 0.0), 1, keepdims=True) - 1.0)
            columns.append(jnp.sum(jnp.where(here, rel, 0.0), 1, keepdims=True))
            edges.append(
                jnp.sum(jnp.where(here, lane.astype(f32) + 1.0, 0.0), 1, keepdims=True) - 1.0
            )
        return edges

    edges = slots(head_owner, head_row)
    head_edge[...] = jnp.where(lane == 0, edges[0], jnp.where(lane == 1, edges[1], -1.0))
    edges = slots(tail_owner, tail_row)
    both = jnp.where(lane == 0, edges[0], jnp.where(lane == 1, edges[1], -1.0)).T
    tail_edge[...] = jnp.where(both[:8, :] < 0.0, -2.0, both[:8, :])

    hot = jnp.where(lanes((8, 512)) == neg_at[0], 1.0, 0.0).astype(bf16)
    re = pick(hot, parts(table_t[0:200, :], 3), NT)[0:1, :]
    im = pick(hot, parts(table_t[200:400, :], 3), NT)[0:1, :]

    def wide(x):
        return jnp.broadcast_to(x, (n, x.shape[1]))

    send[pl.ds(0, n, stride=TILES1), :] = wide(re[:, :LANE])
    send[pl.ds(2, n, stride=TILES1), :] = wide(im[:, :LANE])
    pad = jnp.zeros((1, 56), f32)
    tile = wide(jnp.concatenate([re[:, LANE:], pad], 1))
    for i, col in enumerate(columns):
        tile = jnp.where(lane == 72 + i, col, tile)
    send[pl.ds(1, n, stride=TILES1), :] = tile
    send[pl.ds(3, n, stride=TILES1), :] = wide(jnp.concatenate([im[:, LANE:], pad], 1))


def table_halves(table_t):
    pad = jnp.zeros((56, table_t.shape[1]), f32)
    return [jnp.concatenate([table_t[i : i + 200, :], pad], 0) for i in (0, 200)]


def rel_vectors(tile, slot, rel_ref):
    ids = column(tile, 72 + 2 * slot + 1)
    hot = jnp.where(lanes((tile.shape[0], 64)).astype(f32) == ids, 1.0, 0.0).astype(bf16)
    both = pick(hot, parts(rel_ref[...], 3), NN)
    return (both[:, :256], both[:, 256:])


def fetch_kernel(recv, table_t, rel_ref, send, rows):
    n = LANE
    tile = recv[pl.ds(1, n, stride=TILES1), :]
    pieces = [parts(half, 3) for half in table_halves(table_t)]
    halves = []
    for s in range(4):
        at = column(tile, 72 + 2 * s)
        hot = jnp.where(lanes((n, 512)).astype(f32) == at, 1.0, 0.0).astype(bf16)
        vec = tuple(pick(hot, p, NT) for p in pieces)
        if s < 2:
            vec = cmul(vec, rel_vectors(tile, s, rel_ref))
        halves += vec
        rows[s * n : (s + 1) * n, 0:256] = vec[0]
        rows[s * n : (s + 1) * n, 256:512] = vec[1]
    pack(send, TILES2, halves)


def negatives_kernel(recv, rows, rel_ref, neg0, neg1, neg2, neg3, near, far, rels, out0, out1, out2, out3):
    n = LANE
    tile = recv[pl.ds(1, n, stride=TILES1), :]
    negs = []
    keep = lanes((n, LANE)) < 72
    for ref in (neg0, neg1, neg2, neg3):
        got = [ref[pl.ds(i, n, stride=TILES1), :] for i in range(4)]
        got[1] = jnp.where(keep, got[1], 0.0)
        negs.append(jnp.concatenate(got, 1))
    negs = jnp.concatenate(negs, 0)
    weight = 1.0 / math.sqrt(512.0)
    total = None
    for side in range(2):
        x, rel, valid = [], [], []
        for s in (2 * side, 2 * side + 1):
            vec = (rows[s * n : (s + 1) * n, 0:256], rows[s * n : (s + 1) * n, 256:512])
            rv = rel_vectors(tile, s, rel_ref)
            if side:
                vec = cmul(conj(rv), vec)
            x.append(jnp.concatenate(vec, 1))
            rel.append(rv)
            valid.append(column(tile, 72 + 2 * s))
        x = jnp.concatenate(x, 0)
        valid = jnp.concatenate(valid, 0)
        scores = dot3(x, negs, NT)
        coef = jnp.where(valid >= 0.0, sigmoid(scores) * weight, 0.0)
        back = dot3(coef, negs, NN)
        for i in range(2):
            part = (back[i * n : (i + 1) * n, 0:256], back[i * n : (i + 1) * n, 256:512])
            s = 2 * side + i
            rv = rel[i]
            if side:
                part = cmul(part, rv)
                far[i * n : (i + 1) * n, 0:256] = part[0]
                far[i * n : (i + 1) * n, 256:512] = part[1]
            else:
                near[i * n : (i + 1) * n, 0:256] = part[0]
                near[i * n : (i + 1) * n, 256:512] = part[1]
                rels[i * n : (i + 1) * n, 0:256] = rv[0]
                rels[i * n : (i + 1) * n, 256:512] = rv[1]
        grad = dot3(coef, x, TN)
        total = grad if total is None else total + grad
    for i, ref in enumerate((out0, out1, out2, out3)):
        ref[...] = total[i * n : (i + 1) * n, :]


def edge_kernel(recv, head_edge, tail_edge, sum0, sum1, sum2, sum3, send):
    n = LANE
    halves = unpack(recv, TILES2, 8, n)
    head_at = jnp.concatenate([head_edge[:, 0:1], head_edge[:, 1:2]], 0)
    tail_at = jnp.concatenate([tail_edge[0:1, :], tail_edge[1:2, :]], 1)
    same = jnp.where(head_at == tail_at, 1.0, 0.0).astype(bf16)
    query = jnp.concatenate(
        [jnp.concatenate(halves[0:2], 1), jnp.concatenate(halves[2:4], 1)], 0
    )
    tails = jnp.concatenate(
        [jnp.concatenate(halves[4:6], 1), jnp.concatenate(halves[6:8], 1)], 0
    )
    met = pick(same, parts(tails, 3), NN)
    pos = jnp.sum(query * met, 1, keepdims=True)
    coef = jnp.where(head_at >= 0.0, -sigmoid(-pos), 0.0)
    to_head = coef * met
    to_tail = pick(same, parts(coef * query, 3), TN)
    neg = sum0[...] + sum1[...] + (sum2[...] + sum3[...])
    out = []
    for block in (to_head[:n], to_head[n:], to_tail[:n], to_tail[n:], neg):
        out += [block[:, :256], block[:, 256:]]
    pack(send, TILES3, out)


def scatter_kernel(neg_at, recv, asks, near, far, rels, out):
    n = LANE
    halves = unpack(recv, TILES3, 10, n)
    tile = asks[pl.ds(1, n, stride=TILES1), :]
    hots, grads = [], []
    for s in range(4):
        vec = (halves[2 * s], halves[2 * s + 1])
        base = (s % 2) * n
        other = near if s < 2 else far
        vec = tuple(
            v + other[base : base + n, i * 256 : (i + 1) * 256] for i, v in enumerate(vec)
        )
        if s < 2:
            rv = (rels[base : base + n, 0:256], rels[base : base + n, 256:512])
            vec = cmul(vec, conj(rv))
        at = column(tile, 72 + 2 * s)
        hots.append(jnp.where(lanes((n, 512)).astype(f32) == at, 1.0, 0.0).astype(bf16))
        grads.append(vec)
    hots.append(jnp.where(lanes((n, 512)) == neg_at[0], 1.0, 0.0).astype(bf16))
    grads.append((halves[8], halves[9]))
    hot = jnp.concatenate(hots, 0)
    for i in range(2):
        grad = jnp.concatenate([g[i] for g in grads], 0)
        pieces = parts(grad, 3)
        total = dot(pieces[0], hot, TN)
        for piece in pieces[1:]:
            total = total + dot(piece, hot, TN)
        for q in range(4):
            out[q, i * 200 : (i + 1) * 200, :] = total[0:200, q * n : (q + 1) * n]


def update_kernel(rep, grads, table_t, state, out):
    n = LANE
    grad = grads[0] + grads[1] + (grads[2] + grads[3])
    start = pl.multiple_of(rep[0] * n, n)
    mean = jnp.sum(grad * grad, 0, keepdims=True) * (1.0 / 400.0)
    new = state[:, pl.ds(start, n)] + mean
    out[0:400, :] = table_t[:, pl.ds(start, n)] - learn_rate * grad / jnp.sqrt(new)
    out[400:408, :] = jnp.broadcast_to(new, (8, n))


def call(kernel, outs, args, scalars=0, name=None):
    space = pl.BlockSpec(memory_space=pltpu.VMEM)
    specs = [pl.BlockSpec(memory_space=pltpu.SMEM)] * scalars + [space] * (len(args) - scalars)
    return pl.pallas_call(
        kernel,
        out_shape=[jax.ShapeDtypeStruct(s, f32) for s in outs],
        in_specs=specs,
        out_specs=[space] * len(outs),
        name=name,
    )(*args)


def exchange(x, axis, tiles):
    n = lax.axis_size(axis)
    x = x.reshape(n, 1, tiles * LANE)
    x = lax.all_to_all(x, axis, split_axis=0, concat_axis=0, tiled=True)
    return x.reshape(n * tiles, LANE)


def shift(x, by):
    n = lax.axis_size("rep")
    return lax.ppermute(x, "rep", [(i, (i + by) % n) for i in range(n)])


def on_device(
    entity_table,
    adagrad_state,
    head_owner,
    head_row,
    relation_ids,
    tail_owner,
    tail_row,
    neg_rows,
    relations,
):
    rep = lax.axis_index("rep")
    table_t = entity_table.T
    neg_at = lax.dynamic_slice(neg_rows, (rep,), (1,))
    ints = jnp.stack([head_owner[:, 0], head_row, relation_ids, tail_owner[:, 0], tail_row])
    zero = jnp.zeros((relations.shape[0], 56), f32)
    rel_wide = jnp.concatenate([relations[:, :200], zero, relations[:, 200:], zero], 1)

    n = LANE
    send1, head_edge, tail_edge = call(
        ask_kernel,
        [(n * TILES1, n), (n, n), (8, n)],
        (neg_at, ints, table_t),
        1,
        "ask",
    )
    recv1 = exchange(send1, "ent", TILES1)
    send2, rows = call(
        fetch_kernel, [(n * TILES2, n), (4 * n, 512)], (recv1, table_t, rel_wide), 0, "fetch"
    )
    recv2 = exchange(send2, "ent", TILES2)
    negs = [recv1] + [shift(recv1, -j) for j in (1, 2, 3)]
    near, far, rels, *owned = call(
        negatives_kernel,
        [(2 * n, 512)] * 3 + [(n, 512)] * 4,
        (recv1, rows, rel_wide, *negs),
        0,
        "negatives",
    )
    sums = [owned[0]] + [shift(owned[j], j) for j in (1, 2, 3)]
    (send3,) = call(
        edge_kernel, [(n * TILES3, n)], (recv2, head_edge, tail_edge, *sums), 0, "edge"
    )
    recv3 = exchange(send3, "ent", TILES3)
    (grads,) = call(
        scatter_kernel, [(4, 400, n)], (neg_at, recv3, recv1, near, far, rels), 1, "scatter"
    )
    grads = lax.all_to_all(grads, "rep", split_axis=0, concat_axis=0, tiled=True)
    (fresh,) = call(
        update_kernel,
        [(408, n)],
        (rep.reshape(1).astype(jnp.int32), grads, table_t, adagrad_state.reshape(1, 512)),
        1,
        "update",
    )
    fresh = lax.all_gather(fresh, "rep", axis=0, tiled=False)
    table_new = fresh[:, :400, :].transpose(0, 2, 1).reshape(512, 400)
    state_new = fresh[:, 400, :].reshape(512)
    return (table_new, state_new)


def solution(mesh):
    placed = (
        P("ent", None),
        P("ent"),
        P(("ent", "rep"), None),
        P(("ent", "rep")),
        P(("ent", "rep")),
        P(("ent", "rep"), None),
        P(("ent", "rep")),
        P("ent"),
        P(),
    )
    return jax.shard_map(
        on_device, mesh=mesh, in_specs=placed, out_specs=(P("ent", None), P("ent")), check_vma=False
    )
```

time: 749 us -> 224 us (0.30)
  waiting for transfers between devices: 452 us -> 37.7 us
  local copies, waits for them, and re-layouts: 67.6 us -> 6.55 us
  Pallas kernels: 0 us -> 25.4 us
  blocking collectives: 127 us -> 102 us
  starting transfers between devices: 65.3 us -> 49.2 us
  between operations: 15.2 us -> 0.78 us
  matrix products: 9.73 us -> 0 us
  other arithmetic: 9.47 us -> 0.75 us
    unnamed x3 -> x0, waiting for transfers between devices: 304 us -> none
    all_gather x1, blocking collectives: 127 us -> 14.1 us  [on_device(): fresh = lax.all_gather(fresh, 'rep', axis=0, tiled=False)]
    all_to_all x0 -> x2, blocking collectives: none -> 87.6 us  [the longest x1 70.1 us: exchange(): x = lax.all_to_all(x, axis, split_axis=0, concat_axis=0, tiled=True)]
    all_to_all x6 -> x2, waiting for transfers between devices: 88.8 us -> 21.8 us  [exchange(): x = lax.all_to_all(x, axis, split_axis=0, concat_axis=0, tiled=True)]
    psum x1 -> x0, waiting for transfers between devices: 59.2 us -> none  [on_device(): total_grad = lax.psum(grad_table, 'rep')]
    scatter x4 -> x0, local copies, waits for them, and re-layouts: 43.9 us -> none  [the longest x1 16.1 us: on_device(): head_buffer = jnp.zeros((owners_count, capacity, width), jnp.float32).at[...]
    all_to_all x6 -> x2, starting transfers between devices: 65.2 us -> 26.4 us  [exchange(): x = lax.all_to_all(x, axis, split_axis=0, concat_axis=0, tiled=True)]
    pallas_call x0 -> x6, Pallas kernels: none -> 25.4 us  [call(): pl.pallas_call(kernel, out_shape=[jax.ShapeDtypeStruct(s, f32) for s in o...]
  transfers between devices with their start and end apart: 8 -> 8, of which waited for: 7 -> 7; matrix products, arithmetic and copies ran while one was open for 6% -> 0% of each run, Pallas kernels for 0% -> 3%
where the time goes in v1:
time: 224 us; the launch traced here: 222 us
  blocking collectives  102 us (46%)
  starting transfers between devices  49.2 us (22%)
  waiting for transfers between devices  37.7 us (17%)
  Pallas kernels  25.4 us (11%)
  local copies, waits for them, and re-layouts  6.55 us (3%)
    all_to_all x1, blocking collectives, exchange(): x = lax.all_to_all(x, axis, split_axis=0, concat_axis=0, tiled=True)  70.1 us
    all_to_all x2, starting transfers between devices, exchange(): x = lax.all_to_all(x, axis, split_axis=0, concat_axis=0, tiled=True)  26.4 us
    pallas_call x6, Pallas kernels, call(): pl.pallas_call(kernel, out_shape=[jax.ShapeDtypeStruct(s, f32) for s in o...  25.4 us
    ppermute x6, starting transfers between devices, shift(): return lax.ppermute(x, 'rep', [(i, (i + by) % n) for i in range(n)])  22.8 us
    all_to_all x2, waiting for transfers between devices, exchange(): x = lax.all_to_all(x, axis, split_axis=0, concat_axis=0, tiled=True)  21.8 us
    all_to_all x1, blocking collectives, on_device(): lax.all_to_all(grads, 'rep', split_axis=0, concat_axis=0, tiled=True)  17.6 us
    ppermute x6, waiting for transfers between devices, shift(): return lax.ppermute(x, 'rep', [(i, (i + by) % n) for i in range(n)])  15.9 us
    all_gather x1, blocking collectives, on_device(): fresh = lax.all_gather(fresh, 'rep', axis=0, tiled=False)  14.1 us
  transfers between devices with their start and end apart: 8, of which 7 were waited for; matrix products, arithmetic and copies ran while one was open for 0% of the time, Pallas kernels for 3%

profile of v1, /device:TPU:24, one launch (start us, length us, event | category | flops | bytes accessed | tf_op | source)
XLA Modules:
  0.0 222.2 jit_solution(9827317871885363605)
XLA Ops:
  0.6 0.6 copy-done.15
  1.3 0.6 dynamic_slice.3.neg_at
  1.9 0.6 copy-done.13
  2.6 0.6 stack.15.ints
  3.2 3.0 %ask.1 = (f32[512,128]{1,0:T(8,128)}, f32[128,128]{1,0:T(8,128)}, f32[8,128]{1,0:T(8,128)}) custom-call(s32[1]{0:T(128)} %dynamic_slice.3.neg_at, s32[5,128]{1,0:T(8,128)} %stack.15.ints, f32[400,512]{1,0:T(8,128)} %bitcast.22), custom_call_target="tpu_custom_call" | custom-call | tf_op jit(solution)/shard_map/ask/pallas_call | solution.py:296
  6.2 19.4 %all-to-all-start = ((f32[128,1,512]{2,1,0:T(1,128)}), f32[128,1,512]{2,1,0:T(1,128)S(1)}, u32[]{:S(2)}, u32[]{:S(2)}) async-start(f32[128,1,512]{2,1,0:T(1,128)} %bitcast.38), calls=%async_computation | async-start | bytes 524288 | tf_op jit(solution)/shard_map/all_to_all | solution.py:308
  25.7 0.8 pad_maximum_fusion.rel_ref
  26.5 21.1 %all-to-all-done = f32[128,1,512]{2,1,0:T(1,128)S(1)} async-done(((f32[128,1,512]{2,1,0:T(1,128)}), f32[128,1,512]{2,1,0:T(1,128)S(1)}, u32[]{:S(2)}, u32[]{:S(2)}) %all-to-all-start) | async-done | bytes 262176 | tf_op jit(solution)/shard_map/all_to_all | solution.py:308
  47.5 0.7 copy-done
  48.2 4.8 %fetch.1 = (f32[1664,128]{1,0:T(8,128)}, f32[512,512]{1,0:T(8,128)}) custom-call(f32[512,128]{1,0:T(8,128)} %bitcast.25, f32[400,512]{1,0:T(8,128)} %bitcast.23, f32[64,512]{1,0:T(8,128)} %pad_maximum_fusion.rel_ref), custom_call_target="tpu_custom_call" | custom-call | tf_op jit(solution)/shard_map/fetch/pallas_call | solution.py:296
  53.1 7.0 %all-to-all-start.1 = ((f32[128,1,1664]{2,1,0:T(1,128)}), f32[128,1,1664]{2,1,0:T(1,128)S(1)}, u32[]{:S(2)}, u32[]{:S(2)}) async-start(f32[128,1,1664]{2,1,0:T(1,128)} %bitcast.37), calls=%async_computation.1 | async-start | bytes 1703936 | tf_op jit(solution)/shard_map/all_to_all | solution.py:308
  60.1 3.4 %collective-permute-start.2 = (f32[512,128]{1,0:T(8,128)S(1)}, f32[512,128]{1,0:T(8,128)S(1)}, u32[]{:S(2)}, u32[]{:S(2)}) collective-permute-start(f32[512,128]{1,0:T(8,128)S(1)} %bitcast.29), channel_id=1, source_target_pairs={{0,1},{1,2},{2,3},{3,0},{4,5},{5,6},{6,7},{7,4},{8,9},{9,10},{10,1... | collective-permute-start | bytes 786440 | tf_op jit(solution)/shard_map/ppermute | solution.py:314
  63.5 4.6 %collective-permute-start.1 = (f32[512,128]{1,0:T(8,128)S(1)}, f32[512,128]{1,0:T(8,128)S(1)}, u32[]{:S(2)}, u32[]{:S(2)}) collective-permute-start(f32[512,128]{1,0:T(8,128)S(1)} %bitcast.30), channel_id=1, source_target_pairs={{0,2},{1,3},{2,0},{3,1},{4,6},{5,7},{6,4},{7,5},{8,10},{9,11},{10,... | collective-permute-start | bytes 786440 | tf_op jit(solution)/shard_map/ppermute | solution.py:314
  68.1 3.3 %collective-permute-start = (f32[512,128]{1,0:T(8,128)S(1)}, f32[512,128]{1,0:T(8,128)S(1)}, u32[]{:S(2)}, u32[]{:S(2)}) collective-permute-start(f32[512,128]{1,0:T(8,128)S(1)} %bitcast.31), channel_id=1, source_target_pairs={{0,3},{1,0},{2,1},{3,2},{4,7},{5,4},{6,5},{7,6},{8,11},{9,8},{10,9... | collective-permute-start | bytes 786440 | tf_op jit(solution)/shard_map/ppermute | solution.py:314
  71.6 6.6 %collective-permute-done.1.neg2 = f32[512,128]{1,0:T(8,128)S(1)} collective-permute-done((f32[512,128]{1,0:T(8,128)S(1)}, f32[512,128]{1,0:T(8,128)S(1)}, u32[]{:S(2)}, u32[]{:S(2)}) %collective-permute-start.1) | collective-permute-done | bytes 262176 | tf_op jit(solution)/shard_map/ppermute | solution.py:314
  78.2 1.5 collective-permute-done.neg1
  79.7 0.7 copy-done.8
  80.4 6.3 %negatives.1 = (f32[256,512]{1,0:T(8,128)}, f32[256,512]{1,0:T(8,128)}, f32[256,512]{1,0:T(8,128)}, f32[128,512]{1,0:T(8,128)}, f32[128,512]{1,0:T(8,128)}, /*index=5*/f32[128,512]{1,0:T(8,128)}, f32[128,512]{1,0:T(8,128)}) custom-call(f32[512,128]{1,0:T(8,128)} %bitcast.26, f32[512,512]{1,0:T(8,128)} %get-tuple-element.18.rows, ...), custom_call_target="tpu_custom_call" | custom-call | tf_op jit(solution)/shard_map/negatives/pallas_call | solution.py:296
  86.7 4.3 %collective-permute-start.3 = (f32[128,512]{1,0:T(8,128)}, f32[128,512]{1,0:T(8,128)S(1)}, u32[]{:S(2)}, u32[]{:S(2)}) collective-permute-start(f32[128,512]{1,0:T(8,128)} %get-tuple-element.20), channel_id=1, source_target_pairs={{0,1},{1,2},{2,3},{3,0},{4,5},{5,6},{6,7},{7,4},{8,9},{9,10},{10,1... | collective-permute-start | bytes 786440 | tf_op jit(solution)/shard_map/ppermute | solution.py:314
  91.0 3.6 %collective-permute-start.4 = (f32[128,512]{1,0:T(8,128)}, f32[128,512]{1,0:T(8,128)S(1)}, u32[]{:S(2)}, u32[]{:S(2)}) collective-permute-start(f32[128,512]{1,0:T(8,128)} %get-tuple-element.21), channel_id=1, source_target_pairs={{0,2},{1,3},{2,0},{3,1},{4,6},{5,7},{6,4},{7,5},{8,10},{9,11},{10,... | collective-permute-start | bytes 786440 | tf_op jit(solution)/shard_map/ppermute | solution.py:314
  94.6 3.5 %collective-permute-start.5 = (f32[128,512]{1,0:T(8,128)}, f32[128,512]{1,0:T(8,128)S(1)}, u32[]{:S(2)}, u32[]{:S(2)}) collective-permute-start(f32[128,512]{1,0:T(8,128)} %get-tuple-element.22), channel_id=1, source_target_pairs={{0,3},{1,0},{2,1},{3,2},{4,7},{5,4},{6,5},{7,6},{8,11},{9,8},{10,9... | collective-permute-start | bytes 786440 | tf_op jit(solution)/shard_map/ppermute | solution.py:314
  98.1 6.4 %collective-permute-done.4.sum2 = f32[128,512]{1,0:T(8,128)S(1)} collective-permute-done((f32[128,512]{1,0:T(8,128)}, f32[128,512]{1,0:T(8,128)S(1)}, u32[]{:S(2)}, u32[]{:S(2)}) %collective-permute-start.4) | collective-permute-done | bytes 262176 | tf_op jit(solution)/shard_map/ppermute | solution.py:314
  104.5 1.3 collective-permute-done.5.sum3
  105.8 0.8 all-to-all-done.1
  106.6 0.9 copy-done.2
  107.5 3.9 %edge.1 = f32[2048,128]{1,0:T(8,128)} custom-call(f32[1664,128]{1,0:T(8,128)} %bitcast.34, f32[128,128]{1,0:T(8,128)} %get-tuple-element.16.head_edge, f32[8,128]{1,0:T(8,128)} %get-tuple-element.17.tail_edge, f32[128,512]{1,0:T(8,128)} %get-tuple-element.19.sum0, f32[128,512]{1,0:T(8,128)} %copy-done.3, f32[128,512]{1,0:T(8,128)} %copy-done.5, ...), custom_call_target="tpu_custom_call" | custom-call | tf_op jit(solution)/shard_map/edge/pallas_call | solution.py:296
  111.4 70.1 %all_to_all.20 = f32[128,1,2048]{2,1,0:T(1,128)} all-to-all(f32[128,1,2048]{2,1,0:T(1,128)} %bitcast.32), channel_id=1, replica_groups=mesh['ent'=128,'rep'=4] {'ent'}, dimensions={0} | all-to-all | bytes 2097152 | tf_op jit(solution)/shard_map/all_to_all | solution.py:308
  181.5 5.2 %scatter.1 = f32[4,400,128]{2,1,0:T(8,128)} custom-call(s32[1]{0:T(128)} %dynamic_slice.3.neg_at, f32[2048,128]{1,0:T(8,128)} %bitcast.33, f32[512,128]{1,0:T(8,128)} %bitcast.28, f32[256,512]{1,0:T(8,128)} %get-tuple-element.23.near, f32[256,512]{1,0:T(8,128)} %get-tuple-element.24.far, f32[256,512]{1,0:T(8,128)} %get-tuple-element.25.rels), custom_call_target="tpu_custom_call" | custom-call | tf_op jit(solution)/shard_map/scatter/pallas_call | solution.py:296
  186.7 17.6 %all_to_all.21.grads = f32[4,400,128]{2,1,0:T(8,128)} all-to-all(f32[4,400,128]{2,1,0:T(8,128)} %scatter.1), channel_id=1, replica_groups=mesh['ent'=128,'rep'=4] {'rep'}, dimensions={0} | all-to-all | bytes 1638400 | tf_op jit(solution)/shard_map/all_to_all | solution.py:364
  204.3 2.2 update.1
  206.5 14.1 %all-gather = f32[1632,128]{1,0:T(8,128)S(1)} all-gather(f32[408,128]{1,0:T(8,128)} %update.1), channel_id=2, replica_groups=mesh['ent'=128,'rep'=4] {'rep'}, dimensions={0}, use_global_device_ids=true | all-gather | bytes 1044480 | tf_op jit(solution)/shard_map/all_gather | solution.py:372
  221.2 1.0 copy_bitcast_fusion
  (32 shorter events, 0.9 us)
Async XLA Ops:
  0.6 0.7 copy-start.15
  1.9 0.7 copy-start.13
  1.9 0.7 copy-start.14
  1.9 0.7 copy-start.10
  1.9 0.7 copy-start.11
  1.9 0.7 copy-start.12
  6.2 19.4 %copy-start.9 = (f32[64,400]{1,0:T(8,128)S(1)}, f32[64,400]{1,0:T(8,128)}, u32[]{:S(2)}) copy-start(f32[64,400]{1,0:T(8,128)} %param.17) | copy-start | bytes 307204
  6.2 41.3 %all-to-all-start = ((f32[128,1,512]{2,1,0:T(1,128)}), f32[128,1,512]{2,1,0:T(1,128)S(1)}, u32[]{:S(2)}, u32[]{:S(2)}) async-start(f32[128,1,512]{2,1,0:T(1,128)} %bitcast.38), calls=%async_computation | async-start | bytes 524288 | tf_op jit(solution)/shard_map/all_to_all | solution.py:308
  47.5 0.7 copy-start
  53.1 7.0 %copy-start.1 = (f32[128,1,512]{2,1,0:T(1,128)S(1)}, f32[128,1,512]{2,1,0:T(1,128)}, u32[]{:S(2)}) copy-start(f32[128,1,512]{2,1,0:T(1,128)} %copy-done) | copy-start | bytes 786436
  53.1 53.5 %all-to-all-start.1 = ((f32[128,1,1664]{2,1,0:T(1,128)}), f32[128,1,1664]{2,1,0:T(1,128)S(1)}, u32[]{:S(2)}, u32[]{:S(2)}) async-start(f32[128,1,1664]{2,1,0:T(1,128)} %bitcast.37), calls=%async_computation.1 | async-start | bytes 1703936 | tf_op jit(solution)/shard_map/all_to_all | solution.py:308
  60.1 11.5 %collective-permute-start.2 = (f32[512,128]{1,0:T(8,128)S(1)}, f32[512,128]{1,0:T(8,128)S(1)}, u32[]{:S(2)}, u32[]{:S(2)}) collective-permute-start(f32[512,128]{1,0:T(8,128)S(1)} %bitcast.29), channel_id=1, source_target_pairs={{0,1},{1,2},{2,3},{3,0},{4,5},{5,6},{6,7},{7,4},{8,9},{9,10},{10,1... | collective-permute-start | bytes 786440 | tf_op jit(solution)/shard_map/ppermute | solution.py:314
  63.5 14.7 %collective-permute-start.1 = (f32[512,128]{1,0:T(8,128)S(1)}, f32[512,128]{1,0:T(8,128)S(1)}, u32[]{:S(2)}, u32[]{:S(2)}) collective-permute-start(f32[512,128]{1,0:T(8,128)S(1)} %bitcast.30), channel_id=1, source_target_pairs={{0,2},{1,3},{2,0},{3,1},{4,6},{5,7},{6,4},{7,5},{8,10},{9,11},{10,... | collective-permute-start | bytes 786440 | tf_op jit(solution)/shard_map/ppermute | solution.py:314
  68.1 11.5 %collective-permute-start = (f32[512,128]{1,0:T(8,128)S(1)}, f32[512,128]{1,0:T(8,128)S(1)}, u32[]{:S(2)}, u32[]{:S(2)}) collective-permute-start(f32[512,128]{1,0:T(8,128)S(1)} %bitcast.31), channel_id=1, source_target_pairs={{0,3},{1,0},{2,1},{3,2},{4,7},{5,4},{6,5},{7,6},{8,11},{9,8},{10,9... | collective-permute-start | bytes 786440 | tf_op jit(solution)/shard_map/ppermute | solution.py:314
  71.6 8.1 %copy-start.4 = (f32[512,128]{1,0:T(8,128)}, f32[512,128]{1,0:T(8,128)S(1)}, u32[]{:S(2)}) copy-start(f32[512,128]{1,0:T(8,128)S(1)} %collective-permute-done.2.neg3) | copy-start | bytes 786436
  78.1 1.5 copy-start.6
  79.7 0.7 copy-start.8
  86.7 11.4 %collective-permute-start.3 = (f32[128,512]{1,0:T(8,128)}, f32[128,512]{1,0:T(8,128)S(1)}, u32[]{:S(2)}, u32[]{:S(2)}) collective-permute-start(f32[128,512]{1,0:T(8,128)} %get-tuple-element.20), channel_id=1, source_target_pairs={{0,1},{1,2},{2,3},{3,0},{4,5},{5,6},{6,7},{7,4},{8,9},{9,10},{10,1... | collective-permute-start | bytes 786440 | tf_op jit(solution)/shard_map/ppermute | solution.py:314
  91.0 13.5 %collective-permute-start.4 = (f32[128,512]{1,0:T(8,128)}, f32[128,512]{1,0:T(8,128)S(1)}, u32[]{:S(2)}, u32[]{:S(2)}) collective-permute-start(f32[128,512]{1,0:T(8,128)} %get-tuple-element.21), channel_id=1, source_target_pairs={{0,2},{1,3},{2,0},{3,1},{4,6},{5,7},{6,4},{7,5},{8,10},{9,11},{10,... | collective-permute-start | bytes 786440 | tf_op jit(solution)/shard_map/ppermute | solution.py:314
  94.6 11.2 %collective-permute-start.5 = (f32[128,512]{1,0:T(8,128)}, f32[128,512]{1,0:T(8,128)S(1)}, u32[]{:S(2)}, u32[]{:S(2)}) collective-permute-start(f32[128,512]{1,0:T(8,128)} %get-tuple-element.22), channel_id=1, source_target_pairs={{0,3},{1,0},{2,1},{3,2},{4,7},{5,4},{6,5},{7,6},{8,11},{9,8},{10,9... | collective-permute-start | bytes 786440 | tf_op jit(solution)/shard_map/ppermute | solution.py:314
  98.1 8.5 %copy-start.3 = (f32[128,512]{1,0:T(8,128)}, f32[128,512]{1,0:T(8,128)S(1)}, u32[]{:S(2)}) copy-start(f32[128,512]{1,0:T(8,128)S(1)} %collective-permute-done.3.sum1) | copy-start | bytes 786436
  104.5 2.1 copy-start.5
  105.8 0.8 copy-start.7
  106.6 0.9 copy-start.2

commit v2 on v1

v2 whole, which is shorter than its diff:
```python
import math

import jax
import jax.numpy as jnp
from jax import lax
from jax.experimental import pallas as pl
from jax.experimental.pallas import tpu as pltpu
from jax.sharding import PartitionSpec as P

learn_rate = 0.1

LANE = 128
f32 = jnp.float32
bf16 = jnp.bfloat16
NN = (((1,), (0,)), ((), ()))
NT = (((1,), (1,)), ((), ()))
TN = (((0,), (0,)), ((), ()))
PIECES = 2
TILES1 = 4
TILES2 = 13
TILES3 = 16
GROUP = 32


def dot(a, b, dims):
    return lax.dot_general(a, b, dims, preferred_element_type=f32)


def parts(x, count):
    out = []
    for _ in range(count):
        head = x.astype(bf16)
        out.append(head)
        x = x - head.astype(f32)
    return out


def pick(onehot, pieces, dims):
    total = dot(onehot, pieces[0], dims)
    for piece in pieces[1:]:
        total = total + dot(onehot, piece, dims)
    return total


def dot3(a, b, dims):
    a0, a1 = parts(a, 2)
    b0, b1 = parts(b, 2)
    return dot(a0, b0, dims) + (dot(a0, b1, dims) + dot(a1, b0, dims))


def lanes(shape):
    return lax.broadcasted_iota(jnp.int32, shape, len(shape) - 1)


def cmul(a, b):
    return (a[0] * b[0] - a[1] * b[1], a[0] * b[1] + a[1] * b[0])


def conj(a):
    return (a[0], -a[1])


def sigmoid(x):
    return 1.0 / (1.0 + jnp.exp(-x))


def column(tile, lane):
    return jnp.sum(jnp.where(lanes(tile.shape) == lane, tile, 0.0), 1, keepdims=True)


def pack(ref, tiles, halves, base=0):
    n = halves[0].shape[0]
    at = lanes((n, LANE))
    tail = jnp.zeros((n, LANE), f32)
    for i, half in enumerate(halves):
        ref[pl.ds(base + i, n, stride=tiles), :] = half[:, :LANE]
        rest = half[:, LANE:]
        shift = (8 * i - 64) % LANE
        moved = pltpu.roll(rest, shift, 1) if shift else rest
        tail = jnp.where((at >= 8 * i) & (at < 8 * i + 8), moved, tail)
    for i in range(0, len(halves), 2):
        low, high = halves[i][:, LANE:], halves[i + 1][:, LANE:]
        ref[pl.ds(base + len(halves) + i // 2, n, stride=tiles), :] = jnp.where(
            at < 64, low, pltpu.roll(high, 64, 1)
        )
    ref[pl.ds(base + len(halves) * 3 // 2, n, stride=tiles), :] = tail


def unpack(ref, tiles, count, n):
    at = lanes((n, LANE))
    tail = ref[pl.ds(count * 3 // 2, n, stride=tiles), :]
    out = []
    for i in range(count):
        full = ref[pl.ds(i, n, stride=tiles), :]
        pair = ref[pl.ds(count + i // 2, n, stride=tiles), :]
        if i % 2:
            pair = pltpu.roll(pair, 64, 1)
        shift = (64 - 8 * i) % LANE
        moved = pltpu.roll(tail, shift, 1) if shift else tail
        rest = jnp.where(at < 64, pair, jnp.where(at < 72, moved, 0.0))
        out.append(jnp.concatenate([full, rest], 1))
    return out


def ask_kernel(rep, neg_rows, head_owner, head_row, rel, tail_owner, tail_row, table_t, send, head_edge, tail_edge):
    n = LANE
    sub = lax.broadcasted_iota(jnp.int32, (n, n), 0)
    lane = lanes((n, n))

    def wide(x):
        return jnp.broadcast_to(x, (n, x.shape[1]))

    head_owner, head_row, rel, tail_owner, tail_row = (
        wide(ref[...].astype(f32)) for ref in (head_owner, head_row, rel, tail_owner, tail_row)
    )
    owner_id = sub.astype(f32)
    columns = []

    def slots(owner, named):
        owner_c = owner.T
        rank = jnp.sum(jnp.where((owner == owner_c) & (sub < lane), 1.0, 0.0), 0, keepdims=True)
        edges = []
        for s in range(2):
            here = (owner == owner_id) & (wide(rank) == float(s))
            columns.append(jnp.sum(jnp.where(here, named + 1.0, 0.0), 1, keepdims=True) - 1.0)
            columns.append(jnp.sum(jnp.where(here, rel, 0.0), 1, keepdims=True))
            edges.append(
                jnp.sum(jnp.where(here, lane.astype(f32) + 1.0, 0.0), 1, keepdims=True) - 1.0
            )
        return jnp.where(lane == 0, edges[0], jnp.where(lane == 1, edges[1], -1.0))

    head_edge[...] = slots(head_owner, head_row)
    tail_edge[...] = slots(tail_owner, tail_row)

    neg_at = neg_rows[rep[0]]
    block = table_t[:, pl.ds(pl.multiple_of(neg_at // n * n, n), n)]
    pad = jnp.zeros((56, n), f32)
    for i in range(2):
        half = jnp.concatenate([block[200 * i : 200 * i + 200, :], pad], 0).T
        picked = lax.broadcasted_iota(jnp.int32, (n, 256), 0) == neg_at % n
        line = jnp.sum(jnp.where(picked, half, 0.0), 0, keepdims=True)
        send[pl.ds(2 * i, n, stride=TILES1), :] = wide(line[:, :n])
        tile = wide(line[:, n:])
        if i == 0:
            for j, col in enumerate(columns):
                tile = jnp.where(lane == 72 + j, col, tile)
        send[pl.ds(2 * i + 1, n, stride=TILES1), :] = tile


def ahead_kernel(table_t, relations, head_edge, tail_edge, *outs):
    pad = jnp.zeros((56, 512), f32)
    whole = jnp.concatenate([table_t[0:200, :], pad, table_t[200:400, :], pad], 0).T
    for ref, piece in zip(outs[:PIECES], parts(whole, PIECES), strict=True):
        ref[...] = piece
    pad = jnp.zeros((64, 56), f32)
    whole = jnp.concatenate([relations[:, :200], pad, relations[:, 200:], pad], 1)
    for ref, piece in zip(outs[PIECES : 2 * PIECES], parts(whole, PIECES), strict=True):
        ref[...] = piece
    same, same_t = outs[2 * PIECES :]

    def stack(ref, by_rows):
        if by_rows:
            turned = ref[...].T
            return jnp.concatenate([turned[0:1, :], turned[1:2, :]], 1)
        return jnp.concatenate([ref[:, 0:1], ref[:, 1:2]], 0)

    for ref, one, other in ((same, head_edge, tail_edge), (same_t, tail_edge, head_edge)):
        col, row = stack(one, False), stack(other, True)
        ref[...] = jnp.where((col == row) & (col >= 0.0), 1.0, 0.0).astype(bf16)


def rel_vectors(tile, slots, pieces):
    ids = jnp.concatenate([column(tile, 72 + 2 * s + 1) for s in slots], 0)
    hot = jnp.where(lanes((ids.shape[0], 64)).astype(f32) == ids, 1.0, 0.0).astype(bf16)
    both = pick(hot, [p[...] for p in pieces], NN)
    return (both[:, :256], both[:, 256:])


def split(x):
    return (x[:, :256], x[:, 256:])


def fetch_kernel(recv, *refs):
    n = LANE
    table, rel = refs[:PIECES], refs[PIECES : 2 * PIECES]
    send, rows = refs[2 * PIECES :]
    tile = recv[pl.ds(1, n, stride=TILES1), :]
    halves = []
    for side in range(2):
        slots = (2 * side, 2 * side + 1)
        at = jnp.concatenate([column(tile, 72 + 2 * s) for s in slots], 0)
        hot = jnp.where(lanes((2 * n, 512)).astype(f32) == at, 1.0, 0.0).astype(bf16)
        vec = split(pick(hot, [p[...] for p in table], NN))
        if side == 0:
            vec = cmul(vec, rel_vectors(tile, slots, rel))
        for i in range(2):
            halves += [v[i * n : (i + 1) * n, :] for v in vec]
        for i in range(2):
            rows[2 * n * side : 2 * n * (side + 1), i * 256 : (i + 1) * 256] = vec[i]
    pack(send, TILES2, halves)


def negatives_kernel(recv, rows, *refs):
    n = LANE
    rel = refs[:PIECES]
    *negs, near, far, rels, out0, out1, out2, out3 = refs[PIECES:]
    tile = recv[pl.ds(1, n, stride=TILES1), :]
    keep = lanes((n, LANE)) < 72
    tiles = []
    for ref in negs:
        got = [ref[pl.ds(i, n, stride=TILES1), :] for i in range(4)]
        got[1] = jnp.where(keep, got[1], 0.0)
        tiles.append(jnp.concatenate(got, 1))
    negs = jnp.concatenate(tiles, 0)
    weight = 1.0 / math.sqrt(512.0)
    total = None
    for side in range(2):
        slots = (2 * side, 2 * side + 1)
        x = rows[2 * n * side : 2 * n * (side + 1), :]
        rv = rel_vectors(tile, slots, rel)
        if side:
            x = jnp.concatenate(cmul(conj(rv), split(x)), 1)
        valid = jnp.concatenate([column(tile, 72 + 2 * s) for s in slots], 0)
        scores = dot3(x, negs, NT)
        coef = jnp.where(valid >= 0.0, sigmoid(scores) * weight, 0.0)
        back = dot3(coef, negs, NN)
        if side:
            far[...] = jnp.concatenate(cmul(split(back), rv), 1)
        else:
            near[...] = back
            rels[...] = jnp.concatenate(rv, 1)
        grad = dot3(coef, x, TN)
        total = grad if total is None else total + grad
    for i, ref in enumerate((out0, out1, out2, out3)):
        ref[...] = total[i * n : (i + 1) * n, :]


def edge_kernel(recv, same, same_t, head_edge, sum0, sum1, sum2, sum3, send, token):
    n = LANE
    halves = unpack(recv, TILES2, 8, n)
    head_at = jnp.concatenate([head_edge[:, 0:1], head_edge[:, 1:2]], 0)
    query, tails = (
        jnp.concatenate(
            [jnp.concatenate(halves[i : i + 2], 1), jnp.concatenate(halves[i + 2 : i + 4], 1)], 0
        )
        for i in (0, 4)
    )
    met = pick(same[...], parts(tails, PIECES), NN)
    pos = jnp.sum(query * met, 1, keepdims=True)
    coef = jnp.where(head_at >= 0.0, -sigmoid(-pos), 0.0)
    to_head = coef * met
    to_tail = pick(same_t[...], parts(coef * query, PIECES), NN)
    neg = sum0[...] + sum1[...] + (sum2[...] + sum3[...])
    out = []
    for block in (to_head[:n], to_head[n:], to_tail[:n], to_tail[n:], neg):
        out += [block[:, :256], block[:, 256:]]
    pack(send, TILES3, out)
    token[...] = neg[0:8, 0:128]


def place_kernel(rep, neg_rows, asks, token, *refs):
    n = LANE
    *sides, side, hot = refs
    for i, source in enumerate(sides):
        side[i * 2 * n : (i + 1) * 2 * n, :] = source[...]
    turned = asks[pl.ds(1, n, stride=TILES1), :].T
    sub = lax.broadcasted_iota(jnp.int32, (512, n), 0)
    for s in range(4):
        at = turned[72 + 2 * s : 73 + 2 * s, :]
        hot[:, s * n : (s + 1) * n] = jnp.where(sub.astype(f32) == at, 1.0, 0.0).astype(bf16)
    hot[:, 4 * n :] = jnp.where(sub == neg_rows[rep[0]], 1.0, 0.0).astype(bf16)


def scatter_kernel(recv, hot, side, out):
    n = LANE
    halves = unpack(recv, TILES3, 10, n)
    blocks = [jnp.concatenate(halves[i : i + 2], 1) for i in range(0, 10, 2)]
    head = split(jnp.concatenate(blocks[0:2], 0) + side[0 : 2 * n, :])
    head = jnp.concatenate(cmul(head, conj(split(side[4 * n :, :]))), 1)
    tail = jnp.concatenate(blocks[2:4], 0) + side[2 * n : 4 * n, :]
    grad = jnp.concatenate([head, tail, blocks[4]], 0)
    total = pick(hot[...], parts(grad, PIECES), NN)
    for q in range(4):
        groups = []
        for g in range(4):
            start = q * n + g * GROUP
            groups += split(total[start : start + GROUP, :])
        pack(out, TILES2, groups, q * TILES2 * GROUP)


def update_kernel(rep, grads, table_t, state, out, sums):
    n = LANE
    rows = TILES2 * GROUP
    sums[...] = (
        grads[0:rows, :] + grads[rows : 2 * rows, :]
        + (grads[2 * rows : 3 * rows, :] + grads[3 * rows :, :])
    )
    halves = unpack(sums, TILES2, 8, GROUP)
    grad = jnp.concatenate(
        [jnp.concatenate(halves[i::2], 0).T[0:200, :] for i in range(2)], 0
    )
    start = pl.multiple_of(rep[0] * n, n)
    mean = jnp.sum(grad * grad, 0, keepdims=True) * (1.0 / 400.0)
    new = state[:, pl.ds(start, n)] + mean
    out[0:400, :] = table_t[:, pl.ds(start, n)] - learn_rate * grad / jnp.sqrt(new)
    out[400:408, :] = jnp.broadcast_to(new, (8, n))


def join_kernel(parts_in, table_new, state_new):
    for q in range(4):
        table_new[:, q * LANE : (q + 1) * LANE] = parts_in[q, 0:400, :]
        state_new[:, q * LANE : (q + 1) * LANE] = parts_in[q, 400:401, :]


def call(kernel, outs, args, scalars=(), name=None, scratch=()):
    space = pl.BlockSpec(memory_space=pltpu.VMEM)
    return pl.pallas_call(
        kernel,
        out_shape=[
            (pltpu.VMEM if near else pltpu.HBM)(shape, kind)
            for shape, kind, near in outs
        ],
        in_specs=[pl.BlockSpec(memory_space=pltpu.SMEM)] * len(scalars) + [space] * len(args),
        out_specs=[space] * len(outs),
        scratch_shapes=list(scratch),
        compiler_params=pltpu.CompilerParams(vmem_limit_bytes=24 << 20),
        name=name,
    )(*scalars, *args)


def near(x):
    return pltpu.with_memory_space_constraint(x, pltpu.VMEM)


def far(x):
    return pltpu.with_memory_space_constraint(x, pltpu.HBM)


def exchange(x, axis, tiles):
    n = lax.axis_size(axis)
    x = x.reshape(n, 1, tiles * LANE)
    x = lax.all_to_all(x, axis, split_axis=0, concat_axis=0, tiled=True)
    return x.reshape(n * tiles, LANE)


def shift(x, by):
    n = lax.axis_size("rep")
    return lax.ppermute(x, "rep", [(i, (i + by) % n) for i in range(n)])


def on_device(
    entity_table,
    adagrad_state,
    head_owner,
    head_row,
    relation_ids,
    tail_owner,
    tail_row,
    neg_rows,
    relations,
):
    rep = lax.axis_index("rep").reshape(1).astype(jnp.int32)
    table_t = entity_table.T
    n = LANE

    def line(x):
        return x.reshape(1, n)

    send1, head_edge, tail_edge = call(
        ask_kernel,
        [((n * TILES1, n), f32, False), ((n, n), f32, False), ((n, n), f32, False)],
        (
            line(head_owner),
            line(head_row),
            line(relation_ids),
            line(tail_owner),
            line(tail_row),
            table_t,
        ),
        (rep, neg_rows),
        "ask",
    )
    recv1 = exchange(send1, "ent", TILES1)
    *pieces, same, same_t = call(
        ahead_kernel,
        [((4 * n, 512), bf16, True)] * PIECES
        + [((64, 512), bf16, True)] * PIECES
        + [((2 * n, 2 * n), bf16, False)] * 2,
        (table_t, relations, far(head_edge), far(tail_edge)),
        name="ahead",
    )
    rel_pieces = pieces[PIECES:]
    send2, rows = call(
        fetch_kernel,
        [((n * TILES2, n), f32, False), ((4 * n, 512), f32, True)],
        (near(recv1), *map(near, pieces)),
        name="fetch",
    )
    recv2 = exchange(send2, "ent", TILES2)
    negs = [recv1] + [shift(recv1, -j) for j in (1, 2, 3)]
    query_side, tail_side, rels, *owned = call(
        negatives_kernel,
        [((2 * n, 512), f32, False)] * 3 + [((n, 512), f32, i > 0) for i in range(4)],
        (near(recv1), near(rows), *map(far, rel_pieces), *map(near, negs)),
        name="negatives",
    )
    sums = [owned[0]] + [shift(owned[j], j) for j in (1, 2, 3)]
    send3, token = call(
        edge_kernel,
        [((n * TILES3, n), f32, False), ((8, n), f32, False)],
        (near(recv2), far(same), far(same_t), far(head_edge), far(sums[0]), *map(near, sums[1:])),
        name="edge",
    )
    recv3 = exchange(send3, "ent", TILES3)
    side, hot = call(
        place_kernel,
        [((6 * n, 512), f32, True), ((4 * n, 5 * n), bf16, True)],
        (recv1, far(token), far(query_side), far(tail_side), far(rels)),
        (rep, neg_rows),
        "place",
    )
    (grads,) = call(
        scatter_kernel,
        [((4 * TILES2 * GROUP, n), f32, False)],
        (near(recv3), near(hot), near(side)),
        name="scatter",
    )
    grads = lax.all_to_all(grads, "rep", split_axis=0, concat_axis=0, tiled=True)
    (fresh,) = call(
        update_kernel,
        [((408, n), f32, True)],
        (near(grads), table_t, adagrad_state.reshape(1, 512)),
        (rep,),
        "update",
        (pltpu.VMEM((TILES2 * GROUP, n), f32),),
    )
    fresh = lax.all_gather(fresh, "rep", axis=0, tiled=False)
    table_new, state_new = call(
        join_kernel, [((400, 512), f32, False), ((1, 512), f32, False)], (near(fresh),), name="join"
    )
    return (table_new.T, state_new.reshape(512))


def solution(mesh):
    placed = (
        P("ent", None),
        P("ent"),
        P(("ent", "rep"), None),
        P(("ent", "rep")),
        P(("ent", "rep")),
        P(("ent", "rep"), None),
        P(("ent", "rep")),
        P("ent"),
        P(),
    )
    return jax.shard_map(
        on_device, mesh=mesh, in_specs=placed, out_specs=(P("ent", None), P("ent")), check_vma=False
    )
```

time: 224 us -> 215 us (0.960)
  blocking collectives: 102 us -> 32.5 us
  waiting for transfers between devices: 37.7 us -> 89 us
  starting transfers between devices: 49.2 us -> 62.3 us
  Pallas kernels: 25.4 us -> 19.8 us
    all_to_all x1 -> x0, blocking collectives: 70.1 us -> none  [exchange(): x = lax.all_to_all(x, axis, split_axis=0, concat_axis=0, tiled=True)]
    all_to_all x2 -> x3, waiting for transfers between devices: 21.8 us -> 73.3 us  [exchange(): x = lax.all_to_all(x, axis, split_axis=0, concat_axis=0, tiled=True)]
    all_to_all x2 -> x3, starting transfers between devices: 26.4 us -> 39.5 us  [exchange(): x = lax.all_to_all(x, axis, split_axis=0, concat_axis=0, tiled=True)]
    pallas_call x6 -> x9, Pallas kernels: 25.4 us -> 19.8 us  [call(): pl.pallas_call(kernel, out_shape=[(pltpu.VMEM if near else pltpu.HBM)(sha...]
    unnamed x32 -> x30, local copies, waits for them, and re-layouts: 3.67 us -> 8.57 us
  transfers between devices with their start and end apart: 8 -> 9, of which waited for: 7 -> 8; matrix products, arithmetic and copies ran while one was open for 0% -> 0% of each run, Pallas kernels for 3% -> 4%
where the time goes in v2:
time: 215 us; the launch traced here: 213 us
  waiting for transfers between devices  89 us (41%)
  starting transfers between devices  62.3 us (29%)
  blocking collectives  32.5 us (15%)
  Pallas kernels  19.8 us (9%)
  local copies, waits for them, and re-layouts  8.57 us (4%)
    all_to_all x3, waiting for transfers between devices, exchange(): x = lax.all_to_all(x, axis, split_axis=0, concat_axis=0, tiled=True)  73.3 us
    all_to_all x3, starting transfers between devices, exchange(): x = lax.all_to_all(x, axis, split_axis=0, concat_axis=0, tiled=True)  39.5 us
    ppermute x6, starting transfers between devices, shift(): return lax.ppermute(x, 'rep', [(i, (i + by) % n) for i in range(n)])  22.8 us
    pallas_call x9, Pallas kernels, call(): pl.pallas_call(kernel, out_shape=[(pltpu.VMEM if near else pltpu.HBM)(sha...  19.8 us
    all_to_all x1, blocking collectives, on_device(): lax.all_to_all(grads, 'rep', split_axis=0, concat_axis=0, tiled=True)  18 us
    ppermute x6, waiting for transfers between devices, shift(): return lax.ppermute(x, 'rep', [(i, (i + by) % n) for i in range(n)])  15.7 us
    all_gather x1, blocking collectives, on_device(): fresh = lax.all_gather(fresh, 'rep', axis=0, tiled=False)  14.5 us
    unnamed x30, local copies, waits for them, and re-layouts  8.57 us
  transfers between devices with their start and end apart: 9, of which 8 were waited for; matrix products, arithmetic and copies ran while one was open for 0% of the time, Pallas kernels for 4%

profile of v2, /device:TPU:24, one launch (start us, length us, event | category | flops | bytes accessed | tf_op | source)
XLA Modules:
  0.0 212.9 jit_solution(2058441811644671363)
XLA Ops:
  0.6 1.1 copy-done
  1.8 0.7 copy-done.8
  2.4 0.7 copy-done.10
  5.7 1.8 ask.1
  7.5 19.3 %all-to-all-start = ((f32[128,1,512]{2,1,0:T(1,128)}), f32[128,1,512]{2,1,0:T(1,128)S(1)}, u32[]{:S(2)}, u32[]{:S(2)}) async-start(f32[128,1,512]{2,1,0:T(1,128)} %bitcast.42), calls=%async_computation | async-start | bytes 524288 | tf_op jit(solution)/shard_map/all_to_all | solution.py:342
  26.8 0.9 copy-done.6
  27.7 2.2 %ahead.1 = (bf16[512,512]{1,0:T(8,128)(2,1)S(1)}, bf16[512,512]{1,0:T(8,128)(2,1)S(1)}, bf16[64,512]{1,0:T(8,128)(2,1)S(1)}, bf16[64,512]{1,0:T(8,128)(2,1)S(1)}...) custom-call(f32[400,512]{1,0:T(8,128)S(1)} %bitcast.20, f32[64,400]{1,0:T(8,128)S(1)} %copy-done.6, ...), custom_call_target="tpu_custom_call" | custom-call | tf_op jit(solution)/shard_map/ahead/pallas_call | solution.py:317
  29.9 18.8 %all-to-all-done = f32[128,1,512]{2,1,0:T(1,128)S(1)} async-done(((f32[128,1,512]{2,1,0:T(1,128)}), f32[128,1,512]{2,1,0:T(1,128)S(1)}, u32[]{:S(2)}, u32[]{:S(2)}) %all-to-all-start) | async-done | bytes 262176 | tf_op jit(solution)/shard_map/all_to_all | solution.py:342
  48.7 2.1 fetch.1
  50.8 6.9 %all-to-all-start.1 = ((f32[128,1,1664]{2,1,0:T(1,128)}), f32[128,1,1664]{2,1,0:T(1,128)S(1)}, u32[]{:S(2)}, u32[]{:S(2)}) async-start(f32[128,1,1664]{2,1,0:T(1,128)} %bitcast.41), calls=%async_computation.1 | async-start | bytes 1703936 | tf_op jit(solution)/shard_map/all_to_all | solution.py:342
  57.7 3.4 %collective-permute-start.2 = (f32[512,128]{1,0:T(8,128)S(1)}, f32[512,128]{1,0:T(8,128)S(1)}, u32[]{:S(2)}, u32[]{:S(2)}) collective-permute-start(f32[512,128]{1,0:T(8,128)S(1)} %bitcast.23), channel_id=1, source_target_pairs={{0,1},{1,2},{2,3},{3,0},{4,5},{5,6},{6,7},{7,4},{8,9},{9,10},{10,1... | collective-permute-start | bytes 786440 | tf_op jit(solution)/shard_map/ppermute | solution.py:348
  61.1 4.6 %collective-permute-start.1 = (f32[512,128]{1,0:T(8,128)S(1)}, f32[512,128]{1,0:T(8,128)S(1)}, u32[]{:S(2)}, u32[]{:S(2)}) collective-permute-start(f32[512,128]{1,0:T(8,128)S(1)} %bitcast.24), channel_id=1, source_target_pairs={{0,2},{1,3},{2,0},{3,1},{4,6},{5,7},{6,4},{7,5},{8,10},{9,11},{10,... | collective-permute-start | bytes 786440 | tf_op jit(solution)/shard_map/ppermute | solution.py:348
  65.7 3.3 %collective-permute-start = (f32[512,128]{1,0:T(8,128)S(1)}, f32[512,128]{1,0:T(8,128)S(1)}, u32[]{:S(2)}, u32[]{:S(2)}) collective-permute-start(f32[512,128]{1,0:T(8,128)S(1)} %bitcast.25), channel_id=1, source_target_pairs={{0,3},{1,0},{2,1},{3,2},{4,7},{5,4},{6,5},{7,6},{8,11},{9,8},{10,9... | collective-permute-start | bytes 786440 | tf_op jit(solution)/shard_map/ppermute | solution.py:348
  69.1 6.6 %collective-permute-done.1.refs_4_ = f32[512,128]{1,0:T(8,128)S(1)} collective-permute-done((f32[512,128]{1,0:T(8,128)S(1)}, f32[512,128]{1,0:T(8,128)S(1)}, u32[]{:S(2)}, u32[]{:S(2)}) %collective-permute-start.1) | collective-permute-done | bytes 262176 | tf_op jit(solution)/shard_map/ppermute | solution.py:348
  75.7 1.5 collective-permute-done.refs_3_
  77.2 5.1 %negatives.1 = (f32[256,512]{1,0:T(8,128)}, f32[256,512]{1,0:T(8,128)}, f32[256,512]{1,0:T(8,128)}, f32[128,512]{1,0:T(8,128)}, f32[128,512]{1,0:T(8,128)S(1)}, ...) custom-call(f32[512,128]{1,0:T(8,128)S(1)} %bitcast.26, f32[512,512]{1,0:T(8,128)S(1)} %get-tuple-element.36.rows, ...), custom_call_target="tpu_custom_call" | custom-call | tf_op jit(solution)/shard_map/negatives/pallas_call | solution.py:317
  82.3 4.3 %collective-permute-start.3 = (f32[128,512]{1,0:T(8,128)S(1)}, f32[128,512]{1,0:T(8,128)S(1)}, u32[]{:S(2)}, u32[]{:S(2)}) collective-permute-start(f32[128,512]{1,0:T(8,128)S(1)} %get-tuple-element.38), channel_id=1, source_target_pairs={{0,1},{1,2},{2,3},{3,0},{4,5},{5,6},{6,7},{7,4},{8,9},{9,10},{10,1... | collective-permute-start | bytes 786440 | tf_op jit(solution)/shard_map/ppermute | solution.py:348
  86.6 3.6 %collective-permute-start.4 = (f32[128,512]{1,0:T(8,128)S(1)}, f32[128,512]{1,0:T(8,128)S(1)}, u32[]{:S(2)}, u32[]{:S(2)}) collective-permute-start(f32[128,512]{1,0:T(8,128)S(1)} %get-tuple-element.39), channel_id=1, source_target_pairs={{0,2},{1,3},{2,0},{3,1},{4,6},{5,7},{6,4},{7,5},{8,10},{9,11},{10,... | collective-permute-start | bytes 786440 | tf_op jit(solution)/shard_map/ppermute | solution.py:348
  90.3 3.5 %collective-permute-start.5 = (f32[128,512]{1,0:T(8,128)S(1)}, f32[128,512]{1,0:T(8,128)S(1)}, u32[]{:S(2)}, u32[]{:S(2)}) collective-permute-start(f32[128,512]{1,0:T(8,128)S(1)} %get-tuple-element.40), channel_id=1, source_target_pairs={{0,3},{1,0},{2,1},{3,2},{4,7},{5,4},{6,5},{7,6},{8,11},{9,8},{10,9... | collective-permute-start | bytes 786440 | tf_op jit(solution)/shard_map/ppermute | solution.py:348
  93.7 6.2 %collective-permute-done.4.sum2 = f32[128,512]{1,0:T(8,128)S(1)} collective-permute-done((f32[128,512]{1,0:T(8,128)S(1)}, f32[128,512]{1,0:T(8,128)S(1)}, u32[]{:S(2)}, u32[]{:S(2)}) %collective-permute-start.4) | collective-permute-done | bytes 262176 | tf_op jit(solution)/shard_map/ppermute | solution.py:348
  99.9 1.3 collective-permute-done.5.sum3
  101.2 2.9 %all-to-all-done.1 = f32[128,1,1664]{2,1,0:T(1,128)S(1)} async-done(((f32[128,1,1664]{2,1,0:T(1,128)}), f32[128,1,1664]{2,1,0:T(1,128)S(1)}, u32[]{:S(2)}, u32[]{:S(2)}) %all-to-all-start.1) | async-done | bytes 852000 | tf_op jit(solution)/shard_map/all_to_all | solution.py:342
  104.2 3.3 %edge.1 = (f32[2048,128]{1,0:T(8,128)}, f32[8,128]{1,0:T(8,128)}) custom-call(f32[1664,128]{1,0:T(8,128)S(1)} %bitcast.30, bf16[256,256]{1,0:T(8,128)(2,1)} %get-tuple-element.34.same, bf16[256,256]{1,0:T(8,128)(2,1)} %get-tuple-element.35.same_t, f32[128,128]{1,0:T(8,128)} %get-tuple-element.27.head_edge, f32[128,512]{1,0:T(8,128)} %get-tuple-element.37.sum0, ...), custom_call_target="tpu_custom_call" | custom-call | tf_op jit(solution)/shard_map/edge/pallas_call | solution.py:317
  107.5 13.3 %all-to-all-start.2 = ((f32[128,1,2048]{2,1,0:T(1,128)}), f32[128,1,2048]{2,1,0:T(1,128)S(1)}, u32[]{:S(2)}, u32[]{:S(2)}) async-start(f32[128,1,2048]{2,1,0:T(1,128)} %bitcast.40), calls=%async_computation.2 | async-start | bytes 2097152 | tf_op jit(solution)/shard_map/all_to_all | solution.py:342
  120.8 1.8 place.1
  122.6 1.2 copy-done.2
  123.8 51.6 %all-to-all-done.2 = f32[128,1,2048]{2,1,0:T(1,128)S(1)} async-done(((f32[128,1,2048]{2,1,0:T(1,128)}), f32[128,1,2048]{2,1,0:T(1,128)S(1)}, u32[]{:S(2)}, u32[]{:S(2)}) %all-to-all-start.2) | async-done | bytes 1048608 | tf_op jit(solution)/shard_map/all_to_all | solution.py:342
  175.4 1.4 copy-done.3
  176.8 2.3 %scatter.1 = f32[1664,128]{1,0:T(8,128)} custom-call(f32[2048,128]{1,0:T(8,128)S(1)} %bitcast.29, bf16[512,640]{1,0:T(8,128)(2,1)S(1)} %get-tuple-element.46.hot, f32[768,512]{1,0:T(8,128)S(1)} %copy-done.3), custom_call_target="tpu_custom_call" | custom-call | tf_op jit(solution)/shard_map/scatter/pallas_call | solution.py:317
  179.1 18.0 %all_to_all.26 = f32[4,416,128]{2,1,0:T(8,128)S(1)} all-to-all(f32[4,416,128]{2,1,0:T(8,128)} %bitcast.39), channel_id=1, replica_groups=mesh['ent'=128,'rep'=4] {'rep'}, dimensions={0} | all-to-all | bytes 1703936 | tf_op jit(solution)/shard_map/all_to_all | solution.py:428
  197.4 14.5 %all-gather = f32[1632,128]{1,0:T(8,128)S(1)} all-gather(f32[408,128]{1,0:T(8,128)S(1)} %update.1), channel_id=2, replica_groups=mesh['ent'=128,'rep'=4] {'rep'}, dimensions={0}, use_global_device_ids=true | all-gather | bytes 1044480 | tf_op jit(solution)/shard_map/all_gather | solution.py:437
  211.9 1.0 join.1
  (27 shorter events, 3.0 us)
Async XLA Ops:
  0.6 1.1 copy-start
  1.8 0.7 copy-start.8
  2.4 0.7 copy-start.10
  3.1 0.7 copy-start.11
  3.7 0.7 copy-start.12
  4.4 0.7 copy-start.13
  5.1 0.7 copy-start.14
  5.7 21.1 %copy-start.1 = (f32[512,400]{0,1:T(8,128)S(1)}, f32[512,400]{0,1:T(8,128)}, u32[]{:S(2)}) copy-start(f32[512,400]{0,1:T(8,128)} %param.9) | copy-start | bytes 2457604
  7.5 41.2 %all-to-all-start = ((f32[128,1,512]{2,1,0:T(1,128)}), f32[128,1,512]{2,1,0:T(1,128)S(1)}, u32[]{:S(2)}, u32[]{:S(2)}) async-start(f32[128,1,512]{2,1,0:T(1,128)} %bitcast.42), calls=%async_computation | async-start | bytes 524288 | tf_op jit(solution)/shard_map/all_to_all | solution.py:342
  26.8 0.9 copy-start.6
  29.9 20.9 %copy-start.4 = (bf16[64,512]{1,0:T(8,128)(2,1)}, bf16[64,512]{1,0:T(8,128)(2,1)S(1)}, u32[]{:S(2)}) copy-start(bf16[64,512]{1,0:T(8,128)(2,1)S(1)} %get-tuple-element.31.refs_2_.refs_0_) | copy-start | bytes 196612
  29.9 20.9 %copy-start.5 = (bf16[64,512]{1,0:T(8,128)(2,1)}, bf16[64,512]{1,0:T(8,128)(2,1)S(1)}, u32[]{:S(2)}) copy-start(bf16[64,512]{1,0:T(8,128)(2,1)S(1)} %get-tuple-element.32.refs_3_.refs_1_) | copy-start | bytes 196612
  50.8 53.4 %all-to-all-start.1 = ((f32[128,1,1664]{2,1,0:T(1,128)}), f32[128,1,1664]{2,1,0:T(1,128)S(1)}, u32[]{:S(2)}, u32[]{:S(2)}) async-start(f32[128,1,1664]{2,1,0:T(1,128)} %bitcast.41), calls=%async_computation.1 | async-start | bytes 1703936 | tf_op jit(solution)/shard_map/all_to_all | solution.py:342
  57.7 11.5 %collective-permute-start.2 = (f32[512,128]{1,0:T(8,128)S(1)}, f32[512,128]{1,0:T(8,128)S(1)}, u32[]{:S(2)}, u32[]{:S(2)}) collective-permute-start(f32[512,128]{1,0:T(8,128)S(1)} %bitcast.23), channel_id=1, source_target_pairs={{0,1},{1,2},{2,3},{3,0},{4,5},{5,6},{6,7},{7,4},{8,9},{9,10},{10,1... | collective-permute-start | bytes 786440 | tf_op jit(solution)/shard_map/ppermute | solution.py:348
  61.1 14.7 %collective-permute-start.1 = (f32[512,128]{1,0:T(8,128)S(1)}, f32[512,128]{1,0:T(8,128)S(1)}, u32[]{:S(2)}, u32[]{:S(2)}) collective-permute-start(f32[512,128]{1,0:T(8,128)S(1)} %bitcast.24), channel_id=1, source_target_pairs={{0,2},{1,3},{2,0},{3,1},{4,6},{5,7},{6,4},{7,5},{8,10},{9,11},{10,... | collective-permute-start | bytes 786440 | tf_op jit(solution)/shard_map/ppermute | solution.py:348
  65.7 11.5 %collective-permute-start = (f32[512,128]{1,0:T(8,128)S(1)}, f32[512,128]{1,0:T(8,128)S(1)}, u32[]{:S(2)}, u32[]{:S(2)}) collective-permute-start(f32[512,128]{1,0:T(8,128)S(1)} %bitcast.25), channel_id=1, source_target_pairs={{0,3},{1,0},{2,1},{3,2},{4,7},{5,4},{6,5},{7,6},{8,11},{9,8},{10,9... | collective-permute-start | bytes 786440 | tf_op jit(solution)/shard_map/ppermute | solution.py:348
  82.3 11.4 %collective-permute-start.3 = (f32[128,512]{1,0:T(8,128)S(1)}, f32[128,512]{1,0:T(8,128)S(1)}, u32[]{:S(2)}, u32[]{:S(2)}) collective-permute-start(f32[128,512]{1,0:T(8,128)S(1)} %get-tuple-element.38), channel_id=1, source_target_pairs={{0,1},{1,2},{2,3},{3,0},{4,5},{5,6},{6,7},{7,4},{8,9},{9,10},{10,1... | collective-permute-start | bytes 786440 | tf_op jit(solution)/shard_map/ppermute | solution.py:348
  86.6 13.3 %collective-permute-start.4 = (f32[128,512]{1,0:T(8,128)S(1)}, f32[128,512]{1,0:T(8,128)S(1)}, u32[]{:S(2)}, u32[]{:S(2)}) collective-permute-start(f32[128,512]{1,0:T(8,128)S(1)} %get-tuple-element.39), channel_id=1, source_target_pairs={{0,2},{1,3},{2,0},{3,1},{4,6},{5,7},{6,4},{7,5},{8,10},{9,11},{10,... | collective-permute-start | bytes 786440 | tf_op jit(solution)/shard_map/ppermute | solution.py:348
  90.3 11.0 %collective-permute-start.5 = (f32[128,512]{1,0:T(8,128)S(1)}, f32[128,512]{1,0:T(8,128)S(1)}, u32[]{:S(2)}, u32[]{:S(2)}) collective-permute-start(f32[128,512]{1,0:T(8,128)S(1)} %get-tuple-element.40), channel_id=1, source_target_pairs={{0,3},{1,0},{2,1},{3,2},{4,7},{5,4},{6,5},{7,6},{8,11},{9,8},{10,9... | collective-permute-start | bytes 786440 | tf_op jit(solution)/shard_map/ppermute | solution.py:348
  107.5 13.3 %copy-start.9 = (s32[4]{0:T(128)S(1)}, s32[4]{0:T(128)}, u32[]{:S(2)}) copy-start(s32[4]{0:T(128)} %neg_rows.3) | copy-start | bytes 52
  107.5 67.9 %all-to-all-start.2 = ((f32[128,1,2048]{2,1,0:T(1,128)}), f32[128,1,2048]{2,1,0:T(1,128)S(1)}, u32[]{:S(2)}, u32[]{:S(2)}) async-start(f32[128,1,2048]{2,1,0:T(1,128)} %bitcast.40), calls=%async_computation.2 | async-start | bytes 2097152 | tf_op jit(solution)/shard_map/all_to_all | solution.py:342
  122.6 1.2 copy-start.2
  175.4 1.4 copy-start.3
  179.1 18.0 %copy-start.7 = (f32[512]{0:T(512)S(1)}, f32[512]{0:T(512)}, u32[]{:S(2)}) copy-start(f32[512]{0:T(512)} %param.10) | copy-start | bytes 6148

commit v3 on v2

--- a/solution.py
+++ b/solution.py
@@ -16,9 +16,9 @@
 NT = (((1,), (1,)), ((), ()))
 TN = (((0,), (0,)), ((), ()))
 PIECES = 2
-TILES1 = 4
+TILES1 = 2
 TILES2 = 13
-TILES3 = 16
+TILES3 = 15
 GROUP = 32
 
 
@@ -79,16 +79,16 @@
         moved = pltpu.roll(rest, shift, 1) if shift else rest
         tail = jnp.where((at >= 8 * i) & (at < 8 * i + 8), moved, tail)
     for i in range(0, len(halves), 2):
-        low, high = halves[i][:, LANE:], halves[i + 1][:, LANE:]
-        ref[pl.ds(base + len(halves) + i // 2, n, stride=tiles), :] = jnp.where(
-            at < 64, low, pltpu.roll(high, 64, 1)
-        )
-    ref[pl.ds(base + len(halves) * 3 // 2, n, stride=tiles), :] = tail
+        pair = halves[i][:, LANE:]
+        if i + 1 < len(halves):
+            pair = jnp.where(at < 64, pair, pltpu.roll(halves[i + 1][:, LANE:], 64, 1))
+        ref[pl.ds(base + len(halves) + i // 2, n, stride=tiles), :] = pair
+    ref[pl.ds(base + tiles - 1, n, stride=tiles), :] = tail
 
 
 def unpack(ref, tiles, count, n):
     at = lanes((n, LANE))
-    tail = ref[pl.ds(count * 3 // 2, n, stride=tiles), :]
+    tail = ref[pl.ds(tiles - 1, n, stride=tiles), :]
     out = []
     for i in range(count):
         full = ref[pl.ds(i, n, stride=tiles), :]
@@ -102,8 +102,16 @@
     return out
 
 
-def ask_kernel(rep, neg_rows, head_owner, head_row, rel, tail_owner, tail_row, table_t, send, head_edge, tail_edge):
-    n = LANE
+def ask_kernel(
+    rep, neg_rows, head_owner, head_row, rel, tail_owner, tail_row, table_t,
+    send, head_edge, tail_edge, block, done,
+):
+    n = LANE
+    neg_at = neg_rows[rep[0]]
+    copy = pltpu.make_async_copy(
+        table_t.at[:, pl.ds(pl.multiple_of(neg_at // n * n, n), n)], block, done
+    )
+    copy.start()
     sub = lax.broadcasted_iota(jnp.int32, (n, n), 0)
     lane = lanes((n, n))
 
@@ -132,19 +140,19 @@
     head_edge[...] = slots(head_owner, head_row)
     tail_edge[...] = slots(tail_owner, tail_row)
 
-    neg_at = neg_rows[rep[0]]
-    block = table_t[:, pl.ds(pl.multiple_of(neg_at // n * n, n), n)]
+    copy.wait()
     pad = jnp.zeros((56, n), f32)
+    line = []
     for i in range(2):
         half = jnp.concatenate([block[200 * i : 200 * i + 200, :], pad], 0).T
         picked = lax.broadcasted_iota(jnp.int32, (n, 256), 0) == neg_at % n
-        line = jnp.sum(jnp.where(picked, half, 0.0), 0, keepdims=True)
-        send[pl.ds(2 * i, n, stride=TILES1), :] = wide(line[:, :n])
-        tile = wide(line[:, n:])
-        if i == 0:
-            for j, col in enumerate(columns):
-                tile = jnp.where(lane == 72 + j, col, tile)
-        send[pl.ds(2 * i + 1, n, stride=TILES1), :] = tile
+        line.append(jnp.sum(jnp.where(picked, half, 0.0), 0, keepdims=True))
+    even = sub % 2 == 0
+    send[pl.ds(0, n, stride=TILES1), :] = jnp.where(even, wide(line[0][:, :n]), wide(line[1][:, :n]))
+    tile = jnp.where(even, wide(line[0][:, n:]), wide(line[1][:, n:]))
+    for j, col in enumerate(columns):
+        tile = jnp.where(lane == 72 + j, col, tile)
+    send[pl.ds(1, n, stride=TILES1), :] = tile
 
 
 def ahead_kernel(table_t, relations, head_edge, tail_edge, *outs):
@@ -200,18 +208,29 @@
     pack(send, TILES2, halves)
 
 
-def negatives_kernel(recv, rows, *refs):
+def join_rows_kernel(*refs):
+    *ins, out = refs
+    for i, ref in enumerate(ins):
+        out[i * ref.shape[0] : (i + 1) * ref.shape[0], :] = ref[...]
+
+
+def negatives_kernel(odd, recv, rows, *refs):
     n = LANE
     rel = refs[:PIECES]
-    *negs, near, far, rels, out0, out1, out2, out3 = refs[PIECES:]
+    mine, other, query_side, tail_side, rels, keep, give = refs[PIECES:]
     tile = recv[pl.ds(1, n, stride=TILES1), :]
-    keep = lanes((n, LANE)) < 72
-    tiles = []
-    for ref in negs:
-        got = [ref[pl.ds(i, n, stride=TILES1), :] for i in range(4)]
-        got[1] = jnp.where(keep, got[1], 0.0)
-        tiles.append(jnp.concatenate(got, 1))
-    negs = jnp.concatenate(tiles, 0)
+    mask = lanes((n, LANE)) < 72
+
+    def half(ref, base):
+        low = ref[pl.ds(base, n, stride=TILES1), :]
+        high = jnp.where(mask, ref[pl.ds(base + 1, n, stride=TILES1), :], 0.0)
+        return jnp.concatenate([low, high], 1)
+
+    flip = odd[0] > 0
+    own, got = (
+        jnp.concatenate([half(ref, TILES1 * n * j) for j in range(4)], 0) for ref in (mine, other)
+    )
+    negs = jnp.concatenate([jnp.where(flip, got, own), jnp.where(flip, own, got)], 1)
     weight = 1.0 / math.sqrt(512.0)
     total = None
     for side in range(2):
@@ -225,14 +244,21 @@
         coef = jnp.where(valid >= 0.0, sigmoid(scores) * weight, 0.0)
         back = dot3(coef, negs, NN)
         if side:
-            far[...] = jnp.concatenate(cmul(split(back), rv), 1)
+            tail_side[...] = jnp.concatenate(cmul(split(back), rv), 1)
         else:
-            near[...] = back
+            query_side[...] = back
             rels[...] = jnp.concatenate(rv, 1)
         grad = dot3(coef, x, TN)
         total = grad if total is None else total + grad
-    for i, ref in enumerate((out0, out1, out2, out3)):
-        ref[...] = total[i * n : (i + 1) * n, :]
+    re, im = split(total)
+    keep[...] = jnp.where(flip, im, re)
+    give[...] = jnp.where(flip, re, im)
+
+
+def fold_kernel(keep, got, *outs):
+    for i, ref in enumerate(outs):
+        at = pl.ds(i * LANE, LANE)
+        ref[...] = keep[at, :] + got[at, :]
 
 
 def edge_kernel(recv, same, same_t, head_edge, sum0, sum1, sum2, sum3, send, token):
@@ -252,9 +278,9 @@
     to_tail = pick(same_t[...], parts(coef * query, PIECES), NN)
     neg = sum0[...] + sum1[...] + (sum2[...] + sum3[...])
     out = []
-    for block in (to_head[:n], to_head[n:], to_tail[:n], to_tail[n:], neg):
-        out += [block[:, :256], block[:, 256:]]
-    pack(send, TILES3, out)
+    for block in (to_head[:n], to_head[n:], to_tail[:n], to_tail[n:]):
+        out += split(block)
+    pack(send, TILES3, out + [neg])
     token[...] = neg[0:8, 0:128]
 
 
@@ -273,7 +299,9 @@
 
 def scatter_kernel(recv, hot, side, out):
     n = LANE
-    halves = unpack(recv, TILES3, 10, n)
+    halves = unpack(recv, TILES3, 9, n)
+    even = lax.broadcasted_iota(jnp.int32, (n, 256), 0) % 2 == 0
+    halves = halves[:8] + [jnp.where(even, halves[8], 0.0), jnp.where(even, 0.0, halves[8])]
     blocks = [jnp.concatenate(halves[i : i + 2], 1) for i in range(0, 10, 2)]
     head = split(jnp.concatenate(blocks[0:2], 0) + side[0 : 2 * n, :])
     head = jnp.concatenate(cmul(head, conj(split(side[4 * n :, :]))), 1)
@@ -312,7 +340,7 @@
         state_new[:, q * LANE : (q + 1) * LANE] = parts_in[q, 400:401, :]
 
 
-def call(kernel, outs, args, scalars=(), name=None, scratch=()):
+def call(kernel, outs, args, scalars=(), name=None, scratch=(), whole=0):
     space = pl.BlockSpec(memory_space=pltpu.VMEM)
     return pl.pallas_call(
         kernel,
@@ -320,7 +348,9 @@
             (pltpu.VMEM if near else pltpu.HBM)(shape, kind)
             for shape, kind, near in outs
         ],
-        in_specs=[pl.BlockSpec(memory_space=pltpu.SMEM)] * len(scalars) + [space] * len(args),
+        in_specs=[pl.BlockSpec(memory_space=pltpu.SMEM)] * len(scalars)
+        + [space] * (len(args) - whole)
+        + [pl.BlockSpec(memory_space=pltpu.HBM)] * whole,
         out_specs=[space] * len(outs),
         scratch_shapes=list(scratch),
         compiler_params=pltpu.CompilerParams(vmem_limit_bytes=24 << 20),
@@ -346,6 +376,10 @@
 def shift(x, by):
     n = lax.axis_size("rep")
     return lax.ppermute(x, "rep", [(i, (i + by) % n) for i in range(n)])
+
+
+def swap_cores(x):
+    return lax.ppermute(x, "ent", [(i, i ^ 1) for i in range(lax.axis_size("ent"))])
 
 
 def on_device(
@@ -360,11 +394,13 @@
     relations,
 ):
     rep = lax.axis_index("rep").reshape(1).astype(jnp.int32)
+    odd = (lax.axis_index("ent") & 1).reshape(1).astype(jnp.int32)
     table_t = entity_table.T
+    neg_rows = far(neg_rows)
     n = LANE
 
     def line(x):
-        return x.reshape(1, n)
+        return far(x.reshape(1, n))
 
     send1, head_edge, tail_edge = call(
         ask_kernel,
@@ -375,10 +411,12 @@
             line(relation_ids),
             line(tail_owner),
             line(tail_row),
-            table_t,
+            far(table_t),
         ),
         (rep, neg_rows),
         "ask",
+        (pltpu.VMEM((400, n), f32), pltpu.SemaphoreType.DMA),
+        1,
     )
     recv1 = exchange(send1, "ent", TILES1)
     *pieces, same, same_t = call(
@@ -397,12 +435,23 @@
         name="fetch",
     )
     recv2 = exchange(send2, "ent", TILES2)
-    negs = [recv1] + [shift(recv1, -j) for j in (1, 2, 3)]
-    query_side, tail_side, rels, *owned = call(
+    mine = [recv1] + [shift(recv1, -j) for j in (1, 2, 3)]
+    (mine,) = call(
+        join_rows_kernel, [((4 * TILES1 * n, n), f32, True)], list(map(near, mine)), name="join_rows"
+    )
+    other = swap_cores(mine)
+    query_side, tail_side, rels, keep, give = call(
         negatives_kernel,
-        [((2 * n, 512), f32, False)] * 3 + [((n, 512), f32, i > 0) for i in range(4)],
-        (near(recv1), near(rows), *map(far, rel_pieces), *map(near, negs)),
-        name="negatives",
+        [((2 * n, 512), f32, False)] * 3 + [((4 * n, 256), f32, True)] * 2,
+        (near(recv1), near(rows), *map(far, rel_pieces), near(mine), near(other)),
+        (odd,),
+        "negatives",
+    )
+    owned = call(
+        fold_kernel,
+        [((n, 256), f32, i > 0) for i in range(4)],
+        (near(keep), near(swap_cores(give))),
+        name="fold",
     )
     sums = [owned[0]] + [shift(owned[j], j) for j in (1, 2, 3)]
     send3, token = call(
@@ -414,7 +463,7 @@
     recv3 = exchange(send3, "ent", TILES3)
     side, hot = call(
         place_kernel,
-        [((6 * n, 512), f32, True), ((4 * n, 5 * n), bf16, True)],
+        [((6 * n, 512), f32, False), ((4 * n, 5 * n), bf16, True)],
         (recv1, far(token), far(query_side), far(tail_side), far(rels)),
         (rep, neg_rows),
         "place",
@@ -422,7 +471,7 @@
     (grads,) = call(
         scatter_kernel,
         [((4 * TILES2 * GROUP, n), f32, False)],
-        (near(recv3), near(hot), near(side)),
+        (near(recv3), near(hot), far(side)),
         name="scatter",
     )
     grads = lax.all_to_all(grads, "rep", split_axis=0, concat_axis=0, tiled=True)

time: 215 us -> 200 us (0.930)
  waiting for transfers between devices: 89 us -> 76.9 us
  local copies, waits for them, and re-layouts: 8.57 us -> 0.91 us
  Pallas kernels: 19.8 us -> 23.5 us
  starting transfers between devices: 62.3 us -> 65.2 us
    all_to_all x3, waiting for transfers between devices: 73.3 us -> 65.3 us  [exchange(): x = lax.all_to_all(x, axis, split_axis=0, concat_axis=0, tiled=True)]
    ppermute x6, waiting for transfers between devices: 15.7 us -> 7.9 us  [shift(): return lax.ppermute(x, 'rep', [(i, (i + by) % n) for i in range(n)])]
    unnamed x30 -> x10, local copies, waits for them, and re-layouts: 8.57 us -> 0.91 us
    ppermute x0 -> x2, starting transfers between devices: none -> 3.95 us  [swap_cores(): lax.ppermute(x, 'ent', [(i, i ^ 1) for i in range(lax.axis_size('ent'))])]
    ppermute x0 -> x2, waiting for transfers between devices: none -> 3.76 us  [swap_cores(): lax.ppermute(x, 'ent', [(i, i ^ 1) for i in range(lax.axis_size('ent'))])]
    pallas_call x9 -> x11, Pallas kernels: 19.8 us -> 23.5 us  [call(): pl.pallas_call(kernel, out_shape=[(pltpu.VMEM if near else pltpu.HBM)(sha...]
  transfers between devices with their start and end apart: 9 -> 11, of which waited for: 8 -> 9; matrix products, arithmetic and copies ran while one was open for 0% -> 0% of each run, Pallas kernels for 4% -> 5%
where the time goes in v3:
time: 200 us; the launch traced here: 199 us
  waiting for transfers between devices  76.9 us (38%)
  starting transfers between devices  65.2 us (33%)
  blocking collectives  31.5 us (16%)
  Pallas kernels  23.5 us (12%)
    all_to_all x3, waiting for transfers between devices, exchange(): x = lax.all_to_all(x, axis, split_axis=0, concat_axis=0, tiled=True)  65.3 us
    all_to_all x3, starting transfers between devices, exchange(): x = lax.all_to_all(x, axis, split_axis=0, concat_axis=0, tiled=True)  39.4 us
    pallas_call x11, Pallas kernels, call(): pl.pallas_call(kernel, out_shape=[(pltpu.VMEM if near else pltpu.HBM)(sha...  23.5 us
    ppermute x6, starting transfers between devices, shift(): return lax.ppermute(x, 'rep', [(i, (i + by) % n) for i in range(n)])  21.8 us
    all_to_all x1, blocking collectives, on_device(): lax.all_to_all(grads, 'rep', split_axis=0, concat_axis=0, tiled=True)  17.2 us
    all_gather x1, blocking collectives, on_device(): fresh = lax.all_gather(fresh, 'rep', axis=0, tiled=False)  14.4 us
    ppermute x6, waiting for transfers between devices, shift(): return lax.ppermute(x, 'rep', [(i, (i + by) % n) for i in range(n)])  7.9 us
  transfers between devices with their start and end apart: 11, of which 9 were waited for; matrix products, arithmetic and copies ran while one was open for 0% of the time, Pallas kernels for 5%

profile of v3, /device:TPU:24, one launch (start us, length us, event | category | flops | bytes accessed | tf_op | source)
XLA Modules:
  0.0 198.8 jit_solution(1330079035054163953)
XLA Ops:
  0.6 2.6 %ask.1 = (f32[256,128]{1,0:T(8,128)}, f32[128,128]{1,0:T(8,128)}, f32[128,128]{1,0:T(8,128)}) custom-call(s32[1]{0:T(128)} %bitcast.rep, s32[4]{0:T(128)} %neg_rows.3, s32[1,128]{1,0:T(1,128)} %bitcast.39, s32[1,128]{1,0:T(1,128)} %bitcast.40, s32[1,128]{1,0:T(1,128)} %bitcast.41, s32[1,128]{1,0:T(1,128)} %bitcast.42, s32[1,128]{1,0:T(1,128)} %bitcast.43, ...), custom_call_target="tpu_custom_call" | custom-call | tf_op jit(solution)/shard_map/ask/pallas_call | solution.py:345
  3.2 19.3 %all-to-all-start = ((f32[128,1,256]{2,1,0:T(1,128)}), f32[128,1,256]{2,1,0:T(1,128)S(1)}, u32[]{:S(2)}, u32[]{:S(2)}) async-start(f32[128,1,256]{2,1,0:T(1,128)} %bitcast.38), calls=%async_computation | async-start | bytes 262144 | tf_op jit(solution)/shard_map/all_to_all | solution.py:372
  22.6 0.9 copy-done.3
  23.5 2.2 %ahead.1 = (bf16[512,512]{1,0:T(8,128)(2,1)S(1)}, bf16[512,512]{1,0:T(8,128)(2,1)S(1)}, bf16[64,512]{1,0:T(8,128)(2,1)S(1)}, bf16[64,512]{1,0:T(8,128)(2,1)S(1)}...) custom-call(f32[400,512]{1,0:T(8,128)S(1)} %bitcast.21, f32[64,400]{1,0:T(8,128)S(1)} %copy-done.3, ...), custom_call_target="tpu_custom_call" | custom-call | tf_op jit(solution)/shard_map/ahead/pallas_call | solution.py:345
  25.7 13.0 %all-to-all-done = f32[128,1,256]{2,1,0:T(1,128)S(1)} async-done(((f32[128,1,256]{2,1,0:T(1,128)}), f32[128,1,256]{2,1,0:T(1,128)S(1)}, u32[]{:S(2)}, u32[]{:S(2)}) %all-to-all-start) | async-done | bytes 131104 | tf_op jit(solution)/shard_map/all_to_all | solution.py:372
  38.7 2.1 %fetch.1 = (f32[1664,128]{1,0:T(8,128)}, f32[512,512]{1,0:T(8,128)S(1)}) custom-call(f32[256,128]{1,0:T(8,128)S(1)} %bitcast.27, bf16[512,512]{1,0:T(8,128)(2,1)S(1)} %get-tuple-element.31.refs_0_, bf16[512,512]{1,0:T(8,128)(2,1)S(1)} %get-tuple-element.32.refs_1_, bf16[64,512]{1,0:T(8,128)(2,1)S(1)} %get-tuple-element.33.refs_2_.refs_0_, ...), custom_call_target="tpu_custom_call" | custom-call | tf_op jit(solution)/shard_map/fetch/pallas_call | solution.py:345
  40.8 7.1 %all-to-all-start.1 = ((f32[128,1,1664]{2,1,0:T(1,128)}), f32[128,1,1664]{2,1,0:T(1,128)S(1)}, u32[]{:S(2)}, u32[]{:S(2)}) async-start(f32[128,1,1664]{2,1,0:T(1,128)} %bitcast.37), calls=%async_computation.1 | async-start | bytes 1703936 | tf_op jit(solution)/shard_map/all_to_all | solution.py:372
  47.8 3.4 %collective-permute-start.2 = (f32[256,128]{1,0:T(8,128)S(1)}, f32[256,128]{1,0:T(8,128)S(1)}, u32[]{:S(2)}, u32[]{:S(2)}) collective-permute-start(f32[256,128]{1,0:T(8,128)S(1)} %bitcast.28), channel_id=1, source_target_pairs={{0,1},{1,2},{2,3},{3,0},{4,5},{5,6},{6,7},{7,4},{8,9},{9,10},{10,1... | collective-permute-start | bytes 393224 | tf_op jit(solution)/shard_map/ppermute | solution.py:378
  51.3 4.6 %collective-permute-start.1 = (f32[256,128]{1,0:T(8,128)S(1)}, f32[256,128]{1,0:T(8,128)S(1)}, u32[]{:S(2)}, u32[]{:S(2)}) collective-permute-start(f32[256,128]{1,0:T(8,128)S(1)} %bitcast.29), channel_id=1, source_target_pairs={{0,2},{1,3},{2,0},{3,1},{4,6},{5,7},{6,4},{7,5},{8,10},{9,11},{10,... | collective-permute-start | bytes 393224 | tf_op jit(solution)/shard_map/ppermute | solution.py:378
  55.9 3.3 %collective-permute-start = (f32[256,128]{1,0:T(8,128)S(1)}, f32[256,128]{1,0:T(8,128)S(1)}, u32[]{:S(2)}, u32[]{:S(2)}) collective-permute-start(f32[256,128]{1,0:T(8,128)S(1)} %bitcast.30), channel_id=1, source_target_pairs={{0,3},{1,0},{2,1},{3,2},{4,7},{5,4},{6,5},{7,6},{8,11},{9,8},{10,9... | collective-permute-start | bytes 393224 | tf_op jit(solution)/shard_map/ppermute | solution.py:378
  59.3 1.0 collective-permute-done.1.refs_2_
  60.3 2.5 %collective-permute-done.refs_1_ = f32[256,128]{1,0:T(8,128)S(1)} collective-permute-done((f32[256,128]{1,0:T(8,128)S(1)}, f32[256,128]{1,0:T(8,128)S(1)}, u32[]{:S(2)}, u32[]{:S(2)}) %collective-permute-start) | collective-permute-done | bytes 131104 | tf_op jit(solution)/shard_map/ppermute | solution.py:378
  62.8 1.9 collective-permute-start.3
  64.8 2.0 %collective-permute-done.3.refs_3_ = f32[1024,128]{1,0:T(8,128)} collective-permute-done((f32[1024,128]{1,0:T(8,128)S(1)}, f32[1024,128]{1,0:T(8,128)}, u32[]{:S(2)}, u32[]{:S(2)}) %collective-permute-start.3) | collective-permute-done | bytes 524320 | tf_op jit(solution)/shard_map/ppermute | solution.py:382
  66.8 5.2 %negatives.1 = (f32[256,512]{1,0:T(8,128)}, f32[256,512]{1,0:T(8,128)}, f32[256,512]{1,0:T(8,128)}, f32[512,256]{1,0:T(8,128)S(1)}, f32[512,256]{1,0:T(8,128)S(1)}) custom-call(s32[1]{0:T(128)} %bitcast.11.odd, f32[256,128]{1,0:T(8,128)S(1)} %bitcast.32, f32[512,512]{1,0:T(8,128)S(1)} %get-tuple-element.38.rows, bf16[64,512]{1,0:T(8,128)(2,1)} %copy-done.1, ...), custom_call_target="tpu_custom_call" | custom-call | tf_op jit(solution)/shard_map/negatives/pallas_call | solution.py:345
  72.0 2.0 %collective-permute-start.4 = (f32[512,256]{1,0:T(8,128)S(1)}, f32[512,256]{1,0:T(8,128)S(1)}, u32[]{:S(2)}, u32[]{:S(2)}) collective-permute-start(f32[512,256]{1,0:T(8,128)S(1)} %get-tuple-element.40), channel_id=1, source_target_pairs={{0,4},{4,0},{8,12},{12,8},{16,20},{20,16},{24,28},{28,24},{32,36},... | collective-permute-start | bytes 1572872 | tf_op jit(solution)/shard_map/ppermute | solution.py:382
  74.0 1.8 collective-permute-done.4.got
  75.8 0.7 fold.1
  76.5 3.3 %collective-permute-start.5 = (f32[128,256]{1,0:T(8,128)S(1)}, f32[128,256]{1,0:T(8,128)S(1)}, u32[]{:S(2)}, u32[]{:S(2)}) collective-permute-start(f32[128,256]{1,0:T(8,128)S(1)} %get-tuple-element.42), channel_id=1, source_target_pairs={{0,1},{1,2},{2,3},{3,0},{4,5},{5,6},{6,7},{7,4},{8,9},{9,10},{10,1... | collective-permute-start | bytes 393224 | tf_op jit(solution)/shard_map/ppermute | solution.py:378
  79.8 4.6 %collective-permute-start.6 = (f32[128,256]{1,0:T(8,128)S(1)}, f32[128,256]{1,0:T(8,128)S(1)}, u32[]{:S(2)}, u32[]{:S(2)}) collective-permute-start(f32[128,256]{1,0:T(8,128)S(1)} %get-tuple-element.43), channel_id=1, source_target_pairs={{0,2},{1,3},{2,0},{3,1},{4,6},{5,7},{6,4},{7,5},{8,10},{9,11},{10,... | collective-permute-start | bytes 393224 | tf_op jit(solution)/shard_map/ppermute | solution.py:378
  84.4 2.5 %collective-permute-start.7 = (f32[128,256]{1,0:T(8,128)S(1)}, f32[128,256]{1,0:T(8,128)S(1)}, u32[]{:S(2)}, u32[]{:S(2)}) collective-permute-start(f32[128,256]{1,0:T(8,128)S(1)} %get-tuple-element.44), channel_id=1, source_target_pairs={{0,3},{1,0},{2,1},{3,2},{4,7},{5,4},{6,5},{7,6},{8,11},{9,8},{10,9... | collective-permute-start | bytes 393224 | tf_op jit(solution)/shard_map/ppermute | solution.py:378
  86.9 1.9 collective-permute-done.6.sum2
  88.8 2.5 %collective-permute-done.7.sum3 = f32[128,256]{1,0:T(8,128)S(1)} collective-permute-done((f32[128,256]{1,0:T(8,128)S(1)}, f32[128,256]{1,0:T(8,128)S(1)}, u32[]{:S(2)}, u32[]{:S(2)}) %collective-permute-start.7) | collective-permute-done | bytes 131104 | tf_op jit(solution)/shard_map/ppermute | solution.py:378
  91.3 3.1 %all-to-all-done.1 = f32[128,1,1664]{2,1,0:T(1,128)S(1)} async-done(((f32[128,1,1664]{2,1,0:T(1,128)}), f32[128,1,1664]{2,1,0:T(1,128)S(1)}, u32[]{:S(2)}, u32[]{:S(2)}) %all-to-all-start.1) | async-done | bytes 852000 | tf_op jit(solution)/shard_map/all_to_all | solution.py:372
  94.4 3.1 %edge.1 = (f32[1920,128]{1,0:T(8,128)}, f32[8,128]{1,0:T(8,128)}) custom-call(f32[1664,128]{1,0:T(8,128)S(1)} %bitcast.25, bf16[256,256]{1,0:T(8,128)(2,1)} %get-tuple-element.36.same, bf16[256,256]{1,0:T(8,128)(2,1)} %get-tuple-element.37.same_t, f32[128,128]{1,0:T(8,128)} %get-tuple-element.29.head_edge, f32[128,256]{1,0:T(8,128)} %get-tuple-element.41.sum0, ...), custom_call_target="tpu_custom_call" | custom-call | tf_op jit(solution)/shard_map/edge/pallas_call | solution.py:345
  97.4 13.0 %all-to-all-start.2 = ((f32[128,1,1920]{2,1,0:T(1,128)}), f32[128,1,1920]{2,1,0:T(1,128)S(1)}, u32[]{:S(2)}, u32[]{:S(2)}) async-start(f32[128,1,1920]{2,1,0:T(1,128)} %bitcast.36), calls=%async_computation.2 | async-start | bytes 1966080 | tf_op jit(solution)/shard_map/all_to_all | solution.py:372
  110.5 2.7 %place.1 = (f32[768,512]{1,0:T(8,128)}, bf16[512,640]{1,0:T(8,128)(2,1)S(1)}) custom-call(s32[1]{0:T(128)} %bitcast.rep, s32[4]{0:T(128)} %neg_rows.3, f32[256,128]{1,0:T(8,128)S(1)} %bitcast.33, f32[8,128]{1,0:T(8,128)} %get-tuple-element.46.token, f32[256,512]{1,0:T(8,128)} %get-tuple-element.47.refs_0_, f32[256,512]{1,0:T(8,128)} %get-tuple-element.48.refs_1_, ...), custom_call_target="tpu_custom_call" | custom-call | tf_op jit(solution)/shard_map/place/pallas_call | solution.py:345
  113.1 49.2 %all-to-all-done.2 = f32[128,1,1920]{2,1,0:T(1,128)S(1)} async-done(((f32[128,1,1920]{2,1,0:T(1,128)}), f32[128,1,1920]{2,1,0:T(1,128)S(1)}, u32[]{:S(2)}, u32[]{:S(2)}) %all-to-all-start.2) | async-done | bytes 983072 | tf_op jit(solution)/shard_map/all_to_all | solution.py:372
  162.4 3.6 %scatter.1 = f32[1664,128]{1,0:T(8,128)} custom-call(f32[1920,128]{1,0:T(8,128)S(1)} %bitcast.23, bf16[512,640]{1,0:T(8,128)(2,1)S(1)} %get-tuple-element.50.hot, f32[768,512]{1,0:T(8,128)} %get-tuple-element.51.side), custom_call_target="tpu_custom_call" | custom-call | tf_op jit(solution)/shard_map/scatter/pallas_call | solution.py:345
  166.0 17.2 %all_to_all.26 = f32[4,416,128]{2,1,0:T(8,128)S(1)} all-to-all(f32[4,416,128]{2,1,0:T(8,128)} %bitcast.35), channel_id=1, replica_groups=mesh['ent'=128,'rep'=4] {'rep'}, dimensions={0} | all-to-all | bytes 1703936 | tf_op jit(solution)/shard_map/all_to_all | solution.py:477
  183.4 14.4 %all-gather = f32[1632,128]{1,0:T(8,128)S(1)} all-gather(f32[408,128]{1,0:T(8,128)S(1)} %update.1), channel_id=2, replica_groups=mesh['ent'=128,'rep'=4] {'rep'}, dimensions={0}, use_global_device_ids=true | all-gather | bytes 1044480 | tf_op jit(solution)/shard_map/all_gather | solution.py:486
  197.8 1.0 join.1
  (13 shorter events, 0.4 us)
Async XLA Ops:
  0.6 21.9 %copy-start = (f32[512,400]{0,1:T(8,128)S(1)}, f32[512,400]{0,1:T(8,128)}, u32[]{:S(2)}) copy-start(f32[512,400]{0,1:T(8,128)} %param.9) | copy-start | bytes 2457604
  3.2 35.4 %all-to-all-start = ((f32[128,1,256]{2,1,0:T(1,128)}), f32[128,1,256]{2,1,0:T(1,128)S(1)}, u32[]{:S(2)}, u32[]{:S(2)}) async-start(f32[128,1,256]{2,1,0:T(1,128)} %bitcast.38), calls=%async_computation | async-start | bytes 262144 | tf_op jit(solution)/shard_map/all_to_all | solution.py:372
  22.6 0.9 copy-start.3
  25.7 37.1 %copy-start.1 = (bf16[64,512]{1,0:T(8,128)(2,1)}, bf16[64,512]{1,0:T(8,128)(2,1)S(1)}, u32[]{:S(2)}) copy-start(bf16[64,512]{1,0:T(8,128)(2,1)S(1)} %get-tuple-element.33.refs_2_.refs_0_) | copy-start | bytes 196612
  25.7 37.1 %copy-start.2 = (bf16[64,512]{1,0:T(8,128)(2,1)}, bf16[64,512]{1,0:T(8,128)(2,1)S(1)}, u32[]{:S(2)}) copy-start(bf16[64,512]{1,0:T(8,128)(2,1)S(1)} %get-tuple-element.34.refs_3_.refs_1_) | copy-start | bytes 196612
  40.8 53.6 %all-to-all-start.1 = ((f32[128,1,1664]{2,1,0:T(1,128)}), f32[128,1,1664]{2,1,0:T(1,128)S(1)}, u32[]{:S(2)}, u32[]{:S(2)}) async-start(f32[128,1,1664]{2,1,0:T(1,128)} %bitcast.37), calls=%async_computation.1 | async-start | bytes 1703936 | tf_op jit(solution)/shard_map/all_to_all | solution.py:372
  47.8 11.4 %collective-permute-start.2 = (f32[256,128]{1,0:T(8,128)S(1)}, f32[256,128]{1,0:T(8,128)S(1)}, u32[]{:S(2)}, u32[]{:S(2)}) collective-permute-start(f32[256,128]{1,0:T(8,128)S(1)} %bitcast.28), channel_id=1, source_target_pairs={{0,1},{1,2},{2,3},{3,0},{4,5},{5,6},{6,7},{7,4},{8,9},{9,10},{10,1... | collective-permute-start | bytes 393224 | tf_op jit(solution)/shard_map/ppermute | solution.py:378
  51.3 9.0 %collective-permute-start.1 = (f32[256,128]{1,0:T(8,128)S(1)}, f32[256,128]{1,0:T(8,128)S(1)}, u32[]{:S(2)}, u32[]{:S(2)}) collective-permute-start(f32[256,128]{1,0:T(8,128)S(1)} %bitcast.29), channel_id=1, source_target_pairs={{0,2},{1,3},{2,0},{3,1},{4,6},{5,7},{6,4},{7,5},{8,10},{9,11},{10,... | collective-permute-start | bytes 393224 | tf_op jit(solution)/shard_map/ppermute | solution.py:378
  55.9 6.9 %collective-permute-start = (f32[256,128]{1,0:T(8,128)S(1)}, f32[256,128]{1,0:T(8,128)S(1)}, u32[]{:S(2)}, u32[]{:S(2)}) collective-permute-start(f32[256,128]{1,0:T(8,128)S(1)} %bitcast.30), channel_id=1, source_target_pairs={{0,3},{1,0},{2,1},{3,2},{4,7},{5,4},{6,5},{7,6},{8,11},{9,8},{10,9... | collective-permute-start | bytes 393224 | tf_op jit(solution)/shard_map/ppermute | solution.py:378
  62.8 3.9 %collective-permute-start.3 = (f32[1024,128]{1,0:T(8,128)S(1)}, f32[1024,128]{1,0:T(8,128)}, u32[]{:S(2)}, u32[]{:S(2)}) collective-permute-start(f32[1024,128]{1,0:T(8,128)S(1)} %join_rows.1.refs_2_), channel_id=1, source_target_pairs={{0,4},{4,0},{8,12},{12,8},{16,20},{20,16},{24,28},{28,24},{32,36},... | collective-permute-start | bytes 1572872 | tf_op jit(solution)/shard_map/ppermute | solution.py:382
  72.0 3.8 %collective-permute-start.4 = (f32[512,256]{1,0:T(8,128)S(1)}, f32[512,256]{1,0:T(8,128)S(1)}, u32[]{:S(2)}, u32[]{:S(2)}) collective-permute-start(f32[512,256]{1,0:T(8,128)S(1)} %get-tuple-element.40), channel_id=1, source_target_pairs={{0,4},{4,0},{8,12},{12,8},{16,20},{20,16},{24,28},{28,24},{32,36},... | collective-permute-start | bytes 1572872 | tf_op jit(solution)/shard_map/ppermute | solution.py:382
  76.5 10.4 %collective-permute-start.5 = (f32[128,256]{1,0:T(8,128)S(1)}, f32[128,256]{1,0:T(8,128)S(1)}, u32[]{:S(2)}, u32[]{:S(2)}) collective-permute-start(f32[128,256]{1,0:T(8,128)S(1)} %get-tuple-element.42), channel_id=1, source_target_pairs={{0,1},{1,2},{2,3},{3,0},{4,5},{5,6},{6,7},{7,4},{8,9},{9,10},{10,1... | collective-permute-start | bytes 393224 | tf_op jit(solution)/shard_map/ppermute | solution.py:378
  79.8 9.0 %collective-permute-start.6 = (f32[128,256]{1,0:T(8,128)S(1)}, f32[128,256]{1,0:T(8,128)S(1)}, u32[]{:S(2)}, u32[]{:S(2)}) collective-permute-start(f32[128,256]{1,0:T(8,128)S(1)} %get-tuple-element.43), channel_id=1, source_target_pairs={{0,2},{1,3},{2,0},{3,1},{4,6},{5,7},{6,4},{7,5},{8,10},{9,11},{10,... | collective-permute-start | bytes 393224 | tf_op jit(solution)/shard_map/ppermute | solution.py:378
  84.4 6.9 %collective-permute-start.7 = (f32[128,256]{1,0:T(8,128)S(1)}, f32[128,256]{1,0:T(8,128)S(1)}, u32[]{:S(2)}, u32[]{:S(2)}) collective-permute-start(f32[128,256]{1,0:T(8,128)S(1)} %get-tuple-element.44), channel_id=1, source_target_pairs={{0,3},{1,0},{2,1},{3,2},{4,7},{5,4},{6,5},{7,6},{8,11},{9,8},{10,9... | collective-permute-start | bytes 393224 | tf_op jit(solution)/shard_map/ppermute | solution.py:378
  97.4 64.9 %all-to-all-start.2 = ((f32[128,1,1920]{2,1,0:T(1,128)}), f32[128,1,1920]{2,1,0:T(1,128)S(1)}, u32[]{:S(2)}, u32[]{:S(2)}) async-start(f32[128,1,1920]{2,1,0:T(1,128)} %bitcast.36), calls=%async_computation.2 | async-start | bytes 1966080 | tf_op jit(solution)/shard_map/all_to_all | solution.py:372
  166.0 17.2 %copy-start.4 = (f32[512]{0:T(512)S(1)}, f32[512]{0:T(512)}, u32[]{:S(2)}) copy-start(f32[512]{0:T(512)} %param.10) | copy-start | bytes 6148

commit v4 on v3

--- a/solution.py
+++ b/solution.py
@@ -191,7 +191,8 @@
 def fetch_kernel(recv, *refs):
     n = LANE
     table, rel = refs[:PIECES], refs[PIECES : 2 * PIECES]
-    send, rows = refs[2 * PIECES :]
+    send, rows, negs = refs[2 * PIECES :]
+    negs[...] = recv[...]
     tile = recv[pl.ds(1, n, stride=TILES1), :]
     halves = []
     for side in range(2):
@@ -206,12 +207,6 @@
         for i in range(2):
             rows[2 * n * side : 2 * n * (side + 1), i * 256 : (i + 1) * 256] = vec[i]
     pack(send, TILES2, halves)
-
-
-def join_rows_kernel(*refs):
-    *ins, out = refs
-    for i, ref in enumerate(ins):
-        out[i * ref.shape[0] : (i + 1) * ref.shape[0], :] = ref[...]
 
 
 def negatives_kernel(odd, recv, rows, *refs):
@@ -255,9 +250,9 @@
     give[...] = jnp.where(flip, re, im)
 
 
-def fold_kernel(keep, got, *outs):
+def fold_kernel(rep, keep, got, *outs):
     for i, ref in enumerate(outs):
-        at = pl.ds(i * LANE, LANE)
+        at = pl.ds(pl.multiple_of((rep[0] + i) % 4 * LANE, LANE), LANE)
         ref[...] = keep[at, :] + got[at, :]
 
 
@@ -284,11 +279,14 @@
     token[...] = neg[0:8, 0:128]
 
 
-def place_kernel(rep, neg_rows, asks, token, *refs):
-    n = LANE
-    *sides, side, hot = refs
+def carry_kernel(token, *refs):
+    *sides, side = refs
     for i, source in enumerate(sides):
-        side[i * 2 * n : (i + 1) * 2 * n, :] = source[...]
+        side[i * 2 * LANE : (i + 1) * 2 * LANE, :] = source[...]
+
+
+def place_kernel(rep, neg_rows, asks, token, hot):
+    n = LANE
     turned = asks[pl.ds(1, n, stride=TILES1), :].T
     sub = lax.broadcasted_iota(jnp.int32, (512, n), 0)
     for s in range(4):
@@ -316,8 +314,11 @@
         pack(out, TILES2, groups, q * TILES2 * GROUP)
 
 
-def update_kernel(rep, grads, table_t, state, out, sums):
-    n = LANE
+def update_kernel(rep, grads, state, table_t, out, sums, block, done):
+    n = LANE
+    start = pl.multiple_of(rep[0] * n, n)
+    copy = pltpu.make_async_copy(table_t.at[:, pl.ds(start, n)], block, done)
+    copy.start()
     rows = TILES2 * GROUP
     sums[...] = (
         grads[0:rows, :] + grads[rows : 2 * rows, :]
@@ -327,20 +328,28 @@
     grad = jnp.concatenate(
         [jnp.concatenate(halves[i::2], 0).T[0:200, :] for i in range(2)], 0
     )
-    start = pl.multiple_of(rep[0] * n, n)
     mean = jnp.sum(grad * grad, 0, keepdims=True) * (1.0 / 400.0)
     new = state[:, pl.ds(start, n)] + mean
-    out[0:400, :] = table_t[:, pl.ds(start, n)] - learn_rate * grad / jnp.sqrt(new)
+    copy.wait()
+    out[0:400, :] = block[...] - learn_rate * grad / jnp.sqrt(new)
     out[400:408, :] = jnp.broadcast_to(new, (8, n))
 
 
-def join_kernel(parts_in, table_new, state_new):
+def join_kernel(parts_in, table_new, state_new, done):
+    copies = []
     for q in range(4):
-        table_new[:, q * LANE : (q + 1) * LANE] = parts_in[q, 0:400, :]
+        at = pl.ds(q * LANE, LANE)
+        copies.append((parts_in.at[q, pl.ds(0, 400), :], table_new.at[:, at]))
+    copies = [pltpu.make_async_copy(a, b, done.at[q]) for q, (a, b) in enumerate(copies)]
+    for copy in copies:
+        copy.start()
+    for q in range(4):
         state_new[:, q * LANE : (q + 1) * LANE] = parts_in[q, 400:401, :]
-
-
-def call(kernel, outs, args, scalars=(), name=None, scratch=(), whole=0):
+    for copy in copies:
+        copy.wait()
+
+
+def call(kernel, outs, args, scalars=(), name=None, scratch=(), whole=0, direct=0):
     space = pl.BlockSpec(memory_space=pltpu.VMEM)
     return pl.pallas_call(
         kernel,
@@ -351,7 +360,7 @@
         in_specs=[pl.BlockSpec(memory_space=pltpu.SMEM)] * len(scalars)
         + [space] * (len(args) - whole)
         + [pl.BlockSpec(memory_space=pltpu.HBM)] * whole,
-        out_specs=[space] * len(outs),
+        out_specs=[pl.BlockSpec(memory_space=pltpu.HBM)] * direct + [space] * (len(outs) - direct),
         scratch_shapes=list(scratch),
         compiler_params=pltpu.CompilerParams(vmem_limit_bytes=24 << 20),
         name=name,
@@ -428,17 +437,18 @@
         name="ahead",
     )
     rel_pieces = pieces[PIECES:]
-    send2, rows = call(
+    send2, rows, own_negs = call(
         fetch_kernel,
-        [((n * TILES2, n), f32, False), ((4 * n, 512), f32, True)],
+        [
+            ((n * TILES2, n), f32, False),
+            ((4 * n, 512), f32, True),
+            ((n * TILES1, n), f32, True),
+        ],
         (near(recv1), *map(near, pieces)),
         name="fetch",
     )
     recv2 = exchange(send2, "ent", TILES2)
-    mine = [recv1] + [shift(recv1, -j) for j in (1, 2, 3)]
-    (mine,) = call(
-        join_rows_kernel, [((4 * TILES1 * n, n), f32, True)], list(map(near, mine)), name="join_rows"
-    )
+    mine = lax.all_gather(own_negs, "rep", axis=0, tiled=True)
     other = swap_cores(mine)
     query_side, tail_side, rels, keep, give = call(
         negatives_kernel,
@@ -451,7 +461,8 @@
         fold_kernel,
         [((n, 256), f32, i > 0) for i in range(4)],
         (near(keep), near(swap_cores(give))),
-        name="fold",
+        (rep,),
+        "fold",
     )
     sums = [owned[0]] + [shift(owned[j], j) for j in (1, 2, 3)]
     send3, token = call(
@@ -461,31 +472,40 @@
         name="edge",
     )
     recv3 = exchange(send3, "ent", TILES3)
-    side, hot = call(
-        place_kernel,
-        [((6 * n, 512), f32, False), ((4 * n, 5 * n), bf16, True)],
-        (recv1, far(token), far(query_side), far(tail_side), far(rels)),
-        (rep, neg_rows),
-        "place",
+    token = far(token)
+    (side,) = call(
+        carry_kernel,
+        [((6 * n, 512), f32, True)],
+        (token, far(query_side), far(tail_side), far(rels)),
+        name="carry",
+    )
+    (hot,) = call(
+        place_kernel, [((4 * n, 5 * n), bf16, True)], (recv1, token), (rep, neg_rows), "place"
     )
     (grads,) = call(
         scatter_kernel,
         [((4 * TILES2 * GROUP, n), f32, False)],
-        (near(recv3), near(hot), far(side)),
+        (near(recv3), near(hot), near(side)),
         name="scatter",
     )
     grads = lax.all_to_all(grads, "rep", split_axis=0, concat_axis=0, tiled=True)
     (fresh,) = call(
         update_kernel,
         [((408, n), f32, True)],
-        (near(grads), table_t, adagrad_state.reshape(1, 512)),
+        (near(grads), adagrad_state.reshape(1, 512), far(table_t)),
         (rep,),
         "update",
-        (pltpu.VMEM((TILES2 * GROUP, n), f32),),
+        (
+            pltpu.VMEM((TILES2 * GROUP, n), f32),
+            pltpu.VMEM((400, n), f32),
+            pltpu.SemaphoreType.DMA,
+        ),
+        1,
     )
     fresh = lax.all_gather(fresh, "rep", axis=0, tiled=False)
     table_new, state_new = call(
-        join_kernel, [((400, 512), f32, False), ((1, 512), f32, False)], (near(fresh),), name="join"
+        join_kernel, [((400, 512), f32, False), ((1, 512), f32, False)], (near(fresh),), name="join",
+        scratch=(pltpu.SemaphoreType.DMA((4,)),), direct=1,
     )
     return (table_new.T, state_new.reshape(512))
 

time: 200 us -> 198 us (0.990)
  starting transfers between devices: 65.2 us -> 51 us
  blocking collectives: 31.5 us -> 44.7 us
    all_gather x0 -> x1, blocking collectives: none -> 13.1 us  [on_device(): mine = lax.all_gather(own_negs, 'rep', axis=0, tiled=True)]
    ppermute x6 -> x3, starting transfers between devices: 21.8 us -> 9.82 us  [shift(): return lax.ppermute(x, 'rep', [(i, (i + by) % n) for i in range(n)])]
    ppermute x6 -> x3, waiting for transfers between devices: 7.9 us -> 4.94 us  [shift(): return lax.ppermute(x, 'rep', [(i, (i + by) % n) for i in range(n)])]
    all_to_all x3, waiting for transfers between devices: 65.3 us -> 67.7 us  [exchange(): x = lax.all_to_all(x, axis, split_axis=0, concat_axis=0, tiled=True)]
    all_to_all x3, starting transfers between devices: 39.4 us -> 37.2 us  [exchange(): x = lax.all_to_all(x, axis, split_axis=0, concat_axis=0, tiled=True)]
  transfers between devices with their start and end apart: 11 -> 8, of which waited for: 9 -> 7; matrix products, arithmetic and copies ran while one was open for 0% -> 0% of each run, Pallas kernels for 5% -> 5%
where the time goes in v4:
time: 198 us; the launch traced here: 196 us
  waiting for transfers between devices  76.3 us (39%)
  starting transfers between devices  51 us (26%)
  blocking collectives  44.7 us (23%)
  Pallas kernels  22.8 us (12%)
    all_to_all x3, waiting for transfers between devices, exchange(): x = lax.all_to_all(x, axis, split_axis=0, concat_axis=0, tiled=True)  67.7 us
    all_to_all x3, starting transfers between devices, exchange(): x = lax.all_to_all(x, axis, split_axis=0, concat_axis=0, tiled=True)  37.2 us
    pallas_call x11, Pallas kernels, call(): pl.pallas_call(kernel, out_shape=[(pltpu.VMEM if near else pltpu.HBM)(sha...  22.8 us
    all_to_all x1, blocking collectives, on_device(): lax.all_to_all(grads, 'rep', split_axis=0, concat_axis=0, tiled=True)  17.1 us
    all_gather x1, blocking collectives, on_device(): fresh = lax.all_gather(fresh, 'rep', axis=0, tiled=False)  14.4 us
    all_gather x1, blocking collectives, on_device(): mine = lax.all_gather(own_negs, 'rep', axis=0, tiled=True)  13.1 us
    ppermute x3, starting transfers between devices, shift(): return lax.ppermute(x, 'rep', [(i, (i + by) % n) for i in range(n)])  9.82 us
    ppermute x3, waiting for transfers between devices, shift(): return lax.ppermute(x, 'rep', [(i, (i + by) % n) for i in range(n)])  4.94 us
  transfers between devices with their start and end apart: 8, of which 7 were waited for; matrix products, arithmetic and copies ran while one was open for 0% of the time, Pallas kernels for 5%

profile of v4, /device:TPU:24, one launch (start us, length us, event | category | flops | bytes accessed | tf_op | source)
XLA Modules:
  0.0 196.4 jit_solution(3302810118502230043)
XLA Ops:
  0.6 0.0 copy-start
  0.6 2.6 %ask.1 = (f32[256,128]{1,0:T(8,128)}, f32[128,128]{1,0:T(8,128)}, f32[128,128]{1,0:T(8,128)}) custom-call(s32[1]{0:T(128)} %bitcast.rep, s32[4]{0:T(128)} %neg_rows.3, s32[1,128]{1,0:T(1,128)} %bitcast.35, s32[1,128]{1,0:T(1,128)} %bitcast.36, s32[1,128]{1,0:T(1,128)} %bitcast.37, s32[1,128]{1,0:T(1,128)} %bitcast.38, s32[1,128]{1,0:T(1,128)} %bitcast.39, ...), custom_call_target="tpu_custom_call" | custom-call | tf_op jit(solution)/shard_map/ask/pallas_call | solution.py:354
  3.2 19.3 %all-to-all-start = ((f32[128,1,256]{2,1,0:T(1,128)}), f32[128,1,256]{2,1,0:T(1,128)S(1)}, u32[]{:S(2)}, u32[]{:S(2)}) async-start(f32[128,1,256]{2,1,0:T(1,128)} %bitcast.34), calls=%async_computation | async-start | bytes 262144 | tf_op jit(solution)/shard_map/all_to_all | solution.py:381
  22.6 0.0 copy-start.3
  22.6 0.9 copy-done.3
  23.5 2.2 %ahead.1 = (bf16[512,512]{1,0:T(8,128)(2,1)S(1)}, bf16[512,512]{1,0:T(8,128)(2,1)S(1)}, bf16[64,512]{1,0:T(8,128)(2,1)S(1)}, bf16[64,512]{1,0:T(8,128)(2,1)S(1)}...) custom-call(f32[400,512]{1,0:T(8,128)S(1)} %bitcast.22, f32[64,400]{1,0:T(8,128)S(1)} %copy-done.3, ...), custom_call_target="tpu_custom_call" | custom-call | tf_op jit(solution)/shard_map/ahead/pallas_call | solution.py:354
  25.7 13.0 %all-to-all-done = f32[128,1,256]{2,1,0:T(1,128)S(1)} async-done(((f32[128,1,256]{2,1,0:T(1,128)}), f32[128,1,256]{2,1,0:T(1,128)S(1)}, u32[]{:S(2)}, u32[]{:S(2)}) %all-to-all-start) | async-done | bytes 131104 | tf_op jit(solution)/shard_map/all_to_all | solution.py:381
  38.7 2.1 %fetch.1 = (f32[1664,128]{1,0:T(8,128)}, f32[512,512]{1,0:T(8,128)S(1)}, f32[256,128]{1,0:T(8,128)S(1)}) custom-call(f32[256,128]{1,0:T(8,128)S(1)} %bitcast.27, bf16[512,512]{1,0:T(8,128)(2,1)S(1)} %get-tuple-element.30.refs_0_, bf16[512,512]{1,0:T(8,128)(2,1)S(1)} %get-tuple-element.31.refs_1_, bf16[64,512]{1,0:T(8,128)(2,1)S(1)} %get-tuple-element.32.refs_2_.refs_0_, ...), custom_call_target="tpu_custom_call" | custom-call | tf_op jit(solution)/shard_map/fetch/pallas_call | solution.py:354
  40.7 7.1 %all-to-all-start.1 = ((f32[128,1,1664]{2,1,0:T(1,128)}), f32[128,1,1664]{2,1,0:T(1,128)S(1)}, u32[]{:S(2)}, u32[]{:S(2)}) async-start(f32[128,1,1664]{2,1,0:T(1,128)} %bitcast.33), calls=%async_computation.1 | async-start | bytes 1703936 | tf_op jit(solution)/shard_map/all_to_all | solution.py:381
  47.8 13.1 %all_gather.9.refs_2_ = f32[1024,128]{1,0:T(8,128)S(1)} all-gather(f32[256,128]{1,0:T(8,128)S(1)} %get-tuple-element.38), channel_id=1, replica_groups=mesh['ent'=128,'rep'=4] {'rep'}, dimensions={0}, use_global_device_ids=true | all-gather | bytes 655360 | tf_op jit(solution)/shard_map/all_gather | solution.py:451
  61.0 1.9 collective-permute-start
  62.9 1.9 collective-permute-done.refs_3_
  64.8 5.0 %negatives.1 = (f32[256,512]{1,0:T(8,128)}, f32[256,512]{1,0:T(8,128)}, f32[256,512]{1,0:T(8,128)}, f32[512,256]{1,0:T(8,128)S(1)}, f32[512,256]{1,0:T(8,128)S(1)}) custom-call(s32[1]{0:T(128)} %bitcast.11.odd, f32[256,128]{1,0:T(8,128)S(1)} %bitcast.28, f32[512,512]{1,0:T(8,128)S(1)} %get-tuple-element.37.rows, bf16[64,512]{1,0:T(8,128)(2,1)} %copy-done.1, ...), custom_call_target="tpu_custom_call" | custom-call | tf_op jit(solution)/shard_map/negatives/pallas_call | solution.py:354
  69.8 2.0 %collective-permute-start.1 = (f32[512,256]{1,0:T(8,128)S(1)}, f32[512,256]{1,0:T(8,128)S(1)}, u32[]{:S(2)}, u32[]{:S(2)}) collective-permute-start(f32[512,256]{1,0:T(8,128)S(1)} %get-tuple-element.40), channel_id=1, source_target_pairs={{0,4},{4,0},{8,12},{12,8},{16,20},{20,16},{24,28},{28,24},{32,36},... | collective-permute-start | bytes 1572872 | tf_op jit(solution)/shard_map/ppermute | solution.py:391
  71.8 1.8 collective-permute-done.1.got
  73.6 0.7 fold.1
  74.3 3.3 %collective-permute-start.2 = (f32[128,256]{1,0:T(8,128)S(1)}, f32[128,256]{1,0:T(8,128)S(1)}, u32[]{:S(2)}, u32[]{:S(2)}) collective-permute-start(f32[128,256]{1,0:T(8,128)S(1)} %get-tuple-element.42), channel_id=1, source_target_pairs={{0,1},{1,2},{2,3},{3,0},{4,5},{5,6},{6,7},{7,4},{8,9},{9,10},{10,1... | collective-permute-start | bytes 393224 | tf_op jit(solution)/shard_map/ppermute | solution.py:387
  77.6 4.6 %collective-permute-start.3 = (f32[128,256]{1,0:T(8,128)S(1)}, f32[128,256]{1,0:T(8,128)S(1)}, u32[]{:S(2)}, u32[]{:S(2)}) collective-permute-start(f32[128,256]{1,0:T(8,128)S(1)} %get-tuple-element.43), channel_id=1, source_target_pairs={{0,2},{1,3},{2,0},{3,1},{4,6},{5,7},{6,4},{7,5},{8,10},{9,11},{10,... | collective-permute-start | bytes 393224 | tf_op jit(solution)/shard_map/ppermute | solution.py:387
  82.2 1.9 collective-permute-start.4
  84.1 2.4 %collective-permute-done.3.sum2 = f32[128,256]{1,0:T(8,128)S(1)} collective-permute-done((f32[128,256]{1,0:T(8,128)S(1)}, f32[128,256]{1,0:T(8,128)S(1)}, u32[]{:S(2)}, u32[]{:S(2)}) %collective-permute-start.3) | collective-permute-done | bytes 131104 | tf_op jit(solution)/shard_map/ppermute | solution.py:387
  86.6 2.5 %collective-permute-done.4.sum3 = f32[128,256]{1,0:T(8,128)S(1)} collective-permute-done((f32[128,256]{1,0:T(8,128)S(1)}, f32[128,256]{1,0:T(8,128)S(1)}, u32[]{:S(2)}, u32[]{:S(2)}) %collective-permute-start.4) | collective-permute-done | bytes 131104 | tf_op jit(solution)/shard_map/ppermute | solution.py:387
  89.1 5.3 %all-to-all-done.1 = f32[128,1,1664]{2,1,0:T(1,128)S(1)} async-done(((f32[128,1,1664]{2,1,0:T(1,128)}), f32[128,1,1664]{2,1,0:T(1,128)S(1)}, u32[]{:S(2)}, u32[]{:S(2)}) %all-to-all-start.1) | async-done | bytes 852000 | tf_op jit(solution)/shard_map/all_to_all | solution.py:381
  94.4 3.1 %edge.1 = (f32[1920,128]{1,0:T(8,128)}, f32[8,128]{1,0:T(8,128)}) custom-call(f32[1664,128]{1,0:T(8,128)S(1)} %bitcast.25, bf16[256,256]{1,0:T(8,128)(2,1)} %get-tuple-element.35.same, bf16[256,256]{1,0:T(8,128)(2,1)} %get-tuple-element.36.same_t, f32[128,128]{1,0:T(8,128)} %get-tuple-element.28.head_edge, f32[128,256]{1,0:T(8,128)} %get-tuple-element.41.sum0, ...), custom_call_target="tpu_custom_call" | custom-call | tf_op jit(solution)/shard_map/edge/pallas_call | solution.py:354
  97.4 10.8 %all-to-all-start.2 = ((f32[128,1,1920]{2,1,0:T(1,128)}), f32[128,1,1920]{2,1,0:T(1,128)S(1)}, u32[]{:S(2)}, u32[]{:S(2)}) async-start(f32[128,1,1920]{2,1,0:T(1,128)} %bitcast.32), calls=%async_computation.2 | async-start | bytes 1966080 | tf_op jit(solution)/shard_map/all_to_all | solution.py:381
  108.2 1.0 place.1.hot
  109.2 1.5 carry.1.side
  110.7 49.4 %all-to-all-done.2 = f32[128,1,1920]{2,1,0:T(1,128)S(1)} async-done(((f32[128,1,1920]{2,1,0:T(1,128)}), f32[128,1,1920]{2,1,0:T(1,128)S(1)}, u32[]{:S(2)}, u32[]{:S(2)}) %all-to-all-start.2) | async-done | bytes 983072 | tf_op jit(solution)/shard_map/all_to_all | solution.py:381
  160.1 2.2 %scatter.1 = f32[1664,128]{1,0:T(8,128)} custom-call(f32[1920,128]{1,0:T(8,128)S(1)} %bitcast.23, bf16[512,640]{1,0:T(8,128)(2,1)S(1)} %place.1.hot, f32[768,512]{1,0:T(8,128)S(1)} %carry.1.side), custom_call_target="tpu_custom_call" | custom-call | tf_op jit(solution)/shard_map/scatter/pallas_call | solution.py:354
  162.3 17.1 %all_to_all.26 = f32[4,416,128]{2,1,0:T(8,128)S(1)} all-to-all(f32[4,416,128]{2,1,0:T(8,128)} %bitcast.31), channel_id=1, replica_groups=mesh['ent'=128,'rep'=4] {'rep'}, dimensions={0} | all-to-all | bytes 1703936 | tf_op jit(solution)/shard_map/all_to_all | solution.py:491
  179.5 1.0 update.1
  180.5 14.4 %all-gather = f32[1632,128]{1,0:T(8,128)S(1)} all-gather(f32[408,128]{1,0:T(8,128)S(1)} %update.1), channel_id=2, replica_groups=mesh['ent'=128,'rep'=4] {'rep'}, dimensions={0}, use_global_device_ids=true | all-gather | bytes 1044480 | tf_op jit(solution)/shard_map/all_gather | solution.py:505
  194.9 1.5 join.1
  (8 shorter events, 0.0 us)
Async XLA Ops:
  0.6 21.9 %copy-start = (f32[512,400]{0,1:T(8,128)S(1)}, f32[512,400]{0,1:T(8,128)}, u32[]{:S(2)}) copy-start(f32[512,400]{0,1:T(8,128)} %param.9) | copy-start | bytes 2457604
  3.2 35.4 %all-to-all-start = ((f32[128,1,256]{2,1,0:T(1,128)}), f32[128,1,256]{2,1,0:T(1,128)S(1)}, u32[]{:S(2)}, u32[]{:S(2)}) async-start(f32[128,1,256]{2,1,0:T(1,128)} %bitcast.34), calls=%async_computation | async-start | bytes 262144 | tf_op jit(solution)/shard_map/all_to_all | solution.py:381
  22.6 0.9 copy-start.3
  25.7 35.3 %copy-start.1 = (bf16[64,512]{1,0:T(8,128)(2,1)}, bf16[64,512]{1,0:T(8,128)(2,1)S(1)}, u32[]{:S(2)}) copy-start(bf16[64,512]{1,0:T(8,128)(2,1)S(1)} %get-tuple-element.32.refs_2_.refs_0_) | copy-start | bytes 196612
  25.7 35.3 %copy-start.2 = (bf16[64,512]{1,0:T(8,128)(2,1)}, bf16[64,512]{1,0:T(8,128)(2,1)S(1)}, u32[]{:S(2)}) copy-start(bf16[64,512]{1,0:T(8,128)(2,1)S(1)} %get-tuple-element.33.refs_3_.refs_1_) | copy-start | bytes 196612
  40.7 53.6 %all-to-all-start.1 = ((f32[128,1,1664]{2,1,0:T(1,128)}), f32[128,1,1664]{2,1,0:T(1,128)S(1)}, u32[]{:S(2)}, u32[]{:S(2)}) async-start(f32[128,1,1664]{2,1,0:T(1,128)} %bitcast.33), calls=%async_computation.1 | async-start | bytes 1703936 | tf_op jit(solution)/shard_map/all_to_all | solution.py:381
  61.0 3.8 %collective-permute-start = (f32[1024,128]{1,0:T(8,128)S(1)}, f32[1024,128]{1,0:T(8,128)S(1)}, u32[]{:S(2)}, u32[]{:S(2)}) collective-permute-start(f32[1024,128]{1,0:T(8,128)S(1)} %all_gather.9.refs_2_), channel_id=1, source_target_pairs={{0,4},{4,0},{8,12},{12,8},{16,20},{20,16},{24,28},{28,24},{32,36},... | collective-permute-start | bytes 1572872 | tf_op jit(solution)/shard_map/ppermute | solution.py:391
  69.8 3.8 %collective-permute-start.1 = (f32[512,256]{1,0:T(8,128)S(1)}, f32[512,256]{1,0:T(8,128)S(1)}, u32[]{:S(2)}, u32[]{:S(2)}) collective-permute-start(f32[512,256]{1,0:T(8,128)S(1)} %get-tuple-element.40), channel_id=1, source_target_pairs={{0,4},{4,0},{8,12},{12,8},{16,20},{20,16},{24,28},{28,24},{32,36},... | collective-permute-start | bytes 1572872 | tf_op jit(solution)/shard_map/ppermute | solution.py:391
  74.3 9.8 %collective-permute-start.2 = (f32[128,256]{1,0:T(8,128)S(1)}, f32[128,256]{1,0:T(8,128)S(1)}, u32[]{:S(2)}, u32[]{:S(2)}) collective-permute-start(f32[128,256]{1,0:T(8,128)S(1)} %get-tuple-element.42), channel_id=1, source_target_pairs={{0,1},{1,2},{2,3},{3,0},{4,5},{5,6},{6,7},{7,4},{8,9},{9,10},{10,1... | collective-permute-start | bytes 393224 | tf_op jit(solution)/shard_map/ppermute | solution.py:387
  77.6 9.0 %collective-permute-start.3 = (f32[128,256]{1,0:T(8,128)S(1)}, f32[128,256]{1,0:T(8,128)S(1)}, u32[]{:S(2)}, u32[]{:S(2)}) collective-permute-start(f32[128,256]{1,0:T(8,128)S(1)} %get-tuple-element.43), channel_id=1, source_target_pairs={{0,2},{1,3},{2,0},{3,1},{4,6},{5,7},{6,4},{7,5},{8,10},{9,11},{10,... | collective-permute-start | bytes 393224 | tf_op jit(solution)/shard_map/ppermute | solution.py:387
  82.2 6.9 %collective-permute-start.4 = (f32[128,256]{1,0:T(8,128)S(1)}, f32[128,256]{1,0:T(8,128)S(1)}, u32[]{:S(2)}, u32[]{:S(2)}) collective-permute-start(f32[128,256]{1,0:T(8,128)S(1)} %get-tuple-element.44), channel_id=1, source_target_pairs={{0,3},{1,0},{2,1},{3,2},{4,7},{5,4},{6,5},{7,6},{8,11},{9,8},{10,9... | collective-permute-start | bytes 393224 | tf_op jit(solution)/shard_map/ppermute | solution.py:387
  97.4 62.7 %all-to-all-start.2 = ((f32[128,1,1920]{2,1,0:T(1,128)}), f32[128,1,1920]{2,1,0:T(1,128)S(1)}, u32[]{:S(2)}, u32[]{:S(2)}) async-start(f32[128,1,1920]{2,1,0:T(1,128)} %bitcast.32), calls=%async_computation.2 | async-start | bytes 1966080 | tf_op jit(solution)/shard_map/all_to_all | solution.py:381
  162.3 17.1 %copy-start.4 = (f32[512]{0:T(512)S(1)}, f32[512]{0:T(512)}, u32[]{:S(2)}) copy-start(f32[512]{0:T(512)} %param.10) | copy-start | bytes 6148

commit v5 on v4

--- a/solution.py
+++ b/solution.py
@@ -155,7 +155,7 @@
     send[pl.ds(1, n, stride=TILES1), :] = tile
 
 
-def ahead_kernel(table_t, relations, head_edge, tail_edge, *outs):
+def ahead_kernel(table_t, relations, *outs):
     pad = jnp.zeros((56, 512), f32)
     whole = jnp.concatenate([table_t[0:200, :], pad, table_t[200:400, :], pad], 0).T
     for ref, piece in zip(outs[:PIECES], parts(whole, PIECES), strict=True):
@@ -164,7 +164,10 @@
     whole = jnp.concatenate([relations[:, :200], pad, relations[:, 200:], pad], 1)
     for ref, piece in zip(outs[PIECES : 2 * PIECES], parts(whole, PIECES), strict=True):
         ref[...] = piece
-    same, same_t = outs[2 * PIECES :]
+
+
+def pair_kernel(head_edge, tail_edge, same):
+    n = 2 * LANE
 
     def stack(ref, by_rows):
         if by_rows:
@@ -172,9 +175,11 @@
             return jnp.concatenate([turned[0:1, :], turned[1:2, :]], 1)
         return jnp.concatenate([ref[:, 0:1], ref[:, 1:2]], 0)
 
-    for ref, one, other in ((same, head_edge, tail_edge), (same_t, tail_edge, head_edge)):
+    for i, (one, other) in enumerate(((head_edge, tail_edge), (tail_edge, head_edge))):
         col, row = stack(one, False), stack(other, True)
-        ref[...] = jnp.where((col == row) & (col >= 0.0), 1.0, 0.0).astype(bf16)
+        same[i * n : (i + 1) * n, :] = jnp.where(
+            (col == row) & (col >= 0.0), 1.0, 0.0
+        ).astype(bf16)
 
 
 def rel_vectors(tile, slots, pieces):
@@ -212,7 +217,7 @@
 def negatives_kernel(odd, recv, rows, *refs):
     n = LANE
     rel = refs[:PIECES]
-    mine, other, query_side, tail_side, rels, keep, give = refs[PIECES:]
+    mine, other, back, keep, give = refs[PIECES:]
     tile = recv[pl.ds(1, n, stride=TILES1), :]
     mask = lanes((n, LANE)) < 72
 
@@ -226,25 +231,13 @@
         jnp.concatenate([half(ref, TILES1 * n * j) for j in range(4)], 0) for ref in (mine, other)
     )
     negs = jnp.concatenate([jnp.where(flip, got, own), jnp.where(flip, own, got)], 1)
-    weight = 1.0 / math.sqrt(512.0)
-    total = None
-    for side in range(2):
-        slots = (2 * side, 2 * side + 1)
-        x = rows[2 * n * side : 2 * n * (side + 1), :]
-        rv = rel_vectors(tile, slots, rel)
-        if side:
-            x = jnp.concatenate(cmul(conj(rv), split(x)), 1)
-        valid = jnp.concatenate([column(tile, 72 + 2 * s) for s in slots], 0)
-        scores = dot3(x, negs, NT)
-        coef = jnp.where(valid >= 0.0, sigmoid(scores) * weight, 0.0)
-        back = dot3(coef, negs, NN)
-        if side:
-            tail_side[...] = jnp.concatenate(cmul(split(back), rv), 1)
-        else:
-            query_side[...] = back
-            rels[...] = jnp.concatenate(rv, 1)
-        grad = dot3(coef, x, TN)
-        total = grad if total is None else total + grad
+    probe = cmul(conj(rel_vectors(tile, (2, 3), rel)), split(rows[2 * n :, :]))
+    x = jnp.concatenate([rows[0 : 2 * n, :], jnp.concatenate(probe, 1)], 0)
+    valid = jnp.concatenate([column(tile, 72 + 2 * s) for s in range(4)], 0)
+    coef = sigmoid(dot3(x, negs, NT)) * (1.0 / math.sqrt(512.0))
+    coef = jnp.where(valid >= 0.0, coef, 0.0)
+    back[...] = dot3(coef, negs, NN)
+    total = dot3(coef, x, TN)
     re, im = split(total)
     keep[...] = jnp.where(flip, im, re)
     give[...] = jnp.where(flip, re, im)
@@ -256,21 +249,20 @@
         ref[...] = keep[at, :] + got[at, :]
 
 
-def edge_kernel(recv, same, same_t, head_edge, sum0, sum1, sum2, sum3, send, token):
+def edge_kernel(recv, same, sum0, sum1, sum2, sum3, send, token):
     n = LANE
     halves = unpack(recv, TILES2, 8, n)
-    head_at = jnp.concatenate([head_edge[:, 0:1], head_edge[:, 1:2]], 0)
     query, tails = (
         jnp.concatenate(
             [jnp.concatenate(halves[i : i + 2], 1), jnp.concatenate(halves[i + 2 : i + 4], 1)], 0
         )
         for i in (0, 4)
     )
-    met = pick(same[...], parts(tails, PIECES), NN)
+    met = pick(same[0 : 2 * n, :], parts(tails, PIECES), NN)
     pos = jnp.sum(query * met, 1, keepdims=True)
-    coef = jnp.where(head_at >= 0.0, -sigmoid(-pos), 0.0)
+    coef = -sigmoid(-pos)
     to_head = coef * met
-    to_tail = pick(same_t[...], parts(coef * query, PIECES), NN)
+    to_tail = pick(same[2 * n :, :], parts(coef * query, PIECES), NN)
     neg = sum0[...] + sum1[...] + (sum2[...] + sum3[...])
     out = []
     for block in (to_head[:n], to_head[n:], to_tail[:n], to_tail[n:]):
@@ -279,10 +271,14 @@
     token[...] = neg[0:8, 0:128]
 
 
-def carry_kernel(token, *refs):
-    *sides, side = refs
-    for i, source in enumerate(sides):
-        side[i * 2 * LANE : (i + 1) * 2 * LANE, :] = source[...]
+def carry_kernel(token, asks, back, *refs):
+    n = 2 * LANE
+    *rel, side = refs
+    tile = asks[pl.ds(1, LANE, stride=TILES1), :]
+    side[0:n, :] = back[0:n, :]
+    turned = cmul(split(back[n:, :]), rel_vectors(tile, (2, 3), rel))
+    side[n : 2 * n, :] = jnp.concatenate(turned, 1)
+    side[2 * n :, :] = jnp.concatenate(rel_vectors(tile, (0, 1), rel), 1)
 
 
 def place_kernel(rep, neg_rows, asks, token, hot):
@@ -314,11 +310,8 @@
         pack(out, TILES2, groups, q * TILES2 * GROUP)
 
 
-def update_kernel(rep, grads, state, table_t, out, sums, block, done):
-    n = LANE
-    start = pl.multiple_of(rep[0] * n, n)
-    copy = pltpu.make_async_copy(table_t.at[:, pl.ds(start, n)], block, done)
-    copy.start()
+def update_kernel(rep, grads, block, state, out, sums):
+    n = LANE
     rows = TILES2 * GROUP
     sums[...] = (
         grads[0:rows, :] + grads[rows : 2 * rows, :]
@@ -328,28 +321,27 @@
     grad = jnp.concatenate(
         [jnp.concatenate(halves[i::2], 0).T[0:200, :] for i in range(2)], 0
     )
+    start = pl.multiple_of(rep[0] * n, n)
     mean = jnp.sum(grad * grad, 0, keepdims=True) * (1.0 / 400.0)
     new = state[:, pl.ds(start, n)] + mean
-    copy.wait()
     out[0:400, :] = block[...] - learn_rate * grad / jnp.sqrt(new)
     out[400:408, :] = jnp.broadcast_to(new, (8, n))
 
 
-def join_kernel(parts_in, table_new, state_new, done):
-    copies = []
+def cut_kernel(rep, token, table_t, block, done):
+    start = pl.multiple_of(rep[0] * LANE, LANE)
+    copy = pltpu.make_async_copy(table_t.at[:, pl.ds(start, LANE)], block, done)
+    copy.start()
+    copy.wait()
+
+
+def join_kernel(parts_in, table_new, state_new):
     for q in range(4):
-        at = pl.ds(q * LANE, LANE)
-        copies.append((parts_in.at[q, pl.ds(0, 400), :], table_new.at[:, at]))
-    copies = [pltpu.make_async_copy(a, b, done.at[q]) for q, (a, b) in enumerate(copies)]
-    for copy in copies:
-        copy.start()
-    for q in range(4):
+        table_new[:, q * LANE : (q + 1) * LANE] = parts_in[q, 0:400, :]
         state_new[:, q * LANE : (q + 1) * LANE] = parts_in[q, 400:401, :]
-    for copy in copies:
-        copy.wait()
-
-
-def call(kernel, outs, args, scalars=(), name=None, scratch=(), whole=0, direct=0):
+
+
+def call(kernel, outs, args, scalars=(), name=None, scratch=(), whole=0):
     space = pl.BlockSpec(memory_space=pltpu.VMEM)
     return pl.pallas_call(
         kernel,
@@ -360,7 +352,7 @@
         in_specs=[pl.BlockSpec(memory_space=pltpu.SMEM)] * len(scalars)
         + [space] * (len(args) - whole)
         + [pl.BlockSpec(memory_space=pltpu.HBM)] * whole,
-        out_specs=[pl.BlockSpec(memory_space=pltpu.HBM)] * direct + [space] * (len(outs) - direct),
+        out_specs=[space] * len(outs),
         scratch_shapes=list(scratch),
         compiler_params=pltpu.CompilerParams(vmem_limit_bytes=24 << 20),
         name=name,
@@ -428,13 +420,17 @@
         1,
     )
     recv1 = exchange(send1, "ent", TILES1)
-    *pieces, same, same_t = call(
+    pieces = call(
         ahead_kernel,
-        [((4 * n, 512), bf16, True)] * PIECES
-        + [((64, 512), bf16, True)] * PIECES
-        + [((2 * n, 2 * n), bf16, False)] * 2,
-        (table_t, relations, far(head_edge), far(tail_edge)),
+        [((4 * n, 512), bf16, True)] * PIECES + [((64, 512), bf16, True)] * PIECES,
+        (table_t, relations),
         name="ahead",
+    )
+    (same,) = call(
+        pair_kernel,
+        [((4 * n, 2 * n), bf16, True)],
+        (far(head_edge), far(tail_edge)),
+        name="pair",
     )
     rel_pieces = pieces[PIECES:]
     send2, rows, own_negs = call(
@@ -450,16 +446,16 @@
     recv2 = exchange(send2, "ent", TILES2)
     mine = lax.all_gather(own_negs, "rep", axis=0, tiled=True)
     other = swap_cores(mine)
-    query_side, tail_side, rels, keep, give = call(
+    back, keep, give = call(
         negatives_kernel,
-        [((2 * n, 512), f32, False)] * 3 + [((4 * n, 256), f32, True)] * 2,
+        [((4 * n, 512), f32, True)] + [((4 * n, 256), f32, True)] * 2,
         (near(recv1), near(rows), *map(far, rel_pieces), near(mine), near(other)),
         (odd,),
         "negatives",
     )
     owned = call(
         fold_kernel,
-        [((n, 256), f32, i > 0) for i in range(4)],
+        [((n, 256), f32, True)] * 4,
         (near(keep), near(swap_cores(give))),
         (rep,),
         "fold",
@@ -468,7 +464,7 @@
     send3, token = call(
         edge_kernel,
         [((n * TILES3, n), f32, False), ((8, n), f32, False)],
-        (near(recv2), far(same), far(same_t), far(head_edge), far(sums[0]), *map(near, sums[1:])),
+        (near(recv2), near(same), far(sums[0]), *map(near, sums[1:])),
         name="edge",
     )
     recv3 = exchange(send3, "ent", TILES3)
@@ -476,11 +472,20 @@
     (side,) = call(
         carry_kernel,
         [((6 * n, 512), f32, True)],
-        (token, far(query_side), far(tail_side), far(rels)),
+        (token, recv1, far(back), *map(far, rel_pieces)),
         name="carry",
     )
     (hot,) = call(
         place_kernel, [((4 * n, 5 * n), bf16, True)], (recv1, token), (rep, neg_rows), "place"
+    )
+    (block,) = call(
+        cut_kernel,
+        [((400, n), f32, True)],
+        (token, far(table_t)),
+        (rep,),
+        "cut",
+        (pltpu.SemaphoreType.DMA,),
+        1,
     )
     (grads,) = call(
         scatter_kernel,
@@ -492,20 +497,14 @@
     (fresh,) = call(
         update_kernel,
         [((408, n), f32, True)],
-        (near(grads), adagrad_state.reshape(1, 512), far(table_t)),
+        (near(grads), near(block), adagrad_state.reshape(1, 512)),
         (rep,),
         "update",
-        (
-            pltpu.VMEM((TILES2 * GROUP, n), f32),
-            pltpu.VMEM((400, n), f32),
-            pltpu.SemaphoreType.DMA,
-        ),
-        1,
+        (pltpu.VMEM((TILES2 * GROUP, n), f32),),
     )
     fresh = lax.all_gather(fresh, "rep", axis=0, tiled=False)
     table_new, state_new = call(
-        join_kernel, [((400, 512), f32, False), ((1, 512), f32, False)], (near(fresh),), name="join",
-        scratch=(pltpu.SemaphoreType.DMA((4,)),), direct=1,
+        join_kernel, [((400, 512), f32, False), ((1, 512), f32, False)], (near(fresh),), name="join"
     )
     return (table_new.T, state_new.reshape(512))
 

time: 198 us -> 195 us (0.985)
  blocking collectives: 44.7 us -> 27.6 us
  waiting for transfers between devices: 76.3 us -> 89.8 us
  starting transfers between devices: 51 us -> 53 us
    all_to_all x1 -> x0, blocking collectives: 17.1 us -> none  [on_device(): lax.all_to_all(grads, 'rep', split_axis=0, concat_axis=0, tiled=True)]
    all_to_all x0 -> x1, waiting for transfers between devices: none -> 11.9 us  [on_device(): lax.all_to_all(grads, 'rep', split_axis=0, concat_axis=0, tiled=True)]
    all_to_all x0 -> x1, starting transfers between devices: none -> 3.63 us  [on_device(): lax.all_to_all(grads, 'rep', split_axis=0, concat_axis=0, tiled=True)]
    all_to_all x3, waiting for transfers between devices: 67.7 us -> 70.6 us  [exchange(): x = lax.all_to_all(x, axis, split_axis=0, concat_axis=0, tiled=True)]
    pallas_call x11 -> x13, Pallas kernels: 22.8 us -> 21.2 us  [call(): pl.pallas_call(kernel, out_shape=[(pltpu.VMEM if near else pltpu.HBM)(sha...]
  transfers between devices with their start and end apart: 8 -> 9, of which waited for: 7 -> 8; matrix products, arithmetic and copies ran while one was open for 0% -> 0% of each run, Pallas kernels for 5% -> 5%
where the time goes in v5:
time: 195 us; the launch traced here: 193 us
  waiting for transfers between devices  89.8 us (46%)
  starting transfers between devices  53 us (27%)
  blocking collectives  27.6 us (14%)
  Pallas kernels  21.2 us (11%)
    all_to_all x3, waiting for transfers between devices, exchange(): x = lax.all_to_all(x, axis, split_axis=0, concat_axis=0, tiled=True)  70.6 us
    all_to_all x3, starting transfers between devices, exchange(): x = lax.all_to_all(x, axis, split_axis=0, concat_axis=0, tiled=True)  35.6 us
    pallas_call x13, Pallas kernels, call(): pl.pallas_call(kernel, out_shape=[(pltpu.VMEM if near else pltpu.HBM)(sha...  21.2 us
    all_gather x1, blocking collectives, on_device(): fresh = lax.all_gather(fresh, 'rep', axis=0, tiled=False)  14.5 us
    all_gather x1, blocking collectives, on_device(): mine = lax.all_gather(own_negs, 'rep', axis=0, tiled=True)  13.1 us
    all_to_all x1, waiting for transfers between devices, on_device(): lax.all_to_all(grads, 'rep', split_axis=0, concat_axis=0, tiled=True)  11.9 us
    ppermute x3, starting transfers between devices, shift(): return lax.ppermute(x, 'rep', [(i, (i + by) % n) for i in range(n)])  9.83 us
    ppermute x2, starting transfers between devices, swap_cores(): lax.ppermute(x, 'ent', [(i, i ^ 1) for i in range(lax.axis_size('ent'))])  3.96 us
  transfers between devices with their start and end apart: 9, of which 8 were waited for; matrix products, arithmetic and copies ran while one was open for 0% of the time, Pallas kernels for 5%

profile of v5, /device:TPU:24, one launch (start us, length us, event | category | flops | bytes accessed | tf_op | source)
XLA Modules:
  0.0 193.5 jit_solution(12753865583710852525)
XLA Ops:
  0.6 2.6 %ask.1 = (f32[256,128]{1,0:T(8,128)}, f32[128,128]{1,0:T(8,128)}, f32[128,128]{1,0:T(8,128)}) custom-call(s32[1]{0:T(128)} %bitcast.rep, s32[4]{0:T(128)} %neg_rows.3, s32[1,128]{1,0:T(1,128)} %bitcast.36, s32[1,128]{1,0:T(1,128)} %bitcast.37, s32[1,128]{1,0:T(1,128)} %bitcast.38, s32[1,128]{1,0:T(1,128)} %bitcast.39, s32[1,128]{1,0:T(1,128)} %bitcast.40, ...), custom_call_target="tpu_custom_call" | custom-call | tf_op jit(solution)/shard_map/ask/pallas_call | solution.py:346
  3.2 19.3 %all-to-all-start = ((f32[128,1,256]{2,1,0:T(1,128)}), f32[128,1,256]{2,1,0:T(1,128)S(1)}, u32[]{:S(2)}, u32[]{:S(2)}) async-start(f32[128,1,256]{2,1,0:T(1,128)} %bitcast.35), calls=%async_computation | async-start | bytes 262144 | tf_op jit(solution)/shard_map/all_to_all | solution.py:373
  22.6 0.9 copy-done.5
  23.5 0.4 ahead.1
  23.9 14.8 %all-to-all-done = f32[128,1,256]{2,1,0:T(1,128)S(1)} async-done(((f32[128,1,256]{2,1,0:T(1,128)}), f32[128,1,256]{2,1,0:T(1,128)S(1)}, u32[]{:S(2)}, u32[]{:S(2)}) %all-to-all-start) | async-done | bytes 131104 | tf_op jit(solution)/shard_map/all_to_all | solution.py:373
  38.7 2.1 %fetch.1 = (f32[1664,128]{1,0:T(8,128)}, f32[512,512]{1,0:T(8,128)S(1)}, f32[256,128]{1,0:T(8,128)S(1)}) custom-call(f32[256,128]{1,0:T(8,128)S(1)} %bitcast.27, bf16[512,512]{1,0:T(8,128)(2,1)S(1)} %get-tuple-element.24.refs_0_, bf16[512,512]{1,0:T(8,128)(2,1)S(1)} %get-tuple-element.25.refs_1_, bf16[64,512]{1,0:T(8,128)(2,1)S(1)} %get-tuple-element.26.refs_2_.refs_0_, ...), custom_call_target="tpu_custom_call" | custom-call | tf_op jit(solution)/shard_map/fetch/pallas_call | solution.py:346
  40.7 7.1 %all-to-all-start.1 = ((f32[128,1,1664]{2,1,0:T(1,128)}), f32[128,1,1664]{2,1,0:T(1,128)S(1)}, u32[]{:S(2)}, u32[]{:S(2)}) async-start(f32[128,1,1664]{2,1,0:T(1,128)} %bitcast.34), calls=%async_computation.1 | async-start | bytes 1703936 | tf_op jit(solution)/shard_map/all_to_all | solution.py:373
  47.8 13.1 %all_gather.9.refs_2_ = f32[1024,128]{1,0:T(8,128)S(1)} all-gather(f32[256,128]{1,0:T(8,128)S(1)} %get-tuple-element.32), channel_id=1, replica_groups=mesh['ent'=128,'rep'=4] {'rep'}, dimensions={0}, use_global_device_ids=true | all-gather | bytes 655360 | tf_op jit(solution)/shard_map/all_gather | solution.py:447
  61.0 1.9 collective-permute-start
  62.9 1.9 collective-permute-done.refs_3_
  64.8 4.0 %negatives.1 = (f32[512,512]{1,0:T(8,128)S(1)}, f32[512,256]{1,0:T(8,128)S(1)}, f32[512,256]{1,0:T(8,128)S(1)}) custom-call(s32[1]{0:T(128)} %bitcast.11.odd, f32[256,128]{1,0:T(8,128)S(1)} %bitcast.28, f32[512,512]{1,0:T(8,128)S(1)} %get-tuple-element.31.rows, bf16[64,512]{1,0:T(8,128)(2,1)} %copy-done.2, bf16[64,512]{1,0:T(8,128)(2,1)} %copy-done.3, ...), custom_call_target="tpu_custom_call" | custom-call | tf_op jit(solution)/shard_map/negatives/pallas_call | solution.py:346
  68.8 2.0 %collective-permute-start.1 = (f32[512,256]{1,0:T(8,128)S(1)}, f32[512,256]{1,0:T(8,128)S(1)}, u32[]{:S(2)}, u32[]{:S(2)}) collective-permute-start(f32[512,256]{1,0:T(8,128)S(1)} %get-tuple-element.34), channel_id=1, source_target_pairs={{0,4},{4,0},{8,12},{12,8},{16,20},{20,16},{24,28},{28,24},{32,36},... | collective-permute-start | bytes 1572872 | tf_op jit(solution)/shard_map/ppermute | solution.py:383
  70.9 1.8 collective-permute-done.1.got
  72.7 3.3 %collective-permute-start.2 = (f32[128,256]{1,0:T(8,128)S(1)}, f32[128,256]{1,0:T(8,128)S(1)}, u32[]{:S(2)}, u32[]{:S(2)}) collective-permute-start(f32[128,256]{1,0:T(8,128)S(1)} %get-tuple-element.36), channel_id=1, source_target_pairs={{0,1},{1,2},{2,3},{3,0},{4,5},{5,6},{6,7},{7,4},{8,9},{9,10},{10,1... | collective-permute-start | bytes 393224 | tf_op jit(solution)/shard_map/ppermute | solution.py:379
  76.0 4.6 %collective-permute-start.3 = (f32[128,256]{1,0:T(8,128)S(1)}, f32[128,256]{1,0:T(8,128)S(1)}, u32[]{:S(2)}, u32[]{:S(2)}) collective-permute-start(f32[128,256]{1,0:T(8,128)S(1)} %get-tuple-element.37), channel_id=1, source_target_pairs={{0,2},{1,3},{2,0},{3,1},{4,6},{5,7},{6,4},{7,5},{8,10},{9,11},{10,... | collective-permute-start | bytes 393224 | tf_op jit(solution)/shard_map/ppermute | solution.py:379
  80.6 1.9 collective-permute-start.4
  82.6 1.2 pair.1.same
  83.8 1.2 collective-permute-done.3.sum2
  85.0 2.5 %collective-permute-done.4.sum3 = f32[128,256]{1,0:T(8,128)S(1)} collective-permute-done((f32[128,256]{1,0:T(8,128)S(1)}, f32[128,256]{1,0:T(8,128)S(1)}, u32[]{:S(2)}, u32[]{:S(2)}) %collective-permute-start.4) | collective-permute-done | bytes 131104 | tf_op jit(solution)/shard_map/ppermute | solution.py:379
  87.5 6.9 %all-to-all-done.1 = f32[128,1,1664]{2,1,0:T(1,128)S(1)} async-done(((f32[128,1,1664]{2,1,0:T(1,128)}), f32[128,1,1664]{2,1,0:T(1,128)S(1)}, u32[]{:S(2)}, u32[]{:S(2)}) %all-to-all-start.1) | async-done | bytes 852000 | tf_op jit(solution)/shard_map/all_to_all | solution.py:373
  94.4 2.8 %edge.1 = (f32[1920,128]{1,0:T(8,128)}, f32[8,128]{1,0:T(8,128)}) custom-call(f32[1664,128]{1,0:T(8,128)S(1)} %bitcast.24, bf16[512,256]{1,0:T(8,128)(2,1)S(1)} %pair.1.same, f32[128,256]{1,0:T(8,128)} %copy-done.4, f32[128,256]{1,0:T(8,128)S(1)} %collective-permute-done.2.sum1, f32[128,256]{1,0:T(8,128)S(1)} %collective-permute-done.3.sum2, ...), custom_call_target="tpu_custom_call" | custom-call | tf_op jit(solution)/shard_map/edge/pallas_call | solution.py:346
  97.2 9.2 %all-to-all-start.2 = ((f32[128,1,1920]{2,1,0:T(1,128)}), f32[128,1,1920]{2,1,0:T(1,128)S(1)}, u32[]{:S(2)}, u32[]{:S(2)}) async-start(f32[128,1,1920]{2,1,0:T(1,128)} %bitcast.33), calls=%async_computation.2 | async-start | bytes 1966080 | tf_op jit(solution)/shard_map/all_to_all | solution.py:373
  106.4 1.0 place.1.hot
  107.4 1.9 %carry.1.side = f32[768,512]{1,0:T(8,128)S(1)} custom-call(f32[8,128]{1,0:T(8,128)} %get-tuple-element.40.token, f32[256,128]{1,0:T(8,128)S(1)} %bitcast.30, f32[512,512]{1,0:T(8,128)} %copy-done.1, bf16[64,512]{1,0:T(8,128)(2,1)} %copy-done.2, bf16[64,512]{1,0:T(8,128)(2,1)} %copy-done.3), custom_call_target="tpu_custom_call" | custom-call | tf_op jit(solution)/shard_map/carry/pallas_call | solution.py:346
  109.4 48.9 %all-to-all-done.2 = f32[128,1,1920]{2,1,0:T(1,128)S(1)} async-done(((f32[128,1,1920]{2,1,0:T(1,128)}), f32[128,1,1920]{2,1,0:T(1,128)S(1)}, u32[]{:S(2)}, u32[]{:S(2)}) %all-to-all-start.2) | async-done | bytes 983072 | tf_op jit(solution)/shard_map/all_to_all | solution.py:373
  158.3 2.2 %scatter.1 = f32[1664,128]{1,0:T(8,128)} custom-call(f32[1920,128]{1,0:T(8,128)S(1)} %bitcast.23, bf16[512,640]{1,0:T(8,128)(2,1)S(1)} %place.1.hot, f32[768,512]{1,0:T(8,128)S(1)} %carry.1.side), custom_call_target="tpu_custom_call" | custom-call | tf_op jit(solution)/shard_map/scatter/pallas_call | solution.py:346
  160.5 3.6 %all-to-all-start.3 = ((f32[4,416,128]{2,1,0:T(8,128)}), f32[4,416,128]{2,1,0:T(8,128)S(1)}, u32[]{:S(2)}, u32[]{:S(2)}) async-start(f32[4,416,128]{2,1,0:T(8,128)} %bitcast.32), calls=%async_computation.3 | async-start | bytes 1703936 | tf_op jit(solution)/shard_map/all_to_all | solution.py:496
  164.2 1.6 cut.1.block
  165.8 11.9 %all-to-all-done.3 = f32[4,416,128]{2,1,0:T(8,128)S(1)} async-done(((f32[4,416,128]{2,1,0:T(8,128)}), f32[4,416,128]{2,1,0:T(8,128)S(1)}, u32[]{:S(2)}, u32[]{:S(2)}) %all-to-all-start.3) | async-done | bytes 852000 | tf_op jit(solution)/shard_map/all_to_all | solution.py:496
  177.7 0.3 update.1
  178.0 14.5 %all-gather = f32[1632,128]{1,0:T(8,128)S(1)} all-gather(f32[408,128]{1,0:T(8,128)S(1)} %update.1), channel_id=2, replica_groups=mesh['ent'=128,'rep'=4] {'rep'}, dimensions={0}, use_global_device_ids=true | all-gather | bytes 1044480 | tf_op jit(solution)/shard_map/all_gather | solution.py:505
  192.5 1.0 join.1
  (15 shorter events, 0.1 us)
Async XLA Ops:
  0.6 21.9 %copy-start = (f32[512,400]{0,1:T(8,128)S(1)}, f32[512,400]{0,1:T(8,128)}, u32[]{:S(2)}) copy-start(f32[512,400]{0,1:T(8,128)} %param.9) | copy-start | bytes 2457604
  3.2 35.4 %all-to-all-start = ((f32[128,1,256]{2,1,0:T(1,128)}), f32[128,1,256]{2,1,0:T(1,128)S(1)}, u32[]{:S(2)}, u32[]{:S(2)}) async-start(f32[128,1,256]{2,1,0:T(1,128)} %bitcast.35), calls=%async_computation | async-start | bytes 262144 | tf_op jit(solution)/shard_map/all_to_all | solution.py:373
  22.6 0.9 copy-start.5
  23.9 37.1 %copy-start.2 = (bf16[64,512]{1,0:T(8,128)(2,1)}, bf16[64,512]{1,0:T(8,128)(2,1)S(1)}, u32[]{:S(2)}) copy-start(bf16[64,512]{1,0:T(8,128)(2,1)S(1)} %get-tuple-element.26.refs_2_.refs_0_) | copy-start | bytes 196612
  23.9 37.1 %copy-start.3 = (bf16[64,512]{1,0:T(8,128)(2,1)}, bf16[64,512]{1,0:T(8,128)(2,1)S(1)}, u32[]{:S(2)}) copy-start(bf16[64,512]{1,0:T(8,128)(2,1)S(1)} %get-tuple-element.27.refs_3_.refs_1_) | copy-start | bytes 196612
  40.7 53.6 %all-to-all-start.1 = ((f32[128,1,1664]{2,1,0:T(1,128)}), f32[128,1,1664]{2,1,0:T(1,128)S(1)}, u32[]{:S(2)}, u32[]{:S(2)}) async-start(f32[128,1,1664]{2,1,0:T(1,128)} %bitcast.34), calls=%async_computation.1 | async-start | bytes 1703936 | tf_op jit(solution)/shard_map/all_to_all | solution.py:373
  61.0 3.8 %collective-permute-start = (f32[1024,128]{1,0:T(8,128)S(1)}, f32[1024,128]{1,0:T(8,128)S(1)}, u32[]{:S(2)}, u32[]{:S(2)}) collective-permute-start(f32[1024,128]{1,0:T(8,128)S(1)} %all_gather.9.refs_2_), channel_id=1, source_target_pairs={{0,4},{4,0},{8,12},{12,8},{16,20},{20,16},{24,28},{28,24},{32,36},... | collective-permute-start | bytes 1572872 | tf_op jit(solution)/shard_map/ppermute | solution.py:383
  68.8 16.2 %copy-start.1 = (f32[512,512]{1,0:T(8,128)}, f32[512,512]{1,0:T(8,128)S(1)}, u32[]{:S(2)}) copy-start(f32[512,512]{1,0:T(8,128)S(1)} %get-tuple-element.41.back) | copy-start | bytes 3145732
  68.8 3.8 %collective-permute-start.1 = (f32[512,256]{1,0:T(8,128)S(1)}, f32[512,256]{1,0:T(8,128)S(1)}, u32[]{:S(2)}, u32[]{:S(2)}) collective-permute-start(f32[512,256]{1,0:T(8,128)S(1)} %get-tuple-element.34), channel_id=1, source_target_pairs={{0,4},{4,0},{8,12},{12,8},{16,20},{20,16},{24,28},{28,24},{32,36},... | collective-permute-start | bytes 1572872 | tf_op jit(solution)/shard_map/ppermute | solution.py:383
  72.7 12.3 %copy-start.4 = (f32[128,256]{1,0:T(8,128)}, f32[128,256]{1,0:T(8,128)S(1)}, u32[]{:S(2)}) copy-start(f32[128,256]{1,0:T(8,128)S(1)} %get-tuple-element.35.sum0) | copy-start | bytes 393220
  72.7 11.1 %collective-permute-start.2 = (f32[128,256]{1,0:T(8,128)S(1)}, f32[128,256]{1,0:T(8,128)S(1)}, u32[]{:S(2)}, u32[]{:S(2)}) collective-permute-start(f32[128,256]{1,0:T(8,128)S(1)} %get-tuple-element.36), channel_id=1, source_target_pairs={{0,1},{1,2},{2,3},{3,0},{4,5},{5,6},{6,7},{7,4},{8,9},{9,10},{10,1... | collective-permute-start | bytes 393224 | tf_op jit(solution)/shard_map/ppermute | solution.py:379
  76.0 9.0 %collective-permute-start.3 = (f32[128,256]{1,0:T(8,128)S(1)}, f32[128,256]{1,0:T(8,128)S(1)}, u32[]{:S(2)}, u32[]{:S(2)}) collective-permute-start(f32[128,256]{1,0:T(8,128)S(1)} %get-tuple-element.37), channel_id=1, source_target_pairs={{0,2},{1,3},{2,0},{3,1},{4,6},{5,7},{6,4},{7,5},{8,10},{9,11},{10,... | collective-permute-start | bytes 393224 | tf_op jit(solution)/shard_map/ppermute | solution.py:379
  80.6 6.9 %collective-permute-start.4 = (f32[128,256]{1,0:T(8,128)S(1)}, f32[128,256]{1,0:T(8,128)S(1)}, u32[]{:S(2)}, u32[]{:S(2)}) collective-permute-start(f32[128,256]{1,0:T(8,128)S(1)} %get-tuple-element.38), channel_id=1, source_target_pairs={{0,3},{1,0},{2,1},{3,2},{4,7},{5,4},{6,5},{7,6},{8,11},{9,8},{10,9... | collective-permute-start | bytes 393224 | tf_op jit(solution)/shard_map/ppermute | solution.py:379
  97.2 61.1 %all-to-all-start.2 = ((f32[128,1,1920]{2,1,0:T(1,128)}), f32[128,1,1920]{2,1,0:T(1,128)S(1)}, u32[]{:S(2)}, u32[]{:S(2)}) async-start(f32[128,1,1920]{2,1,0:T(1,128)} %bitcast.33), calls=%async_computation.2 | async-start | bytes 1966080 | tf_op jit(solution)/shard_map/all_to_all | solution.py:373
  160.5 17.2 %copy-start.6 = (f32[512]{0:T(512)S(1)}, f32[512]{0:T(512)}, u32[]{:S(2)}) copy-start(f32[512]{0:T(512)} %param.10) | copy-start | bytes 6148
  160.5 17.1 %all-to-all-start.3 = ((f32[4,416,128]{2,1,0:T(8,128)}), f32[4,416,128]{2,1,0:T(8,128)S(1)}, u32[]{:S(2)}, u32[]{:S(2)}) async-start(f32[4,416,128]{2,1,0:T(8,128)} %bitcast.32), calls=%async_computation.3 | async-start | bytes 1703936 | tf_op jit(solution)/shard_map/all_to_all | solution.py:496

commit v6 on v5

--- a/solution.py
+++ b/solution.py
@@ -18,8 +18,9 @@
 PIECES = 2
 TILES1 = 2
 TILES2 = 13
-TILES3 = 15
-GROUP = 32
+TILES3 = 4
+STARTS = (0, 56, 104, 152)
+SIZES = (56, 48, 48, 48)
 
 
 def dot(a, b, dims):
@@ -68,12 +69,12 @@
     return jnp.sum(jnp.where(lanes(tile.shape) == lane, tile, 0.0), 1, keepdims=True)
 
 
-def pack(ref, tiles, halves, base=0):
+def pack(ref, tiles, halves):
     n = halves[0].shape[0]
     at = lanes((n, LANE))
     tail = jnp.zeros((n, LANE), f32)
     for i, half in enumerate(halves):
-        ref[pl.ds(base + i, n, stride=tiles), :] = half[:, :LANE]
+        ref[pl.ds(i, n, stride=tiles), :] = half[:, :LANE]
         rest = half[:, LANE:]
         shift = (8 * i - 64) % LANE
         moved = pltpu.roll(rest, shift, 1) if shift else rest
@@ -82,8 +83,8 @@
         pair = halves[i][:, LANE:]
         if i + 1 < len(halves):
             pair = jnp.where(at < 64, pair, pltpu.roll(halves[i + 1][:, LANE:], 64, 1))
-        ref[pl.ds(base + len(halves) + i // 2, n, stride=tiles), :] = pair
-    ref[pl.ds(base + tiles - 1, n, stride=tiles), :] = tail
+        ref[pl.ds(len(halves) + i // 2, n, stride=tiles), :] = pair
+    ref[pl.ds(tiles - 1, n, stride=tiles), :] = tail
 
 
 def unpack(ref, tiles, count, n):
@@ -99,6 +100,26 @@
         moved = pltpu.roll(tail, shift, 1) if shift else tail
         rest = jnp.where(at < 64, pair, jnp.where(at < 72, moved, 0.0))
         out.append(jnp.concatenate([full, rest], 1))
+    return out
+
+
+def window(into, low, high, start, size, dest):
+    at = lanes(into.shape)
+    for src, first in ((low, 0), (high, LANE)):
+        begin, end = max(start, first), min(start + size, first + LANE)
+        if begin < end:
+            goal = dest + begin - start
+            shift = (goal - (begin - first)) % LANE
+            moved = pltpu.roll(src, shift, 1) if shift else src
+            into = jnp.where((at >= goal) & (at < goal + end - begin), moved, into)
+    return into
+
+
+def quarter(wide, q):
+    out = jnp.zeros((wide.shape[0], LANE), f32)
+    for i in range(2):
+        low, high = (wide[:, (2 * i + j) * LANE : (2 * i + j + 1) * LANE] for j in range(2))
+        out = window(out, low, high, STARTS[q], SIZES[q], 64 * i)
     return out
 
 
@@ -264,81 +285,128 @@
     to_head = coef * met
     to_tail = pick(same[2 * n :, :], parts(coef * query, PIECES), NN)
     neg = sum0[...] + sum1[...] + (sum2[...] + sum3[...])
-    out = []
-    for block in (to_head[:n], to_head[n:], to_tail[:n], to_tail[n:]):
-        out += split(block)
-    pack(send, TILES3, out + [neg])
+    low, high = neg[:, :LANE], neg[:, LANE:]
+    for s, block in enumerate((to_head[:n], to_head[n:], to_tail[:n], to_tail[n:])):
+        for q in range(4):
+            tile = quarter(block, q)
+            for i in range(2):
+                word = 16 * s + 8 * i
+                if word < 56:
+                    tile = window(tile, low, high, STARTS[q] + word, 8, 56 + 64 * i)
+            send[pl.ds(4 * q + s, n, stride=4 * TILES3), :] = tile
     token[...] = neg[0:8, 0:128]
 
 
-def carry_kernel(token, asks, back, *refs):
+def local_kernel(rep, token, asks, back, *refs):
     n = 2 * LANE
-    *rel, side = refs
+    *rel, out0, out1, out2, out3, quarters = refs
     tile = asks[pl.ds(1, LANE, stride=TILES1), :]
-    side[0:n, :] = back[0:n, :]
-    turned = cmul(split(back[n:, :]), rel_vectors(tile, (2, 3), rel))
-    side[n : 2 * n, :] = jnp.concatenate(turned, 1)
-    side[2 * n :, :] = jnp.concatenate(rel_vectors(tile, (0, 1), rel), 1)
-
-
-def place_kernel(rep, neg_rows, asks, token, hot):
-    n = LANE
-    turned = asks[pl.ds(1, n, stride=TILES1), :].T
-    sub = lax.broadcasted_iota(jnp.int32, (512, n), 0)
+    turned = tile.T
+    sub = lax.broadcasted_iota(jnp.int32, (512, LANE), 0).astype(f32)
+    hot = jnp.concatenate(
+        [
+            jnp.where(sub == turned[72 + 2 * s : 73 + 2 * s, :], 1.0, 0.0).astype(bf16)
+            for s in range(4)
+        ],
+        1,
+    )
+    head = cmul(split(back[0:n, :]), conj(rel_vectors(tile, (0, 1), rel)))
+    tail = cmul(split(back[n:, :]), rel_vectors(tile, (2, 3), rel))
+    grad = jnp.concatenate([jnp.concatenate(head, 1), jnp.concatenate(tail, 1)], 0)
+    total = pick(hot, parts(grad, PIECES), NN)
+    for q in range(4):
+        quarters[q] = quarter(total, q)
+    for i, ref in enumerate((out0, out1, out2, out3)):
+        ref[...] = quarters[(rep[0] + i) % 4]
+
+
+def gather_local_kernel(part0, part1, part2, part3, out):
+    out[...] = part0[...] + part1[...] + (part2[...] + part3[...])
+
+
+def rels_kernel(rep, token, asks, relations, out):
+    pad = jnp.zeros((64, 56), f32)
+    wide = jnp.concatenate([relations[:, :200], pad, relations[:, 200:], pad], 1)
+    mine = jnp.zeros((64, LANE), f32)
+    for q in range(4):
+        mine = jnp.where(rep[0] == q, quarter(wide, q), mine)
+    pieces = parts(mine, PIECES)
+    for x in range(4):
+        tile = asks[pl.ds(x * TILES1 * LANE + 1, LANE, stride=TILES1), :]
+        ids = jnp.concatenate([column(tile, 73), column(tile, 75)], 0)
+        hot = jnp.where(lanes((2 * LANE, 64)).astype(f32) == ids, 1.0, 0.0).astype(bf16)
+        out[2 * x * LANE : 2 * (x + 1) * LANE, :] = pick(hot, pieces, NN)
+
+
+def place_kernel(neg_rows, asks, token, hot):
+    n = LANE
+    sub = lax.broadcasted_iota(jnp.int32, (512, n), 0).astype(f32)
+    for x in range(4):
+        turned = asks[pl.ds(x * TILES1 * n + 1, n, stride=TILES1), :].T
+        for s in range(4):
+            at = turned[72 + 2 * s : 73 + 2 * s, :]
+            b = 4 * x + s
+            hot[:, b * n : (b + 1) * n] = jnp.where(sub == at, 1.0, 0.0).astype(bf16)
+    at = jnp.full((1, n), -1.0, f32)
+    for x in range(4):
+        at = jnp.where(lanes((1, n)) == x, neg_rows[x].astype(f32), at)
+    hot[:, 16 * n :] = jnp.where(sub == at, 1.0, 0.0).astype(bf16)
+
+
+def scatter_kernel(recv, hot, rels, local, out):
+    n = LANE
+    at = lanes((n, n))
+    even = lax.broadcasted_iota(jnp.int32, (n, n), 0) % 2 == 0
+    which = lax.broadcasted_iota(jnp.int32, (8, n), 0)
+    sums = [[jnp.zeros((8, n), f32) for _ in range(2)] for _ in range(4)]
+    blocks = []
+    for x in range(4):
+        for s in range(4):
+            tile = recv[pl.ds(4 * x + s, n, stride=4 * TILES3), :]
+            reals = jnp.sum(jnp.where(even, tile, 0.0), 0, keepdims=True)
+            imags = jnp.sum(jnp.where(even, 0.0, tile), 0, keepdims=True)
+            sums[s] = [
+                jnp.where(which == x, new, old) for old, new in zip(sums[s], (reals, imags))
+            ]
+            if s < 2:
+                rel = rels[(2 * x + s) * n : (2 * x + s + 1) * n, :]
+                other = pltpu.roll(rel, 64, 1)
+                tile = tile * jnp.where(at < 64, rel, other) + pltpu.roll(
+                    tile, 64, 1
+                ) * jnp.where(at < 64, other, -rel)
+            blocks.append(tile)
+    neg = jnp.zeros((8, n), f32)
+    lane = lanes((8, n))
     for s in range(4):
-        at = turned[72 + 2 * s : 73 + 2 * s, :]
-        hot[:, s * n : (s + 1) * n] = jnp.where(sub.astype(f32) == at, 1.0, 0.0).astype(bf16)
-    hot[:, 4 * n :] = jnp.where(sub == neg_rows[rep[0]], 1.0, 0.0).astype(bf16)
-
-
-def scatter_kernel(recv, hot, side, out):
-    n = LANE
-    halves = unpack(recv, TILES3, 9, n)
-    even = lax.broadcasted_iota(jnp.int32, (n, 256), 0) % 2 == 0
-    halves = halves[:8] + [jnp.where(even, halves[8], 0.0), jnp.where(even, 0.0, halves[8])]
-    blocks = [jnp.concatenate(halves[i : i + 2], 1) for i in range(0, 10, 2)]
-    head = split(jnp.concatenate(blocks[0:2], 0) + side[0 : 2 * n, :])
-    head = jnp.concatenate(cmul(head, conj(split(side[4 * n :, :]))), 1)
-    tail = jnp.concatenate(blocks[2:4], 0) + side[2 * n : 4 * n, :]
-    grad = jnp.concatenate([head, tail, blocks[4]], 0)
-    total = pick(hot[...], parts(grad, PIECES), NN)
-    for q in range(4):
-        groups = []
-        for g in range(4):
-            start = q * n + g * GROUP
-            groups += split(total[start : start + GROUP, :])
-        pack(out, TILES2, groups, q * TILES2 * GROUP)
-
-
-def update_kernel(rep, grads, block, state, out, sums):
-    n = LANE
-    rows = TILES2 * GROUP
-    sums[...] = (
-        grads[0:rows, :] + grads[rows : 2 * rows, :]
-        + (grads[2 * rows : 3 * rows, :] + grads[3 * rows :, :])
-    )
-    halves = unpack(sums, TILES2, 8, GROUP)
-    grad = jnp.concatenate(
-        [jnp.concatenate(halves[i::2], 0).T[0:200, :] for i in range(2)], 0
-    )
-    start = pl.multiple_of(rep[0] * n, n)
-    mean = jnp.sum(grad * grad, 0, keepdims=True) * (1.0 / 400.0)
-    new = state[:, pl.ds(start, n)] + mean
-    out[0:400, :] = block[...] - learn_rate * grad / jnp.sqrt(new)
-    out[400:408, :] = jnp.broadcast_to(new, (8, n))
-
-
-def cut_kernel(rep, token, table_t, block, done):
-    start = pl.multiple_of(rep[0] * LANE, LANE)
-    copy = pltpu.make_async_copy(table_t.at[:, pl.ds(start, LANE)], block, done)
-    copy.start()
-    copy.wait()
-
-
-def join_kernel(parts_in, table_new, state_new):
-    for q in range(4):
-        table_new[:, q * LANE : (q + 1) * LANE] = parts_in[q, 0:400, :]
-        state_new[:, q * LANE : (q + 1) * LANE] = parts_in[q, 400:401, :]
+        for i in range(2):
+            word = 16 * s + 8 * i
+            if word < 56:
+                for side in range(2):
+                    goal = 64 * side + word
+                    shift = (goal - (56 + 64 * i)) % n
+                    moved = pltpu.roll(sums[s][side], shift, 1) if shift else sums[s][side]
+                    neg = jnp.where((lane >= goal) & (lane < goal + 8), moved, neg)
+    blocks += [neg, jnp.zeros((n - 8, n), f32)]
+    both = jnp.concatenate(parts(jnp.concatenate(blocks, 0), 2), 1)
+    total = dot(hot[...], both, NN)
+    turned = (total[:, :n] + total[:, n:] + local[...]).T
+    out[0:56, :] = turned[0:56, :]
+    out[56:112, :] = turned[64:120, :]
+
+
+def finish_kernel(grads, table_t, state, table_new, state_new):
+    spans = [
+        (q * 112 + i * 56, i * 200 + STARTS[q], SIZES[q]) for q in range(4) for i in range(2)
+    ]
+    total = jnp.zeros((1, 512), f32)
+    for at, _, size in spans:
+        grad = grads[at : at + size, :]
+        total = total + jnp.sum(grad * grad, 0, keepdims=True)
+    new = state[...] + total * (1.0 / 400.0)
+    state_new[...] = new
+    step = learn_rate / jnp.sqrt(new)
+    for at, to, size in spans:
+        table_new[to : to + size, :] = table_t[to : to + size, :] - grads[at : at + size, :] * step
 
 
 def call(kernel, outs, args, scalars=(), name=None, scratch=(), whole=0):
@@ -368,7 +436,7 @@
 
 
 def exchange(x, axis, tiles):
-    n = lax.axis_size(axis)
+    n = x.shape[0] // tiles
     x = x.reshape(n, 1, tiles * LANE)
     x = lax.all_to_all(x, axis, split_axis=0, concat_axis=0, tiled=True)
     return x.reshape(n * tiles, LANE)
@@ -463,48 +531,44 @@
     sums = [owned[0]] + [shift(owned[j], j) for j in (1, 2, 3)]
     send3, token = call(
         edge_kernel,
-        [((n * TILES3, n), f32, False), ((8, n), f32, False)],
+        [((4 * n * TILES3, n), f32, False), ((8, n), f32, False)],
         (near(recv2), near(same), far(sums[0]), *map(near, sums[1:])),
         name="edge",
     )
-    recv3 = exchange(send3, "ent", TILES3)
+    recv3 = exchange(send3, ("ent", "rep"), TILES3)
     token = far(token)
-    (side,) = call(
-        carry_kernel,
-        [((6 * n, 512), f32, True)],
+    local = call(
+        local_kernel,
+        [((4 * n, n), f32, True)] * 4,
         (token, recv1, far(back), *map(far, rel_pieces)),
-        name="carry",
+        (rep,),
+        "local",
+        (pltpu.VMEM((4, 4 * n, n), f32),),
+    )
+    (local,) = call(
+        gather_local_kernel,
+        [((4 * n, n), f32, True)],
+        [far(local[0])] + [far(shift(local[j], j)) for j in (1, 2, 3)],
+        name="gather_local",
     )
     (hot,) = call(
-        place_kernel, [((4 * n, 5 * n), bf16, True)], (recv1, token), (rep, neg_rows), "place"
-    )
-    (block,) = call(
-        cut_kernel,
-        [((400, n), f32, True)],
-        (token, far(table_t)),
-        (rep,),
-        "cut",
-        (pltpu.SemaphoreType.DMA,),
-        1,
+        place_kernel, [((4 * n, 17 * n), bf16, True)], (far(mine), token), (neg_rows,), "place"
+    )
+    (rels,) = call(
+        rels_kernel, [((8 * n, n), f32, True)], (near(local), far(mine), relations), (rep,), "rels"
     )
     (grads,) = call(
         scatter_kernel,
-        [((4 * TILES2 * GROUP, n), f32, False)],
-        (near(recv3), near(hot), near(side)),
+        [((112, 512), f32, True)],
+        (near(recv3), near(hot), near(rels), near(local)),
         name="scatter",
     )
-    grads = lax.all_to_all(grads, "rep", split_axis=0, concat_axis=0, tiled=True)
-    (fresh,) = call(
-        update_kernel,
-        [((408, n), f32, True)],
-        (near(grads), near(block), adagrad_state.reshape(1, 512)),
-        (rep,),
-        "update",
-        (pltpu.VMEM((TILES2 * GROUP, n), f32),),
-    )
-    fresh = lax.all_gather(fresh, "rep", axis=0, tiled=False)
+    grads = lax.all_gather(grads, "rep", axis=0, tiled=True)
     table_new, state_new = call(
-        join_kernel, [((400, 512), f32, False), ((1, 512), f32, False)], (near(fresh),), name="join"
+        finish_kernel,
+        [((400, 512), f32, False), ((1, 512), f32, False)],
+        (near(grads), table_t, adagrad_state.reshape(1, 512)),
+        name="finish",
     )
     return (table_new.T, state_new.reshape(512))
 

time: 195 us -> 187 us (0.959); the launches traced: 193 us -> 183 us
  waiting for transfers between devices: 89.8 us -> 62.2 us
  starting transfers between devices: 53 us -> 63.5 us
  local copies, waits for them, and re-layouts: 0.93 us -> 5.3 us
  Pallas kernels: 21.2 us -> 24.2 us
    all_to_all x3, waiting for transfers between devices: 70.6 us -> 45 us  [exchange(): x = lax.all_to_all(x, axis, split_axis=0, concat_axis=0, tiled=True)]
    all_to_all x1 -> x0, waiting for transfers between devices: 11.9 us -> none  [on_device(): lax.all_to_all(grads, 'rep', split_axis=0, concat_axis=0, tiled=True)]
    ppermute x3 -> x6, starting transfers between devices: 9.83 us -> 21.3 us  [shift(): return lax.ppermute(x, 'rep', [(i, (i + by) % n) for i in range(n)])]
    ppermute x3 -> x6, waiting for transfers between devices: 3.7 us -> 13.6 us  [shift(): return lax.ppermute(x, 'rep', [(i, (i + by) % n) for i in range(n)])]
    unnamed x14 -> x32, local copies, waits for them, and re-layouts: 0.93 us -> 5.3 us
    all_to_all x1 -> x0, starting transfers between devices: 3.63 us -> none  [on_device(): lax.all_to_all(grads, 'rep', split_axis=0, concat_axis=0, tiled=True)]
    pallas_call x13, Pallas kernels: 21.2 us -> 24.2 us  [call(): pl.pallas_call(kernel, out_shape=[(pltpu.VMEM if near else pltpu.HBM)(sha...]
    all_to_all x3, starting transfers between devices: 35.6 us -> 38.2 us  [exchange(): x = lax.all_to_all(x, axis, split_axis=0, concat_axis=0, tiled=True)]
  transfers between devices with their start and end apart: 9 -> 11, of which waited for: 8 -> 9; matrix products, arithmetic and copies ran while one was open for 0% -> 0% of each run, Pallas kernels for 5% -> 7%
where the time goes in v6:
time: 187 us; the launch traced here: 183 us
  starting transfers between devices  63.5 us (34%)
  waiting for transfers between devices  62.2 us (33%)
  blocking collectives  27.3 us (15%)
  Pallas kernels  24.2 us (13%)
  local copies, waits for them, and re-layouts  5.3 us (3%)
    all_to_all x3, waiting for transfers between devices, exchange(): x = lax.all_to_all(x, axis, split_axis=0, concat_axis=0, tiled=True)  45 us
    all_to_all x3, starting transfers between devices, exchange(): x = lax.all_to_all(x, axis, split_axis=0, concat_axis=0, tiled=True)  38.2 us
    pallas_call x13, Pallas kernels, call(): pl.pallas_call(kernel, out_shape=[(pltpu.VMEM if near else pltpu.HBM)(sha...  24.2 us
    ppermute x6, starting transfers between devices, shift(): return lax.ppermute(x, 'rep', [(i, (i + by) % n) for i in range(n)])  21.3 us
    all_gather x1, blocking collectives, on_device(): grads = lax.all_gather(grads, 'rep', axis=0, tiled=True)  14.2 us
    ppermute x6, waiting for transfers between devices, shift(): return lax.ppermute(x, 'rep', [(i, (i + by) % n) for i in range(n)])  13.6 us
    all_gather x1, blocking collectives, on_device(): mine = lax.all_gather(own_negs, 'rep', axis=0, tiled=True)  13.1 us
    unnamed x32, local copies, waits for them, and re-layouts  5.3 us
  transfers between devices with their start and end apart: 11, of which 9 were waited for; matrix products, arithmetic and copies ran while one was open for 0% of the time, Pallas kernels for 7%

profile of v6, /device:TPU:24, one launch (start us, length us, event | category | flops | bytes accessed | tf_op | source)
XLA Modules:
  0.0 183.4 jit_solution(4335205856067781202)
XLA Ops:
  0.6 2.6 %ask.1 = (f32[256,128]{1,0:T(8,128)}, f32[128,128]{1,0:T(8,128)}, f32[128,128]{1,0:T(8,128)}) custom-call(s32[1]{0:T(128)} %bitcast.rep, s32[4]{0:T(128)} %neg_rows.3, s32[1,128]{1,0:T(1,128)} %bitcast.29, s32[1,128]{1,0:T(1,128)} %bitcast.30, s32[1,128]{1,0:T(1,128)} %bitcast.31, s32[1,128]{1,0:T(1,128)} %bitcast.32, s32[1,128]{1,0:T(1,128)} %bitcast.33, ...), custom_call_target="tpu_custom_call" | custom-call | tf_op jit(solution)/shard_map/ask/pallas_call | solution.py:414
  3.2 19.3 %all-to-all-start = ((f32[128,1,256]{2,1,0:T(1,128)}), f32[128,1,256]{2,1,0:T(1,128)S(1)}, u32[]{:S(2)}, u32[]{:S(2)}) async-start(f32[128,1,256]{2,1,0:T(1,128)} %bitcast.28), calls=%async_computation | async-start | bytes 262144 | tf_op jit(solution)/shard_map/all_to_all | solution.py:441
  25.0 13.7 %all-to-all-done = f32[128,1,256]{2,1,0:T(1,128)S(1)} async-done(((f32[128,1,256]{2,1,0:T(1,128)}), f32[128,1,256]{2,1,0:T(1,128)S(1)}, u32[]{:S(2)}, u32[]{:S(2)}) %all-to-all-start) | async-done | bytes 131104 | tf_op jit(solution)/shard_map/all_to_all | solution.py:441
  38.7 2.1 %fetch.1 = (f32[1664,128]{1,0:T(8,128)}, f32[512,512]{1,0:T(8,128)S(1)}, f32[256,128]{1,0:T(8,128)S(1)}) custom-call(f32[256,128]{1,0:T(8,128)S(1)} %bitcast.22, bf16[512,512]{1,0:T(8,128)(2,1)S(1)} %get-tuple-element.28.refs_0_, bf16[512,512]{1,0:T(8,128)(2,1)S(1)} %get-tuple-element.29.refs_1_, bf16[64,512]{1,0:T(8,128)(2,1)S(1)} %get-tuple-element.30.refs_2_.refs_0_, ...), custom_call_target="tpu_custom_call" | custom-call | tf_op jit(solution)/shard_map/fetch/pallas_call | solution.py:414
  40.7 7.1 %all-to-all-start.1 = ((f32[128,1,1664]{2,1,0:T(1,128)}), f32[128,1,1664]{2,1,0:T(1,128)S(1)}, u32[]{:S(2)}, u32[]{:S(2)}) async-start(f32[128,1,1664]{2,1,0:T(1,128)} %bitcast.27), calls=%async_computation.1 | async-start | bytes 1703936 | tf_op jit(solution)/shard_map/all_to_all | solution.py:441
  47.8 13.1 %all_gather.6.refs_2_.asks = f32[1024,128]{1,0:T(8,128)S(1)} all-gather(f32[256,128]{1,0:T(8,128)S(1)} %get-tuple-element.36), channel_id=1, replica_groups=mesh['ent'=128,'rep'=4] {'rep'}, dimensions={0}, use_global_device_ids=true | all-gather | bytes 655360 | tf_op jit(solution)/shard_map/all_gather | solution.py:515
  61.0 1.9 %collective-permute-start = (f32[1024,128]{1,0:T(8,128)S(1)}, f32[1024,128]{1,0:T(8,128)S(1)}, u32[]{:S(2)}, u32[]{:S(2)}) collective-permute-start(f32[1024,128]{1,0:T(8,128)S(1)} %all_gather.6.refs_2_.asks), channel_id=1, source_target_pairs={{0,4},{4,0},{8,12},{12,8},{16,20},{20,16},{24,28},{28,24},{32,36},... | collective-permute-start | bytes 1572872 | tf_op jit(solution)/shard_map/ppermute | solution.py:451
  62.9 1.9 %collective-permute-done.refs_3_ = f32[1024,128]{1,0:T(8,128)S(1)} collective-permute-done((f32[1024,128]{1,0:T(8,128)S(1)}, f32[1024,128]{1,0:T(8,128)S(1)}, u32[]{:S(2)}, u32[]{:S(2)}) %collective-permute-start) | collective-permute-done | bytes 524320 | tf_op jit(solution)/shard_map/ppermute | solution.py:451
  64.8 4.0 %negatives.1 = (f32[512,512]{1,0:T(8,128)S(1)}, f32[512,256]{1,0:T(8,128)S(1)}, f32[512,256]{1,0:T(8,128)S(1)}) custom-call(s32[1]{0:T(128)} %bitcast.11.odd, f32[256,128]{1,0:T(8,128)S(1)} %bitcast.23, f32[512,512]{1,0:T(8,128)S(1)} %get-tuple-element.35.rows, bf16[64,512]{1,0:T(8,128)(2,1)} %copy-done.6, bf16[64,512]{1,0:T(8,128)(2,1)} %copy-done.7, ...), custom_call_target="tpu_custom_call" | custom-call | tf_op jit(solution)/shard_map/negatives/pallas_call | solution.py:414
  68.8 2.0 %collective-permute-start.1 = (f32[512,256]{1,0:T(8,128)S(1)}, f32[512,256]{1,0:T(8,128)S(1)}, u32[]{:S(2)}, u32[]{:S(2)}) collective-permute-start(f32[512,256]{1,0:T(8,128)S(1)} %get-tuple-element.38), channel_id=1, source_target_pairs={{0,4},{4,0},{8,12},{12,8},{16,20},{20,16},{24,28},{28,24},{32,36},... | collective-permute-start | bytes 1572872 | tf_op jit(solution)/shard_map/ppermute | solution.py:451
  70.9 1.8 collective-permute-done.1.got
  72.7 3.3 %collective-permute-start.2 = (f32[128,256]{1,0:T(8,128)S(1)}, f32[128,256]{1,0:T(8,128)S(1)}, u32[]{:S(2)}, u32[]{:S(2)}) collective-permute-start(f32[128,256]{1,0:T(8,128)S(1)} %get-tuple-element.40), channel_id=1, source_target_pairs={{0,1},{1,2},{2,3},{3,0},{4,5},{5,6},{6,7},{7,4},{8,9},{9,10},{10,1... | collective-permute-start | bytes 393224 | tf_op jit(solution)/shard_map/ppermute | solution.py:447
  76.0 4.6 %collective-permute-start.3 = (f32[128,256]{1,0:T(8,128)S(1)}, f32[128,256]{1,0:T(8,128)S(1)}, u32[]{:S(2)}, u32[]{:S(2)}) collective-permute-start(f32[128,256]{1,0:T(8,128)S(1)} %get-tuple-element.41), channel_id=1, source_target_pairs={{0,2},{1,3},{2,0},{3,1},{4,6},{5,7},{6,4},{7,5},{8,10},{9,11},{10,... | collective-permute-start | bytes 393224 | tf_op jit(solution)/shard_map/ppermute | solution.py:447
  80.6 1.9 %collective-permute-start.4 = (f32[128,256]{1,0:T(8,128)S(1)}, f32[128,256]{1,0:T(8,128)S(1)}, u32[]{:S(2)}, u32[]{:S(2)}) collective-permute-start(f32[128,256]{1,0:T(8,128)S(1)} %get-tuple-element.42), channel_id=1, source_target_pairs={{0,3},{1,0},{2,1},{3,2},{4,7},{5,4},{6,5},{7,6},{8,11},{9,8},{10,9... | collective-permute-start | bytes 393224 | tf_op jit(solution)/shard_map/ppermute | solution.py:447
  82.5 1.2 pair.1.same
  83.8 1.2 collective-permute-done.3.sum2
  85.0 2.5 %collective-permute-done.4.sum3 = f32[128,256]{1,0:T(8,128)S(1)} collective-permute-done((f32[128,256]{1,0:T(8,128)S(1)}, f32[128,256]{1,0:T(8,128)S(1)}, u32[]{:S(2)}, u32[]{:S(2)}) %collective-permute-start.4) | collective-permute-done | bytes 131104 | tf_op jit(solution)/shard_map/ppermute | solution.py:447
  87.5 6.9 %all-to-all-done.1 = f32[128,1,1664]{2,1,0:T(1,128)S(1)} async-done(((f32[128,1,1664]{2,1,0:T(1,128)}), f32[128,1,1664]{2,1,0:T(1,128)S(1)}, u32[]{:S(2)}, u32[]{:S(2)}) %all-to-all-start.1) | async-done | bytes 852000 | tf_op jit(solution)/shard_map/all_to_all | solution.py:441
  94.3 3.7 %edge.1 = (f32[2048,128]{1,0:T(8,128)}, f32[8,128]{1,0:T(8,128)}) custom-call(f32[1664,128]{1,0:T(8,128)S(1)} %bitcast.21, bf16[512,256]{1,0:T(8,128)(2,1)S(1)} %pair.1.same, f32[128,256]{1,0:T(8,128)} %copy-done.11, f32[128,256]{1,0:T(8,128)S(1)} %collective-permute-done.2.sum1, f32[128,256]{1,0:T(8,128)S(1)} %collective-permute-done.3.sum2, ...), custom_call_target="tpu_custom_call" | custom-call | tf_op jit(solution)/shard_map/edge/pallas_call | solution.py:414
  98.0 11.8 %all-to-all-start.2 = ((f32[512,1,512]{2,1,0:T(1,128)}), f32[512,1,512]{2,1,0:T(1,128)S(1)}, u32[]{:S(2)}, u32[]{:S(2)}) async-start(f32[512,1,512]{2,1,0:T(1,128)} %bitcast.26), calls=%async_computation.2 | async-start | bytes 2097152 | tf_op jit(solution)/shard_map/all_to_all | solution.py:441
  109.9 3.2 %local.1 = (f32[512,128]{1,0:T(8,128)S(1)}, f32[512,128]{1,0:T(8,128)S(1)}, f32[512,128]{1,0:T(8,128)S(1)}, f32[512,128]{1,0:T(8,128)S(1)}) custom-call(s32[1]{0:T(128)} %bitcast.rep, f32[8,128]{1,0:T(8,128)} %get-tuple-element.44.token, f32[256,128]{1,0:T(8,128)S(1)} %bitcast.24, f32[512,512]{1,0:T(8,128)} %copy-done.5, bf16[64,512]{1,0:T(8,128)(2,1)} %copy-done.6, ...), custom_call_target="tpu_custom_call" | custom-call | tf_op jit(solution)/shard_map/local/pallas_call | solution.py:414
  113.8 3.5 %collective-permute-start.5 = (f32[512,128]{1,0:T(8,128)S(1)}, f32[512,128]{1,0:T(8,128)S(1)}, u32[]{:S(2)}, u32[]{:S(2)}) collective-permute-start(f32[512,128]{1,0:T(8,128)S(1)} %get-tuple-element.47), channel_id=1, source_target_pairs={{0,1},{1,2},{2,3},{3,0},{4,5},{5,6},{6,7},{7,4},{8,9},{9,10},{10,1... | collective-permute-start | bytes 786440 | tf_op jit(solution)/shard_map/ppermute | solution.py:447
  117.3 4.6 %collective-permute-start.6 = (f32[512,128]{1,0:T(8,128)S(1)}, f32[512,128]{1,0:T(8,128)S(1)}, u32[]{:S(2)}, u32[]{:S(2)}) collective-permute-start(f32[512,128]{1,0:T(8,128)S(1)} %get-tuple-element.48), channel_id=1, source_target_pairs={{0,2},{1,3},{2,0},{3,1},{4,6},{5,7},{6,4},{7,5},{8,10},{9,11},{10,... | collective-permute-start | bytes 786440 | tf_op jit(solution)/shard_map/ppermute | solution.py:447
  121.9 3.4 %collective-permute-start.7 = (f32[512,128]{1,0:T(8,128)S(1)}, f32[512,128]{1,0:T(8,128)S(1)}, u32[]{:S(2)}, u32[]{:S(2)}) collective-permute-start(f32[512,128]{1,0:T(8,128)S(1)} %get-tuple-element.49), channel_id=1, source_target_pairs={{0,3},{1,0},{2,1},{3,2},{4,7},{5,4},{6,5},{7,6},{8,11},{9,8},{10,9... | collective-permute-start | bytes 786440 | tf_op jit(solution)/shard_map/ppermute | solution.py:447
  125.3 1.7 place.1.hot
  127.1 8.4 %collective-permute-done.6.part2 = f32[512,128]{1,0:T(8,128)S(1)} collective-permute-done((f32[512,128]{1,0:T(8,128)S(1)}, f32[512,128]{1,0:T(8,128)S(1)}, u32[]{:S(2)}, u32[]{:S(2)}) %collective-permute-start.6) | collective-permute-done | bytes 262176 | tf_op jit(solution)/shard_map/ppermute | solution.py:447
  135.5 1.5 collective-permute-done.7.part3
  137.7 1.2 gather_local.1.token.local
  138.9 1.7 rels.1
  141.5 24.4 %all-to-all-done.2 = f32[512,1,512]{2,1,0:T(1,128)S(1)} async-done(((f32[512,1,512]{2,1,0:T(1,128)}), f32[512,1,512]{2,1,0:T(1,128)S(1)}, u32[]{:S(2)}, u32[]{:S(2)}) %all-to-all-start.2) | async-done | bytes 1048608 | tf_op jit(solution)/shard_map/all_to_all | solution.py:441
  167.0 1.2 scatter.1
  168.2 14.2 %all_gather.7.grads = f32[448,512]{1,0:T(8,128)S(1)} all-gather(f32[112,512]{1,0:T(8,128)S(1)} %scatter.1), channel_id=1, replica_groups=mesh['ent'=128,'rep'=4] {'rep'}, dimensions={0}, use_global_device_ids=true | all-gather | bytes 1146880 | tf_op jit(solution)/shard_map/all_gather | solution.py:566
  (37 shorter events, 6.8 us)
Async XLA Ops:
  3.2 35.4 %all-to-all-start = ((f32[128,1,256]{2,1,0:T(1,128)}), f32[128,1,256]{2,1,0:T(1,128)S(1)}, u32[]{:S(2)}, u32[]{:S(2)}) async-start(f32[128,1,256]{2,1,0:T(1,128)} %bitcast.28), calls=%async_computation | async-start | bytes 262144 | tf_op jit(solution)/shard_map/all_to_all | solution.py:441
  22.5 1.1 copy-start.1
  23.7 0.9 copy-start.8
  25.0 39.8 %copy-start.6 = (bf16[64,512]{1,0:T(8,128)(2,1)}, bf16[64,512]{1,0:T(8,128)(2,1)S(1)}, u32[]{:S(2)}) copy-start(bf16[64,512]{1,0:T(8,128)(2,1)S(1)} %get-tuple-element.30.refs_2_.refs_0_) | copy-start | bytes 196612
  25.0 39.8 %copy-start.7 = (bf16[64,512]{1,0:T(8,128)(2,1)}, bf16[64,512]{1,0:T(8,128)(2,1)S(1)}, u32[]{:S(2)}) copy-start(bf16[64,512]{1,0:T(8,128)(2,1)S(1)} %get-tuple-element.31.refs_3_.refs_1_) | copy-start | bytes 196612
  40.7 53.6 %all-to-all-start.1 = ((f32[128,1,1664]{2,1,0:T(1,128)}), f32[128,1,1664]{2,1,0:T(1,128)S(1)}, u32[]{:S(2)}, u32[]{:S(2)}) async-start(f32[128,1,1664]{2,1,0:T(1,128)} %bitcast.27), calls=%async_computation.1 | async-start | bytes 1703936 | tf_op jit(solution)/shard_map/all_to_all | solution.py:441
  61.0 37.1 %copy-start = (f32[1024,128]{1,0:T(8,128)}, f32[1024,128]{1,0:T(8,128)S(1)}, u32[]{:S(2)}) copy-start(f32[1024,128]{1,0:T(8,128)S(1)} %all_gather.6.refs_2_.asks) | copy-start | bytes 1572868
  61.0 3.8 %collective-permute-start = (f32[1024,128]{1,0:T(8,128)S(1)}, f32[1024,128]{1,0:T(8,128)S(1)}, u32[]{:S(2)}, u32[]{:S(2)}) collective-permute-start(f32[1024,128]{1,0:T(8,128)S(1)} %all_gather.6.refs_2_.asks), channel_id=1, source_target_pairs={{0,4},{4,0},{8,12},{12,8},{16,20},{20,16},{24,28},{28,24},{32,36},... | collective-permute-start | bytes 1572872 | tf_op jit(solution)/shard_map/ppermute | solution.py:451
  68.8 16.2 %copy-start.5 = (f32[512,512]{1,0:T(8,128)}, f32[512,512]{1,0:T(8,128)S(1)}, u32[]{:S(2)}) copy-start(f32[512,512]{1,0:T(8,128)S(1)} %get-tuple-element.45.back) | copy-start | bytes 3145732
  68.8 3.8 %collective-permute-start.1 = (f32[512,256]{1,0:T(8,128)S(1)}, f32[512,256]{1,0:T(8,128)S(1)}, u32[]{:S(2)}, u32[]{:S(2)}) collective-permute-start(f32[512,256]{1,0:T(8,128)S(1)} %get-tuple-element.38), channel_id=1, source_target_pairs={{0,4},{4,0},{8,12},{12,8},{16,20},{20,16},{24,28},{28,24},{32,36},... | collective-permute-start | bytes 1572872 | tf_op jit(solution)/shard_map/ppermute | solution.py:451
  72.7 12.3 %copy-start.11 = (f32[128,256]{1,0:T(8,128)}, f32[128,256]{1,0:T(8,128)S(1)}, u32[]{:S(2)}) copy-start(f32[128,256]{1,0:T(8,128)S(1)} %get-tuple-element.39.sum0) | copy-start | bytes 393220
  72.7 11.1 %collective-permute-start.2 = (f32[128,256]{1,0:T(8,128)S(1)}, f32[128,256]{1,0:T(8,128)S(1)}, u32[]{:S(2)}, u32[]{:S(2)}) collective-permute-start(f32[128,256]{1,0:T(8,128)S(1)} %get-tuple-element.40), channel_id=1, source_target_pairs={{0,1},{1,2},{2,3},{3,0},{4,5},{5,6},{6,7},{7,4},{8,9},{9,10},{10,1... | collective-permute-start | bytes 393224 | tf_op jit(solution)/shard_map/ppermute | solution.py:447
  76.0 9.0 %collective-permute-start.3 = (f32[128,256]{1,0:T(8,128)S(1)}, f32[128,256]{1,0:T(8,128)S(1)}, u32[]{:S(2)}, u32[]{:S(2)}) collective-permute-start(f32[128,256]{1,0:T(8,128)S(1)} %get-tuple-element.41), channel_id=1, source_target_pairs={{0,2},{1,3},{2,0},{3,1},{4,6},{5,7},{6,4},{7,5},{8,10},{9,11},{10,... | collective-permute-start | bytes 393224 | tf_op jit(solution)/shard_map/ppermute | solution.py:447
  80.6 6.9 %collective-permute-start.4 = (f32[128,256]{1,0:T(8,128)S(1)}, f32[128,256]{1,0:T(8,128)S(1)}, u32[]{:S(2)}, u32[]{:S(2)}) collective-permute-start(f32[128,256]{1,0:T(8,128)S(1)} %get-tuple-element.42), channel_id=1, source_target_pairs={{0,3},{1,0},{2,1},{3,2},{4,7},{5,4},{6,5},{7,6},{8,11},{9,8},{10,9... | collective-permute-start | bytes 393224 | tf_op jit(solution)/shard_map/ppermute | solution.py:447
  98.0 67.9 %all-to-all-start.2 = ((f32[512,1,512]{2,1,0:T(1,128)}), f32[512,1,512]{2,1,0:T(1,128)S(1)}, u32[]{:S(2)}, u32[]{:S(2)}) async-start(f32[512,1,512]{2,1,0:T(1,128)} %bitcast.26), calls=%async_computation.2 | async-start | bytes 2097152 | tf_op jit(solution)/shard_map/all_to_all | solution.py:441
  113.1 0.7 copy-start.10
  113.8 25.1 %copy-start.9 = (f32[64,400]{1,0:T(8,128)S(1)}, f32[64,400]{1,0:T(8,128)}, u32[]{:S(2)}) copy-start(f32[64,400]{1,0:T(8,128)} %relations.3) | copy-start | bytes 307204
  113.8 13.3 %collective-permute-start.5 = (f32[512,128]{1,0:T(8,128)S(1)}, f32[512,128]{1,0:T(8,128)S(1)}, u32[]{:S(2)}, u32[]{:S(2)}) collective-permute-start(f32[512,128]{1,0:T(8,128)S(1)} %get-tuple-element.47), channel_id=1, source_target_pairs={{0,1},{1,2},{2,3},{3,0},{4,5},{5,6},{6,7},{7,4},{8,9},{9,10},{10,1... | collective-permute-start | bytes 786440 | tf_op jit(solution)/shard_map/ppermute | solution.py:447
  117.3 18.2 %collective-permute-start.6 = (f32[512,128]{1,0:T(8,128)S(1)}, f32[512,128]{1,0:T(8,128)S(1)}, u32[]{:S(2)}, u32[]{:S(2)}) collective-permute-start(f32[512,128]{1,0:T(8,128)S(1)} %get-tuple-element.48), channel_id=1, source_target_pairs={{0,2},{1,3},{2,0},{3,1},{4,6},{5,7},{6,4},{7,5},{8,10},{9,11},{10,... | collective-permute-start | bytes 786440 | tf_op jit(solution)/shard_map/ppermute | solution.py:447
  121.9 15.0 %collective-permute-start.7 = (f32[512,128]{1,0:T(8,128)S(1)}, f32[512,128]{1,0:T(8,128)S(1)}, u32[]{:S(2)}, u32[]{:S(2)}) collective-permute-start(f32[512,128]{1,0:T(8,128)S(1)} %get-tuple-element.49), channel_id=1, source_target_pairs={{0,3},{1,0},{2,1},{3,2},{4,7},{5,4},{6,5},{7,6},{8,11},{9,8},{10,9... | collective-permute-start | bytes 786440 | tf_op jit(solution)/shard_map/ppermute | solution.py:447
  127.1 9.9 %copy-start.13 = (f32[512,128]{1,0:T(8,128)}, f32[512,128]{1,0:T(8,128)S(1)}, u32[]{:S(2)}) copy-start(f32[512,128]{1,0:T(8,128)S(1)} %collective-permute-done.5.part1) | copy-start | bytes 786436
  135.5 1.5 copy-start.14
  137.0 0.7 copy-start.15
  140.7 0.8 copy-start.3
  165.9 1.0 copy-start.4
  167.0 15.4 %copy-start.2 = (f32[512,400]{0,1:T(8,128)S(1)}, f32[512,400]{0,1:T(8,128)}, u32[]{:S(2)}) copy-start(f32[512,400]{0,1:T(8,128)} %param.9) | copy-start | bytes 2457604
  167.0 15.4 %copy-start.12 = (f32[512]{0:T(512)S(1)}, f32[512]{0:T(512)}, u32[]{:S(2)}) copy-start(f32[512]{0:T(512)} %param.10) | copy-start | bytes 6148

commit v7 on v6

--- a/solution.py
+++ b/solution.py
@@ -19,6 +19,7 @@
 TILES1 = 2
 TILES2 = 13
 TILES3 = 4
+ASKS = 112
 STARTS = (0, 56, 104, 152)
 SIZES = (56, 48, 48, 48)
 
@@ -53,12 +54,19 @@
     return lax.broadcasted_iota(jnp.int32, shape, len(shape) - 1)
 
 
-def cmul(a, b):
-    return (a[0] * b[0] - a[1] * b[1], a[0] * b[1] + a[1] * b[0])
-
-
-def conj(a):
-    return (a[0], -a[1])
+def tile_of(x, q):
+    return x[:, q * LANE : (q + 1) * LANE]
+
+
+def turn(x):
+    return jnp.concatenate([pltpu.roll(tile_of(x, q), 64, 1) for q in range(4)], 1)
+
+
+def cmul(a, b, conj=False):
+    low = lanes(b.shape) % LANE < 64
+    other = turn(b)
+    second = jnp.where(low, other, -b) if conj else jnp.where(low, -other, b)
+    return a * jnp.where(low, b, other) + turn(a) * second
 
 
 def sigmoid(x):
@@ -69,37 +77,34 @@
     return jnp.sum(jnp.where(lanes(tile.shape) == lane, tile, 0.0), 1, keepdims=True)
 
 
-def pack(ref, tiles, halves):
-    n = halves[0].shape[0]
-    at = lanes((n, LANE))
+def pack(ref, slots):
+    n = slots[0].shape[0]
+    at = lanes((n, LANE)) % 64
     tail = jnp.zeros((n, LANE), f32)
-    for i, half in enumerate(halves):
-        ref[pl.ds(i, n, stride=tiles), :] = half[:, :LANE]
-        rest = half[:, LANE:]
-        shift = (8 * i - 64) % LANE
-        moved = pltpu.roll(rest, shift, 1) if shift else rest
-        tail = jnp.where((at >= 8 * i) & (at < 8 * i + 8), moved, tail)
-    for i in range(0, len(halves), 2):
-        pair = halves[i][:, LANE:]
-        if i + 1 < len(halves):
-            pair = jnp.where(at < 64, pair, pltpu.roll(halves[i + 1][:, LANE:], 64, 1))
-        ref[pl.ds(len(halves) + i // 2, n, stride=tiles), :] = pair
-    ref[pl.ds(tiles - 1, n, stride=tiles), :] = tail
-
-
-def unpack(ref, tiles, count, n):
-    at = lanes((n, LANE))
-    tail = ref[pl.ds(tiles - 1, n, stride=tiles), :]
+    for s, slot in enumerate(slots):
+        first = tile_of(slot, 0)
+        for j in range(1, 4):
+            moved = pltpu.roll(first, 64 - 16 * j, 1)
+            ref[pl.ds(3 * s + j - 1, n, stride=TILES2), :] = jnp.where(
+                at < 48, tile_of(slot, j), moved
+            )
+        moved = pltpu.roll(first, (8 * s - 48) % LANE, 1)
+        tail = jnp.where((at >= 8 * s) & (at < 8 * s + 8), moved, tail)
+    ref[pl.ds(12, n, stride=TILES2), :] = tail
+
+
+def unpack(ref, n):
+    at = lanes((n, LANE)) % 64
+    tail = ref[pl.ds(12, n, stride=TILES2), :]
     out = []
-    for i in range(count):
-        full = ref[pl.ds(i, n, stride=tiles), :]
-        pair = ref[pl.ds(count + i // 2, n, stride=tiles), :]
-        if i % 2:
-            pair = pltpu.roll(pair, 64, 1)
-        shift = (64 - 8 * i) % LANE
-        moved = pltpu.roll(tail, shift, 1) if shift else tail
-        rest = jnp.where(at < 64, pair, jnp.where(at < 72, moved, 0.0))
-        out.append(jnp.concatenate([full, rest], 1))
+    for s in range(4):
+        first = jnp.where(at < 56, pltpu.roll(tail, 48 - 8 * s, 1), 0.0)
+        others = []
+        for j in range(3, 0, -1):
+            dense = ref[pl.ds(3 * s + j - 1, n, stride=TILES2), :]
+            first = jnp.where(at < 16 * j, pltpu.roll(dense, 64 + 16 * j, 1), first)
+            others.append(jnp.where(at < 48, dense, 0.0))
+        out.append(jnp.concatenate([first] + others[::-1], 1))
     return out
 
 
@@ -121,6 +126,16 @@
         low, high = (wide[:, (2 * i + j) * LANE : (2 * i + j + 1) * LANE] for j in range(2))
         out = window(out, low, high, STARTS[q], SIZES[q], 64 * i)
     return out
+
+
+def spread(rows, sides):
+    out = []
+    for q in range(4):
+        for i in sides:
+            at = 200 * i + STARTS[q]
+            out.append(rows[at : at + SIZES[q], :])
+            out.append(jnp.zeros((64 - SIZES[q], rows.shape[1]), f32))
+    return jnp.concatenate(out, 0)
 
 
 def ask_kernel(
@@ -158,33 +173,38 @@
             )
         return jnp.where(lane == 0, edges[0], jnp.where(lane == 1, edges[1], -1.0))
 
-    head_edge[...] = slots(head_owner, head_row)
+    edges = slots(head_owner, head_row)
+    edges = jnp.where(lane == 2, columns[1], jnp.where(lane == 3, columns[3], edges))
+    head_edge[...] = edges
     tail_edge[...] = slots(tail_owner, tail_row)
 
     copy.wait()
-    pad = jnp.zeros((56, n), f32)
     line = []
     for i in range(2):
-        half = jnp.concatenate([block[200 * i : 200 * i + 200, :], pad], 0).T
+        half = spread(block, (i,)).T
         picked = lax.broadcasted_iota(jnp.int32, (n, 256), 0) == neg_at % n
         line.append(jnp.sum(jnp.where(picked, half, 0.0), 0, keepdims=True))
     even = sub % 2 == 0
     send[pl.ds(0, n, stride=TILES1), :] = jnp.where(even, wide(line[0][:, :n]), wide(line[1][:, :n]))
     tile = jnp.where(even, wide(line[0][:, n:]), wide(line[1][:, n:]))
     for j, col in enumerate(columns):
-        tile = jnp.where(lane == 72 + j, col, tile)
+        tile = jnp.where(lane == ASKS + j, col, tile)
     send[pl.ds(1, n, stride=TILES1), :] = tile
 
 
-def ahead_kernel(table_t, relations, *outs):
-    pad = jnp.zeros((56, 512), f32)
-    whole = jnp.concatenate([table_t[0:200, :], pad, table_t[200:400, :], pad], 0).T
+def ahead_kernel(table_t, relations, head_edge, *outs):
+    whole = spread(table_t[...], (0, 1)).T
     for ref, piece in zip(outs[:PIECES], parts(whole, PIECES), strict=True):
         ref[...] = piece
     pad = jnp.zeros((64, 56), f32)
     whole = jnp.concatenate([relations[:, :200], pad, relations[:, 200:], pad], 1)
-    for ref, piece in zip(outs[PIECES : 2 * PIECES], parts(whole, PIECES), strict=True):
+    whole = jnp.concatenate([quarter(whole, q) for q in range(4)], 1)
+    pieces = parts(whole, PIECES)
+    for ref, piece in zip(outs[PIECES:-1], pieces, strict=True):
         ref[...] = piece
+    ids = jnp.concatenate([head_edge[:, 2:3], head_edge[:, 3:4]], 0)
+    hot = jnp.where(lanes((2 * LANE, 64)).astype(f32) == ids, 1.0, 0.0).astype(bf16)
+    outs[-1][...] = pick(hot, pieces, NN)
 
 
 def pair_kernel(head_edge, tail_edge, same):
@@ -204,14 +224,9 @@
 
 
 def rel_vectors(tile, slots, pieces):
-    ids = jnp.concatenate([column(tile, 72 + 2 * s + 1) for s in slots], 0)
+    ids = jnp.concatenate([column(tile, ASKS + 2 * s + 1) for s in slots], 0)
     hot = jnp.where(lanes((ids.shape[0], 64)).astype(f32) == ids, 1.0, 0.0).astype(bf16)
-    both = pick(hot, [p[...] for p in pieces], NN)
-    return (both[:, :256], both[:, 256:])
-
-
-def split(x):
-    return (x[:, :256], x[:, 256:])
+    return pick(hot, [p[...] for p in pieces], NN)
 
 
 def fetch_kernel(recv, *refs):
@@ -220,19 +235,17 @@
     send, rows, negs = refs[2 * PIECES :]
     negs[...] = recv[...]
     tile = recv[pl.ds(1, n, stride=TILES1), :]
-    halves = []
+    packed = []
     for side in range(2):
         slots = (2 * side, 2 * side + 1)
-        at = jnp.concatenate([column(tile, 72 + 2 * s) for s in slots], 0)
+        at = jnp.concatenate([column(tile, ASKS + 2 * s) for s in slots], 0)
         hot = jnp.where(lanes((2 * n, 512)).astype(f32) == at, 1.0, 0.0).astype(bf16)
-        vec = split(pick(hot, [p[...] for p in table], NN))
+        vec = pick(hot, [p[...] for p in table], NN)
         if side == 0:
             vec = cmul(vec, rel_vectors(tile, slots, rel))
-        for i in range(2):
-            halves += [v[i * n : (i + 1) * n, :] for v in vec]
-        for i in range(2):
-            rows[2 * n * side : 2 * n * (side + 1), i * 256 : (i + 1) * 256] = vec[i]
-    pack(send, TILES2, halves)
+        packed += [vec[:n, :], vec[n:, :]]
+        rows[2 * n * side : 2 * n * (side + 1), :] = vec
+    pack(send, packed)
 
 
 def negatives_kernel(odd, recv, rows, *refs):
@@ -240,28 +253,35 @@
     rel = refs[:PIECES]
     mine, other, back, keep, give = refs[PIECES:]
     tile = recv[pl.ds(1, n, stride=TILES1), :]
-    mask = lanes((n, LANE)) < 72
-
-    def half(ref, base):
-        low = ref[pl.ds(base, n, stride=TILES1), :]
-        high = jnp.where(mask, ref[pl.ds(base + 1, n, stride=TILES1), :], 0.0)
-        return jnp.concatenate([low, high], 1)
+    at = lanes((n, LANE))
+    low = lanes((4 * n, LANE)) < 64
+
+    def half(ref):
+        first = [ref[pl.ds(TILES1 * n * j, n, stride=TILES1), :] for j in range(4)]
+        second = [ref[pl.ds(TILES1 * n * j + 1, n, stride=TILES1), :] for j in range(4)]
+        second = [jnp.where(at < ASKS, x, 0.0) for x in second]
+        return jnp.concatenate(first, 0), jnp.concatenate(second, 0)
 
     flip = odd[0] > 0
-    own, got = (
-        jnp.concatenate([half(ref, TILES1 * n * j) for j in range(4)], 0) for ref in (mine, other)
-    )
-    negs = jnp.concatenate([jnp.where(flip, got, own), jnp.where(flip, own, got)], 1)
-    probe = cmul(conj(rel_vectors(tile, (2, 3), rel)), split(rows[2 * n :, :]))
-    x = jnp.concatenate([rows[0 : 2 * n, :], jnp.concatenate(probe, 1)], 0)
-    valid = jnp.concatenate([column(tile, 72 + 2 * s) for s in range(4)], 0)
+    negs = []
+    for own, got in zip(half(mine), half(other)):
+        re, im = jnp.where(flip, got, own), jnp.where(flip, own, got)
+        negs.append(jnp.where(low, re, pltpu.roll(im, 64, 1)))
+        negs.append(jnp.where(low, pltpu.roll(re, 64, 1), im))
+    negs = jnp.concatenate(negs, 1)
+    probe = cmul(rows[2 * n :, :], rel_vectors(tile, (2, 3), rel), True)
+    x = jnp.concatenate([rows[0 : 2 * n, :], probe], 0)
+    valid = jnp.concatenate([column(tile, ASKS + 2 * s) for s in range(4)], 0)
     coef = sigmoid(dot3(x, negs, NT)) * (1.0 / math.sqrt(512.0))
     coef = jnp.where(valid >= 0.0, coef, 0.0)
     back[...] = dot3(coef, negs, NN)
     total = dot3(coef, x, TN)
-    re, im = split(total)
-    keep[...] = jnp.where(flip, im, re)
-    give[...] = jnp.where(flip, re, im)
+    for i in range(2):
+        first, second = tile_of(total, 2 * i), tile_of(total, 2 * i + 1)
+        re = jnp.where(low, first, pltpu.roll(second, 64, 1))
+        im = jnp.where(low, pltpu.roll(first, 64, 1), second)
+        keep[:, i * n : (i + 1) * n] = jnp.where(flip, im, re)
+        give[:, i * n : (i + 1) * n] = jnp.where(flip, re, im)
 
 
 def fold_kernel(rep, keep, got, *outs):
@@ -270,30 +290,27 @@
         ref[...] = keep[at, :] + got[at, :]
 
 
-def edge_kernel(recv, same, sum0, sum1, sum2, sum3, send, token):
-    n = LANE
-    halves = unpack(recv, TILES2, 8, n)
-    query, tails = (
-        jnp.concatenate(
-            [jnp.concatenate(halves[i : i + 2], 1), jnp.concatenate(halves[i + 2 : i + 4], 1)], 0
-        )
-        for i in (0, 4)
-    )
+def edge_kernel(recv, same, rels, sum0, sum1, sum2, sum3, send, token):
+    n = LANE
+    slots = unpack(recv, n)
+    query, tails = jnp.concatenate(slots[:2], 0), jnp.concatenate(slots[2:], 0)
     met = pick(same[0 : 2 * n, :], parts(tails, PIECES), NN)
     pos = jnp.sum(query * met, 1, keepdims=True)
     coef = -sigmoid(-pos)
-    to_head = coef * met
+    to_head = cmul(coef * met, rels[...], True)
     to_tail = pick(same[2 * n :, :], parts(coef * query, PIECES), NN)
     neg = sum0[...] + sum1[...] + (sum2[...] + sum3[...])
-    low, high = neg[:, :LANE], neg[:, LANE:]
-    for s, block in enumerate((to_head[:n], to_head[n:], to_tail[:n], to_tail[n:])):
-        for q in range(4):
-            tile = quarter(block, q)
-            for i in range(2):
-                word = 16 * s + 8 * i
-                if word < 56:
-                    tile = window(tile, low, high, STARTS[q] + word, 8, 56 + 64 * i)
-            send[pl.ds(4 * q + s, n, stride=4 * TILES3), :] = tile
+    at = lanes((n, LANE))
+    for q in range(4):
+        words = tile_of(neg, q // 2)
+        if q % 2:
+            words = pltpu.roll(words, 64, 1)
+        words = jnp.where(at < 64, words, pltpu.roll(words, 32, 1))
+        for s, block in enumerate((to_head[:n], to_head[n:], to_tail[:n], to_tail[n:])):
+            moved = pltpu.roll(words, 56 - 8 * s, 1)
+            send[pl.ds(4 * q + s, n, stride=4 * TILES3), :] = jnp.where(
+                at % 64 < 56, tile_of(block, q), moved
+            )
     token[...] = neg[0:8, 0:128]
 
 
@@ -305,37 +322,23 @@
     sub = lax.broadcasted_iota(jnp.int32, (512, LANE), 0).astype(f32)
     hot = jnp.concatenate(
         [
-            jnp.where(sub == turned[72 + 2 * s : 73 + 2 * s, :], 1.0, 0.0).astype(bf16)
+            jnp.where(sub == turned[ASKS + 2 * s : ASKS + 2 * s + 1, :], 1.0, 0.0).astype(bf16)
             for s in range(4)
         ],
         1,
     )
-    head = cmul(split(back[0:n, :]), conj(rel_vectors(tile, (0, 1), rel)))
-    tail = cmul(split(back[n:, :]), rel_vectors(tile, (2, 3), rel))
-    grad = jnp.concatenate([jnp.concatenate(head, 1), jnp.concatenate(tail, 1)], 0)
+    head = cmul(back[0:n, :], rel_vectors(tile, (0, 1), rel), True)
+    tail = cmul(back[n:, :], rel_vectors(tile, (2, 3), rel))
+    grad = jnp.concatenate([head, tail], 0)
     total = pick(hot, parts(grad, PIECES), NN)
     for q in range(4):
-        quarters[q] = quarter(total, q)
+        quarters[q] = tile_of(total, q)
     for i, ref in enumerate((out0, out1, out2, out3)):
         ref[...] = quarters[(rep[0] + i) % 4]
 
 
 def gather_local_kernel(part0, part1, part2, part3, out):
     out[...] = part0[...] + part1[...] + (part2[...] + part3[...])
-
-
-def rels_kernel(rep, token, asks, relations, out):
-    pad = jnp.zeros((64, 56), f32)
-    wide = jnp.concatenate([relations[:, :200], pad, relations[:, 200:], pad], 1)
-    mine = jnp.zeros((64, LANE), f32)
-    for q in range(4):
-        mine = jnp.where(rep[0] == q, quarter(wide, q), mine)
-    pieces = parts(mine, PIECES)
-    for x in range(4):
-        tile = asks[pl.ds(x * TILES1 * LANE + 1, LANE, stride=TILES1), :]
-        ids = jnp.concatenate([column(tile, 73), column(tile, 75)], 0)
-        hot = jnp.where(lanes((2 * LANE, 64)).astype(f32) == ids, 1.0, 0.0).astype(bf16)
-        out[2 * x * LANE : 2 * (x + 1) * LANE, :] = pick(hot, pieces, NN)
 
 
 def place_kernel(neg_rows, asks, token, hot):
@@ -344,7 +347,7 @@
     for x in range(4):
         turned = asks[pl.ds(x * TILES1 * n + 1, n, stride=TILES1), :].T
         for s in range(4):
-            at = turned[72 + 2 * s : 73 + 2 * s, :]
+            at = turned[ASKS + 2 * s : ASKS + 2 * s + 1, :]
             b = 4 * x + s
             hot[:, b * n : (b + 1) * n] = jnp.where(sub == at, 1.0, 0.0).astype(bf16)
     at = jnp.full((1, n), -1.0, f32)
@@ -353,9 +356,8 @@
     hot[:, 16 * n :] = jnp.where(sub == at, 1.0, 0.0).astype(bf16)
 
 
-def scatter_kernel(recv, hot, rels, local, out):
-    n = LANE
-    at = lanes((n, n))
+def scatter_kernel(recv, hot, local, out):
+    n = LANE
     even = lax.broadcasted_iota(jnp.int32, (n, n), 0) % 2 == 0
     which = lax.broadcasted_iota(jnp.int32, (8, n), 0)
     sums = [[jnp.zeros((8, n), f32) for _ in range(2)] for _ in range(4)]
@@ -368,18 +370,12 @@
             sums[s] = [
                 jnp.where(which == x, new, old) for old, new in zip(sums[s], (reals, imags))
             ]
-            if s < 2:
-                rel = rels[(2 * x + s) * n : (2 * x + s + 1) * n, :]
-                other = pltpu.roll(rel, 64, 1)
-                tile = tile * jnp.where(at < 64, rel, other) + pltpu.roll(
-                    tile, 64, 1
-                ) * jnp.where(at < 64, other, -rel)
             blocks.append(tile)
     neg = jnp.zeros((8, n), f32)
     lane = lanes((8, n))
     for s in range(4):
         for i in range(2):
-            word = 16 * s + 8 * i
+            word = 32 * i + 8 * s
             if word < 56:
                 for side in range(2):
                     goal = 64 * side + word
@@ -488,10 +484,12 @@
         1,
     )
     recv1 = exchange(send1, "ent", TILES1)
-    pieces = call(
+    *pieces, edge_rels = call(
         ahead_kernel,
-        [((4 * n, 512), bf16, True)] * PIECES + [((64, 512), bf16, True)] * PIECES,
-        (table_t, relations),
+        [((4 * n, 512), bf16, True)] * PIECES
+        + [((64, 512), bf16, True)] * PIECES
+        + [((2 * n, 512), f32, True)],
+        (table_t, relations, far(head_edge)),
         name="ahead",
     )
     (same,) = call(
@@ -532,7 +530,7 @@
     send3, token = call(
         edge_kernel,
         [((4 * n * TILES3, n), f32, False), ((8, n), f32, False)],
-        (near(recv2), near(same), far(sums[0]), *map(near, sums[1:])),
+        (near(recv2), near(same), far(edge_rels), far(sums[0]), *map(near, sums[1:])),
         name="edge",
     )
     recv3 = exchange(send3, ("ent", "rep"), TILES3)
@@ -554,13 +552,10 @@
     (hot,) = call(
         place_kernel, [((4 * n, 17 * n), bf16, True)], (far(mine), token), (neg_rows,), "place"
     )
-    (rels,) = call(
-        rels_kernel, [((8 * n, n), f32, True)], (near(local), far(mine), relations), (rep,), "rels"
-    )
     (grads,) = call(
         scatter_kernel,
         [((112, 512), f32, True)],
-        (near(recv3), near(hot), near(rels), near(local)),
+        (near(recv3), near(hot), near(local)),
         name="scatter",
     )
     grads = lax.all_gather(grads, "rep", axis=0, tiled=True)

time: 187 us -> 186 us (level)
    unnamed x32 -> x28, local copies, waits for them, and re-layouts: 5.3 us -> 3.58 us
    pallas_call x13 -> x12, Pallas kernels: 24.2 us -> 24 us  [call(): pl.pallas_call(kernel, out_shape=[(pltpu.VMEM if near else pltpu.HBM)(sha...]
where the time goes in v7:
time: 186 us; the launch traced here: 183 us
  starting transfers between devices  63.7 us (34%)
  waiting for transfers between devices  63.5 us (34%)
  blocking collectives  27.3 us (15%)
  Pallas kernels  24 us (13%)
  local copies, waits for them, and re-layouts  3.58 us (2%)
    all_to_all x3, waiting for transfers between devices, exchange(): x = lax.all_to_all(x, axis, split_axis=0, concat_axis=0, tiled=True)  46.3 us
    all_to_all x3, starting transfers between devices, exchange(): x = lax.all_to_all(x, axis, split_axis=0, concat_axis=0, tiled=True)  38.6 us
    pallas_call x12, Pallas kernels, call(): pl.pallas_call(kernel, out_shape=[(pltpu.VMEM if near else pltpu.HBM)(sha...  24 us
    ppermute x6, starting transfers between devices, shift(): return lax.ppermute(x, 'rep', [(i, (i + by) % n) for i in range(n)])  21.2 us
    all_gather x1, blocking collectives, on_device(): grads = lax.all_gather(grads, 'rep', axis=0, tiled=True)  14.2 us
    ppermute x6, waiting for transfers between devices, shift(): return lax.ppermute(x, 'rep', [(i, (i + by) % n) for i in range(n)])  13.6 us
    all_gather x1, blocking collectives, on_device(): mine = lax.all_gather(own_negs, 'rep', axis=0, tiled=True)  13.1 us
    ppermute x2, starting transfers between devices, swap_cores(): lax.ppermute(x, 'ent', [(i, i ^ 1) for i in range(lax.axis_size('ent'))])  3.96 us
  transfers between devices with their start and end apart: 11, of which 9 were waited for; matrix products, arithmetic and copies ran while one was open for 0% of the time, Pallas kernels for 7%

profile of v7, /device:TPU:24, one launch (start us, length us, event | category | flops | bytes accessed | tf_op | source)
XLA Modules:
  0.0 183.1 jit_solution(1304946531949883906)
XLA Ops:
  0.6 2.6 %ask.1 = (f32[256,128]{1,0:T(8,128)}, f32[128,128]{1,0:T(8,128)}, f32[128,128]{1,0:T(8,128)}) custom-call(s32[1]{0:T(128)} %bitcast.rep, s32[4]{0:T(128)} %neg_rows.3, s32[1,128]{1,0:T(1,128)} %bitcast.29, s32[1,128]{1,0:T(1,128)} %bitcast.30, s32[1,128]{1,0:T(1,128)} %bitcast.31, s32[1,128]{1,0:T(1,128)} %bitcast.32, s32[1,128]{1,0:T(1,128)} %bitcast.33, ...), custom_call_target="tpu_custom_call" | custom-call | tf_op jit(solution)/shard_map/ask/pallas_call | solution.py:410
  3.2 19.3 %all-to-all-start = ((f32[128,1,256]{2,1,0:T(1,128)}), f32[128,1,256]{2,1,0:T(1,128)S(1)}, u32[]{:S(2)}, u32[]{:S(2)}) async-start(f32[128,1,256]{2,1,0:T(1,128)} %bitcast.28), calls=%async_computation | async-start | bytes 262144 | tf_op jit(solution)/shard_map/all_to_all | solution.py:437
  22.5 1.1 copy-done
  24.6 1.5 ahead.1
  26.9 11.8 %all-to-all-done = f32[128,1,256]{2,1,0:T(1,128)S(1)} async-done(((f32[128,1,256]{2,1,0:T(1,128)}), f32[128,1,256]{2,1,0:T(1,128)S(1)}, u32[]{:S(2)}, u32[]{:S(2)}) %all-to-all-start) | async-done | bytes 131104 | tf_op jit(solution)/shard_map/all_to_all | solution.py:437
  38.7 2.1 %fetch.1 = (f32[1664,128]{1,0:T(8,128)}, f32[512,512]{1,0:T(8,128)S(1)}, f32[256,128]{1,0:T(8,128)S(1)}) custom-call(f32[256,128]{1,0:T(8,128)S(1)} %bitcast.22, bf16[512,512]{1,0:T(8,128)(2,1)S(1)} %get-tuple-element.30.refs_0_, bf16[512,512]{1,0:T(8,128)(2,1)S(1)} %get-tuple-element.31.refs_1_, bf16[64,512]{1,0:T(8,128)(2,1)S(1)} %get-tuple-element.32.refs_2_.refs_0_, ...), custom_call_target="tpu_custom_call" | custom-call | tf_op jit(solution)/shard_map/fetch/pallas_call | solution.py:410
  40.8 7.1 %all-to-all-start.1 = ((f32[128,1,1664]{2,1,0:T(1,128)}), f32[128,1,1664]{2,1,0:T(1,128)S(1)}, u32[]{:S(2)}, u32[]{:S(2)}) async-start(f32[128,1,1664]{2,1,0:T(1,128)} %bitcast.27), calls=%async_computation.1 | async-start | bytes 1703936 | tf_op jit(solution)/shard_map/all_to_all | solution.py:437
  47.9 13.1 %all_gather.6.refs_2_.asks = f32[1024,128]{1,0:T(8,128)S(1)} all-gather(f32[256,128]{1,0:T(8,128)S(1)} %get-tuple-element.38), channel_id=1, replica_groups=mesh['ent'=128,'rep'=4] {'rep'}, dimensions={0}, use_global_device_ids=true | all-gather | bytes 655360 | tf_op jit(solution)/shard_map/all_gather | solution.py:513
  61.0 1.9 %collective-permute-start = (f32[1024,128]{1,0:T(8,128)S(1)}, f32[1024,128]{1,0:T(8,128)S(1)}, u32[]{:S(2)}, u32[]{:S(2)}) collective-permute-start(f32[1024,128]{1,0:T(8,128)S(1)} %all_gather.6.refs_2_.asks), channel_id=1, source_target_pairs={{0,4},{4,0},{8,12},{12,8},{16,20},{20,16},{24,28},{28,24},{32,36},... | collective-permute-start | bytes 1572872 | tf_op jit(solution)/shard_map/ppermute | solution.py:447
  62.9 1.9 %collective-permute-done.refs_3_ = f32[1024,128]{1,0:T(8,128)S(1)} collective-permute-done((f32[1024,128]{1,0:T(8,128)S(1)}, f32[1024,128]{1,0:T(8,128)S(1)}, u32[]{:S(2)}, u32[]{:S(2)}) %collective-permute-start) | collective-permute-done | bytes 524320 | tf_op jit(solution)/shard_map/ppermute | solution.py:447
  64.8 4.4 %negatives.1 = (f32[512,512]{1,0:T(8,128)S(1)}, f32[512,256]{1,0:T(8,128)S(1)}, f32[512,256]{1,0:T(8,128)S(1)}) custom-call(s32[1]{0:T(128)} %bitcast.11.odd, f32[256,128]{1,0:T(8,128)S(1)} %bitcast.23, f32[512,512]{1,0:T(8,128)S(1)} %get-tuple-element.37.rows, bf16[64,512]{1,0:T(8,128)(2,1)} %copy-done.4, bf16[64,512]{1,0:T(8,128)(2,1)} %copy-done.5, ...), custom_call_target="tpu_custom_call" | custom-call | tf_op jit(solution)/shard_map/negatives/pallas_call | solution.py:410
  69.3 2.0 %collective-permute-start.1 = (f32[512,256]{1,0:T(8,128)S(1)}, f32[512,256]{1,0:T(8,128)S(1)}, u32[]{:S(2)}, u32[]{:S(2)}) collective-permute-start(f32[512,256]{1,0:T(8,128)S(1)} %get-tuple-element.40), channel_id=1, source_target_pairs={{0,4},{4,0},{8,12},{12,8},{16,20},{20,16},{24,28},{28,24},{32,36},... | collective-permute-start | bytes 1572872 | tf_op jit(solution)/shard_map/ppermute | solution.py:447
  71.3 1.7 collective-permute-done.1.got
  73.1 3.3 %collective-permute-start.2 = (f32[128,256]{1,0:T(8,128)S(1)}, f32[128,256]{1,0:T(8,128)S(1)}, u32[]{:S(2)}, u32[]{:S(2)}) collective-permute-start(f32[128,256]{1,0:T(8,128)S(1)} %get-tuple-element.42), channel_id=1, source_target_pairs={{0,1},{1,2},{2,3},{3,0},{4,5},{5,6},{6,7},{7,4},{8,9},{9,10},{10,1... | collective-permute-start | bytes 393224 | tf_op jit(solution)/shard_map/ppermute | solution.py:443
  76.5 4.6 %collective-permute-start.3 = (f32[128,256]{1,0:T(8,128)S(1)}, f32[128,256]{1,0:T(8,128)S(1)}, u32[]{:S(2)}, u32[]{:S(2)}) collective-permute-start(f32[128,256]{1,0:T(8,128)S(1)} %get-tuple-element.43), channel_id=1, source_target_pairs={{0,2},{1,3},{2,0},{3,1},{4,6},{5,7},{6,4},{7,5},{8,10},{9,11},{10,... | collective-permute-start | bytes 393224 | tf_op jit(solution)/shard_map/ppermute | solution.py:443
  81.1 1.9 %collective-permute-start.4 = (f32[128,256]{1,0:T(8,128)S(1)}, f32[128,256]{1,0:T(8,128)S(1)}, u32[]{:S(2)}, u32[]{:S(2)}) collective-permute-start(f32[128,256]{1,0:T(8,128)S(1)} %get-tuple-element.44), channel_id=1, source_target_pairs={{0,3},{1,0},{2,1},{3,2},{4,7},{5,4},{6,5},{7,6},{8,11},{9,8},{10,9... | collective-permute-start | bytes 393224 | tf_op jit(solution)/shard_map/ppermute | solution.py:443
  83.0 1.2 pair.1.same
  84.2 1.2 collective-permute-done.3.sum2
  85.4 2.5 %collective-permute-done.4.sum3 = f32[128,256]{1,0:T(8,128)S(1)} collective-permute-done((f32[128,256]{1,0:T(8,128)S(1)}, f32[128,256]{1,0:T(8,128)S(1)}, u32[]{:S(2)}, u32[]{:S(2)}) %collective-permute-start.4) | collective-permute-done | bytes 131104 | tf_op jit(solution)/shard_map/ppermute | solution.py:443
  87.9 6.5 %all-to-all-done.1 = f32[128,1,1664]{2,1,0:T(1,128)S(1)} async-done(((f32[128,1,1664]{2,1,0:T(1,128)}), f32[128,1,1664]{2,1,0:T(1,128)S(1)}, u32[]{:S(2)}, u32[]{:S(2)}) %all-to-all-start.1) | async-done | bytes 852000 | tf_op jit(solution)/shard_map/all_to_all | solution.py:437
  94.4 4.1 %edge.1 = (f32[2048,128]{1,0:T(8,128)}, f32[8,128]{1,0:T(8,128)}) custom-call(f32[1664,128]{1,0:T(8,128)S(1)} %bitcast.21, bf16[512,256]{1,0:T(8,128)(2,1)S(1)} %pair.1.same, f32[256,512]{1,0:T(8,128)} %copy-done.6, f32[128,256]{1,0:T(8,128)} %copy-done.8, f32[128,256]{1,0:T(8,128)S(1)} %collective-permute-done.2.sum1, ...), custom_call_target="tpu_custom_call" | custom-call | tf_op jit(solution)/shard_map/edge/pallas_call | solution.py:410
  98.5 12.2 %all-to-all-start.2 = ((f32[512,1,512]{2,1,0:T(1,128)}), f32[512,1,512]{2,1,0:T(1,128)S(1)}, u32[]{:S(2)}, u32[]{:S(2)}) async-start(f32[512,1,512]{2,1,0:T(1,128)} %bitcast.26), calls=%async_computation.2 | async-start | bytes 2097152 | tf_op jit(solution)/shard_map/all_to_all | solution.py:437
  110.8 2.9 %local.1 = (f32[512,128]{1,0:T(8,128)S(1)}, f32[512,128]{1,0:T(8,128)S(1)}, f32[512,128]{1,0:T(8,128)S(1)}, f32[512,128]{1,0:T(8,128)S(1)}) custom-call(s32[1]{0:T(128)} %bitcast.rep, f32[8,128]{1,0:T(8,128)} %get-tuple-element.46.token, f32[256,128]{1,0:T(8,128)S(1)} %bitcast.24, f32[512,512]{1,0:T(8,128)} %copy-done.3, bf16[64,512]{1,0:T(8,128)(2,1)} %copy-done.4, ...), custom_call_target="tpu_custom_call" | custom-call | tf_op jit(solution)/shard_map/local/pallas_call | solution.py:410
  113.7 3.4 %collective-permute-start.5 = (f32[512,128]{1,0:T(8,128)S(1)}, f32[512,128]{1,0:T(8,128)S(1)}, u32[]{:S(2)}, u32[]{:S(2)}) collective-permute-start(f32[512,128]{1,0:T(8,128)S(1)} %get-tuple-element.49), channel_id=1, source_target_pairs={{0,1},{1,2},{2,3},{3,0},{4,5},{5,6},{6,7},{7,4},{8,9},{9,10},{10,1... | collective-permute-start | bytes 786440 | tf_op jit(solution)/shard_map/ppermute | solution.py:443
  117.1 4.6 %collective-permute-start.6 = (f32[512,128]{1,0:T(8,128)S(1)}, f32[512,128]{1,0:T(8,128)S(1)}, u32[]{:S(2)}, u32[]{:S(2)}) collective-permute-start(f32[512,128]{1,0:T(8,128)S(1)} %get-tuple-element.50), channel_id=1, source_target_pairs={{0,2},{1,3},{2,0},{3,1},{4,6},{5,7},{6,4},{7,5},{8,10},{9,11},{10,... | collective-permute-start | bytes 786440 | tf_op jit(solution)/shard_map/ppermute | solution.py:443
  121.7 3.4 %collective-permute-start.7 = (f32[512,128]{1,0:T(8,128)S(1)}, f32[512,128]{1,0:T(8,128)S(1)}, u32[]{:S(2)}, u32[]{:S(2)}) collective-permute-start(f32[512,128]{1,0:T(8,128)S(1)} %get-tuple-element.51), channel_id=1, source_target_pairs={{0,3},{1,0},{2,1},{3,2},{4,7},{5,4},{6,5},{7,6},{8,11},{9,8},{10,9... | collective-permute-start | bytes 786440 | tf_op jit(solution)/shard_map/ppermute | solution.py:443
  125.1 1.7 place.1.hot
  126.9 8.3 %collective-permute-done.6.part2 = f32[512,128]{1,0:T(8,128)S(1)} collective-permute-done((f32[512,128]{1,0:T(8,128)S(1)}, f32[512,128]{1,0:T(8,128)S(1)}, u32[]{:S(2)}, u32[]{:S(2)}) %collective-permute-start.6) | collective-permute-done | bytes 262176 | tf_op jit(solution)/shard_map/ppermute | solution.py:443
  135.2 1.5 collective-permute-done.7.part3
  137.4 1.2 gather_local.1.local
  138.7 28.1 %all-to-all-done.2 = f32[512,1,512]{2,1,0:T(1,128)S(1)} async-done(((f32[512,1,512]{2,1,0:T(1,128)}), f32[512,1,512]{2,1,0:T(1,128)S(1)}, u32[]{:S(2)}, u32[]{:S(2)}) %all-to-all-start.2) | async-done | bytes 1048608 | tf_op jit(solution)/shard_map/all_to_all | solution.py:437
  167.8 14.2 %all_gather.7.grads = f32[448,512]{1,0:T(8,128)S(1)} all-gather(f32[112,512]{1,0:T(8,128)S(1)} %scatter.1), channel_id=1, replica_groups=mesh['ent'=128,'rep'=4] {'rep'}, dimensions={0}, use_global_device_ids=true | all-gather | bytes 1146880 | tf_op jit(solution)/shard_map/all_gather | solution.py:561
  (32 shorter events, 4.6 us)
Async XLA Ops:
  3.2 35.4 %all-to-all-start = ((f32[128,1,256]{2,1,0:T(1,128)}), f32[128,1,256]{2,1,0:T(1,128)S(1)}, u32[]{:S(2)}, u32[]{:S(2)}) async-start(f32[128,1,256]{2,1,0:T(1,128)} %bitcast.28), calls=%async_computation | async-start | bytes 262144 | tf_op jit(solution)/shard_map/all_to_all | solution.py:437
  22.5 1.1 copy-start
  23.7 0.9 copy-start.9
  26.1 0.8 copy-start.6
  26.9 37.9 %copy-start.4 = (bf16[64,512]{1,0:T(8,128)(2,1)}, bf16[64,512]{1,0:T(8,128)(2,1)S(1)}, u32[]{:S(2)}) copy-start(bf16[64,512]{1,0:T(8,128)(2,1)S(1)} %get-tuple-element.32.refs_2_.refs_0_) | copy-start | bytes 196612
  26.9 37.9 %copy-start.5 = (bf16[64,512]{1,0:T(8,128)(2,1)}, bf16[64,512]{1,0:T(8,128)(2,1)S(1)}, u32[]{:S(2)}) copy-start(bf16[64,512]{1,0:T(8,128)(2,1)S(1)} %get-tuple-element.33.refs_3_.refs_1_) | copy-start | bytes 196612
  40.8 53.6 %all-to-all-start.1 = ((f32[128,1,1664]{2,1,0:T(1,128)}), f32[128,1,1664]{2,1,0:T(1,128)S(1)}, u32[]{:S(2)}, u32[]{:S(2)}) async-start(f32[128,1,1664]{2,1,0:T(1,128)} %bitcast.27), calls=%async_computation.1 | async-start | bytes 1703936 | tf_op jit(solution)/shard_map/all_to_all | solution.py:437
  61.0 37.5 %copy-start.2 = (f32[1024,128]{1,0:T(8,128)}, f32[1024,128]{1,0:T(8,128)S(1)}, u32[]{:S(2)}) copy-start(f32[1024,128]{1,0:T(8,128)S(1)} %all_gather.6.refs_2_.asks) | copy-start | bytes 1572868
  61.0 3.8 %collective-permute-start = (f32[1024,128]{1,0:T(8,128)S(1)}, f32[1024,128]{1,0:T(8,128)S(1)}, u32[]{:S(2)}, u32[]{:S(2)}) collective-permute-start(f32[1024,128]{1,0:T(8,128)S(1)} %all_gather.6.refs_2_.asks), channel_id=1, source_target_pairs={{0,4},{4,0},{8,12},{12,8},{16,20},{20,16},{24,28},{28,24},{32,36},... | collective-permute-start | bytes 1572872 | tf_op jit(solution)/shard_map/ppermute | solution.py:447
  69.3 16.2 %copy-start.3 = (f32[512,512]{1,0:T(8,128)}, f32[512,512]{1,0:T(8,128)S(1)}, u32[]{:S(2)}) copy-start(f32[512,512]{1,0:T(8,128)S(1)} %get-tuple-element.47.back) | copy-start | bytes 3145732
  69.3 3.8 %collective-permute-start.1 = (f32[512,256]{1,0:T(8,128)S(1)}, f32[512,256]{1,0:T(8,128)S(1)}, u32[]{:S(2)}, u32[]{:S(2)}) collective-permute-start(f32[512,256]{1,0:T(8,128)S(1)} %get-tuple-element.40), channel_id=1, source_target_pairs={{0,4},{4,0},{8,12},{12,8},{16,20},{20,16},{24,28},{28,24},{32,36},... | collective-permute-start | bytes 1572872 | tf_op jit(solution)/shard_map/ppermute | solution.py:447
  73.1 12.3 %copy-start.8 = (f32[128,256]{1,0:T(8,128)}, f32[128,256]{1,0:T(8,128)S(1)}, u32[]{:S(2)}) copy-start(f32[128,256]{1,0:T(8,128)S(1)} %get-tuple-element.41.sum0) | copy-start | bytes 393220
  73.1 11.1 %collective-permute-start.2 = (f32[128,256]{1,0:T(8,128)S(1)}, f32[128,256]{1,0:T(8,128)S(1)}, u32[]{:S(2)}, u32[]{:S(2)}) collective-permute-start(f32[128,256]{1,0:T(8,128)S(1)} %get-tuple-element.42), channel_id=1, source_target_pairs={{0,1},{1,2},{2,3},{3,0},{4,5},{5,6},{6,7},{7,4},{8,9},{9,10},{10,1... | collective-permute-start | bytes 393224 | tf_op jit(solution)/shard_map/ppermute | solution.py:443
  76.5 9.0 %collective-permute-start.3 = (f32[128,256]{1,0:T(8,128)S(1)}, f32[128,256]{1,0:T(8,128)S(1)}, u32[]{:S(2)}, u32[]{:S(2)}) collective-permute-start(f32[128,256]{1,0:T(8,128)S(1)} %get-tuple-element.43), channel_id=1, source_target_pairs={{0,2},{1,3},{2,0},{3,1},{4,6},{5,7},{6,4},{7,5},{8,10},{9,11},{10,... | collective-permute-start | bytes 393224 | tf_op jit(solution)/shard_map/ppermute | solution.py:443
  81.1 6.9 %collective-permute-start.4 = (f32[128,256]{1,0:T(8,128)S(1)}, f32[128,256]{1,0:T(8,128)S(1)}, u32[]{:S(2)}, u32[]{:S(2)}) collective-permute-start(f32[128,256]{1,0:T(8,128)S(1)} %get-tuple-element.44), channel_id=1, source_target_pairs={{0,3},{1,0},{2,1},{3,2},{4,7},{5,4},{6,5},{7,6},{8,11},{9,8},{10,9... | collective-permute-start | bytes 393224 | tf_op jit(solution)/shard_map/ppermute | solution.py:443
  98.5 68.3 %all-to-all-start.2 = ((f32[512,1,512]{2,1,0:T(1,128)}), f32[512,1,512]{2,1,0:T(1,128)S(1)}, u32[]{:S(2)}, u32[]{:S(2)}) async-start(f32[512,1,512]{2,1,0:T(1,128)} %bitcast.26), calls=%async_computation.2 | async-start | bytes 2097152 | tf_op jit(solution)/shard_map/all_to_all | solution.py:437
  113.7 23.0 %copy-start.7 = (f32[512,128]{1,0:T(8,128)}, f32[512,128]{1,0:T(8,128)S(1)}, u32[]{:S(2)}) copy-start(f32[512,128]{1,0:T(8,128)S(1)} %get-tuple-element.48.part0) | copy-start | bytes 786436
  113.7 13.2 %collective-permute-start.5 = (f32[512,128]{1,0:T(8,128)S(1)}, f32[512,128]{1,0:T(8,128)S(1)}, u32[]{:S(2)}, u32[]{:S(2)}) collective-permute-start(f32[512,128]{1,0:T(8,128)S(1)} %get-tuple-element.49), channel_id=1, source_target_pairs={{0,1},{1,2},{2,3},{3,0},{4,5},{5,6},{6,7},{7,4},{8,9},{9,10},{10,1... | collective-permute-start | bytes 786440 | tf_op jit(solution)/shard_map/ppermute | solution.py:443
  117.1 18.1 %collective-permute-start.6 = (f32[512,128]{1,0:T(8,128)S(1)}, f32[512,128]{1,0:T(8,128)S(1)}, u32[]{:S(2)}, u32[]{:S(2)}) collective-permute-start(f32[512,128]{1,0:T(8,128)S(1)} %get-tuple-element.50), channel_id=1, source_target_pairs={{0,2},{1,3},{2,0},{3,1},{4,6},{5,7},{6,4},{7,5},{8,10},{9,11},{10,... | collective-permute-start | bytes 786440 | tf_op jit(solution)/shard_map/ppermute | solution.py:443
  121.7 15.0 %collective-permute-start.7 = (f32[512,128]{1,0:T(8,128)S(1)}, f32[512,128]{1,0:T(8,128)S(1)}, u32[]{:S(2)}, u32[]{:S(2)}) collective-permute-start(f32[512,128]{1,0:T(8,128)S(1)} %get-tuple-element.51), channel_id=1, source_target_pairs={{0,3},{1,0},{2,1},{3,2},{4,7},{5,4},{6,5},{7,6},{8,11},{9,8},{10,9... | collective-permute-start | bytes 786440 | tf_op jit(solution)/shard_map/ppermute | solution.py:443
  126.9 9.9 %copy-start.11 = (f32[512,128]{1,0:T(8,128)}, f32[512,128]{1,0:T(8,128)S(1)}, u32[]{:S(2)}) copy-start(f32[512,128]{1,0:T(8,128)S(1)} %collective-permute-done.5.part1) | copy-start | bytes 786436
  135.2 1.6 copy-start.12
  136.7 0.7 copy-start.13
  166.8 15.2 %copy-start.1 = (f32[512,400]{0,1:T(8,128)S(1)}, f32[512,400]{0,1:T(8,128)}, u32[]{:S(2)}) copy-start(f32[512,400]{0,1:T(8,128)} %param.9) | copy-start | bytes 2457604
  166.8 15.2 %copy-start.10 = (f32[512]{0:T(512)S(1)}, f32[512]{0:T(512)}, u32[]{:S(2)}) copy-start(f32[512]{0:T(512)} %param.10) | copy-start | bytes 6148

commit v8 on v7

--- a/solution.py
+++ b/solution.py
@@ -62,11 +62,27 @@
     return jnp.concatenate([pltpu.roll(tile_of(x, q), 64, 1) for q in range(4)], 1)
 
 
-def cmul(a, b, conj=False):
+def factors(b, conj=False):
     low = lanes(b.shape) % LANE < 64
     other = turn(b)
     second = jnp.where(low, other, -b) if conj else jnp.where(low, -other, b)
-    return a * jnp.where(low, b, other) + turn(a) * second
+    return jnp.where(low, b, other), second
+
+
+def cmul(a, b, conj=False):
+    first, second = factors(b, conj)
+    return a * first + turn(a) * second
+
+
+def in_parts(write, rows, stage, out, done):
+    copies = []
+    for c in range(4):
+        write(c)
+        at = pl.ds(c * rows, rows)
+        copies.append(pltpu.make_async_copy(stage.at[at, :], out.at[at, :], done.at[c]))
+        copies[-1].start()
+    for copy in copies:
+        copy.wait()
 
 
 def sigmoid(x):
@@ -77,7 +93,7 @@
     return jnp.sum(jnp.where(lanes(tile.shape) == lane, tile, 0.0), 1, keepdims=True)
 
 
-def pack(ref, slots):
+def pack(ref, slots, base):
     n = slots[0].shape[0]
     at = lanes((n, LANE)) % 64
     tail = jnp.zeros((n, LANE), f32)
@@ -85,12 +101,12 @@
         first = tile_of(slot, 0)
         for j in range(1, 4):
             moved = pltpu.roll(first, 64 - 16 * j, 1)
-            ref[pl.ds(3 * s + j - 1, n, stride=TILES2), :] = jnp.where(
+            ref[pl.ds(base + 3 * s + j - 1, n, stride=TILES2), :] = jnp.where(
                 at < 48, tile_of(slot, j), moved
             )
         moved = pltpu.roll(first, (8 * s - 48) % LANE, 1)
         tail = jnp.where((at >= 8 * s) & (at < 8 * s + 8), moved, tail)
-    ref[pl.ds(12, n, stride=TILES2), :] = tail
+    ref[pl.ds(base + 12, n, stride=TILES2), :] = tail
 
 
 def unpack(ref, n):
@@ -207,8 +223,9 @@
     outs[-1][...] = pick(hot, pieces, NN)
 
 
-def pair_kernel(head_edge, tail_edge, same):
+def pair_kernel(head_edge, tail_edge, rels, out):
     n = 2 * LANE
+    out[0:n, :], out[n : 2 * n, :] = factors(rels[...], True)
 
     def stack(ref, by_rows):
         if by_rows:
@@ -218,9 +235,7 @@
 
     for i, (one, other) in enumerate(((head_edge, tail_edge), (tail_edge, head_edge))):
         col, row = stack(one, False), stack(other, True)
-        same[i * n : (i + 1) * n, :] = jnp.where(
-            (col == row) & (col >= 0.0), 1.0, 0.0
-        ).astype(bf16)
+        out[2 * n :, i * n : (i + 1) * n] = jnp.where((col == row) & (col >= 0.0), 1.0, 0.0)
 
 
 def rel_vectors(tile, slots, pieces):
@@ -232,7 +247,7 @@
 def fetch_kernel(recv, *refs):
     n = LANE
     table, rel = refs[:PIECES], refs[PIECES : 2 * PIECES]
-    send, rows, negs = refs[2 * PIECES :]
+    send, rows, negs, stage, done = refs[2 * PIECES :]
     negs[...] = recv[...]
     tile = recv[pl.ds(1, n, stride=TILES1), :]
     packed = []
@@ -245,7 +260,12 @@
             vec = cmul(vec, rel_vectors(tile, slots, rel))
         packed += [vec[:n, :], vec[n:, :]]
         rows[2 * n * side : 2 * n * (side + 1), :] = vec
-    pack(send, packed)
+
+    def write(c):
+        part = n // 4
+        pack(stage, [x[c * part : (c + 1) * part, :] for x in packed], c * part * TILES2)
+
+    in_parts(write, n // 4 * TILES2, stage, send, done)
 
 
 def negatives_kernel(odd, recv, rows, *refs):
@@ -290,28 +310,36 @@
         ref[...] = keep[at, :] + got[at, :]
 
 
-def edge_kernel(recv, same, rels, sum0, sum1, sum2, sum3, send, token):
+def edge_kernel(recv, aids, sum0, sum1, sum2, sum3, send, token, stage, done):
     n = LANE
     slots = unpack(recv, n)
     query, tails = jnp.concatenate(slots[:2], 0), jnp.concatenate(slots[2:], 0)
-    met = pick(same[0 : 2 * n, :], parts(tails, PIECES), NN)
+    met = pick(aids[4 * n :, 0 : 2 * n].astype(bf16), parts(tails, PIECES), NN)
     pos = jnp.sum(query * met, 1, keepdims=True)
     coef = -sigmoid(-pos)
-    to_head = cmul(coef * met, rels[...], True)
-    to_tail = pick(same[2 * n :, :], parts(coef * query, PIECES), NN)
+    met = coef * met
+    to_head = met * aids[0 : 2 * n, :] + turn(met) * aids[2 * n : 4 * n, :]
+    to_tail = pick(aids[4 * n :, 2 * n :].astype(bf16), parts(coef * query, PIECES), NN)
     neg = sum0[...] + sum1[...] + (sum2[...] + sum3[...])
-    at = lanes((n, LANE))
-    for q in range(4):
-        words = tile_of(neg, q // 2)
-        if q % 2:
-            words = pltpu.roll(words, 64, 1)
-        words = jnp.where(at < 64, words, pltpu.roll(words, 32, 1))
-        for s, block in enumerate((to_head[:n], to_head[n:], to_tail[:n], to_tail[n:])):
-            moved = pltpu.roll(words, 56 - 8 * s, 1)
-            send[pl.ds(4 * q + s, n, stride=4 * TILES3), :] = jnp.where(
-                at % 64 < 56, tile_of(block, q), moved
-            )
     token[...] = neg[0:8, 0:128]
+    part = n // 4
+    at = lanes((part, LANE))
+
+    def write(c):
+        rows = slice(c * part, (c + 1) * part)
+        for q in range(4):
+            words = tile_of(neg[rows, :], q // 2)
+            if q % 2:
+                words = pltpu.roll(words, 64, 1)
+            words = jnp.where(at < 64, words, pltpu.roll(words, 32, 1))
+            for s, block in enumerate((to_head[:n], to_head[n:], to_tail[:n], to_tail[n:])):
+                moved = pltpu.roll(words, 56 - 8 * s, 1)
+                first = c * part * 4 * TILES3 + 4 * q + s
+                stage[pl.ds(first, part, stride=4 * TILES3), :] = jnp.where(
+                    at % 64 < 56, tile_of(block[rows, :], q), moved
+                )
+
+    in_parts(write, part * 4 * TILES3, stage, send, done)
 
 
 def local_kernel(rep, token, asks, back, *refs):
@@ -405,7 +433,7 @@
         table_new[to : to + size, :] = table_t[to : to + size, :] - grads[at : at + size, :] * step
 
 
-def call(kernel, outs, args, scalars=(), name=None, scratch=(), whole=0):
+def call(kernel, outs, args, scalars=(), name=None, scratch=(), whole=0, direct=0):
     space = pl.BlockSpec(memory_space=pltpu.VMEM)
     return pl.pallas_call(
         kernel,
@@ -416,7 +444,7 @@
         in_specs=[pl.BlockSpec(memory_space=pltpu.SMEM)] * len(scalars)
         + [space] * (len(args) - whole)
         + [pl.BlockSpec(memory_space=pltpu.HBM)] * whole,
-        out_specs=[space] * len(outs),
+        out_specs=[pl.BlockSpec(memory_space=pltpu.HBM)] * direct + [space] * (len(outs) - direct),
         scratch_shapes=list(scratch),
         compiler_params=pltpu.CompilerParams(vmem_limit_bytes=24 << 20),
         name=name,
@@ -492,10 +520,10 @@
         (table_t, relations, far(head_edge)),
         name="ahead",
     )
-    (same,) = call(
+    (aids,) = call(
         pair_kernel,
-        [((4 * n, 2 * n), bf16, True)],
-        (far(head_edge), far(tail_edge)),
+        [((6 * n, 512), f32, True)],
+        (far(head_edge), far(tail_edge), far(edge_rels)),
         name="pair",
     )
     rel_pieces = pieces[PIECES:]
@@ -508,6 +536,8 @@
         ],
         (near(recv1), *map(near, pieces)),
         name="fetch",
+        scratch=(pltpu.VMEM((n * TILES2, n), f32), pltpu.SemaphoreType.DMA((4,))),
+        direct=1,
     )
     recv2 = exchange(send2, "ent", TILES2)
     mine = lax.all_gather(own_negs, "rep", axis=0, tiled=True)
@@ -530,8 +560,10 @@
     send3, token = call(
         edge_kernel,
         [((4 * n * TILES3, n), f32, False), ((8, n), f32, False)],
-        (near(recv2), near(same), far(edge_rels), far(sums[0]), *map(near, sums[1:])),
+        (near(recv2), near(aids), far(sums[0]), *map(near, sums[1:])),
         name="edge",
+        scratch=(pltpu.VMEM((4 * n * TILES3, n), f32), pltpu.SemaphoreType.DMA((4,))),
+        direct=1,
     )
     recv3 = exchange(send3, ("ent", "rep"), TILES3)
     token = far(token)

time: 186 us -> 188 us (1.011)
  transfers between devices with their start and end apart: 11 -> 11, of which waited for: 9 -> 10; matrix products, arithmetic and copies ran while one was open for 0% -> 0% of each run, Pallas kernels for 7% -> 7%
where the time goes in v8:
time: 188 us; the launch traced here: 184 us
  starting transfers between devices  64.5 us (34%)
  waiting for transfers between devices  62.8 us (33%)
  blocking collectives  27.3 us (15%)
  Pallas kernels  25.4 us (14%)
  local copies, waits for them, and re-layouts  3.58 us (2%)
    all_to_all x3, waiting for transfers between devices, exchange(): x = lax.all_to_all(x, axis, split_axis=0, concat_axis=0, tiled=True)  46.3 us
    all_to_all x3, starting transfers between devices, exchange(): x = lax.all_to_all(x, axis, split_axis=0, concat_axis=0, tiled=True)  39.3 us
    pallas_call x12, Pallas kernels, call(): pl.pallas_call(kernel, out_shape=[(pltpu.VMEM if near else pltpu.HBM)(sha...  25.4 us
    ppermute x6, starting transfers between devices, shift(): return lax.ppermute(x, 'rep', [(i, (i + by) % n) for i in range(n)])  21.2 us
    all_gather x1, blocking collectives, on_device(): grads = lax.all_gather(grads, 'rep', axis=0, tiled=True)  14.2 us
    all_gather x1, blocking collectives, on_device(): mine = lax.all_gather(own_negs, 'rep', axis=0, tiled=True)  13.1 us
    ppermute x6, waiting for transfers between devices, shift(): return lax.ppermute(x, 'rep', [(i, (i + by) % n) for i in range(n)])  13 us
    ppermute x2, starting transfers between devices, swap_cores(): lax.ppermute(x, 'ent', [(i, i ^ 1) for i in range(lax.axis_size('ent'))])  3.96 us
  transfers between devices with their start and end apart: 11, of which 10 were waited for; matrix products, arithmetic and copies ran while one was open for 0% of the time, Pallas kernels for 7%

profile of v8, /device:TPU:24, one launch (start us, length us, event | category | flops | bytes accessed | tf_op | source)
XLA Modules:
  0.0 184.5 jit_solution(15286411183493824564)
XLA Ops:
  0.6 2.6 %ask.1 = (f32[256,128]{1,0:T(8,128)}, f32[128,128]{1,0:T(8,128)}, f32[128,128]{1,0:T(8,128)}) custom-call(s32[1]{0:T(128)} %bitcast.rep, s32[4]{0:T(128)} %neg_rows.3, s32[1,128]{1,0:T(1,128)} %bitcast.28, s32[1,128]{1,0:T(1,128)} %bitcast.29, s32[1,128]{1,0:T(1,128)} %bitcast.30, s32[1,128]{1,0:T(1,128)} %bitcast.31, s32[1,128]{1,0:T(1,128)} %bitcast.32, ...), custom_call_target="tpu_custom_call" | custom-call | tf_op jit(solution)/shard_map/ask/pallas_call | solution.py:438
  3.2 19.3 %all-to-all-start = ((f32[128,1,256]{2,1,0:T(1,128)}), f32[128,1,256]{2,1,0:T(1,128)S(1)}, u32[]{:S(2)}, u32[]{:S(2)}) async-start(f32[128,1,256]{2,1,0:T(1,128)} %bitcast.27), calls=%async_computation | async-start | bytes 262144 | tf_op jit(solution)/shard_map/all_to_all | solution.py:465
  22.5 1.1 copy-done
  24.6 1.5 ahead.1
  26.9 11.8 %all-to-all-done = f32[128,1,256]{2,1,0:T(1,128)S(1)} async-done(((f32[128,1,256]{2,1,0:T(1,128)}), f32[128,1,256]{2,1,0:T(1,128)S(1)}, u32[]{:S(2)}, u32[]{:S(2)}) %all-to-all-start) | async-done | bytes 131104 | tf_op jit(solution)/shard_map/all_to_all | solution.py:465
  38.7 2.1 %fetch.1 = (f32[1664,128]{1,0:T(8,128)}, f32[512,512]{1,0:T(8,128)S(1)}, f32[256,128]{1,0:T(8,128)S(1)}) custom-call(f32[256,128]{1,0:T(8,128)S(1)} %bitcast.21, bf16[512,512]{1,0:T(8,128)(2,1)S(1)} %get-tuple-element.30.refs_0_, bf16[512,512]{1,0:T(8,128)(2,1)S(1)} %get-tuple-element.31.refs_1_, bf16[64,512]{1,0:T(8,128)(2,1)S(1)} %get-tuple-element.32.refs_2_.refs_0_, ...), custom_call_target="tpu_custom_call" | custom-call | tf_op jit(solution)/shard_map/fetch/pallas_call | solution.py:438
  40.8 7.5 %all-to-all-start.1 = ((f32[128,1,1664]{2,1,0:T(1,128)}), f32[128,1,1664]{2,1,0:T(1,128)}, u32[]{:S(2)}, u32[]{:S(2)}) async-start(f32[128,1,1664]{2,1,0:T(1,128)} %bitcast.26), calls=%async_computation.1 | async-start | bytes 1703936 | tf_op jit(solution)/shard_map/all_to_all | solution.py:465
  48.3 13.1 %all_gather.6.refs_2_.asks = f32[1024,128]{1,0:T(8,128)S(1)} all-gather(f32[256,128]{1,0:T(8,128)S(1)} %get-tuple-element.38), channel_id=1, replica_groups=mesh['ent'=128,'rep'=4] {'rep'}, dimensions={0}, use_global_device_ids=true | all-gather | bytes 655360 | tf_op jit(solution)/shard_map/all_gather | solution.py:543
  61.4 1.9 %collective-permute-start = (f32[1024,128]{1,0:T(8,128)S(1)}, f32[1024,128]{1,0:T(8,128)S(1)}, u32[]{:S(2)}, u32[]{:S(2)}) collective-permute-start(f32[1024,128]{1,0:T(8,128)S(1)} %all_gather.6.refs_2_.asks), channel_id=1, source_target_pairs={{0,4},{4,0},{8,12},{12,8},{16,20},{20,16},{24,28},{28,24},{32,36},... | collective-permute-start | bytes 1572872 | tf_op jit(solution)/shard_map/ppermute | solution.py:475
  63.3 1.9 %collective-permute-done.refs_3_ = f32[1024,128]{1,0:T(8,128)S(1)} collective-permute-done((f32[1024,128]{1,0:T(8,128)S(1)}, f32[1024,128]{1,0:T(8,128)S(1)}, u32[]{:S(2)}, u32[]{:S(2)}) %collective-permute-start) | collective-permute-done | bytes 524320 | tf_op jit(solution)/shard_map/ppermute | solution.py:475
  65.2 4.4 %negatives.1 = (f32[512,512]{1,0:T(8,128)S(1)}, f32[512,256]{1,0:T(8,128)S(1)}, f32[512,256]{1,0:T(8,128)S(1)}) custom-call(s32[1]{0:T(128)} %bitcast.11.odd, f32[256,128]{1,0:T(8,128)S(1)} %bitcast.22, f32[512,512]{1,0:T(8,128)S(1)} %get-tuple-element.37.rows, bf16[64,512]{1,0:T(8,128)(2,1)} %copy-done.4, bf16[64,512]{1,0:T(8,128)(2,1)} %copy-done.5, ...), custom_call_target="tpu_custom_call" | custom-call | tf_op jit(solution)/shard_map/negatives/pallas_call | solution.py:438
  69.7 2.0 %collective-permute-start.1 = (f32[512,256]{1,0:T(8,128)S(1)}, f32[512,256]{1,0:T(8,128)S(1)}, u32[]{:S(2)}, u32[]{:S(2)}) collective-permute-start(f32[512,256]{1,0:T(8,128)S(1)} %get-tuple-element.40), channel_id=1, source_target_pairs={{0,4},{4,0},{8,12},{12,8},{16,20},{20,16},{24,28},{28,24},{32,36},... | collective-permute-start | bytes 1572872 | tf_op jit(solution)/shard_map/ppermute | solution.py:475
  71.7 1.7 collective-permute-done.1.got
  73.5 3.1 %collective-permute-start.2 = (f32[128,256]{1,0:T(8,128)S(1)}, f32[128,256]{1,0:T(8,128)S(1)}, u32[]{:S(2)}, u32[]{:S(2)}) collective-permute-start(f32[128,256]{1,0:T(8,128)S(1)} %get-tuple-element.42), channel_id=1, source_target_pairs={{0,1},{1,2},{2,3},{3,0},{4,5},{5,6},{6,7},{7,4},{8,9},{9,10},{10,1... | collective-permute-start | bytes 393224 | tf_op jit(solution)/shard_map/ppermute | solution.py:471
  76.6 4.6 %collective-permute-start.3 = (f32[128,256]{1,0:T(8,128)S(1)}, f32[128,256]{1,0:T(8,128)S(1)}, u32[]{:S(2)}, u32[]{:S(2)}) collective-permute-start(f32[128,256]{1,0:T(8,128)S(1)} %get-tuple-element.43), channel_id=1, source_target_pairs={{0,2},{1,3},{2,0},{3,1},{4,6},{5,7},{6,4},{7,5},{8,10},{9,11},{10,... | collective-permute-start | bytes 393224 | tf_op jit(solution)/shard_map/ppermute | solution.py:471
  81.2 2.1 %collective-permute-start.4 = (f32[128,256]{1,0:T(8,128)S(1)}, f32[128,256]{1,0:T(8,128)S(1)}, u32[]{:S(2)}, u32[]{:S(2)}) collective-permute-start(f32[128,256]{1,0:T(8,128)S(1)} %get-tuple-element.44), channel_id=1, source_target_pairs={{0,3},{1,0},{2,1},{3,2},{4,7},{5,4},{6,5},{7,6},{8,11},{9,8},{10,9... | collective-permute-start | bytes 393224 | tf_op jit(solution)/shard_map/ppermute | solution.py:471
  83.4 1.6 pair.1.aids
  85.6 2.5 %collective-permute-done.4.sum3 = f32[128,256]{1,0:T(8,128)S(1)} collective-permute-done((f32[128,256]{1,0:T(8,128)S(1)}, f32[128,256]{1,0:T(8,128)S(1)}, u32[]{:S(2)}, u32[]{:S(2)}) %collective-permute-start.4) | collective-permute-done | bytes 131104 | tf_op jit(solution)/shard_map/ppermute | solution.py:471
  88.1 6.4 %all-to-all-done.1 = f32[128,1,1664]{2,1,0:T(1,128)} async-done(((f32[128,1,1664]{2,1,0:T(1,128)}), f32[128,1,1664]{2,1,0:T(1,128)}, u32[]{:S(2)}, u32[]{:S(2)}) %all-to-all-start.1) | async-done | bytes 852000 | tf_op jit(solution)/shard_map/all_to_all | solution.py:465
  94.5 5.1 %edge.1 = (f32[2048,128]{1,0:T(8,128)}, f32[8,128]{1,0:T(8,128)}) custom-call(f32[1664,128]{1,0:T(8,128)} %bitcast.10.recv, f32[768,512]{1,0:T(8,128)S(1)} %pair.1.aids, f32[128,256]{1,0:T(8,128)} %copy-done.8, f32[128,256]{1,0:T(8,128)S(1)} %collective-permute-done.2.sum1, f32[128,256]{1,0:T(8,128)S(1)} %collective-permute-done.3.sum2, ...), custom_call_target="tpu_custom_call" | custom-call | tf_op jit(solution)/shard_map/edge/pallas_call | solution.py:438
  99.6 12.5 %all-to-all-start.2 = ((f32[512,1,512]{2,1,0:T(1,128)}), f32[512,1,512]{2,1,0:T(1,128)S(1)}, u32[]{:S(2)}, u32[]{:S(2)}) async-start(f32[512,1,512]{2,1,0:T(1,128)} %bitcast.25), calls=%async_computation.2 | async-start | bytes 2097152 | tf_op jit(solution)/shard_map/all_to_all | solution.py:465
  112.2 2.9 %local.1 = (f32[512,128]{1,0:T(8,128)S(1)}, f32[512,128]{1,0:T(8,128)S(1)}, f32[512,128]{1,0:T(8,128)S(1)}, f32[512,128]{1,0:T(8,128)S(1)}) custom-call(s32[1]{0:T(128)} %bitcast.rep, f32[8,128]{1,0:T(8,128)} %get-tuple-element.46.token, f32[256,128]{1,0:T(8,128)S(1)} %bitcast.23, f32[512,512]{1,0:T(8,128)} %copy-done.3, bf16[64,512]{1,0:T(8,128)(2,1)} %copy-done.4, ...), custom_call_target="tpu_custom_call" | custom-call | tf_op jit(solution)/shard_map/local/pallas_call | solution.py:438
  115.1 3.4 %collective-permute-start.5 = (f32[512,128]{1,0:T(8,128)S(1)}, f32[512,128]{1,0:T(8,128)S(1)}, u32[]{:S(2)}, u32[]{:S(2)}) collective-permute-start(f32[512,128]{1,0:T(8,128)S(1)} %get-tuple-element.49), channel_id=1, source_target_pairs={{0,1},{1,2},{2,3},{3,0},{4,5},{5,6},{6,7},{7,4},{8,9},{9,10},{10,1... | collective-permute-start | bytes 786440 | tf_op jit(solution)/shard_map/ppermute | solution.py:471
  118.5 4.6 %collective-permute-start.6 = (f32[512,128]{1,0:T(8,128)S(1)}, f32[512,128]{1,0:T(8,128)S(1)}, u32[]{:S(2)}, u32[]{:S(2)}) collective-permute-start(f32[512,128]{1,0:T(8,128)S(1)} %get-tuple-element.50), channel_id=1, source_target_pairs={{0,2},{1,3},{2,0},{3,1},{4,6},{5,7},{6,4},{7,5},{8,10},{9,11},{10,... | collective-permute-start | bytes 786440 | tf_op jit(solution)/shard_map/ppermute | solution.py:471
  123.1 3.4 %collective-permute-start.7 = (f32[512,128]{1,0:T(8,128)S(1)}, f32[512,128]{1,0:T(8,128)S(1)}, u32[]{:S(2)}, u32[]{:S(2)}) collective-permute-start(f32[512,128]{1,0:T(8,128)S(1)} %get-tuple-element.51), channel_id=1, source_target_pairs={{0,3},{1,0},{2,1},{3,2},{4,7},{5,4},{6,5},{7,6},{8,11},{9,8},{10,9... | collective-permute-start | bytes 786440 | tf_op jit(solution)/shard_map/ppermute | solution.py:471
  126.5 1.7 place.1.hot
  128.3 8.3 %collective-permute-done.6.part2 = f32[512,128]{1,0:T(8,128)S(1)} collective-permute-done((f32[512,128]{1,0:T(8,128)S(1)}, f32[512,128]{1,0:T(8,128)S(1)}, u32[]{:S(2)}, u32[]{:S(2)}) %collective-permute-start.6) | collective-permute-done | bytes 262176 | tf_op jit(solution)/shard_map/ppermute | solution.py:471
  136.6 1.6 collective-permute-done.7.part3
  138.8 1.2 gather_local.1.local
  140.1 28.1 %all-to-all-done.2 = f32[512,1,512]{2,1,0:T(1,128)S(1)} async-done(((f32[512,1,512]{2,1,0:T(1,128)}), f32[512,1,512]{2,1,0:T(1,128)S(1)}, u32[]{:S(2)}, u32[]{:S(2)}) %all-to-all-start.2) | async-done | bytes 1048608 | tf_op jit(solution)/shard_map/all_to_all | solution.py:465
  169.2 14.2 %all_gather.7.grads = f32[448,512]{1,0:T(8,128)S(1)} all-gather(f32[112,512]{1,0:T(8,128)S(1)} %scatter.1), channel_id=1, replica_groups=mesh['ent'=128,'rep'=4] {'rep'}, dimensions={0}, use_global_device_ids=true | all-gather | bytes 1146880 | tf_op jit(solution)/shard_map/all_gather | solution.py:593
  183.4 1.1 finish.1
  (32 shorter events, 4.2 us)
Async XLA Ops:
  3.2 35.4 %all-to-all-start = ((f32[128,1,256]{2,1,0:T(1,128)}), f32[128,1,256]{2,1,0:T(1,128)S(1)}, u32[]{:S(2)}, u32[]{:S(2)}) async-start(f32[128,1,256]{2,1,0:T(1,128)} %bitcast.27), calls=%async_computation | async-start | bytes 262144 | tf_op jit(solution)/shard_map/all_to_all | solution.py:465
  22.5 1.1 copy-start
  23.7 0.9 copy-start.9
  26.1 0.8 copy-start.6
  26.9 38.3 %copy-start.4 = (bf16[64,512]{1,0:T(8,128)(2,1)}, bf16[64,512]{1,0:T(8,128)(2,1)S(1)}, u32[]{:S(2)}) copy-start(bf16[64,512]{1,0:T(8,128)(2,1)S(1)} %get-tuple-element.32.refs_2_.refs_0_) | copy-start | bytes 196612
  26.9 38.3 %copy-start.5 = (bf16[64,512]{1,0:T(8,128)(2,1)}, bf16[64,512]{1,0:T(8,128)(2,1)S(1)}, u32[]{:S(2)}) copy-start(bf16[64,512]{1,0:T(8,128)(2,1)S(1)} %get-tuple-element.33.refs_3_.refs_1_) | copy-start | bytes 196612
  40.8 53.7 %all-to-all-start.1 = ((f32[128,1,1664]{2,1,0:T(1,128)}), f32[128,1,1664]{2,1,0:T(1,128)}, u32[]{:S(2)}, u32[]{:S(2)}) async-start(f32[128,1,1664]{2,1,0:T(1,128)} %bitcast.26), calls=%async_computation.1 | async-start | bytes 1703936 | tf_op jit(solution)/shard_map/all_to_all | solution.py:465
  61.4 23.6 %copy-start.2 = (f32[1024,128]{1,0:T(8,128)}, f32[1024,128]{1,0:T(8,128)S(1)}, u32[]{:S(2)}) copy-start(f32[1024,128]{1,0:T(8,128)S(1)} %all_gather.6.refs_2_.asks) | copy-start | bytes 1572868
  61.4 3.8 %collective-permute-start = (f32[1024,128]{1,0:T(8,128)S(1)}, f32[1024,128]{1,0:T(8,128)S(1)}, u32[]{:S(2)}, u32[]{:S(2)}) collective-permute-start(f32[1024,128]{1,0:T(8,128)S(1)} %all_gather.6.refs_2_.asks), channel_id=1, source_target_pairs={{0,4},{4,0},{8,12},{12,8},{16,20},{20,16},{24,28},{28,24},{32,36},... | collective-permute-start | bytes 1572872 | tf_op jit(solution)/shard_map/ppermute | solution.py:475
  69.6 15.4 %copy-start.3 = (f32[512,512]{1,0:T(8,128)}, f32[512,512]{1,0:T(8,128)S(1)}, u32[]{:S(2)}) copy-start(f32[512,512]{1,0:T(8,128)S(1)} %get-tuple-element.47.back) | copy-start | bytes 3145732
  69.7 3.8 %collective-permute-start.1 = (f32[512,256]{1,0:T(8,128)S(1)}, f32[512,256]{1,0:T(8,128)S(1)}, u32[]{:S(2)}, u32[]{:S(2)}) collective-permute-start(f32[512,256]{1,0:T(8,128)S(1)} %get-tuple-element.40), channel_id=1, source_target_pairs={{0,4},{4,0},{8,12},{12,8},{16,20},{20,16},{24,28},{28,24},{32,36},... | collective-permute-start | bytes 1572872 | tf_op jit(solution)/shard_map/ppermute | solution.py:475
  73.5 12.1 %copy-start.8 = (f32[128,256]{1,0:T(8,128)}, f32[128,256]{1,0:T(8,128)S(1)}, u32[]{:S(2)}) copy-start(f32[128,256]{1,0:T(8,128)S(1)} %get-tuple-element.41.sum0) | copy-start | bytes 393220
  73.5 11.5 %collective-permute-start.2 = (f32[128,256]{1,0:T(8,128)S(1)}, f32[128,256]{1,0:T(8,128)S(1)}, u32[]{:S(2)}, u32[]{:S(2)}) collective-permute-start(f32[128,256]{1,0:T(8,128)S(1)} %get-tuple-element.42), channel_id=1, source_target_pairs={{0,1},{1,2},{2,3},{3,0},{4,5},{5,6},{6,7},{7,4},{8,9},{9,10},{10,1... | collective-permute-start | bytes 393224 | tf_op jit(solution)/shard_map/ppermute | solution.py:471
  76.6 9.0 %collective-permute-start.3 = (f32[128,256]{1,0:T(8,128)S(1)}, f32[128,256]{1,0:T(8,128)S(1)}, u32[]{:S(2)}, u32[]{:S(2)}) collective-permute-start(f32[128,256]{1,0:T(8,128)S(1)} %get-tuple-element.43), channel_id=1, source_target_pairs={{0,2},{1,3},{2,0},{3,1},{4,6},{5,7},{6,4},{7,5},{8,10},{9,11},{10,... | collective-permute-start | bytes 393224 | tf_op jit(solution)/shard_map/ppermute | solution.py:471
  81.2 6.9 %collective-permute-start.4 = (f32[128,256]{1,0:T(8,128)S(1)}, f32[128,256]{1,0:T(8,128)S(1)}, u32[]{:S(2)}, u32[]{:S(2)}) collective-permute-start(f32[128,256]{1,0:T(8,128)S(1)} %get-tuple-element.44), channel_id=1, source_target_pairs={{0,3},{1,0},{2,1},{3,2},{4,7},{5,4},{6,5},{7,6},{8,11},{9,8},{10,9... | collective-permute-start | bytes 393224 | tf_op jit(solution)/shard_map/ppermute | solution.py:471
  99.6 68.6 %all-to-all-start.2 = ((f32[512,1,512]{2,1,0:T(1,128)}), f32[512,1,512]{2,1,0:T(1,128)S(1)}, u32[]{:S(2)}, u32[]{:S(2)}) async-start(f32[512,1,512]{2,1,0:T(1,128)} %bitcast.25), calls=%async_computation.2 | async-start | bytes 2097152 | tf_op jit(solution)/shard_map/all_to_all | solution.py:465
  115.1 23.0 %copy-start.7 = (f32[512,128]{1,0:T(8,128)}, f32[512,128]{1,0:T(8,128)S(1)}, u32[]{:S(2)}) copy-start(f32[512,128]{1,0:T(8,128)S(1)} %get-tuple-element.48.part0) | copy-start | bytes 786436
  115.1 13.2 %collective-permute-start.5 = (f32[512,128]{1,0:T(8,128)S(1)}, f32[512,128]{1,0:T(8,128)S(1)}, u32[]{:S(2)}, u32[]{:S(2)}) collective-permute-start(f32[512,128]{1,0:T(8,128)S(1)} %get-tuple-element.49), channel_id=1, source_target_pairs={{0,1},{1,2},{2,3},{3,0},{4,5},{5,6},{6,7},{7,4},{8,9},{9,10},{10,1... | collective-permute-start | bytes 786440 | tf_op jit(solution)/shard_map/ppermute | solution.py:471
  118.5 18.1 %collective-permute-start.6 = (f32[512,128]{1,0:T(8,128)S(1)}, f32[512,128]{1,0:T(8,128)S(1)}, u32[]{:S(2)}, u32[]{:S(2)}) collective-permute-start(f32[512,128]{1,0:T(8,128)S(1)} %get-tuple-element.50), channel_id=1, source_target_pairs={{0,2},{1,3},{2,0},{3,1},{4,6},{5,7},{6,4},{7,5},{8,10},{9,11},{10,... | collective-permute-start | bytes 786440 | tf_op jit(solution)/shard_map/ppermute | solution.py:471
  123.1 15.0 %collective-permute-start.7 = (f32[512,128]{1,0:T(8,128)S(1)}, f32[512,128]{1,0:T(8,128)S(1)}, u32[]{:S(2)}, u32[]{:S(2)}) collective-permute-start(f32[512,128]{1,0:T(8,128)S(1)} %get-tuple-element.51), channel_id=1, source_target_pairs={{0,3},{1,0},{2,1},{3,2},{4,7},{5,4},{6,5},{7,6},{8,11},{9,8},{10,9... | collective-permute-start | bytes 786440 | tf_op jit(solution)/shard_map/ppermute | solution.py:471
  128.3 9.8 %copy-start.11 = (f32[512,128]{1,0:T(8,128)}, f32[512,128]{1,0:T(8,128)S(1)}, u32[]{:S(2)}) copy-start(f32[512,128]{1,0:T(8,128)S(1)} %collective-permute-done.5.part1) | copy-start | bytes 786436
  136.6 1.6 copy-start.12
  138.1 0.7 copy-start.13
  168.2 15.2 %copy-start.1 = (f32[512,400]{0,1:T(8,128)S(1)}, f32[512,400]{0,1:T(8,128)}, u32[]{:S(2)}) copy-start(f32[512,400]{0,1:T(8,128)} %param.9) | copy-start | bytes 2457604
  168.2 15.2 %copy-start.10 = (f32[512]{0:T(512)S(1)}, f32[512]{0:T(512)}, u32[]{:S(2)}) copy-start(f32[512]{0:T(512)} %param.10) | copy-start | bytes 6148

commit v9 on v7

--- a/solution.py
+++ b/solution.py
@@ -62,11 +62,16 @@
     return jnp.concatenate([pltpu.roll(tile_of(x, q), 64, 1) for q in range(4)], 1)
 
 
-def cmul(a, b, conj=False):
+def factors(b, conj=False):
     low = lanes(b.shape) % LANE < 64
     other = turn(b)
     second = jnp.where(low, other, -b) if conj else jnp.where(low, -other, b)
-    return a * jnp.where(low, b, other) + turn(a) * second
+    return jnp.where(low, b, other), second
+
+
+def cmul(a, b, conj=False):
+    first, second = factors(b, conj)
+    return a * first + turn(a) * second
 
 
 def sigmoid(x):
@@ -207,8 +212,9 @@
     outs[-1][...] = pick(hot, pieces, NN)
 
 
-def pair_kernel(head_edge, tail_edge, same):
+def pair_kernel(head_edge, tail_edge, rels, neg, out):
     n = 2 * LANE
+    out[0:n, :], out[n : 2 * n, :] = factors(rels[...], True)
 
     def stack(ref, by_rows):
         if by_rows:
@@ -218,9 +224,11 @@
 
     for i, (one, other) in enumerate(((head_edge, tail_edge), (tail_edge, head_edge))):
         col, row = stack(one, False), stack(other, True)
-        same[i * n : (i + 1) * n, :] = jnp.where(
+        out[2 * n : 3 * n, i * n : (i + 1) * n] = jnp.where(
             (col == row) & (col >= 0.0), 1.0, 0.0
-        ).astype(bf16)
+        )
+    out[3 * n :, 0:n] = neg[...]
+    out[3 * n :, n:] = jnp.zeros((LANE, n), f32)
 
 
 def rel_vectors(tile, slots, pieces):
@@ -290,16 +298,17 @@
         ref[...] = keep[at, :] + got[at, :]
 
 
-def edge_kernel(recv, same, rels, sum0, sum1, sum2, sum3, send, token):
+def edge_kernel(recv, aids, sum1, sum2, sum3, send, token):
     n = LANE
     slots = unpack(recv, n)
     query, tails = jnp.concatenate(slots[:2], 0), jnp.concatenate(slots[2:], 0)
-    met = pick(same[0 : 2 * n, :], parts(tails, PIECES), NN)
+    met = pick(aids[4 * n : 6 * n, 0 : 2 * n].astype(bf16), parts(tails, PIECES), NN)
     pos = jnp.sum(query * met, 1, keepdims=True)
     coef = -sigmoid(-pos)
-    to_head = cmul(coef * met, rels[...], True)
-    to_tail = pick(same[2 * n :, :], parts(coef * query, PIECES), NN)
-    neg = sum0[...] + sum1[...] + (sum2[...] + sum3[...])
+    met = coef * met
+    to_head = met * aids[0 : 2 * n, :] + turn(met) * aids[2 * n : 4 * n, :]
+    to_tail = pick(aids[4 * n : 6 * n, 2 * n :].astype(bf16), parts(coef * query, PIECES), NN)
+    neg = aids[6 * n :, 0 : 2 * n] + sum1[...] + (sum2[...] + sum3[...])
     at = lanes((n, LANE))
     for q in range(4):
         words = tile_of(neg, q // 2)
@@ -492,12 +501,6 @@
         (table_t, relations, far(head_edge)),
         name="ahead",
     )
-    (same,) = call(
-        pair_kernel,
-        [((4 * n, 2 * n), bf16, True)],
-        (far(head_edge), far(tail_edge)),
-        name="pair",
-    )
     rel_pieces = pieces[PIECES:]
     send2, rows, own_negs = call(
         fetch_kernel,
@@ -526,11 +529,17 @@
         (rep,),
         "fold",
     )
-    sums = [owned[0]] + [shift(owned[j], j) for j in (1, 2, 3)]
+    sums = [shift(owned[j], j) for j in (1, 2, 3)]
+    (aids,) = call(
+        pair_kernel,
+        [((7 * n, 512), f32, True)],
+        (far(head_edge), far(tail_edge), far(edge_rels), near(owned[0])),
+        name="pair",
+    )
     send3, token = call(
         edge_kernel,
         [((4 * n * TILES3, n), f32, False), ((8, n), f32, False)],
-        (near(recv2), near(same), far(edge_rels), far(sums[0]), *map(near, sums[1:])),
+        (near(recv2), near(aids), *map(near, sums)),
         name="edge",
     )
     recv3 = exchange(send3, ("ent", "rep"), TILES3)

time: 186 us -> 187 us (level)
    unnamed x28 -> x26, local copies, waits for them, and re-layouts: 3.58 us -> 4.28 us
where the time goes in v9:
time: 187 us; the launch traced here: 183 us
  starting transfers between devices  64.3 us (34%)
  waiting for transfers between devices  62.2 us (33%)
  blocking collectives  27.3 us (15%)
  Pallas kernels  24.3 us (13%)
  local copies, waits for them, and re-layouts  4.28 us (2%)
    all_to_all x3, waiting for transfers between devices, exchange(): x = lax.all_to_all(x, axis, split_axis=0, concat_axis=0, tiled=True)  45.6 us
    all_to_all x3, starting transfers between devices, exchange(): x = lax.all_to_all(x, axis, split_axis=0, concat_axis=0, tiled=True)  39.2 us
    pallas_call x12, Pallas kernels, call(): pl.pallas_call(kernel, out_shape=[(pltpu.VMEM if near else pltpu.HBM)(sha...  24.3 us
    ppermute x6, starting transfers between devices, shift(): return lax.ppermute(x, 'rep', [(i, (i + by) % n) for i in range(n)])  21.2 us
    all_gather x1, blocking collectives, on_device(): grads = lax.all_gather(grads, 'rep', axis=0, tiled=True)  14.2 us
    all_gather x1, blocking collectives, on_device(): mine = lax.all_gather(own_negs, 'rep', axis=0, tiled=True)  13.1 us
    ppermute x6, waiting for transfers between devices, shift(): return lax.ppermute(x, 'rep', [(i, (i + by) % n) for i in range(n)])  13 us
    unnamed x26, local copies, waits for them, and re-layouts  4.28 us
  transfers between devices with their start and end apart: 11, of which 9 were waited for; matrix products, arithmetic and copies ran while one was open for 0% of the time, Pallas kernels for 7%

profile of v9, /device:TPU:24, one launch (start us, length us, event | category | flops | bytes accessed | tf_op | source)
XLA Modules:
  0.0 183.3 jit_solution(4591471937338488686)
XLA Ops:
  0.6 2.6 %ask.1 = (f32[256,128]{1,0:T(8,128)}, f32[128,128]{1,0:T(8,128)}, f32[128,128]{1,0:T(8,128)}) custom-call(s32[1]{0:T(128)} %bitcast.rep, s32[4]{0:T(128)} %neg_rows.3, s32[1,128]{1,0:T(1,128)} %bitcast.28, s32[1,128]{1,0:T(1,128)} %bitcast.29, s32[1,128]{1,0:T(1,128)} %bitcast.30, s32[1,128]{1,0:T(1,128)} %bitcast.31, s32[1,128]{1,0:T(1,128)} %bitcast.32, ...), custom_call_target="tpu_custom_call" | custom-call | tf_op jit(solution)/shard_map/ask/pallas_call | solution.py:419
  3.2 19.3 %all-to-all-start = ((f32[128,1,256]{2,1,0:T(1,128)}), f32[128,1,256]{2,1,0:T(1,128)S(1)}, u32[]{:S(2)}, u32[]{:S(2)}) async-start(f32[128,1,256]{2,1,0:T(1,128)} %bitcast.27), calls=%async_computation | async-start | bytes 262144 | tf_op jit(solution)/shard_map/all_to_all | solution.py:446
  22.5 1.1 copy-done
  24.6 1.5 ahead.1
  26.9 11.8 %all-to-all-done = f32[128,1,256]{2,1,0:T(1,128)S(1)} async-done(((f32[128,1,256]{2,1,0:T(1,128)}), f32[128,1,256]{2,1,0:T(1,128)S(1)}, u32[]{:S(2)}, u32[]{:S(2)}) %all-to-all-start) | async-done | bytes 131104 | tf_op jit(solution)/shard_map/all_to_all | solution.py:446
  38.7 2.1 %fetch.1 = (f32[1664,128]{1,0:T(8,128)}, f32[512,512]{1,0:T(8,128)S(1)}, f32[256,128]{1,0:T(8,128)S(1)}) custom-call(f32[256,128]{1,0:T(8,128)S(1)} %bitcast.21, bf16[512,512]{1,0:T(8,128)(2,1)S(1)} %get-tuple-element.30.refs_0_, bf16[512,512]{1,0:T(8,128)(2,1)S(1)} %get-tuple-element.31.refs_1_, bf16[64,512]{1,0:T(8,128)(2,1)S(1)} %get-tuple-element.32.refs_2_.refs_0_, ...), custom_call_target="tpu_custom_call" | custom-call | tf_op jit(solution)/shard_map/fetch/pallas_call | solution.py:419
  40.9 7.4 %all-to-all-start.1 = ((f32[128,1,1664]{2,1,0:T(1,128)}), f32[128,1,1664]{2,1,0:T(1,128)}, u32[]{:S(2)}, u32[]{:S(2)}) async-start(f32[128,1,1664]{2,1,0:T(1,128)} %bitcast.26), calls=%async_computation.1 | async-start | bytes 1703936 | tf_op jit(solution)/shard_map/all_to_all | solution.py:446
  48.3 13.1 %all_gather.6.refs_2_.asks = f32[1024,128]{1,0:T(8,128)S(1)} all-gather(f32[256,128]{1,0:T(8,128)S(1)} %get-tuple-element.38), channel_id=1, replica_groups=mesh['ent'=128,'rep'=4] {'rep'}, dimensions={0}, use_global_device_ids=true | all-gather | bytes 655360 | tf_op jit(solution)/shard_map/all_gather | solution.py:516
  61.4 1.9 %collective-permute-start = (f32[1024,128]{1,0:T(8,128)S(1)}, f32[1024,128]{1,0:T(8,128)S(1)}, u32[]{:S(2)}, u32[]{:S(2)}) collective-permute-start(f32[1024,128]{1,0:T(8,128)S(1)} %all_gather.6.refs_2_.asks), channel_id=1, source_target_pairs={{0,4},{4,0},{8,12},{12,8},{16,20},{20,16},{24,28},{28,24},{32,36},... | collective-permute-start | bytes 1572872 | tf_op jit(solution)/shard_map/ppermute | solution.py:456
  63.3 1.9 %collective-permute-done.refs_3_ = f32[1024,128]{1,0:T(8,128)S(1)} collective-permute-done((f32[1024,128]{1,0:T(8,128)S(1)}, f32[1024,128]{1,0:T(8,128)S(1)}, u32[]{:S(2)}, u32[]{:S(2)}) %collective-permute-start) | collective-permute-done | bytes 524320 | tf_op jit(solution)/shard_map/ppermute | solution.py:456
  65.2 4.4 %negatives.1 = (f32[512,512]{1,0:T(8,128)S(1)}, f32[512,256]{1,0:T(8,128)S(1)}, f32[512,256]{1,0:T(8,128)S(1)}) custom-call(s32[1]{0:T(128)} %bitcast.11.odd, f32[256,128]{1,0:T(8,128)S(1)} %bitcast.22, f32[512,512]{1,0:T(8,128)S(1)} %get-tuple-element.37.rows, bf16[64,512]{1,0:T(8,128)(2,1)} %copy-done.4, bf16[64,512]{1,0:T(8,128)(2,1)} %copy-done.5, ...), custom_call_target="tpu_custom_call" | custom-call | tf_op jit(solution)/shard_map/negatives/pallas_call | solution.py:419
  69.7 2.0 %collective-permute-start.1 = (f32[512,256]{1,0:T(8,128)S(1)}, f32[512,256]{1,0:T(8,128)S(1)}, u32[]{:S(2)}, u32[]{:S(2)}) collective-permute-start(f32[512,256]{1,0:T(8,128)S(1)} %get-tuple-element.40), channel_id=1, source_target_pairs={{0,4},{4,0},{8,12},{12,8},{16,20},{20,16},{24,28},{28,24},{32,36},... | collective-permute-start | bytes 1572872 | tf_op jit(solution)/shard_map/ppermute | solution.py:456
  71.7 1.8 collective-permute-done.1.got
  73.5 3.1 %collective-permute-start.2 = (f32[128,256]{1,0:T(8,128)S(1)}, f32[128,256]{1,0:T(8,128)S(1)}, u32[]{:S(2)}, u32[]{:S(2)}) collective-permute-start(f32[128,256]{1,0:T(8,128)S(1)} %get-tuple-element.42), channel_id=1, source_target_pairs={{0,1},{1,2},{2,3},{3,0},{4,5},{5,6},{6,7},{7,4},{8,9},{9,10},{10,1... | collective-permute-start | bytes 393224 | tf_op jit(solution)/shard_map/ppermute | solution.py:452
  76.6 4.6 %collective-permute-start.3 = (f32[128,256]{1,0:T(8,128)S(1)}, f32[128,256]{1,0:T(8,128)S(1)}, u32[]{:S(2)}, u32[]{:S(2)}) collective-permute-start(f32[128,256]{1,0:T(8,128)S(1)} %get-tuple-element.43), channel_id=1, source_target_pairs={{0,2},{1,3},{2,0},{3,1},{4,6},{5,7},{6,4},{7,5},{8,10},{9,11},{10,... | collective-permute-start | bytes 393224 | tf_op jit(solution)/shard_map/ppermute | solution.py:452
  81.2 2.1 %collective-permute-start.4 = (f32[128,256]{1,0:T(8,128)S(1)}, f32[128,256]{1,0:T(8,128)S(1)}, u32[]{:S(2)}, u32[]{:S(2)}) collective-permute-start(f32[128,256]{1,0:T(8,128)S(1)} %get-tuple-element.44), channel_id=1, source_target_pairs={{0,3},{1,0},{2,1},{3,2},{4,7},{5,4},{6,5},{7,6},{8,11},{9,8},{10,9... | collective-permute-start | bytes 393224 | tf_op jit(solution)/shard_map/ppermute | solution.py:452
  83.4 1.6 pair.1.aids
  85.6 2.5 %collective-permute-done.4.sum3 = f32[128,256]{1,0:T(8,128)S(1)} collective-permute-done((f32[128,256]{1,0:T(8,128)S(1)}, f32[128,256]{1,0:T(8,128)S(1)}, u32[]{:S(2)}, u32[]{:S(2)}) %collective-permute-start.4) | collective-permute-done | bytes 131104 | tf_op jit(solution)/shard_map/ppermute | solution.py:452
  88.1 6.4 %all-to-all-done.1 = f32[128,1,1664]{2,1,0:T(1,128)} async-done(((f32[128,1,1664]{2,1,0:T(1,128)}), f32[128,1,1664]{2,1,0:T(1,128)}, u32[]{:S(2)}, u32[]{:S(2)}) %all-to-all-start.1) | async-done | bytes 852000 | tf_op jit(solution)/shard_map/all_to_all | solution.py:446
  94.5 4.0 %edge.1 = (f32[2048,128]{1,0:T(8,128)}, f32[8,128]{1,0:T(8,128)}) custom-call(f32[1664,128]{1,0:T(8,128)} %bitcast.10.recv, f32[896,512]{1,0:T(8,128)S(1)} %pair.1.aids, f32[128,256]{1,0:T(8,128)S(1)} %collective-permute-done.2.sum1, f32[128,256]{1,0:T(8,128)S(1)} %collective-permute-done.3.sum2, f32[128,256]{1,0:T(8,128)S(1)} %collective-permute-done.4.sum3), custom_call_target="tpu_custom_call" | custom-call | tf_op jit(solution)/shard_map/edge/pallas_call | solution.py:419
  98.5 12.5 %all-to-all-start.2 = ((f32[512,1,512]{2,1,0:T(1,128)}), f32[512,1,512]{2,1,0:T(1,128)S(1)}, u32[]{:S(2)}, u32[]{:S(2)}) async-start(f32[512,1,512]{2,1,0:T(1,128)} %bitcast.25), calls=%async_computation.2 | async-start | bytes 2097152 | tf_op jit(solution)/shard_map/all_to_all | solution.py:446
  111.0 2.9 %local.1 = (f32[512,128]{1,0:T(8,128)S(1)}, f32[512,128]{1,0:T(8,128)S(1)}, f32[512,128]{1,0:T(8,128)S(1)}, f32[512,128]{1,0:T(8,128)S(1)}) custom-call(s32[1]{0:T(128)} %bitcast.rep, f32[8,128]{1,0:T(8,128)} %get-tuple-element.46.token, f32[256,128]{1,0:T(8,128)S(1)} %bitcast.23, f32[512,512]{1,0:T(8,128)} %copy-done.3, bf16[64,512]{1,0:T(8,128)(2,1)} %copy-done.4, ...), custom_call_target="tpu_custom_call" | custom-call | tf_op jit(solution)/shard_map/local/pallas_call | solution.py:419
  114.6 3.4 %collective-permute-start.5 = (f32[512,128]{1,0:T(8,128)S(1)}, f32[512,128]{1,0:T(8,128)S(1)}, u32[]{:S(2)}, u32[]{:S(2)}) collective-permute-start(f32[512,128]{1,0:T(8,128)S(1)} %get-tuple-element.49), channel_id=1, source_target_pairs={{0,1},{1,2},{2,3},{3,0},{4,5},{5,6},{6,7},{7,4},{8,9},{9,10},{10,1... | collective-permute-start | bytes 786440 | tf_op jit(solution)/shard_map/ppermute | solution.py:452
  118.0 4.6 %collective-permute-start.6 = (f32[512,128]{1,0:T(8,128)S(1)}, f32[512,128]{1,0:T(8,128)S(1)}, u32[]{:S(2)}, u32[]{:S(2)}) collective-permute-start(f32[512,128]{1,0:T(8,128)S(1)} %get-tuple-element.50), channel_id=1, source_target_pairs={{0,2},{1,3},{2,0},{3,1},{4,6},{5,7},{6,4},{7,5},{8,10},{9,11},{10,... | collective-permute-start | bytes 786440 | tf_op jit(solution)/shard_map/ppermute | solution.py:452
  122.6 3.4 %collective-permute-start.7 = (f32[512,128]{1,0:T(8,128)S(1)}, f32[512,128]{1,0:T(8,128)S(1)}, u32[]{:S(2)}, u32[]{:S(2)}) collective-permute-start(f32[512,128]{1,0:T(8,128)S(1)} %get-tuple-element.51), channel_id=1, source_target_pairs={{0,3},{1,0},{2,1},{3,2},{4,7},{5,4},{6,5},{7,6},{8,11},{9,8},{10,9... | collective-permute-start | bytes 786440 | tf_op jit(solution)/shard_map/ppermute | solution.py:452
  126.0 1.7 place.1.hot
  127.8 8.4 %collective-permute-done.6.part2 = f32[512,128]{1,0:T(8,128)S(1)} collective-permute-done((f32[512,128]{1,0:T(8,128)S(1)}, f32[512,128]{1,0:T(8,128)S(1)}, u32[]{:S(2)}, u32[]{:S(2)}) %collective-permute-start.6) | collective-permute-done | bytes 262176 | tf_op jit(solution)/shard_map/ppermute | solution.py:452
  136.2 1.5 collective-permute-done.7.part3
  138.4 1.2 gather_local.1.local
  139.6 27.4 %all-to-all-done.2 = f32[512,1,512]{2,1,0:T(1,128)S(1)} async-done(((f32[512,1,512]{2,1,0:T(1,128)}), f32[512,1,512]{2,1,0:T(1,128)S(1)}, u32[]{:S(2)}, u32[]{:S(2)}) %all-to-all-start.2) | async-done | bytes 1048608 | tf_op jit(solution)/shard_map/all_to_all | solution.py:446
  168.0 14.2 %all_gather.7.grads = f32[448,512]{1,0:T(8,128)S(1)} all-gather(f32[112,512]{1,0:T(8,128)S(1)} %scatter.1), channel_id=1, replica_groups=mesh['ent'=128,'rep'=4] {'rep'}, dimensions={0}, use_global_device_ids=true | all-gather | bytes 1146880 | tf_op jit(solution)/shard_map/all_gather | solution.py:570
  182.2 1.1 finish.1
  (30 shorter events, 4.8 us)
Async XLA Ops:
  3.2 35.5 %all-to-all-start = ((f32[128,1,256]{2,1,0:T(1,128)}), f32[128,1,256]{2,1,0:T(1,128)S(1)}, u32[]{:S(2)}, u32[]{:S(2)}) async-start(f32[128,1,256]{2,1,0:T(1,128)} %bitcast.27), calls=%async_computation | async-start | bytes 262144 | tf_op jit(solution)/shard_map/all_to_all | solution.py:446
  22.5 1.1 copy-start
  23.7 0.9 copy-start.8
  26.1 0.8 copy-start.6
  26.9 38.3 %copy-start.4 = (bf16[64,512]{1,0:T(8,128)(2,1)}, bf16[64,512]{1,0:T(8,128)(2,1)S(1)}, u32[]{:S(2)}) copy-start(bf16[64,512]{1,0:T(8,128)(2,1)S(1)} %get-tuple-element.32.refs_2_.refs_0_) | copy-start | bytes 196612
  26.9 38.3 %copy-start.5 = (bf16[64,512]{1,0:T(8,128)(2,1)}, bf16[64,512]{1,0:T(8,128)(2,1)S(1)}, u32[]{:S(2)}) copy-start(bf16[64,512]{1,0:T(8,128)(2,1)S(1)} %get-tuple-element.33.refs_3_.refs_1_) | copy-start | bytes 196612
  40.9 53.6 %all-to-all-start.1 = ((f32[128,1,1664]{2,1,0:T(1,128)}), f32[128,1,1664]{2,1,0:T(1,128)}, u32[]{:S(2)}, u32[]{:S(2)}) async-start(f32[128,1,1664]{2,1,0:T(1,128)} %bitcast.26), calls=%async_computation.1 | async-start | bytes 1703936 | tf_op jit(solution)/shard_map/all_to_all | solution.py:446
  61.4 23.6 %copy-start.2 = (f32[1024,128]{1,0:T(8,128)}, f32[1024,128]{1,0:T(8,128)S(1)}, u32[]{:S(2)}) copy-start(f32[1024,128]{1,0:T(8,128)S(1)} %all_gather.6.refs_2_.asks) | copy-start | bytes 1572868
  61.4 3.8 %collective-permute-start = (f32[1024,128]{1,0:T(8,128)S(1)}, f32[1024,128]{1,0:T(8,128)S(1)}, u32[]{:S(2)}, u32[]{:S(2)}) collective-permute-start(f32[1024,128]{1,0:T(8,128)S(1)} %all_gather.6.refs_2_.asks), channel_id=1, source_target_pairs={{0,4},{4,0},{8,12},{12,8},{16,20},{20,16},{24,28},{28,24},{32,36},... | collective-permute-start | bytes 1572872 | tf_op jit(solution)/shard_map/ppermute | solution.py:456
  69.7 15.4 %copy-start.3 = (f32[512,512]{1,0:T(8,128)}, f32[512,512]{1,0:T(8,128)S(1)}, u32[]{:S(2)}) copy-start(f32[512,512]{1,0:T(8,128)S(1)} %get-tuple-element.47.back) | copy-start | bytes 3145732
  69.7 3.8 %collective-permute-start.1 = (f32[512,256]{1,0:T(8,128)S(1)}, f32[512,256]{1,0:T(8,128)S(1)}, u32[]{:S(2)}, u32[]{:S(2)}) collective-permute-start(f32[512,256]{1,0:T(8,128)S(1)} %get-tuple-element.40), channel_id=1, source_target_pairs={{0,4},{4,0},{8,12},{12,8},{16,20},{20,16},{24,28},{28,24},{32,36},... | collective-permute-start | bytes 1572872 | tf_op jit(solution)/shard_map/ppermute | solution.py:456
  73.5 11.5 %collective-permute-start.2 = (f32[128,256]{1,0:T(8,128)S(1)}, f32[128,256]{1,0:T(8,128)S(1)}, u32[]{:S(2)}, u32[]{:S(2)}) collective-permute-start(f32[128,256]{1,0:T(8,128)S(1)} %get-tuple-element.42), channel_id=1, source_target_pairs={{0,1},{1,2},{2,3},{3,0},{4,5},{5,6},{6,7},{7,4},{8,9},{9,10},{10,1... | collective-permute-start | bytes 393224 | tf_op jit(solution)/shard_map/ppermute | solution.py:452
  76.6 9.0 %collective-permute-start.3 = (f32[128,256]{1,0:T(8,128)S(1)}, f32[128,256]{1,0:T(8,128)S(1)}, u32[]{:S(2)}, u32[]{:S(2)}) collective-permute-start(f32[128,256]{1,0:T(8,128)S(1)} %get-tuple-element.43), channel_id=1, source_target_pairs={{0,2},{1,3},{2,0},{3,1},{4,6},{5,7},{6,4},{7,5},{8,10},{9,11},{10,... | collective-permute-start | bytes 393224 | tf_op jit(solution)/shard_map/ppermute | solution.py:452
  81.2 6.9 %collective-permute-start.4 = (f32[128,256]{1,0:T(8,128)S(1)}, f32[128,256]{1,0:T(8,128)S(1)}, u32[]{:S(2)}, u32[]{:S(2)}) collective-permute-start(f32[128,256]{1,0:T(8,128)S(1)} %get-tuple-element.44), channel_id=1, source_target_pairs={{0,3},{1,0},{2,1},{3,2},{4,7},{5,4},{6,5},{7,6},{8,11},{9,8},{10,9... | collective-permute-start | bytes 393224 | tf_op jit(solution)/shard_map/ppermute | solution.py:452
  98.5 68.6 %all-to-all-start.2 = ((f32[512,1,512]{2,1,0:T(1,128)}), f32[512,1,512]{2,1,0:T(1,128)S(1)}, u32[]{:S(2)}, u32[]{:S(2)}) async-start(f32[512,1,512]{2,1,0:T(1,128)} %bitcast.25), calls=%async_computation.2 | async-start | bytes 2097152 | tf_op jit(solution)/shard_map/all_to_all | solution.py:446
  113.9 0.7 copy-start.7
  114.6 13.1 %collective-permute-start.5 = (f32[512,128]{1,0:T(8,128)S(1)}, f32[512,128]{1,0:T(8,128)S(1)}, u32[]{:S(2)}, u32[]{:S(2)}) collective-permute-start(f32[512,128]{1,0:T(8,128)S(1)} %get-tuple-element.49), channel_id=1, source_target_pairs={{0,1},{1,2},{2,3},{3,0},{4,5},{5,6},{6,7},{7,4},{8,9},{9,10},{10,1... | collective-permute-start | bytes 786440 | tf_op jit(solution)/shard_map/ppermute | solution.py:452
  118.0 18.1 %collective-permute-start.6 = (f32[512,128]{1,0:T(8,128)S(1)}, f32[512,128]{1,0:T(8,128)S(1)}, u32[]{:S(2)}, u32[]{:S(2)}) collective-permute-start(f32[512,128]{1,0:T(8,128)S(1)} %get-tuple-element.50), channel_id=1, source_target_pairs={{0,2},{1,3},{2,0},{3,1},{4,6},{5,7},{6,4},{7,5},{8,10},{9,11},{10,... | collective-permute-start | bytes 786440 | tf_op jit(solution)/shard_map/ppermute | solution.py:452
  122.6 15.0 %collective-permute-start.7 = (f32[512,128]{1,0:T(8,128)S(1)}, f32[512,128]{1,0:T(8,128)S(1)}, u32[]{:S(2)}, u32[]{:S(2)}) collective-permute-start(f32[512,128]{1,0:T(8,128)S(1)} %get-tuple-element.51), channel_id=1, source_target_pairs={{0,3},{1,0},{2,1},{3,2},{4,7},{5,4},{6,5},{7,6},{8,11},{9,8},{10,9... | collective-permute-start | bytes 786440 | tf_op jit(solution)/shard_map/ppermute | solution.py:452
  127.7 9.9 %copy-start.10 = (f32[512,128]{1,0:T(8,128)}, f32[512,128]{1,0:T(8,128)S(1)}, u32[]{:S(2)}) copy-start(f32[512,128]{1,0:T(8,128)S(1)} %collective-permute-done.5.part1) | copy-start | bytes 786436
  136.2 1.5 copy-start.11
  137.6 0.7 copy-start.12
  167.0 15.2 %copy-start.1 = (f32[512,400]{0,1:T(8,128)S(1)}, f32[512,400]{0,1:T(8,128)}, u32[]{:S(2)}) copy-start(f32[512,400]{0,1:T(8,128)} %param.9) | copy-start | bytes 2457604
  167.0 15.2 %copy-start.9 = (f32[512]{0:T(512)S(1)}, f32[512]{0:T(512)}, u32[]{:S(2)}) copy-start(f32[512]{0:T(512)} %param.10) | copy-start | bytes 6148

commit v10 on v9

--- a/solution.py
+++ b/solution.py
@@ -214,7 +214,7 @@
 
 def pair_kernel(head_edge, tail_edge, rels, neg, out):
     n = 2 * LANE
-    out[0:n, :], out[n : 2 * n, :] = factors(rels[...], True)
+    out[0:n, :] = rels[...]
 
     def stack(ref, by_rows):
         if by_rows:
@@ -224,11 +224,11 @@
 
     for i, (one, other) in enumerate(((head_edge, tail_edge), (tail_edge, head_edge))):
         col, row = stack(one, False), stack(other, True)
-        out[2 * n : 3 * n, i * n : (i + 1) * n] = jnp.where(
+        out[n : 2 * n, i * n : (i + 1) * n] = jnp.where(
             (col == row) & (col >= 0.0), 1.0, 0.0
         )
-    out[3 * n :, 0:n] = neg[...]
-    out[3 * n :, n:] = jnp.zeros((LANE, n), f32)
+    out[2 * n :, 0:n] = neg[...]
+    out[2 * n :, n:] = jnp.zeros((LANE, n), f32)
 
 
 def rel_vectors(tile, slots, pieces):
@@ -302,13 +302,12 @@
     n = LANE
     slots = unpack(recv, n)
     query, tails = jnp.concatenate(slots[:2], 0), jnp.concatenate(slots[2:], 0)
-    met = pick(aids[4 * n : 6 * n, 0 : 2 * n].astype(bf16), parts(tails, PIECES), NN)
+    met = pick(aids[2 * n : 4 * n, 0 : 2 * n].astype(bf16), parts(tails, PIECES), NN)
     pos = jnp.sum(query * met, 1, keepdims=True)
     coef = -sigmoid(-pos)
-    met = coef * met
-    to_head = met * aids[0 : 2 * n, :] + turn(met) * aids[2 * n : 4 * n, :]
-    to_tail = pick(aids[4 * n : 6 * n, 2 * n :].astype(bf16), parts(coef * query, PIECES), NN)
-    neg = aids[6 * n :, 0 : 2 * n] + sum1[...] + (sum2[...] + sum3[...])
+    to_head = cmul(coef * met, aids[0 : 2 * n, :], True)
+    to_tail = pick(aids[2 * n : 4 * n, 2 * n :].astype(bf16), parts(coef * query, PIECES), NN)
+    neg = aids[4 * n :, 0 : 2 * n] + sum1[...] + (sum2[...] + sum3[...])
     at = lanes((n, LANE))
     for q in range(4):
         words = tile_of(neg, q // 2)
@@ -532,7 +531,7 @@
     sums = [shift(owned[j], j) for j in (1, 2, 3)]
     (aids,) = call(
         pair_kernel,
-        [((7 * n, 512), f32, True)],
+        [((5 * n, 512), f32, True)],
         (far(head_edge), far(tail_edge), far(edge_rels), near(owned[0])),
         name="pair",
     )

time: 187 us -> 185 us (0.989)
  no operation moved by 1% of the time
where the time goes in v10:
time: 185 us; the launch traced here: 182 us
  starting transfers between devices  63.7 us (34%)
  waiting for transfers between devices  63.3 us (34%)
  blocking collectives  27.3 us (15%)
  Pallas kernels  23.3 us (13%)
  local copies, waits for them, and re-layouts  3.58 us (2%)
    all_to_all x3, waiting for transfers between devices, exchange(): x = lax.all_to_all(x, axis, split_axis=0, concat_axis=0, tiled=True)  46.4 us
    all_to_all x3, starting transfers between devices, exchange(): x = lax.all_to_all(x, axis, split_axis=0, concat_axis=0, tiled=True)  38.5 us
    pallas_call x12, Pallas kernels, call(): pl.pallas_call(kernel, out_shape=[(pltpu.VMEM if near else pltpu.HBM)(sha...  23.3 us
    ppermute x6, starting transfers between devices, shift(): return lax.ppermute(x, 'rep', [(i, (i + by) % n) for i in range(n)])  21.2 us
    all_gather x1, blocking collectives, on_device(): grads = lax.all_gather(grads, 'rep', axis=0, tiled=True)  14.2 us
    ppermute x6, waiting for transfers between devices, shift(): return lax.ppermute(x, 'rep', [(i, (i + by) % n) for i in range(n)])  13.3 us
    all_gather x1, blocking collectives, on_device(): mine = lax.all_gather(own_negs, 'rep', axis=0, tiled=True)  13.1 us
    ppermute x2, starting transfers between devices, swap_cores(): lax.ppermute(x, 'ent', [(i, i ^ 1) for i in range(lax.axis_size('ent'))])  3.96 us
  transfers between devices with their start and end apart: 11, of which 9 were waited for; matrix products, arithmetic and copies ran while one was open for 0% of the time, Pallas kernels for 7%

profile of v10, /device:TPU:24, one launch (start us, length us, event | category | flops | bytes accessed | tf_op | source)
XLA Modules:
  0.0 182.0 jit_solution(17459887654055603156)
XLA Ops:
  0.6 2.6 %ask.1 = (f32[256,128]{1,0:T(8,128)}, f32[128,128]{1,0:T(8,128)}, f32[128,128]{1,0:T(8,128)}) custom-call(s32[1]{0:T(128)} %bitcast.rep, s32[4]{0:T(128)} %neg_rows.3, s32[1,128]{1,0:T(1,128)} %bitcast.29, s32[1,128]{1,0:T(1,128)} %bitcast.30, s32[1,128]{1,0:T(1,128)} %bitcast.31, s32[1,128]{1,0:T(1,128)} %bitcast.32, s32[1,128]{1,0:T(1,128)} %bitcast.33, ...), custom_call_target="tpu_custom_call" | custom-call | tf_op jit(solution)/shard_map/ask/pallas_call | solution.py:418
  3.2 19.3 %all-to-all-start = ((f32[128,1,256]{2,1,0:T(1,128)}), f32[128,1,256]{2,1,0:T(1,128)S(1)}, u32[]{:S(2)}, u32[]{:S(2)}) async-start(f32[128,1,256]{2,1,0:T(1,128)} %bitcast.28), calls=%async_computation | async-start | bytes 262144 | tf_op jit(solution)/shard_map/all_to_all | solution.py:445
  22.5 1.1 copy-done
  24.6 1.5 ahead.1
  26.9 11.8 %all-to-all-done = f32[128,1,256]{2,1,0:T(1,128)S(1)} async-done(((f32[128,1,256]{2,1,0:T(1,128)}), f32[128,1,256]{2,1,0:T(1,128)S(1)}, u32[]{:S(2)}, u32[]{:S(2)}) %all-to-all-start) | async-done | bytes 131104 | tf_op jit(solution)/shard_map/all_to_all | solution.py:445
  38.7 2.1 %fetch.1 = (f32[1664,128]{1,0:T(8,128)}, f32[512,512]{1,0:T(8,128)S(1)}, f32[256,128]{1,0:T(8,128)S(1)}) custom-call(f32[256,128]{1,0:T(8,128)S(1)} %bitcast.22, bf16[512,512]{1,0:T(8,128)(2,1)S(1)} %get-tuple-element.30.refs_0_, bf16[512,512]{1,0:T(8,128)(2,1)S(1)} %get-tuple-element.31.refs_1_, bf16[64,512]{1,0:T(8,128)(2,1)S(1)} %get-tuple-element.32.refs_2_.refs_0_, ...), custom_call_target="tpu_custom_call" | custom-call | tf_op jit(solution)/shard_map/fetch/pallas_call | solution.py:418
  40.9 7.0 %all-to-all-start.1 = ((f32[128,1,1664]{2,1,0:T(1,128)}), f32[128,1,1664]{2,1,0:T(1,128)S(1)}, u32[]{:S(2)}, u32[]{:S(2)}) async-start(f32[128,1,1664]{2,1,0:T(1,128)} %bitcast.27), calls=%async_computation.1 | async-start | bytes 1703936 | tf_op jit(solution)/shard_map/all_to_all | solution.py:445
  47.9 13.1 %all_gather.6.refs_2_.asks = f32[1024,128]{1,0:T(8,128)S(1)} all-gather(f32[256,128]{1,0:T(8,128)S(1)} %get-tuple-element.38), channel_id=1, replica_groups=mesh['ent'=128,'rep'=4] {'rep'}, dimensions={0}, use_global_device_ids=true | all-gather | bytes 655360 | tf_op jit(solution)/shard_map/all_gather | solution.py:515
  61.0 1.9 %collective-permute-start = (f32[1024,128]{1,0:T(8,128)S(1)}, f32[1024,128]{1,0:T(8,128)S(1)}, u32[]{:S(2)}, u32[]{:S(2)}) collective-permute-start(f32[1024,128]{1,0:T(8,128)S(1)} %all_gather.6.refs_2_.asks), channel_id=1, source_target_pairs={{0,4},{4,0},{8,12},{12,8},{16,20},{20,16},{24,28},{28,24},{32,36},... | collective-permute-start | bytes 1572872 | tf_op jit(solution)/shard_map/ppermute | solution.py:455
  62.9 1.9 %collective-permute-done.refs_3_ = f32[1024,128]{1,0:T(8,128)S(1)} collective-permute-done((f32[1024,128]{1,0:T(8,128)S(1)}, f32[1024,128]{1,0:T(8,128)S(1)}, u32[]{:S(2)}, u32[]{:S(2)}) %collective-permute-start) | collective-permute-done | bytes 524320 | tf_op jit(solution)/shard_map/ppermute | solution.py:455
  64.8 4.4 %negatives.1 = (f32[512,512]{1,0:T(8,128)S(1)}, f32[512,256]{1,0:T(8,128)S(1)}, f32[512,256]{1,0:T(8,128)S(1)}) custom-call(s32[1]{0:T(128)} %bitcast.11.odd, f32[256,128]{1,0:T(8,128)S(1)} %bitcast.23, f32[512,512]{1,0:T(8,128)S(1)} %get-tuple-element.37.rows, bf16[64,512]{1,0:T(8,128)(2,1)} %copy-done.4, bf16[64,512]{1,0:T(8,128)(2,1)} %copy-done.5, ...), custom_call_target="tpu_custom_call" | custom-call | tf_op jit(solution)/shard_map/negatives/pallas_call | solution.py:418
  69.3 2.0 %collective-permute-start.1 = (f32[512,256]{1,0:T(8,128)S(1)}, f32[512,256]{1,0:T(8,128)S(1)}, u32[]{:S(2)}, u32[]{:S(2)}) collective-permute-start(f32[512,256]{1,0:T(8,128)S(1)} %get-tuple-element.40), channel_id=1, source_target_pairs={{0,4},{4,0},{8,12},{12,8},{16,20},{20,16},{24,28},{28,24},{32,36},... | collective-permute-start | bytes 1572872 | tf_op jit(solution)/shard_map/ppermute | solution.py:455
  71.3 1.7 collective-permute-done.1.got
  73.1 3.3 %collective-permute-start.2 = (f32[128,256]{1,0:T(8,128)S(1)}, f32[128,256]{1,0:T(8,128)S(1)}, u32[]{:S(2)}, u32[]{:S(2)}) collective-permute-start(f32[128,256]{1,0:T(8,128)S(1)} %get-tuple-element.42), channel_id=1, source_target_pairs={{0,1},{1,2},{2,3},{3,0},{4,5},{5,6},{6,7},{7,4},{8,9},{9,10},{10,1... | collective-permute-start | bytes 393224 | tf_op jit(solution)/shard_map/ppermute | solution.py:451
  76.5 4.6 %collective-permute-start.3 = (f32[128,256]{1,0:T(8,128)S(1)}, f32[128,256]{1,0:T(8,128)S(1)}, u32[]{:S(2)}, u32[]{:S(2)}) collective-permute-start(f32[128,256]{1,0:T(8,128)S(1)} %get-tuple-element.43), channel_id=1, source_target_pairs={{0,2},{1,3},{2,0},{3,1},{4,6},{5,7},{6,4},{7,5},{8,10},{9,11},{10,... | collective-permute-start | bytes 393224 | tf_op jit(solution)/shard_map/ppermute | solution.py:451
  81.0 1.9 %collective-permute-start.4 = (f32[128,256]{1,0:T(8,128)S(1)}, f32[128,256]{1,0:T(8,128)S(1)}, u32[]{:S(2)}, u32[]{:S(2)}) collective-permute-start(f32[128,256]{1,0:T(8,128)S(1)} %get-tuple-element.44), channel_id=1, source_target_pairs={{0,3},{1,0},{2,1},{3,2},{4,7},{5,4},{6,5},{7,6},{8,11},{9,8},{10,9... | collective-permute-start | bytes 393224 | tf_op jit(solution)/shard_map/ppermute | solution.py:451
  83.0 1.5 pair.1.aids
  85.4 2.5 %collective-permute-done.4.sum3 = f32[128,256]{1,0:T(8,128)S(1)} collective-permute-done((f32[128,256]{1,0:T(8,128)S(1)}, f32[128,256]{1,0:T(8,128)S(1)}, u32[]{:S(2)}, u32[]{:S(2)}) %collective-permute-start.4) | collective-permute-done | bytes 131104 | tf_op jit(solution)/shard_map/ppermute | solution.py:451
  87.9 6.5 %all-to-all-done.1 = f32[128,1,1664]{2,1,0:T(1,128)S(1)} async-done(((f32[128,1,1664]{2,1,0:T(1,128)}), f32[128,1,1664]{2,1,0:T(1,128)S(1)}, u32[]{:S(2)}, u32[]{:S(2)}) %all-to-all-start.1) | async-done | bytes 852000 | tf_op jit(solution)/shard_map/all_to_all | solution.py:445
  94.4 3.0 %edge.1 = (f32[2048,128]{1,0:T(8,128)}, f32[8,128]{1,0:T(8,128)}) custom-call(f32[1664,128]{1,0:T(8,128)S(1)} %bitcast.21, f32[640,512]{1,0:T(8,128)S(1)} %pair.1.aids, f32[128,256]{1,0:T(8,128)S(1)} %collective-permute-done.2.sum1, f32[128,256]{1,0:T(8,128)S(1)} %collective-permute-done.3.sum2, f32[128,256]{1,0:T(8,128)S(1)} %collective-permute-done.4.sum3), custom_call_target="tpu_custom_call" | custom-call | tf_op jit(solution)/shard_map/edge/pallas_call | solution.py:418
  97.4 12.2 %all-to-all-start.2 = ((f32[512,1,512]{2,1,0:T(1,128)}), f32[512,1,512]{2,1,0:T(1,128)S(1)}, u32[]{:S(2)}, u32[]{:S(2)}) async-start(f32[512,1,512]{2,1,0:T(1,128)} %bitcast.26), calls=%async_computation.2 | async-start | bytes 2097152 | tf_op jit(solution)/shard_map/all_to_all | solution.py:445
  109.7 2.9 %local.1 = (f32[512,128]{1,0:T(8,128)S(1)}, f32[512,128]{1,0:T(8,128)S(1)}, f32[512,128]{1,0:T(8,128)S(1)}, f32[512,128]{1,0:T(8,128)S(1)}) custom-call(s32[1]{0:T(128)} %bitcast.rep, f32[8,128]{1,0:T(8,128)} %get-tuple-element.46.token, f32[256,128]{1,0:T(8,128)S(1)} %bitcast.24, f32[512,512]{1,0:T(8,128)} %copy-done.3, bf16[64,512]{1,0:T(8,128)(2,1)} %copy-done.4, ...), custom_call_target="tpu_custom_call" | custom-call | tf_op jit(solution)/shard_map/local/pallas_call | solution.py:418
  112.6 3.4 %collective-permute-start.5 = (f32[512,128]{1,0:T(8,128)S(1)}, f32[512,128]{1,0:T(8,128)S(1)}, u32[]{:S(2)}, u32[]{:S(2)}) collective-permute-start(f32[512,128]{1,0:T(8,128)S(1)} %get-tuple-element.49), channel_id=1, source_target_pairs={{0,1},{1,2},{2,3},{3,0},{4,5},{5,6},{6,7},{7,4},{8,9},{9,10},{10,1... | collective-permute-start | bytes 786440 | tf_op jit(solution)/shard_map/ppermute | solution.py:451
  116.0 4.6 %collective-permute-start.6 = (f32[512,128]{1,0:T(8,128)S(1)}, f32[512,128]{1,0:T(8,128)S(1)}, u32[]{:S(2)}, u32[]{:S(2)}) collective-permute-start(f32[512,128]{1,0:T(8,128)S(1)} %get-tuple-element.50), channel_id=1, source_target_pairs={{0,2},{1,3},{2,0},{3,1},{4,6},{5,7},{6,4},{7,5},{8,10},{9,11},{10,... | collective-permute-start | bytes 786440 | tf_op jit(solution)/shard_map/ppermute | solution.py:451
  120.6 3.4 %collective-permute-start.7 = (f32[512,128]{1,0:T(8,128)S(1)}, f32[512,128]{1,0:T(8,128)S(1)}, u32[]{:S(2)}, u32[]{:S(2)}) collective-permute-start(f32[512,128]{1,0:T(8,128)S(1)} %get-tuple-element.51), channel_id=1, source_target_pairs={{0,3},{1,0},{2,1},{3,2},{4,7},{5,4},{6,5},{7,6},{8,11},{9,8},{10,9... | collective-permute-start | bytes 786440 | tf_op jit(solution)/shard_map/ppermute | solution.py:451
  124.0 1.7 place.1.hot
  125.8 8.3 %collective-permute-done.6.part2 = f32[512,128]{1,0:T(8,128)S(1)} collective-permute-done((f32[512,128]{1,0:T(8,128)S(1)}, f32[512,128]{1,0:T(8,128)S(1)}, u32[]{:S(2)}, u32[]{:S(2)}) %collective-permute-start.6) | collective-permute-done | bytes 262176 | tf_op jit(solution)/shard_map/ppermute | solution.py:451
  134.1 1.5 collective-permute-done.7.part3
  136.3 1.2 gather_local.1.local
  137.6 28.1 %all-to-all-done.2 = f32[512,1,512]{2,1,0:T(1,128)S(1)} async-done(((f32[512,1,512]{2,1,0:T(1,128)}), f32[512,1,512]{2,1,0:T(1,128)S(1)}, u32[]{:S(2)}, u32[]{:S(2)}) %all-to-all-start.2) | async-done | bytes 1048608 | tf_op jit(solution)/shard_map/all_to_all | solution.py:445
  166.7 14.2 %all_gather.7.grads = f32[448,512]{1,0:T(8,128)S(1)} all-gather(f32[112,512]{1,0:T(8,128)S(1)} %scatter.1), channel_id=1, replica_groups=mesh['ent'=128,'rep'=4] {'rep'}, dimensions={0}, use_global_device_ids=true | all-gather | bytes 1146880 | tf_op jit(solution)/shard_map/all_gather | solution.py:569
  180.9 1.1 finish.1
  (30 shorter events, 4.5 us)
Async XLA Ops:
  3.2 35.5 %all-to-all-start = ((f32[128,1,256]{2,1,0:T(1,128)}), f32[128,1,256]{2,1,0:T(1,128)S(1)}, u32[]{:S(2)}, u32[]{:S(2)}) async-start(f32[128,1,256]{2,1,0:T(1,128)} %bitcast.28), calls=%async_computation | async-start | bytes 262144 | tf_op jit(solution)/shard_map/all_to_all | solution.py:445
  22.5 1.1 copy-start
  23.7 0.9 copy-start.8
  26.1 0.8 copy-start.6
  26.9 37.9 %copy-start.4 = (bf16[64,512]{1,0:T(8,128)(2,1)}, bf16[64,512]{1,0:T(8,128)(2,1)S(1)}, u32[]{:S(2)}) copy-start(bf16[64,512]{1,0:T(8,128)(2,1)S(1)} %get-tuple-element.32.refs_2_.refs_0_) | copy-start | bytes 196612
  26.9 37.9 %copy-start.5 = (bf16[64,512]{1,0:T(8,128)(2,1)}, bf16[64,512]{1,0:T(8,128)(2,1)S(1)}, u32[]{:S(2)}) copy-start(bf16[64,512]{1,0:T(8,128)(2,1)S(1)} %get-tuple-element.33.refs_3_.refs_1_) | copy-start | bytes 196612
  40.9 53.5 %all-to-all-start.1 = ((f32[128,1,1664]{2,1,0:T(1,128)}), f32[128,1,1664]{2,1,0:T(1,128)S(1)}, u32[]{:S(2)}, u32[]{:S(2)}) async-start(f32[128,1,1664]{2,1,0:T(1,128)} %bitcast.27), calls=%async_computation.1 | async-start | bytes 1703936 | tf_op jit(solution)/shard_map/all_to_all | solution.py:445
  61.0 23.5 %copy-start.2 = (f32[1024,128]{1,0:T(8,128)}, f32[1024,128]{1,0:T(8,128)S(1)}, u32[]{:S(2)}) copy-start(f32[1024,128]{1,0:T(8,128)S(1)} %all_gather.6.refs_2_.asks) | copy-start | bytes 1572868
  61.0 3.8 %collective-permute-start = (f32[1024,128]{1,0:T(8,128)S(1)}, f32[1024,128]{1,0:T(8,128)S(1)}, u32[]{:S(2)}, u32[]{:S(2)}) collective-permute-start(f32[1024,128]{1,0:T(8,128)S(1)} %all_gather.6.refs_2_.asks), channel_id=1, source_target_pairs={{0,4},{4,0},{8,12},{12,8},{16,20},{20,16},{24,28},{28,24},{32,36},... | collective-permute-start | bytes 1572872 | tf_op jit(solution)/shard_map/ppermute | solution.py:455
  69.2 16.2 %copy-start.3 = (f32[512,512]{1,0:T(8,128)}, f32[512,512]{1,0:T(8,128)S(1)}, u32[]{:S(2)}) copy-start(f32[512,512]{1,0:T(8,128)S(1)} %get-tuple-element.47.back) | copy-start | bytes 3145732
  69.3 3.8 %collective-permute-start.1 = (f32[512,256]{1,0:T(8,128)S(1)}, f32[512,256]{1,0:T(8,128)S(1)}, u32[]{:S(2)}, u32[]{:S(2)}) collective-permute-start(f32[512,256]{1,0:T(8,128)S(1)} %get-tuple-element.40), channel_id=1, source_target_pairs={{0,4},{4,0},{8,12},{12,8},{16,20},{20,16},{24,28},{28,24},{32,36},... | collective-permute-start | bytes 1572872 | tf_op jit(solution)/shard_map/ppermute | solution.py:455
  73.1 11.4 %collective-permute-start.2 = (f32[128,256]{1,0:T(8,128)S(1)}, f32[128,256]{1,0:T(8,128)S(1)}, u32[]{:S(2)}, u32[]{:S(2)}) collective-permute-start(f32[128,256]{1,0:T(8,128)S(1)} %get-tuple-element.42), channel_id=1, source_target_pairs={{0,1},{1,2},{2,3},{3,0},{4,5},{5,6},{6,7},{7,4},{8,9},{9,10},{10,1... | collective-permute-start | bytes 393224 | tf_op jit(solution)/shard_map/ppermute | solution.py:451
  76.5 9.0 %collective-permute-start.3 = (f32[128,256]{1,0:T(8,128)S(1)}, f32[128,256]{1,0:T(8,128)S(1)}, u32[]{:S(2)}, u32[]{:S(2)}) collective-permute-start(f32[128,256]{1,0:T(8,128)S(1)} %get-tuple-element.43), channel_id=1, source_target_pairs={{0,2},{1,3},{2,0},{3,1},{4,6},{5,7},{6,4},{7,5},{8,10},{9,11},{10,... | collective-permute-start | bytes 393224 | tf_op jit(solution)/shard_map/ppermute | solution.py:451
  81.0 6.9 %collective-permute-start.4 = (f32[128,256]{1,0:T(8,128)S(1)}, f32[128,256]{1,0:T(8,128)S(1)}, u32[]{:S(2)}, u32[]{:S(2)}) collective-permute-start(f32[128,256]{1,0:T(8,128)S(1)} %get-tuple-element.44), channel_id=1, source_target_pairs={{0,3},{1,0},{2,1},{3,2},{4,7},{5,4},{6,5},{7,6},{8,11},{9,8},{10,9... | collective-permute-start | bytes 393224 | tf_op jit(solution)/shard_map/ppermute | solution.py:451
  97.4 68.3 %all-to-all-start.2 = ((f32[512,1,512]{2,1,0:T(1,128)}), f32[512,1,512]{2,1,0:T(1,128)S(1)}, u32[]{:S(2)}, u32[]{:S(2)}) async-start(f32[512,1,512]{2,1,0:T(1,128)} %bitcast.26), calls=%async_computation.2 | async-start | bytes 2097152 | tf_op jit(solution)/shard_map/all_to_all | solution.py:445
  112.6 23.0 %copy-start.7 = (f32[512,128]{1,0:T(8,128)}, f32[512,128]{1,0:T(8,128)S(1)}, u32[]{:S(2)}) copy-start(f32[512,128]{1,0:T(8,128)S(1)} %get-tuple-element.48.part0) | copy-start | bytes 786436
  112.6 13.2 %collective-permute-start.5 = (f32[512,128]{1,0:T(8,128)S(1)}, f32[512,128]{1,0:T(8,128)S(1)}, u32[]{:S(2)}, u32[]{:S(2)}) collective-permute-start(f32[512,128]{1,0:T(8,128)S(1)} %get-tuple-element.49), channel_id=1, source_target_pairs={{0,1},{1,2},{2,3},{3,0},{4,5},{5,6},{6,7},{7,4},{8,9},{9,10},{10,1... | collective-permute-start | bytes 786440 | tf_op jit(solution)/shard_map/ppermute | solution.py:451
  116.0 18.1 %collective-permute-start.6 = (f32[512,128]{1,0:T(8,128)S(1)}, f32[512,128]{1,0:T(8,128)S(1)}, u32[]{:S(2)}, u32[]{:S(2)}) collective-permute-start(f32[512,128]{1,0:T(8,128)S(1)} %get-tuple-element.50), channel_id=1, source_target_pairs={{0,2},{1,3},{2,0},{3,1},{4,6},{5,7},{6,4},{7,5},{8,10},{9,11},{10,... | collective-permute-start | bytes 786440 | tf_op jit(solution)/shard_map/ppermute | solution.py:451
  120.6 15.0 %collective-permute-start.7 = (f32[512,128]{1,0:T(8,128)S(1)}, f32[512,128]{1,0:T(8,128)S(1)}, u32[]{:S(2)}, u32[]{:S(2)}) collective-permute-start(f32[512,128]{1,0:T(8,128)S(1)} %get-tuple-element.51), channel_id=1, source_target_pairs={{0,3},{1,0},{2,1},{3,2},{4,7},{5,4},{6,5},{7,6},{8,11},{9,8},{10,9... | collective-permute-start | bytes 786440 | tf_op jit(solution)/shard_map/ppermute | solution.py:451
  125.8 9.9 %copy-start.10 = (f32[512,128]{1,0:T(8,128)}, f32[512,128]{1,0:T(8,128)S(1)}, u32[]{:S(2)}) copy-start(f32[512,128]{1,0:T(8,128)S(1)} %collective-permute-done.5.part1) | copy-start | bytes 786436
  134.1 1.5 copy-start.11
  135.6 0.7 copy-start.12
  165.7 15.2 %copy-start.1 = (f32[512,400]{0,1:T(8,128)S(1)}, f32[512,400]{0,1:T(8,128)}, u32[]{:S(2)}) copy-start(f32[512,400]{0,1:T(8,128)} %param.9) | copy-start | bytes 2457604
  165.7 15.2 %copy-start.9 = (f32[512]{0:T(512)S(1)}, f32[512]{0:T(512)}, u32[]{:S(2)}) copy-start(f32[512]{0:T(512)} %param.10) | copy-start | bytes 6148

commit v11 on v10

--- a/solution.py
+++ b/solution.py
@@ -340,7 +340,9 @@
     grad = jnp.concatenate([head, tail], 0)
     total = pick(hot, parts(grad, PIECES), NN)
     for q in range(4):
-        quarters[q] = tile_of(total, q)
+        turned = tile_of(total, q).T
+        quarters[q, 0:56, :] = turned[0:56, :]
+        quarters[q, 56:112, :] = turned[64:120, :]
     for i, ref in enumerate((out0, out1, out2, out3)):
         ref[...] = quarters[(rep[0] + i) % 4]
 
@@ -393,9 +395,9 @@
     blocks += [neg, jnp.zeros((n - 8, n), f32)]
     both = jnp.concatenate(parts(jnp.concatenate(blocks, 0), 2), 1)
     total = dot(hot[...], both, NN)
-    turned = (total[:, :n] + total[:, n:] + local[...]).T
-    out[0:56, :] = turned[0:56, :]
-    out[56:112, :] = turned[64:120, :]
+    turned = (total[:, :n] + total[:, n:]).T
+    out[0:56, :] = turned[0:56, :] + local[0:56, :]
+    out[56:112, :] = turned[64:120, :] + local[56:112, :]
 
 
 def finish_kernel(grads, table_t, state, table_new, state_new):
@@ -545,15 +547,15 @@
     token = far(token)
     local = call(
         local_kernel,
-        [((4 * n, n), f32, True)] * 4,
+        [((112, 512), f32, True)] * 4,
         (token, recv1, far(back), *map(far, rel_pieces)),
         (rep,),
         "local",
-        (pltpu.VMEM((4, 4 * n, n), f32),),
+        (pltpu.VMEM((4, 112, 512), f32),),
     )
     (local,) = call(
         gather_local_kernel,
-        [((4 * n, n), f32, True)],
+        [((112, 512), f32, True)],
         [far(local[0])] + [far(shift(local[j], j)) for j in (1, 2, 3)],
         name="gather_local",
     )

time: 185 us -> 185 us (level)
    ppermute x6, waiting for transfers between devices: 13.3 us -> 11.2 us  [shift(): return lax.ppermute(x, 'rep', [(i, (i + by) % n) for i in range(n)])]
  transfers between devices with their start and end apart: 11 -> 11, of which waited for: 9 -> 9; matrix products, arithmetic and copies ran while one was open for 0% -> 0% of each run, Pallas kernels for 7% -> 8%
where the time goes in v11:
time: 185 us; the launch traced here: 182 us
  starting transfers between devices  63.7 us (34%)
  waiting for transfers between devices  62.9 us (34%)
  blocking collectives  27.3 us (15%)
  Pallas kernels  23.6 us (13%)
  local copies, waits for them, and re-layouts  3.58 us (2%)
    all_to_all x3, waiting for transfers between devices, exchange(): x = lax.all_to_all(x, axis, split_axis=0, concat_axis=0, tiled=True)  48.1 us
    all_to_all x3, starting transfers between devices, exchange(): x = lax.all_to_all(x, axis, split_axis=0, concat_axis=0, tiled=True)  38.5 us
    pallas_call x12, Pallas kernels, call(): pl.pallas_call(kernel, out_shape=[(pltpu.VMEM if near else pltpu.HBM)(sha...  23.6 us
    ppermute x6, starting transfers between devices, shift(): return lax.ppermute(x, 'rep', [(i, (i + by) % n) for i in range(n)])  21.2 us
    all_gather x1, blocking collectives, on_device(): grads = lax.all_gather(grads, 'rep', axis=0, tiled=True)  14.2 us
    all_gather x1, blocking collectives, on_device(): mine = lax.all_gather(own_negs, 'rep', axis=0, tiled=True)  13.1 us
    ppermute x6, waiting for transfers between devices, shift(): return lax.ppermute(x, 'rep', [(i, (i + by) % n) for i in range(n)])  11.2 us
    ppermute x2, starting transfers between devices, swap_cores(): lax.ppermute(x, 'ent', [(i, i ^ 1) for i in range(lax.axis_size('ent'))])  3.96 us
  transfers between devices with their start and end apart: 11, of which 9 were waited for; matrix products, arithmetic and copies ran while one was open for 0% of the time, Pallas kernels for 8%

profile of v11, /device:TPU:24, one launch (start us, length us, event | category | flops | bytes accessed | tf_op | source)
XLA Modules:
  0.0 182.0 jit_solution(7272309088858589107)
XLA Ops:
  0.6 2.6 %ask.1 = (f32[256,128]{1,0:T(8,128)}, f32[128,128]{1,0:T(8,128)}, f32[128,128]{1,0:T(8,128)}) custom-call(s32[1]{0:T(128)} %bitcast.rep, s32[4]{0:T(128)} %neg_rows.3, s32[1,128]{1,0:T(1,128)} %bitcast.29, s32[1,128]{1,0:T(1,128)} %bitcast.30, s32[1,128]{1,0:T(1,128)} %bitcast.31, s32[1,128]{1,0:T(1,128)} %bitcast.32, s32[1,128]{1,0:T(1,128)} %bitcast.33, ...), custom_call_target="tpu_custom_call" | custom-call | tf_op jit(solution)/shard_map/ask/pallas_call | solution.py:420
  3.2 19.3 %all-to-all-start = ((f32[128,1,256]{2,1,0:T(1,128)}), f32[128,1,256]{2,1,0:T(1,128)S(1)}, u32[]{:S(2)}, u32[]{:S(2)}) async-start(f32[128,1,256]{2,1,0:T(1,128)} %bitcast.28), calls=%async_computation | async-start | bytes 262144 | tf_op jit(solution)/shard_map/all_to_all | solution.py:447
  22.5 1.1 copy-done
  24.6 1.5 ahead.1
  26.9 11.8 %all-to-all-done = f32[128,1,256]{2,1,0:T(1,128)S(1)} async-done(((f32[128,1,256]{2,1,0:T(1,128)}), f32[128,1,256]{2,1,0:T(1,128)S(1)}, u32[]{:S(2)}, u32[]{:S(2)}) %all-to-all-start) | async-done | bytes 131104 | tf_op jit(solution)/shard_map/all_to_all | solution.py:447
  38.7 2.1 %fetch.1 = (f32[1664,128]{1,0:T(8,128)}, f32[512,512]{1,0:T(8,128)S(1)}, f32[256,128]{1,0:T(8,128)S(1)}) custom-call(f32[256,128]{1,0:T(8,128)S(1)} %bitcast.22, bf16[512,512]{1,0:T(8,128)(2,1)S(1)} %get-tuple-element.30.refs_0_, bf16[512,512]{1,0:T(8,128)(2,1)S(1)} %get-tuple-element.31.refs_1_, bf16[64,512]{1,0:T(8,128)(2,1)S(1)} %get-tuple-element.32.refs_2_.refs_0_, ...), custom_call_target="tpu_custom_call" | custom-call | tf_op jit(solution)/shard_map/fetch/pallas_call | solution.py:420
  40.9 7.0 %all-to-all-start.1 = ((f32[128,1,1664]{2,1,0:T(1,128)}), f32[128,1,1664]{2,1,0:T(1,128)S(1)}, u32[]{:S(2)}, u32[]{:S(2)}) async-start(f32[128,1,1664]{2,1,0:T(1,128)} %bitcast.27), calls=%async_computation.1 | async-start | bytes 1703936 | tf_op jit(solution)/shard_map/all_to_all | solution.py:447
  47.9 13.1 %all_gather.6.refs_2_.asks = f32[1024,128]{1,0:T(8,128)S(1)} all-gather(f32[256,128]{1,0:T(8,128)S(1)} %get-tuple-element.38), channel_id=1, replica_groups=mesh['ent'=128,'rep'=4] {'rep'}, dimensions={0}, use_global_device_ids=true | all-gather | bytes 655360 | tf_op jit(solution)/shard_map/all_gather | solution.py:517
  61.0 1.9 %collective-permute-start = (f32[1024,128]{1,0:T(8,128)S(1)}, f32[1024,128]{1,0:T(8,128)S(1)}, u32[]{:S(2)}, u32[]{:S(2)}) collective-permute-start(f32[1024,128]{1,0:T(8,128)S(1)} %all_gather.6.refs_2_.asks), channel_id=1, source_target_pairs={{0,4},{4,0},{8,12},{12,8},{16,20},{20,16},{24,28},{28,24},{32,36},... | collective-permute-start | bytes 1572872 | tf_op jit(solution)/shard_map/ppermute | solution.py:457
  62.9 1.9 %collective-permute-done.refs_3_ = f32[1024,128]{1,0:T(8,128)S(1)} collective-permute-done((f32[1024,128]{1,0:T(8,128)S(1)}, f32[1024,128]{1,0:T(8,128)S(1)}, u32[]{:S(2)}, u32[]{:S(2)}) %collective-permute-start) | collective-permute-done | bytes 524320 | tf_op jit(solution)/shard_map/ppermute | solution.py:457
  64.8 4.4 %negatives.1 = (f32[512,512]{1,0:T(8,128)S(1)}, f32[512,256]{1,0:T(8,128)S(1)}, f32[512,256]{1,0:T(8,128)S(1)}) custom-call(s32[1]{0:T(128)} %bitcast.11.odd, f32[256,128]{1,0:T(8,128)S(1)} %bitcast.23, f32[512,512]{1,0:T(8,128)S(1)} %get-tuple-element.37.rows, bf16[64,512]{1,0:T(8,128)(2,1)} %copy-done.4, bf16[64,512]{1,0:T(8,128)(2,1)} %copy-done.5, ...), custom_call_target="tpu_custom_call" | custom-call | tf_op jit(solution)/shard_map/negatives/pallas_call | solution.py:420
  69.3 2.0 %collective-permute-start.1 = (f32[512,256]{1,0:T(8,128)S(1)}, f32[512,256]{1,0:T(8,128)S(1)}, u32[]{:S(2)}, u32[]{:S(2)}) collective-permute-start(f32[512,256]{1,0:T(8,128)S(1)} %get-tuple-element.40), channel_id=1, source_target_pairs={{0,4},{4,0},{8,12},{12,8},{16,20},{20,16},{24,28},{28,24},{32,36},... | collective-permute-start | bytes 1572872 | tf_op jit(solution)/shard_map/ppermute | solution.py:457
  71.3 1.7 collective-permute-done.1.got
  73.1 3.3 %collective-permute-start.2 = (f32[128,256]{1,0:T(8,128)S(1)}, f32[128,256]{1,0:T(8,128)S(1)}, u32[]{:S(2)}, u32[]{:S(2)}) collective-permute-start(f32[128,256]{1,0:T(8,128)S(1)} %get-tuple-element.42), channel_id=1, source_target_pairs={{0,1},{1,2},{2,3},{3,0},{4,5},{5,6},{6,7},{7,4},{8,9},{9,10},{10,1... | collective-permute-start | bytes 393224 | tf_op jit(solution)/shard_map/ppermute | solution.py:453
  76.5 4.6 %collective-permute-start.3 = (f32[128,256]{1,0:T(8,128)S(1)}, f32[128,256]{1,0:T(8,128)S(1)}, u32[]{:S(2)}, u32[]{:S(2)}) collective-permute-start(f32[128,256]{1,0:T(8,128)S(1)} %get-tuple-element.43), channel_id=1, source_target_pairs={{0,2},{1,3},{2,0},{3,1},{4,6},{5,7},{6,4},{7,5},{8,10},{9,11},{10,... | collective-permute-start | bytes 393224 | tf_op jit(solution)/shard_map/ppermute | solution.py:453
  81.0 1.9 %collective-permute-start.4 = (f32[128,256]{1,0:T(8,128)S(1)}, f32[128,256]{1,0:T(8,128)S(1)}, u32[]{:S(2)}, u32[]{:S(2)}) collective-permute-start(f32[128,256]{1,0:T(8,128)S(1)} %get-tuple-element.44), channel_id=1, source_target_pairs={{0,3},{1,0},{2,1},{3,2},{4,7},{5,4},{6,5},{7,6},{8,11},{9,8},{10,9... | collective-permute-start | bytes 393224 | tf_op jit(solution)/shard_map/ppermute | solution.py:453
  83.0 1.5 pair.1.aids
  85.4 2.5 %collective-permute-done.4.sum3 = f32[128,256]{1,0:T(8,128)S(1)} collective-permute-done((f32[128,256]{1,0:T(8,128)S(1)}, f32[128,256]{1,0:T(8,128)S(1)}, u32[]{:S(2)}, u32[]{:S(2)}) %collective-permute-start.4) | collective-permute-done | bytes 131104 | tf_op jit(solution)/shard_map/ppermute | solution.py:453
  87.9 6.5 %all-to-all-done.1 = f32[128,1,1664]{2,1,0:T(1,128)S(1)} async-done(((f32[128,1,1664]{2,1,0:T(1,128)}), f32[128,1,1664]{2,1,0:T(1,128)S(1)}, u32[]{:S(2)}, u32[]{:S(2)}) %all-to-all-start.1) | async-done | bytes 852000 | tf_op jit(solution)/shard_map/all_to_all | solution.py:447
  94.4 3.0 %edge.1 = (f32[2048,128]{1,0:T(8,128)}, f32[8,128]{1,0:T(8,128)}) custom-call(f32[1664,128]{1,0:T(8,128)S(1)} %bitcast.21, f32[640,512]{1,0:T(8,128)S(1)} %pair.1.aids, f32[128,256]{1,0:T(8,128)S(1)} %collective-permute-done.2.sum1, f32[128,256]{1,0:T(8,128)S(1)} %collective-permute-done.3.sum2, f32[128,256]{1,0:T(8,128)S(1)} %collective-permute-done.4.sum3), custom_call_target="tpu_custom_call" | custom-call | tf_op jit(solution)/shard_map/edge/pallas_call | solution.py:420
  97.4 12.2 %all-to-all-start.2 = ((f32[512,1,512]{2,1,0:T(1,128)}), f32[512,1,512]{2,1,0:T(1,128)S(1)}, u32[]{:S(2)}, u32[]{:S(2)}) async-start(f32[512,1,512]{2,1,0:T(1,128)} %bitcast.26), calls=%async_computation.2 | async-start | bytes 2097152 | tf_op jit(solution)/shard_map/all_to_all | solution.py:447
  109.7 3.2 %local.1 = (f32[112,512]{1,0:T(8,128)S(1)}, f32[112,512]{1,0:T(8,128)S(1)}, f32[112,512]{1,0:T(8,128)S(1)}, f32[112,512]{1,0:T(8,128)S(1)}) custom-call(s32[1]{0:T(128)} %bitcast.rep, f32[8,128]{1,0:T(8,128)} %get-tuple-element.46.token, f32[256,128]{1,0:T(8,128)S(1)} %bitcast.24, f32[512,512]{1,0:T(8,128)} %copy-done.3, bf16[64,512]{1,0:T(8,128)(2,1)} %copy-done.4, ...), custom_call_target="tpu_custom_call" | custom-call | tf_op jit(solution)/shard_map/local/pallas_call | solution.py:420
  112.9 3.4 %collective-permute-start.5 = (f32[112,512]{1,0:T(8,128)S(1)}, f32[112,512]{1,0:T(8,128)S(1)}, u32[]{:S(2)}, u32[]{:S(2)}) collective-permute-start(f32[112,512]{1,0:T(8,128)S(1)} %get-tuple-element.49), channel_id=1, source_target_pairs={{0,1},{1,2},{2,3},{3,0},{4,5},{5,6},{6,7},{7,4},{8,9},{9,10},{10,1... | collective-permute-start | bytes 688136 | tf_op jit(solution)/shard_map/ppermute | solution.py:453
  116.3 4.6 %collective-permute-start.6 = (f32[112,512]{1,0:T(8,128)S(1)}, f32[112,512]{1,0:T(8,128)S(1)}, u32[]{:S(2)}, u32[]{:S(2)}) collective-permute-start(f32[112,512]{1,0:T(8,128)S(1)} %get-tuple-element.50), channel_id=1, source_target_pairs={{0,2},{1,3},{2,0},{3,1},{4,6},{5,7},{6,4},{7,5},{8,10},{9,11},{10,... | collective-permute-start | bytes 688136 | tf_op jit(solution)/shard_map/ppermute | solution.py:453
  120.9 3.4 %collective-permute-start.7 = (f32[112,512]{1,0:T(8,128)S(1)}, f32[112,512]{1,0:T(8,128)S(1)}, u32[]{:S(2)}, u32[]{:S(2)}) collective-permute-start(f32[112,512]{1,0:T(8,128)S(1)} %get-tuple-element.51), channel_id=1, source_target_pairs={{0,3},{1,0},{2,1},{3,2},{4,7},{5,4},{6,5},{7,6},{8,11},{9,8},{10,9... | collective-permute-start | bytes 688136 | tf_op jit(solution)/shard_map/ppermute | solution.py:453
  124.2 1.7 place.1.hot
  126.0 6.6 %collective-permute-done.6.part2 = f32[112,512]{1,0:T(8,128)S(1)} collective-permute-done((f32[112,512]{1,0:T(8,128)S(1)}, f32[112,512]{1,0:T(8,128)S(1)}, u32[]{:S(2)}, u32[]{:S(2)}) %collective-permute-start.6) | collective-permute-done | bytes 229408 | tf_op jit(solution)/shard_map/ppermute | solution.py:453
  132.6 1.2 collective-permute-done.7.part3
  134.6 1.3 gather_local.1.local
  135.9 29.8 %all-to-all-done.2 = f32[512,1,512]{2,1,0:T(1,128)S(1)} async-done(((f32[512,1,512]{2,1,0:T(1,128)}), f32[512,1,512]{2,1,0:T(1,128)S(1)}, u32[]{:S(2)}, u32[]{:S(2)}) %all-to-all-start.2) | async-done | bytes 1048608 | tf_op jit(solution)/shard_map/all_to_all | solution.py:447
  166.7 14.2 %all_gather.7.grads = f32[448,512]{1,0:T(8,128)S(1)} all-gather(f32[112,512]{1,0:T(8,128)S(1)} %scatter.1), channel_id=1, replica_groups=mesh['ent'=128,'rep'=4] {'rep'}, dimensions={0}, use_global_device_ids=true | all-gather | bytes 1146880 | tf_op jit(solution)/shard_map/all_gather | solution.py:571
  180.9 1.1 finish.1
  (30 shorter events, 4.4 us)
Async XLA Ops:
  3.2 35.5 %all-to-all-start = ((f32[128,1,256]{2,1,0:T(1,128)}), f32[128,1,256]{2,1,0:T(1,128)S(1)}, u32[]{:S(2)}, u32[]{:S(2)}) async-start(f32[128,1,256]{2,1,0:T(1,128)} %bitcast.28), calls=%async_computation | async-start | bytes 262144 | tf_op jit(solution)/shard_map/all_to_all | solution.py:447
  22.5 1.1 copy-start
  23.7 0.9 copy-start.8
  26.1 0.8 copy-start.6
  26.9 37.9 %copy-start.4 = (bf16[64,512]{1,0:T(8,128)(2,1)}, bf16[64,512]{1,0:T(8,128)(2,1)S(1)}, u32[]{:S(2)}) copy-start(bf16[64,512]{1,0:T(8,128)(2,1)S(1)} %get-tuple-element.32.refs_2_.refs_0_) | copy-start | bytes 196612
  26.9 37.9 %copy-start.5 = (bf16[64,512]{1,0:T(8,128)(2,1)}, bf16[64,512]{1,0:T(8,128)(2,1)S(1)}, u32[]{:S(2)}) copy-start(bf16[64,512]{1,0:T(8,128)(2,1)S(1)} %get-tuple-element.33.refs_3_.refs_1_) | copy-start | bytes 196612
  40.9 53.5 %all-to-all-start.1 = ((f32[128,1,1664]{2,1,0:T(1,128)}), f32[128,1,1664]{2,1,0:T(1,128)S(1)}, u32[]{:S(2)}, u32[]{:S(2)}) async-start(f32[128,1,1664]{2,1,0:T(1,128)} %bitcast.27), calls=%async_computation.1 | async-start | bytes 1703936 | tf_op jit(solution)/shard_map/all_to_all | solution.py:447
  61.0 23.5 %copy-start.2 = (f32[1024,128]{1,0:T(8,128)}, f32[1024,128]{1,0:T(8,128)S(1)}, u32[]{:S(2)}) copy-start(f32[1024,128]{1,0:T(8,128)S(1)} %all_gather.6.refs_2_.asks) | copy-start | bytes 1572868
  61.0 3.8 %collective-permute-start = (f32[1024,128]{1,0:T(8,128)S(1)}, f32[1024,128]{1,0:T(8,128)S(1)}, u32[]{:S(2)}, u32[]{:S(2)}) collective-permute-start(f32[1024,128]{1,0:T(8,128)S(1)} %all_gather.6.refs_2_.asks), channel_id=1, source_target_pairs={{0,4},{4,0},{8,12},{12,8},{16,20},{20,16},{24,28},{28,24},{32,36},... | collective-permute-start | bytes 1572872 | tf_op jit(solution)/shard_map/ppermute | solution.py:457
  69.2 16.2 %copy-start.3 = (f32[512,512]{1,0:T(8,128)}, f32[512,512]{1,0:T(8,128)S(1)}, u32[]{:S(2)}) copy-start(f32[512,512]{1,0:T(8,128)S(1)} %get-tuple-element.47.back) | copy-start | bytes 3145732
  69.3 3.8 %collective-permute-start.1 = (f32[512,256]{1,0:T(8,128)S(1)}, f32[512,256]{1,0:T(8,128)S(1)}, u32[]{:S(2)}, u32[]{:S(2)}) collective-permute-start(f32[512,256]{1,0:T(8,128)S(1)} %get-tuple-element.40), channel_id=1, source_target_pairs={{0,4},{4,0},{8,12},{12,8},{16,20},{20,16},{24,28},{28,24},{32,36},... | collective-permute-start | bytes 1572872 | tf_op jit(solution)/shard_map/ppermute | solution.py:457
  73.1 11.4 %collective-permute-start.2 = (f32[128,256]{1,0:T(8,128)S(1)}, f32[128,256]{1,0:T(8,128)S(1)}, u32[]{:S(2)}, u32[]{:S(2)}) collective-permute-start(f32[128,256]{1,0:T(8,128)S(1)} %get-tuple-element.42), channel_id=1, source_target_pairs={{0,1},{1,2},{2,3},{3,0},{4,5},{5,6},{6,7},{7,4},{8,9},{9,10},{10,1... | collective-permute-start | bytes 393224 | tf_op jit(solution)/shard_map/ppermute | solution.py:453
  76.5 9.0 %collective-permute-start.3 = (f32[128,256]{1,0:T(8,128)S(1)}, f32[128,256]{1,0:T(8,128)S(1)}, u32[]{:S(2)}, u32[]{:S(2)}) collective-permute-start(f32[128,256]{1,0:T(8,128)S(1)} %get-tuple-element.43), channel_id=1, source_target_pairs={{0,2},{1,3},{2,0},{3,1},{4,6},{5,7},{6,4},{7,5},{8,10},{9,11},{10,... | collective-permute-start | bytes 393224 | tf_op jit(solution)/shard_map/ppermute | solution.py:453
  81.0 6.9 %collective-permute-start.4 = (f32[128,256]{1,0:T(8,128)S(1)}, f32[128,256]{1,0:T(8,128)S(1)}, u32[]{:S(2)}, u32[]{:S(2)}) collective-permute-start(f32[128,256]{1,0:T(8,128)S(1)} %get-tuple-element.44), channel_id=1, source_target_pairs={{0,3},{1,0},{2,1},{3,2},{4,7},{5,4},{6,5},{7,6},{8,11},{9,8},{10,9... | collective-permute-start | bytes 393224 | tf_op jit(solution)/shard_map/ppermute | solution.py:453
  97.4 68.3 %all-to-all-start.2 = ((f32[512,1,512]{2,1,0:T(1,128)}), f32[512,1,512]{2,1,0:T(1,128)S(1)}, u32[]{:S(2)}, u32[]{:S(2)}) async-start(f32[512,1,512]{2,1,0:T(1,128)} %bitcast.26), calls=%async_computation.2 | async-start | bytes 2097152 | tf_op jit(solution)/shard_map/all_to_all | solution.py:447
  112.8 21.0 %copy-start.7 = (f32[112,512]{1,0:T(8,128)}, f32[112,512]{1,0:T(8,128)S(1)}, u32[]{:S(2)}) copy-start(f32[112,512]{1,0:T(8,128)S(1)} %get-tuple-element.48.part0) | copy-start | bytes 688132
  112.9 13.1 %collective-permute-start.5 = (f32[112,512]{1,0:T(8,128)S(1)}, f32[112,512]{1,0:T(8,128)S(1)}, u32[]{:S(2)}, u32[]{:S(2)}) collective-permute-start(f32[112,512]{1,0:T(8,128)S(1)} %get-tuple-element.49), channel_id=1, source_target_pairs={{0,1},{1,2},{2,3},{3,0},{4,5},{5,6},{6,7},{7,4},{8,9},{9,10},{10,1... | collective-permute-start | bytes 688136 | tf_op jit(solution)/shard_map/ppermute | solution.py:453
  116.3 16.4 %collective-permute-start.6 = (f32[112,512]{1,0:T(8,128)S(1)}, f32[112,512]{1,0:T(8,128)S(1)}, u32[]{:S(2)}, u32[]{:S(2)}) collective-permute-start(f32[112,512]{1,0:T(8,128)S(1)} %get-tuple-element.50), channel_id=1, source_target_pairs={{0,2},{1,3},{2,0},{3,1},{4,6},{5,7},{6,4},{7,5},{8,10},{9,11},{10,... | collective-permute-start | bytes 688136 | tf_op jit(solution)/shard_map/ppermute | solution.py:453
  120.9 13.0 %collective-permute-start.7 = (f32[112,512]{1,0:T(8,128)S(1)}, f32[112,512]{1,0:T(8,128)S(1)}, u32[]{:S(2)}, u32[]{:S(2)}) collective-permute-start(f32[112,512]{1,0:T(8,128)S(1)} %get-tuple-element.51), channel_id=1, source_target_pairs={{0,3},{1,0},{2,1},{3,2},{4,7},{5,4},{6,5},{7,6},{8,11},{9,8},{10,9... | collective-permute-start | bytes 688136 | tf_op jit(solution)/shard_map/ppermute | solution.py:453
  126.0 7.9 %copy-start.10 = (f32[112,512]{1,0:T(8,128)}, f32[112,512]{1,0:T(8,128)S(1)}, u32[]{:S(2)}) copy-start(f32[112,512]{1,0:T(8,128)S(1)} %collective-permute-done.5.part1) | copy-start | bytes 688132
  132.6 1.2 copy-start.11
  133.8 0.7 copy-start.12
  165.7 15.2 %copy-start.1 = (f32[512,400]{0,1:T(8,128)S(1)}, f32[512,400]{0,1:T(8,128)}, u32[]{:S(2)}) copy-start(f32[512,400]{0,1:T(8,128)} %param.9) | copy-start | bytes 2457604
  165.7 15.2 %copy-start.9 = (f32[512]{0:T(512)S(1)}, f32[512]{0:T(512)}, u32[]{:S(2)}) copy-start(f32[512]{0:T(512)} %param.10) | copy-start | bytes 6148

commit v12 on v10

--- a/solution.py
+++ b/solution.py
@@ -243,16 +243,13 @@
     send, rows, negs = refs[2 * PIECES :]
     negs[...] = recv[...]
     tile = recv[pl.ds(1, n, stride=TILES1), :]
-    packed = []
-    for side in range(2):
-        slots = (2 * side, 2 * side + 1)
-        at = jnp.concatenate([column(tile, ASKS + 2 * s) for s in slots], 0)
-        hot = jnp.where(lanes((2 * n, 512)).astype(f32) == at, 1.0, 0.0).astype(bf16)
-        vec = pick(hot, [p[...] for p in table], NN)
-        if side == 0:
-            vec = cmul(vec, rel_vectors(tile, slots, rel))
-        packed += [vec[:n, :], vec[n:, :]]
-        rows[2 * n * side : 2 * n * (side + 1), :] = vec
+    at = jnp.concatenate([column(tile, ASKS + 2 * s) for s in range(4)], 0)
+    hot = jnp.where(lanes((4 * n, 512)).astype(f32) == at, 1.0, 0.0).astype(bf16)
+    vec = pick(hot, [p[...] for p in table], NN)
+    query = cmul(vec[: 2 * n, :], rel_vectors(tile, (0, 1), rel))
+    rows[0 : 2 * n, :] = query
+    rows[2 * n :, :] = vec[2 * n :, :]
+    packed = [query[:n, :], query[n:, :], vec[2 * n : 3 * n, :], vec[3 * n :, :]]
     pack(send, packed)
 
 

time: 185 us -> 186 us (level)
  no operation moved by 1% of the time
where the time goes in v12:
time: 186 us; the launch traced here: 182 us
  starting transfers between devices  63.7 us (34%)
  waiting for transfers between devices  63.3 us (34%)
  blocking collectives  27.3 us (15%)
  Pallas kernels  23.5 us (13%)
  local copies, waits for them, and re-layouts  3.58 us (2%)
    all_to_all x3, waiting for transfers between devices, exchange(): x = lax.all_to_all(x, axis, split_axis=0, concat_axis=0, tiled=True)  46.4 us
    all_to_all x3, starting transfers between devices, exchange(): x = lax.all_to_all(x, axis, split_axis=0, concat_axis=0, tiled=True)  38.5 us
    pallas_call x12, Pallas kernels, call(): pl.pallas_call(kernel, out_shape=[(pltpu.VMEM if near else pltpu.HBM)(sha...  23.5 us
    ppermute x6, starting transfers between devices, shift(): return lax.ppermute(x, 'rep', [(i, (i + by) % n) for i in range(n)])  21.2 us
    all_gather x1, blocking collectives, on_device(): grads = lax.all_gather(grads, 'rep', axis=0, tiled=True)  14.2 us
    ppermute x6, waiting for transfers between devices, shift(): return lax.ppermute(x, 'rep', [(i, (i + by) % n) for i in range(n)])  13.3 us
    all_gather x1, blocking collectives, on_device(): mine = lax.all_gather(own_negs, 'rep', axis=0, tiled=True)  13.1 us
    ppermute x2, starting transfers between devices, swap_cores(): lax.ppermute(x, 'ent', [(i, i ^ 1) for i in range(lax.axis_size('ent'))])  3.96 us
  transfers between devices with their start and end apart: 11, of which 9 were waited for; matrix products, arithmetic and copies ran while one was open for 0% of the time, Pallas kernels for 7%

profile of v12, /device:TPU:24, one launch (start us, length us, event | category | flops | bytes accessed | tf_op | source)
XLA Modules:
  0.0 182.2 jit_solution(7285205704387711284)
XLA Ops:
  0.6 2.6 %ask.1 = (f32[256,128]{1,0:T(8,128)}, f32[128,128]{1,0:T(8,128)}, f32[128,128]{1,0:T(8,128)}) custom-call(s32[1]{0:T(128)} %bitcast.rep, s32[4]{0:T(128)} %neg_rows.3, s32[1,128]{1,0:T(1,128)} %bitcast.29, s32[1,128]{1,0:T(1,128)} %bitcast.30, s32[1,128]{1,0:T(1,128)} %bitcast.31, s32[1,128]{1,0:T(1,128)} %bitcast.32, s32[1,128]{1,0:T(1,128)} %bitcast.33, ...), custom_call_target="tpu_custom_call" | custom-call | tf_op jit(solution)/shard_map/ask/pallas_call | solution.py:415
  3.2 19.3 %all-to-all-start = ((f32[128,1,256]{2,1,0:T(1,128)}), f32[128,1,256]{2,1,0:T(1,128)S(1)}, u32[]{:S(2)}, u32[]{:S(2)}) async-start(f32[128,1,256]{2,1,0:T(1,128)} %bitcast.28), calls=%async_computation | async-start | bytes 262144 | tf_op jit(solution)/shard_map/all_to_all | solution.py:442
  22.5 1.1 copy-done
  24.6 1.5 ahead.1
  26.9 11.8 %all-to-all-done = f32[128,1,256]{2,1,0:T(1,128)S(1)} async-done(((f32[128,1,256]{2,1,0:T(1,128)}), f32[128,1,256]{2,1,0:T(1,128)S(1)}, u32[]{:S(2)}, u32[]{:S(2)}) %all-to-all-start) | async-done | bytes 131104 | tf_op jit(solution)/shard_map/all_to_all | solution.py:442
  38.7 2.4 %fetch.1 = (f32[1664,128]{1,0:T(8,128)}, f32[512,512]{1,0:T(8,128)S(1)}, f32[256,128]{1,0:T(8,128)S(1)}) custom-call(f32[256,128]{1,0:T(8,128)S(1)} %bitcast.22, bf16[512,512]{1,0:T(8,128)(2,1)S(1)} %get-tuple-element.30.refs_0_, bf16[512,512]{1,0:T(8,128)(2,1)S(1)} %get-tuple-element.31.refs_1_, bf16[64,512]{1,0:T(8,128)(2,1)S(1)} %get-tuple-element.32.refs_2_.refs_0_, ...), custom_call_target="tpu_custom_call" | custom-call | tf_op jit(solution)/shard_map/fetch/pallas_call | solution.py:415
  41.1 7.0 %all-to-all-start.1 = ((f32[128,1,1664]{2,1,0:T(1,128)}), f32[128,1,1664]{2,1,0:T(1,128)S(1)}, u32[]{:S(2)}, u32[]{:S(2)}) async-start(f32[128,1,1664]{2,1,0:T(1,128)} %bitcast.27), calls=%async_computation.1 | async-start | bytes 1703936 | tf_op jit(solution)/shard_map/all_to_all | solution.py:442
  48.1 13.1 %all_gather.6.refs_2_.asks = f32[1024,128]{1,0:T(8,128)S(1)} all-gather(f32[256,128]{1,0:T(8,128)S(1)} %get-tuple-element.38), channel_id=1, replica_groups=mesh['ent'=128,'rep'=4] {'rep'}, dimensions={0}, use_global_device_ids=true | all-gather | bytes 655360 | tf_op jit(solution)/shard_map/all_gather | solution.py:512
  61.2 1.9 %collective-permute-start = (f32[1024,128]{1,0:T(8,128)S(1)}, f32[1024,128]{1,0:T(8,128)S(1)}, u32[]{:S(2)}, u32[]{:S(2)}) collective-permute-start(f32[1024,128]{1,0:T(8,128)S(1)} %all_gather.6.refs_2_.asks), channel_id=1, source_target_pairs={{0,4},{4,0},{8,12},{12,8},{16,20},{20,16},{24,28},{28,24},{32,36},... | collective-permute-start | bytes 1572872 | tf_op jit(solution)/shard_map/ppermute | solution.py:452
  63.2 1.9 %collective-permute-done.refs_3_ = f32[1024,128]{1,0:T(8,128)S(1)} collective-permute-done((f32[1024,128]{1,0:T(8,128)S(1)}, f32[1024,128]{1,0:T(8,128)S(1)}, u32[]{:S(2)}, u32[]{:S(2)}) %collective-permute-start) | collective-permute-done | bytes 524320 | tf_op jit(solution)/shard_map/ppermute | solution.py:452
  65.0 4.4 %negatives.1 = (f32[512,512]{1,0:T(8,128)S(1)}, f32[512,256]{1,0:T(8,128)S(1)}, f32[512,256]{1,0:T(8,128)S(1)}) custom-call(s32[1]{0:T(128)} %bitcast.11.odd, f32[256,128]{1,0:T(8,128)S(1)} %bitcast.23, f32[512,512]{1,0:T(8,128)S(1)} %get-tuple-element.37.rows, bf16[64,512]{1,0:T(8,128)(2,1)} %copy-done.4, bf16[64,512]{1,0:T(8,128)(2,1)} %copy-done.5, ...), custom_call_target="tpu_custom_call" | custom-call | tf_op jit(solution)/shard_map/negatives/pallas_call | solution.py:415
  69.5 2.0 %collective-permute-start.1 = (f32[512,256]{1,0:T(8,128)S(1)}, f32[512,256]{1,0:T(8,128)S(1)}, u32[]{:S(2)}, u32[]{:S(2)}) collective-permute-start(f32[512,256]{1,0:T(8,128)S(1)} %get-tuple-element.40), channel_id=1, source_target_pairs={{0,4},{4,0},{8,12},{12,8},{16,20},{20,16},{24,28},{28,24},{32,36},... | collective-permute-start | bytes 1572872 | tf_op jit(solution)/shard_map/ppermute | solution.py:452
  71.6 1.7 collective-permute-done.1.got
  73.4 3.3 %collective-permute-start.2 = (f32[128,256]{1,0:T(8,128)S(1)}, f32[128,256]{1,0:T(8,128)S(1)}, u32[]{:S(2)}, u32[]{:S(2)}) collective-permute-start(f32[128,256]{1,0:T(8,128)S(1)} %get-tuple-element.42), channel_id=1, source_target_pairs={{0,1},{1,2},{2,3},{3,0},{4,5},{5,6},{6,7},{7,4},{8,9},{9,10},{10,1... | collective-permute-start | bytes 393224 | tf_op jit(solution)/shard_map/ppermute | solution.py:448
  76.7 4.6 %collective-permute-start.3 = (f32[128,256]{1,0:T(8,128)S(1)}, f32[128,256]{1,0:T(8,128)S(1)}, u32[]{:S(2)}, u32[]{:S(2)}) collective-permute-start(f32[128,256]{1,0:T(8,128)S(1)} %get-tuple-element.43), channel_id=1, source_target_pairs={{0,2},{1,3},{2,0},{3,1},{4,6},{5,7},{6,4},{7,5},{8,10},{9,11},{10,... | collective-permute-start | bytes 393224 | tf_op jit(solution)/shard_map/ppermute | solution.py:448
  81.3 1.9 %collective-permute-start.4 = (f32[128,256]{1,0:T(8,128)S(1)}, f32[128,256]{1,0:T(8,128)S(1)}, u32[]{:S(2)}, u32[]{:S(2)}) collective-permute-start(f32[128,256]{1,0:T(8,128)S(1)} %get-tuple-element.44), channel_id=1, source_target_pairs={{0,3},{1,0},{2,1},{3,2},{4,7},{5,4},{6,5},{7,6},{8,11},{9,8},{10,9... | collective-permute-start | bytes 393224 | tf_op jit(solution)/shard_map/ppermute | solution.py:448
  83.2 1.5 pair.1.aids
  85.7 2.5 %collective-permute-done.4.sum3 = f32[128,256]{1,0:T(8,128)S(1)} collective-permute-done((f32[128,256]{1,0:T(8,128)S(1)}, f32[128,256]{1,0:T(8,128)S(1)}, u32[]{:S(2)}, u32[]{:S(2)}) %collective-permute-start.4) | collective-permute-done | bytes 131104 | tf_op jit(solution)/shard_map/ppermute | solution.py:448
  88.2 6.5 %all-to-all-done.1 = f32[128,1,1664]{2,1,0:T(1,128)S(1)} async-done(((f32[128,1,1664]{2,1,0:T(1,128)}), f32[128,1,1664]{2,1,0:T(1,128)S(1)}, u32[]{:S(2)}, u32[]{:S(2)}) %all-to-all-start.1) | async-done | bytes 852000 | tf_op jit(solution)/shard_map/all_to_all | solution.py:442
  94.6 3.0 %edge.1 = (f32[2048,128]{1,0:T(8,128)}, f32[8,128]{1,0:T(8,128)}) custom-call(f32[1664,128]{1,0:T(8,128)S(1)} %bitcast.21, f32[640,512]{1,0:T(8,128)S(1)} %pair.1.aids, f32[128,256]{1,0:T(8,128)S(1)} %collective-permute-done.2.sum1, f32[128,256]{1,0:T(8,128)S(1)} %collective-permute-done.3.sum2, f32[128,256]{1,0:T(8,128)S(1)} %collective-permute-done.4.sum3), custom_call_target="tpu_custom_call" | custom-call | tf_op jit(solution)/shard_map/edge/pallas_call | solution.py:415
  97.7 12.2 %all-to-all-start.2 = ((f32[512,1,512]{2,1,0:T(1,128)}), f32[512,1,512]{2,1,0:T(1,128)S(1)}, u32[]{:S(2)}, u32[]{:S(2)}) async-start(f32[512,1,512]{2,1,0:T(1,128)} %bitcast.26), calls=%async_computation.2 | async-start | bytes 2097152 | tf_op jit(solution)/shard_map/all_to_all | solution.py:442
  109.9 2.9 %local.1 = (f32[512,128]{1,0:T(8,128)S(1)}, f32[512,128]{1,0:T(8,128)S(1)}, f32[512,128]{1,0:T(8,128)S(1)}, f32[512,128]{1,0:T(8,128)S(1)}) custom-call(s32[1]{0:T(128)} %bitcast.rep, f32[8,128]{1,0:T(8,128)} %get-tuple-element.46.token, f32[256,128]{1,0:T(8,128)S(1)} %bitcast.24, f32[512,512]{1,0:T(8,128)} %copy-done.3, bf16[64,512]{1,0:T(8,128)(2,1)} %copy-done.4, ...), custom_call_target="tpu_custom_call" | custom-call | tf_op jit(solution)/shard_map/local/pallas_call | solution.py:415
  112.8 3.4 %collective-permute-start.5 = (f32[512,128]{1,0:T(8,128)S(1)}, f32[512,128]{1,0:T(8,128)S(1)}, u32[]{:S(2)}, u32[]{:S(2)}) collective-permute-start(f32[512,128]{1,0:T(8,128)S(1)} %get-tuple-element.49), channel_id=1, source_target_pairs={{0,1},{1,2},{2,3},{3,0},{4,5},{5,6},{6,7},{7,4},{8,9},{9,10},{10,1... | collective-permute-start | bytes 786440 | tf_op jit(solution)/shard_map/ppermute | solution.py:448
  116.2 4.6 %collective-permute-start.6 = (f32[512,128]{1,0:T(8,128)S(1)}, f32[512,128]{1,0:T(8,128)S(1)}, u32[]{:S(2)}, u32[]{:S(2)}) collective-permute-start(f32[512,128]{1,0:T(8,128)S(1)} %get-tuple-element.50), channel_id=1, source_target_pairs={{0,2},{1,3},{2,0},{3,1},{4,6},{5,7},{6,4},{7,5},{8,10},{9,11},{10,... | collective-permute-start | bytes 786440 | tf_op jit(solution)/shard_map/ppermute | solution.py:448
  120.9 3.4 %collective-permute-start.7 = (f32[512,128]{1,0:T(8,128)S(1)}, f32[512,128]{1,0:T(8,128)S(1)}, u32[]{:S(2)}, u32[]{:S(2)}) collective-permute-start(f32[512,128]{1,0:T(8,128)S(1)} %get-tuple-element.51), channel_id=1, source_target_pairs={{0,3},{1,0},{2,1},{3,2},{4,7},{5,4},{6,5},{7,6},{8,11},{9,8},{10,9... | collective-permute-start | bytes 786440 | tf_op jit(solution)/shard_map/ppermute | solution.py:448
  124.2 1.7 place.1.hot
  126.0 8.3 %collective-permute-done.6.part2 = f32[512,128]{1,0:T(8,128)S(1)} collective-permute-done((f32[512,128]{1,0:T(8,128)S(1)}, f32[512,128]{1,0:T(8,128)S(1)}, u32[]{:S(2)}, u32[]{:S(2)}) %collective-permute-start.6) | collective-permute-done | bytes 262176 | tf_op jit(solution)/shard_map/ppermute | solution.py:448
  134.3 1.5 collective-permute-done.7.part3
  136.6 1.2 gather_local.1.local
  137.8 28.1 %all-to-all-done.2 = f32[512,1,512]{2,1,0:T(1,128)S(1)} async-done(((f32[512,1,512]{2,1,0:T(1,128)}), f32[512,1,512]{2,1,0:T(1,128)S(1)}, u32[]{:S(2)}, u32[]{:S(2)}) %all-to-all-start.2) | async-done | bytes 1048608 | tf_op jit(solution)/shard_map/all_to_all | solution.py:442
  167.0 14.2 %all_gather.7.grads = f32[448,512]{1,0:T(8,128)S(1)} all-gather(f32[112,512]{1,0:T(8,128)S(1)} %scatter.1), channel_id=1, replica_groups=mesh['ent'=128,'rep'=4] {'rep'}, dimensions={0}, use_global_device_ids=true | all-gather | bytes 1146880 | tf_op jit(solution)/shard_map/all_gather | solution.py:566
  181.2 1.1 finish.1
  (30 shorter events, 4.5 us)
Async XLA Ops:
  3.2 35.5 %all-to-all-start = ((f32[128,1,256]{2,1,0:T(1,128)}), f32[128,1,256]{2,1,0:T(1,128)S(1)}, u32[]{:S(2)}, u32[]{:S(2)}) async-start(f32[128,1,256]{2,1,0:T(1,128)} %bitcast.28), calls=%async_computation | async-start | bytes 262144 | tf_op jit(solution)/shard_map/all_to_all | solution.py:442
  22.5 1.1 copy-start
  23.7 0.9 copy-start.8
  26.1 0.8 copy-start.6
  26.9 38.1 %copy-start.4 = (bf16[64,512]{1,0:T(8,128)(2,1)}, bf16[64,512]{1,0:T(8,128)(2,1)S(1)}, u32[]{:S(2)}) copy-start(bf16[64,512]{1,0:T(8,128)(2,1)S(1)} %get-tuple-element.32.refs_2_.refs_0_) | copy-start | bytes 196612
  26.9 38.1 %copy-start.5 = (bf16[64,512]{1,0:T(8,128)(2,1)}, bf16[64,512]{1,0:T(8,128)(2,1)S(1)}, u32[]{:S(2)}) copy-start(bf16[64,512]{1,0:T(8,128)(2,1)S(1)} %get-tuple-element.33.refs_3_.refs_1_) | copy-start | bytes 196612
  41.1 53.5 %all-to-all-start.1 = ((f32[128,1,1664]{2,1,0:T(1,128)}), f32[128,1,1664]{2,1,0:T(1,128)S(1)}, u32[]{:S(2)}, u32[]{:S(2)}) async-start(f32[128,1,1664]{2,1,0:T(1,128)} %bitcast.27), calls=%async_computation.1 | async-start | bytes 1703936 | tf_op jit(solution)/shard_map/all_to_all | solution.py:442
  61.2 23.5 %copy-start.2 = (f32[1024,128]{1,0:T(8,128)}, f32[1024,128]{1,0:T(8,128)S(1)}, u32[]{:S(2)}) copy-start(f32[1024,128]{1,0:T(8,128)S(1)} %all_gather.6.refs_2_.asks) | copy-start | bytes 1572868
  61.2 3.8 %collective-permute-start = (f32[1024,128]{1,0:T(8,128)S(1)}, f32[1024,128]{1,0:T(8,128)S(1)}, u32[]{:S(2)}, u32[]{:S(2)}) collective-permute-start(f32[1024,128]{1,0:T(8,128)S(1)} %all_gather.6.refs_2_.asks), channel_id=1, source_target_pairs={{0,4},{4,0},{8,12},{12,8},{16,20},{20,16},{24,28},{28,24},{32,36},... | collective-permute-start | bytes 1572872 | tf_op jit(solution)/shard_map/ppermute | solution.py:452
  69.5 16.2 %copy-start.3 = (f32[512,512]{1,0:T(8,128)}, f32[512,512]{1,0:T(8,128)S(1)}, u32[]{:S(2)}) copy-start(f32[512,512]{1,0:T(8,128)S(1)} %get-tuple-element.47.back) | copy-start | bytes 3145732
  69.5 3.8 %collective-permute-start.1 = (f32[512,256]{1,0:T(8,128)S(1)}, f32[512,256]{1,0:T(8,128)S(1)}, u32[]{:S(2)}, u32[]{:S(2)}) collective-permute-start(f32[512,256]{1,0:T(8,128)S(1)} %get-tuple-element.40), channel_id=1, source_target_pairs={{0,4},{4,0},{8,12},{12,8},{16,20},{20,16},{24,28},{28,24},{32,36},... | collective-permute-start | bytes 1572872 | tf_op jit(solution)/shard_map/ppermute | solution.py:452
  73.4 11.4 %collective-permute-start.2 = (f32[128,256]{1,0:T(8,128)S(1)}, f32[128,256]{1,0:T(8,128)S(1)}, u32[]{:S(2)}, u32[]{:S(2)}) collective-permute-start(f32[128,256]{1,0:T(8,128)S(1)} %get-tuple-element.42), channel_id=1, source_target_pairs={{0,1},{1,2},{2,3},{3,0},{4,5},{5,6},{6,7},{7,4},{8,9},{9,10},{10,1... | collective-permute-start | bytes 393224 | tf_op jit(solution)/shard_map/ppermute | solution.py:448
  76.7 9.0 %collective-permute-start.3 = (f32[128,256]{1,0:T(8,128)S(1)}, f32[128,256]{1,0:T(8,128)S(1)}, u32[]{:S(2)}, u32[]{:S(2)}) collective-permute-start(f32[128,256]{1,0:T(8,128)S(1)} %get-tuple-element.43), channel_id=1, source_target_pairs={{0,2},{1,3},{2,0},{3,1},{4,6},{5,7},{6,4},{7,5},{8,10},{9,11},{10,... | collective-permute-start | bytes 393224 | tf_op jit(solution)/shard_map/ppermute | solution.py:448
  81.3 6.9 %collective-permute-start.4 = (f32[128,256]{1,0:T(8,128)S(1)}, f32[128,256]{1,0:T(8,128)S(1)}, u32[]{:S(2)}, u32[]{:S(2)}) collective-permute-start(f32[128,256]{1,0:T(8,128)S(1)} %get-tuple-element.44), channel_id=1, source_target_pairs={{0,3},{1,0},{2,1},{3,2},{4,7},{5,4},{6,5},{7,6},{8,11},{9,8},{10,9... | collective-permute-start | bytes 393224 | tf_op jit(solution)/shard_map/ppermute | solution.py:448
  97.7 68.3 %all-to-all-start.2 = ((f32[512,1,512]{2,1,0:T(1,128)}), f32[512,1,512]{2,1,0:T(1,128)S(1)}, u32[]{:S(2)}, u32[]{:S(2)}) async-start(f32[512,1,512]{2,1,0:T(1,128)} %bitcast.26), calls=%async_computation.2 | async-start | bytes 2097152 | tf_op jit(solution)/shard_map/all_to_all | solution.py:442
  112.8 23.0 %copy-start.7 = (f32[512,128]{1,0:T(8,128)}, f32[512,128]{1,0:T(8,128)S(1)}, u32[]{:S(2)}) copy-start(f32[512,128]{1,0:T(8,128)S(1)} %get-tuple-element.48.part0) | copy-start | bytes 786436
  112.8 13.2 %collective-permute-start.5 = (f32[512,128]{1,0:T(8,128)S(1)}, f32[512,128]{1,0:T(8,128)S(1)}, u32[]{:S(2)}, u32[]{:S(2)}) collective-permute-start(f32[512,128]{1,0:T(8,128)S(1)} %get-tuple-element.49), channel_id=1, source_target_pairs={{0,1},{1,2},{2,3},{3,0},{4,5},{5,6},{6,7},{7,4},{8,9},{9,10},{10,1... | collective-permute-start | bytes 786440 | tf_op jit(solution)/shard_map/ppermute | solution.py:448
  116.2 18.1 %collective-permute-start.6 = (f32[512,128]{1,0:T(8,128)S(1)}, f32[512,128]{1,0:T(8,128)S(1)}, u32[]{:S(2)}, u32[]{:S(2)}) collective-permute-start(f32[512,128]{1,0:T(8,128)S(1)} %get-tuple-element.50), channel_id=1, source_target_pairs={{0,2},{1,3},{2,0},{3,1},{4,6},{5,7},{6,4},{7,5},{8,10},{9,11},{10,... | collective-permute-start | bytes 786440 | tf_op jit(solution)/shard_map/ppermute | solution.py:448
  120.9 15.0 %collective-permute-start.7 = (f32[512,128]{1,0:T(8,128)S(1)}, f32[512,128]{1,0:T(8,128)S(1)}, u32[]{:S(2)}, u32[]{:S(2)}) collective-permute-start(f32[512,128]{1,0:T(8,128)S(1)} %get-tuple-element.51), channel_id=1, source_target_pairs={{0,3},{1,0},{2,1},{3,2},{4,7},{5,4},{6,5},{7,6},{8,11},{9,8},{10,9... | collective-permute-start | bytes 786440 | tf_op jit(solution)/shard_map/ppermute | solution.py:448
  126.0 9.9 %copy-start.10 = (f32[512,128]{1,0:T(8,128)}, f32[512,128]{1,0:T(8,128)S(1)}, u32[]{:S(2)}) copy-start(f32[512,128]{1,0:T(8,128)S(1)} %collective-permute-done.5.part1) | copy-start | bytes 786436
  134.3 1.5 copy-start.11
  135.8 0.7 copy-start.12
  165.9 15.2 %copy-start.1 = (f32[512,400]{0,1:T(8,128)S(1)}, f32[512,400]{0,1:T(8,128)}, u32[]{:S(2)}) copy-start(f32[512,400]{0,1:T(8,128)} %param.9) | copy-start | bytes 2457604
  165.9 15.2 %copy-start.9 = (f32[512]{0:T(512)S(1)}, f32[512]{0:T(512)}, u32[]{:S(2)}) copy-start(f32[512]{0:T(512)} %param.10) | copy-start | bytes 6148
